TPU v7x, 128 devices: a whole 4x4x4 slice. The times are simulated.
128 devices in a mesh: batch: 4 (over z_hi, core), centers: 32 (over x, y, z_lo).
Axes of the slice: x: 4, y: 4, z: 4 (z_hi: 2, z_lo: 2; z = z_hi * 2 + z_lo), core: 2. Of those that a mesh axis runs over, the one named last changes fastest.
Arguments:
- pool_features: float32 [131072, 128], P(('batch', 'centers')), may hold values from -14 to 14
- pool_targets: float32 [131072, 64], P(('batch', 'centers')), may hold values from -6 to 6
- batch_index: int32 [8192], P(('batch', 'centers')), may hold values from 0 to 1023
- centers: float32 [16384, 128], P('centers'), may hold values from -14 to 14
- weights: float32 [16384, 64], P('centers'), as said below
- eig_vectors: float32 [16384, 1024], P(('batch', 'centers')), may hold values from -0.046875 to 0.046875
- eig_scale: float32 [1024], replicated, may hold values from 0.5 to 4
- nys_owner: int32 [16384, 1], P(('batch', 'centers')), may hold values from 0 to 31; in each aligned block of 128 rows (0 to 127, 128 to 255, ...) at most 8 rows name the same one
- nys_offset: int32 [16384], P(('batch', 'centers')), may hold values from 0 to 511
Outputs:
- residual_out: float32 [8192, 64], P(('batch', 'centers'))
- update: float32 [16384, 64], P('centers')
Inputs may be any that keep to these rules, and one draw needn't show every extreme that they name: `nys_owner`: among the 128 rows of one device no owner is named more than 8 times; on some devices one owner is named exactly 8 times. `weights`: every column sums to zero.
All inputs are finite; a program needn't handle non-finite values.
Results may differ from a plain program's by a relative error of at most 0.0003.
Values sent between devices are 32-bit elements; how exact they have to be, the bound alone decides.
No kernel may reach another device: no remote copies, remote signals or barrier semaphores. Data moves between devices by JAX's collectives and lax.ppermute only.
A program may use at most 64 MiB of HBM per device.

v0:
```python
import math

import jax
import jax.numpy as jnp
from jax import lax
from jax.sharding import PartitionSpec as P

DEPTH = 3


epsilon = 1e-06
highest = lax.Precision.HIGHEST


def kernel_rows(row_block, center_block, center_norm):
    inner_prod = (
        lax.dot_general(
            row_block,
            center_block,
            (((1,), (1,)), ((), ())),
            precision=highest,
            preferred_element_type=jnp.float32,
        )
        / row_block.shape[1]
    )
    row_norm = jnp.mean(row_block * row_block, axis=1) + epsilon
    norm_scale = jnp.sqrt(row_norm[:, None] * center_norm[None, :])
    sigma_now = inner_prod
    tangent = inner_prod
    for depth_step in range(DEPTH):
        cosine = sigma_now / norm_scale
        arc_angle = jnp.arccos(cosine)
        remain = (math.pi - arc_angle) / math.pi
        sigma_now = (
            norm_scale
            * (jnp.sqrt(1.0 - cosine * cosine) + (math.pi - arc_angle) * cosine)
            / math.pi
        )
        tangent = sigma_now + tangent * remain
    return tangent


def per_device(
    pool_features,
    pool_targets,
    batch_index,
    centers,
    weights,
    eig_vectors,
    eig_scale,
    nys_owner,
    nys_offset,
):
    local_rows = pool_features[batch_index]
    local_targets = pool_targets[batch_index]
    row_count = local_rows.shape[0]
    group_size = lax.axis_size("centers")
    rows_total = row_count * group_size * lax.axis_size("batch")
    center_count = centers.shape[0]
    outputs = weights.shape[1]
    center_norm = jnp.mean(centers * centers, axis=1) + epsilon
    kernel = kernel_rows(
        lax.all_gather(local_rows, "centers", axis=0, tiled=True), centers, center_norm
    )
    partial_pred = jnp.dot(kernel, weights, precision=highest, preferred_element_type=jnp.float32)
    all_targets = lax.all_gather(local_targets, "centers", axis=0, tiled=True)
    prediction = lax.psum(partial_pred, "centers")
    residual = prediction - all_targets
    own_residual = lax.dynamic_slice_in_dim(
        residual, lax.axis_index("centers") * row_count, row_count, 0
    )
    grads_part = lax.dot_general(
        kernel,
        residual,
        (((0,), (0,)), ((), ())),
        precision=highest,
        preferred_element_type=jnp.float32,
    ) / math.sqrt(rows_total)
    grads = lax.psum(grads_part, "batch")
    owner = nys_owner[:, 0]
    slots = max(2, 2 * owner.shape[0] // group_size)
    owner_hot = (owner[:, None] == jnp.arange(group_size, dtype=jnp.int32)[None, :]).astype(
        jnp.int32
    )
    slot_rank = jnp.sum((jnp.cumsum(owner_hot, axis=0) - owner_hot) * owner_hot, axis=1)
    requests = jnp.zeros((group_size, slots), jnp.int32).at[owner, slot_rank].set(nys_offset)
    received = lax.all_to_all(requests, "centers", split_axis=0, concat_axis=0, tiled=True)
    found = grads[received]
    returned = lax.all_to_all(found, "centers", split_axis=0, concat_axis=0, tiled=True)
    picked_grads = returned[owner, slot_rank]
    coeff_part = lax.dot_general(
        eig_vectors,
        picked_grads,
        (((0,), (0,)), ((), ())),
        precision=highest,
        preferred_element_type=jnp.float32,
    )
    coeff = lax.psum(coeff_part, ("batch", "centers"))
    corr_rows = jnp.dot(
        eig_vectors,
        eig_scale[:, None] * coeff,
        precision=highest,
        preferred_element_type=jnp.float32,
    )
    spread = (
        jnp.zeros((group_size * center_count, outputs), jnp.float32)
        .at[owner * center_count + nys_offset]
        .add(corr_rows)
    )
    corr_part = lax.psum_scatter(spread, "centers", scatter_dimension=0, tiled=True)
    correction = lax.psum(corr_part, "batch")
    return (own_residual, correction - grads)


def solution(mesh):
    placed = (
        P(("batch", "centers"), None),
        P(("batch", "centers"), None),
        P(("batch", "centers")),
        P("centers", None),
        P("centers", None),
        P(("batch", "centers"), None),
        P(),
        P(("batch", "centers"), None),
        P(("batch", "centers")),
    )
    return jax.shard_map(
        per_device,
        mesh=mesh,
        in_specs=placed,
        out_specs=(P(("batch", "centers"), None), P("centers", None)),
        check_vma=False,
    )
```

profile of v0, /device:TPU:1, one launch (start us, length us, event | category | flops | bytes accessed | tf_op | source)
XLA Modules:
  0.0 951.3 jit_solution(6418293287864881805)
XLA Ops:
  7.2 0.7 compare_select_fusion.4
  7.9 2.2 gather_fusion
  10.2 0.7 fusion.4
  11.2 1.1 multiply_reduce_fusion.1
  12.3 130.2 %all-gather.4.cloned.1.call-done = f32[2048,128]{1,0:T(8,128)} async-done(((f32[64,128]{1,0:T(8,128)}), f32[2048,128]{1,0:T(8,128)}) %all-gather.4.cloned.1.call-update) | async-done | bytes 1048592 | tf_op jit(solution)/shard_map/all_gather | solution.py:63
  142.5 1.6 multiply_reduce_fusion
  144.1 37.0 %multiply_add_fusion = f32[2048,512]{1,0:T(8,128)S(1)} fusion(f32[2048,128]{1,0:T(8,128)} %all-gather.4.cloned.1.call-done, f32[512,128]{1,0:T(8,128)} %param.12, f32[512]{0:T(512)S(1)} %multiply_add_fusion.2, f32[2048]{0:T(1024)S(1)} %multiply_add_fusion.1), kind=kOutput, calls=%fused_computation.8 | convolution fusion | flops 1656750080 | bytes 5515264 | tf_op jit(solution)/shard_map/dot_general | solution.py:17
  181.1 1.9 copy-done.1
  183.0 5.0 fusion.8
  188.2 6.4 scatter_fusion
  194.7 0.7 copy.26
  195.4 6.9 all-to-all-start
  202.6 0.6 gather_fusion.1
  203.2 73.5 %all-gather.1 = f32[2048,64]{1,0:T(8,128)S(1)} all-gather(f32[64,64]{1,0:T(8,128)S(1)} %gather_fusion.1), channel_id=3, replica_groups=mesh['batch'=4,'centers'=32] {'centers'}, dimensions={0}, use_global_device_ids=true | all-gather | bytes 540672 | tf_op jit(solution)/shard_map/all_gather | solution.py:66
  277.0 218.7 %all-reduce.5.cloned.1.call-done = f32[2048,64]{0,1:T(8,128)} async-done(((f32[2048,64]{0,1:T(8,128)}), f32[2048,64]{0,1:T(8,128)}) %all-reduce.5.cloned.1.call-update) | async-done | bytes 524304 | tf_op jit(solution)/shard_map/psum | solution.py:67
  495.7 1.1 sub.36
  496.9 5.6 convolution_multiply_fusion
  502.7 62.1 %all-reduce.7.cloned.1.call-done = f32[512,64]{0,1:T(8,128)} async-done(((f32[512,64]{0,1:T(8,128)}), f32[512,64]{0,1:T(8,128)}) %all-reduce.7.cloned.1.call-update) | async-done | bytes 131088 | tf_op jit(solution)/shard_map/psum | solution.py:79
  564.8 1.0 copy.27
  565.8 0.7 gather_fusion.2
  566.7 13.8 %all_to_all.17 = f32[32,1,512]{2,1,0:T(1,128)S(1)} all-to-all(f32[32,1,512]{2,1,0:T(1,128)S(1)} %reshape.108), channel_id=1, replica_groups=mesh['batch'=4,'centers'=32] {'centers'}, dimensions={0} | all-to-all | bytes 131072 | tf_op jit(solution)/shard_map/all_to_all | solution.py:89
  581.0 0.8 reduce
  581.9 1.0 gather_fusion.3
  582.9 1.1 convolution_bitcast_fusion
  584.1 139.3 %all-reduce.9.cloned.1.call-done = f32[1024,64]{0,1:T(8,128)} async-done(((f32[1024,64]{0,1:T(8,128)}), f32[1024,64]{0,1:T(8,128)}) %all-reduce.9.cloned.1.call-update) | async-done | bytes 262160 | tf_op jit(solution)/shard_map/psum | solution.py:98
  723.4 1.6 convolution_bitcast_fusion.1
  725.1 4.7 scatter_custom_fusion.1
  729.9 6.8 copy.29
  736.8 143.3 %reduce-scatter.2.cloned.1.call-done = f32[512,64]{0,1:T(8,128)} async-done(((f32[16384,64]{0,1:T(8,128)}), f32[512,64]{0,1:T(8,128)}) %reduce-scatter.2.cloned.1.call-update) | async-done | bytes 131088 | tf_op jit(solution)/shard_map/reduce_scatter | solution.py:110
  880.1 0.7 copy.30
  880.8 62.0 %all-reduce.11.cloned.1.call-done = f32[512,64]{0,1:T(8,128)} async-done(((f32[512,64]{0,1:T(8,128)}), f32[512,64]{0,1:T(8,128)}) %all-reduce.11.cloned.1.call-update) | async-done | bytes 131088 | tf_op jit(solution)/shard_map/psum | solution.py:111
  942.9 1.6 sub.38
  (46 shorter events, 2.3 us)
Async XLA Ops:
  7.2 575.7 %copy-start = (f32[128,1024]{1,0:T(8,128)S(1)}, f32[128,1024]{1,0:T(8,128)}, u32[]{:S(2)}) copy-start(f32[128,1024]{1,0:T(8,128)} %param.14) | copy-start | bytes 1572868
  7.2 135.3 %all-gather.4.cloned.1.call-start = ((), (), s32[]{:S(2)}) async-start(), calls=%async_computation.8 | async-start | bytes 1081344 | tf_op jit(solution)/shard_map/all_gather | solution.py:63
  10.2 485.5 %all-reduce.5.cloned.1.call-start = ((), (), s32[]{:S(2)}) async-start(), calls=%async_computation.3 | async-start | bytes 1048576 | tf_op jit(solution)/shard_map/psum | solution.py:67
  144.1 38.9 %copy-start.4 = (f32[512,64]{0,1:T(8,128)S(1)}, f32[512,64]{0,1:T(8,128)}, u32[]{:S(2)}) copy-start(f32[512,64]{0,1:T(8,128)} %param.13) | copy-start | bytes 393220
  181.0 1.9 copy-start.1
  183.0 5.0 copy-start.5
  183.0 5.3 copy-start.7
  183.0 19.4 %copy-start.3 = (f32[1024,64]{0,1:T(8,128)S(1)}, f32[1024,64]{0,1:T(8,128)}, u32[]{:S(2)}) copy-start(f32[1024,64]{0,1:T(8,128)} %param.10) | copy-start | bytes 786436
  195.4 307.2 %all-to-all-start = ((s32[32,1,8]{2,1,0:T(1,128)}), s32[32,1,8]{2,1,0:T(1,128)S(1)}, u32[]{:S(2)}, u32[]{:S(2)}) async-start(s32[32,1,8]{2,1,0:T(1,128)} %copy.26), calls=%async_computation | async-start | bytes 32768 | tf_op jit(solution)/shard_map/all_to_all | solution.py:87
  202.3 362.5 %all-reduce.7.cloned.1.call-start = ((), (), s32[]{:S(2)}) async-start(), calls=%async_computation.4 | async-start | bytes 262144 | tf_op jit(solution)/shard_map/psum | solution.py:79
  496.9 226.6 %copy-start.6 = (f32[1024]{0:T(1024)S(1)}, f32[1024]{0:T(1024)}, u32[]{:S(2)}) copy-start(f32[1024]{0:T(1024)} %param.15) | copy-start | bytes 12292
  502.5 220.9 %all-reduce.9.cloned.1.call-start = ((), (), s32[]{:S(2)}) async-start(), calls=%async_computation.5 | async-start | bytes 524288 | tf_op jit(solution)/shard_map/psum | solution.py:98
  584.1 296.0 %reduce-scatter.2.cloned.1.call-start = ((), (), s32[]{:S(2)}) async-start(), calls=%async_computation.6 | async-start | bytes 4325376 | tf_op jit(solution)/shard_map/reduce_scatter | solution.py:110
  736.7 206.2 %copy-start.2 = (f32[512,64]{0,1:T(8,128)S(1)}, f32[512,64]{0,1:T(8,128)}, u32[]{:S(2)}) copy-start(f32[512,64]{0,1:T(8,128)} %all-reduce.7.cloned.1.call-done) | copy-start | bytes 393220
  736.7 206.2 %all-reduce.11.cloned.1.call-start = ((), (), s32[]{:S(2)}) async-start(), calls=%async_computation.7 | async-start | bytes 262144 | tf_op jit(solution)/shard_map/psum | solution.py:111
Sparse Core Ops, SparseCore 0:
  10.3 132.1 all-gather.3
  188.1 307.5 all-reduce.4
  502.6 62.1 all-reduce.6
  584.2 139.2 all-reduce.8
  736.8 143.1 reduce-scatter.1
  882.3 60.4 all-reduce.10
where the time goes:
time: 952 us; the launch traced here: 951 us
  waiting for transfers between devices  756 us (79%)
  blocking collectives  87.4 us (9%)
  matrix products  50.3 us (5%)
  local copies, waits for them, and re-layouts  23.6 us (2%)
  between operations  14.3 us (2%)
  other arithmetic  12.7 us (1%)
    psum x1, waiting for transfers between devices, per_device(): prediction = lax.psum(partial_pred, 'centers')  219 us
    reduce_scatter x1, waiting for transfers between devices, per_device(): lax.psum_scatter(spread, 'centers', scatter_dimension=0, tiled=True)  143 us
    psum x1, waiting for transfers between devices, per_device(): coeff = lax.psum(coeff_part, ('batch', 'centers'))  139 us
    all_gather x1, waiting for transfers between devices, per_device(): lax.all_gather(local_rows, 'centers', axis=0, tiled=True)  130 us
    all_gather x1, blocking collectives, per_device(): all_targets = lax.all_gather(local_targets, 'centers', axis=0, tiled=True)  73.5 us
    psum x1, waiting for transfers between devices, per_device(): grads = lax.psum(grads_part, 'batch')  62.1 us
    psum x1, waiting for transfers between devices, per_device(): correction = lax.psum(corr_part, 'batch')  62 us
    dot_general x1, matrix products, kernel_rows(): lax.dot_general(row_block, center_block, (((1,), (1,)), ((), ())), precis...  37 us
  transfers between devices with their start and end apart: 7, of which 6 were waited for; matrix products, arithmetic and copies ran while one was open for 2% of the time, Pallas kernels for 0%

commit v1 on v0

v1 whole, which is shorter than its diff:
```python
import itertools
import math

import jax
import jax.numpy as jnp
from jax import lax
from jax.experimental import pallas as pl
from jax.experimental.pallas import tpu as pltpu
from jax.sharding import Mesh, PartitionSpec as P

EPS = 1e-06
CAP = 8
BF = jnp.bfloat16
F32 = jnp.float32
SIZES = {"zh": 2, "core": 2, "x": 4, "y": 4, "zl": 2}
ALL = ("zh", "core", "x", "y", "zl")
CENTERS = ("x", "y", "zl")
VMEM = pl.BlockSpec(memory_space=pltpu.VMEM)

ACOS_FULL = (
    0.4999999701976776, -0.31830424070358276, 0.24984024465084076, -0.210431307554245,
    0.17730562388896942, -0.13514360785484314, 0.0806083083152771, -0.031184406951069832,
    0.005619336850941181,
)
ACOS_HIGH = (
    0.4999392330646515, -0.3173876106739044, 0.24387668073177338, -0.18864932656288147,
    0.12859871983528137, -0.06701970100402832, 0.02248113788664341, -0.003529248759150505,
)

NN = (((1,), (0,)), ((), ()))
NT = (((1,), (1,)), ((), ()))


def mm(a, b, dims):
    return lax.dot_general(a, b, dims, preferred_element_type=F32)


def split2(x):
    hi = x.astype(BF)
    return hi, (x - hi.astype(F32)).astype(BF)


def split3(x):
    hi = x.astype(BF)
    rest = x - hi.astype(F32)
    mid = rest.astype(BF)
    return hi, mid, (rest - mid.astype(F32)).astype(BF)


def pick(onehot, x, dims, flip=False):
    parts = split3(x)
    prods = [mm(p, onehot, dims) if flip else mm(onehot, p, dims) for p in parts]
    return prods[0] + prods[1] + prods[2]


def full_nt(a, b):
    a1, a2, a3 = split3(a)
    b1, b2, b3 = split3(b)
    return (
        mm(a1, b1, NT) + (mm(a1, b2, NT) + mm(a2, b1, NT))
        + (mm(a2, b2, NT) + mm(a1, b3, NT) + mm(a3, b1, NT))
    )


def horner(coefs, x):
    acc = coefs[-1] * x + coefs[-2]
    for c in coefs[-3::-1]:
        acc = acc * x + c
    return acc


def ntk_over_scale(c):
    c = jnp.clip(c, -1.0, 1.0)
    inv_pi = 1.0 / math.pi
    ntk = c
    for layer in range(3):
        w = jnp.maximum(1.0 - c * c, 1e-30)
        root = w * lax.rsqrt(w)
        arg = jnp.abs(c) if layer == 0 else c
        angle = root * horner(ACOS_HIGH if layer == 2 else ACOS_FULL, arg)
        remain = 1.0 - angle
        if layer == 0:
            remain = jnp.where(c < 0.0, angle, remain)
        c = root * inv_pi + remain * c
        ntk = c + ntk * remain
    return ntk


def prep_body(pool_f, pool_t, index, eig, owner_row, owner_col, offset_row, send, targ, scale):
    rows, pool = index.shape[0], pool_f.shape[0]
    hot = (index[...] == lax.broadcasted_iota(jnp.int32, (rows, pool), 1)).astype(BF)
    feats = pick(hot, pool_f[...], NN)
    targets = pick(hot, pool_t[...], NN)
    sa = jnp.sqrt(jnp.mean(feats * feats, axis=1, keepdims=True) + EPS)
    unit = feats / sa
    half = rows // 2
    targ[...] = jnp.concatenate([targets[:half], targets[half:]], axis=1)
    wide = jnp.broadcast_to(sa, targets.shape)
    scale[...] = jnp.concatenate([wide[:half], wide[half:]], axis=1)
    count, q = eig.shape
    peers = send.shape[0]
    same = (owner_col[...] == owner_row[...]).astype(jnp.int32)
    earlier = lax.broadcasted_iota(jnp.int32, (count, count), 0) < lax.broadcasted_iota(
        jnp.int32, (count, count), 1
    )
    rank = jnp.sum(jnp.where(earlier, same, 0), axis=0, keepdims=True)
    slot = owner_row[...] * CAP + rank
    place = slot == lax.broadcasted_iota(jnp.int32, (peers * CAP, count), 0)
    offs = jnp.sum(jnp.where(place, offset_row[...].astype(F32), 0.0), axis=1, keepdims=True)
    offs = jnp.broadcast_to(offs, (peers * CAP, 128))
    vectors = pick(place.astype(BF), eig[...], NN)
    for o in range(peers):
        send[o, 0:rows, :] = unit
        own = slice(o * CAP, (o + 1) * CAP)
        for j in range(q // 128):
            send[o, rows + CAP * j : rows + CAP * (j + 1), :] = vectors[own, 128 * j : 128 * (j + 1)]
        send[o, rows + CAP * (q // 128) :, :] = offs[own]


def kernel_body(recv, centers, weights, khi_out, klo_out, pred, cen, wts, cos):
    step = pl.program_id(0)
    src, rows, dim = recv.shape
    out = weights.shape[1]

    @pl.when(step == 0)
    def _():
        b = centers[...]
        sb = jnp.sqrt(jnp.mean(b * b, axis=1, keepdims=True) + EPS)
        b1, b2, b3 = split3(b / sb)
        cen[0] = jnp.concatenate([b1, b1], axis=1)
        cen[1] = jnp.concatenate([b2, b2], axis=1)
        cen[2] = jnp.concatenate([b3, b1], axis=1)
        w1, w2 = split2(weights[...] * sb)
        wts[...] = jnp.concatenate([w1, w2], axis=1)

    a1, a2, a3 = split3(recv[...].reshape(src * rows, dim))
    near = jnp.concatenate([a1, a2], axis=1)
    far = jnp.concatenate([a1, a3], axis=1)
    cos[...] = (mm(near, cen[0], NT) + (mm(near, cen[1], NT) + mm(far, cen[2], NT))) * (1.0 / dim)
    sub = 32

    def body(i, _):
        at = pl.ds(pl.multiple_of(i * sub, sub), sub)
        hi, lo = split2(ntk_over_scale(cos[at, :]))
        khi_out[at, :] = hi
        klo_out[at, :] = lo
        return 0

    lax.fori_loop(0, src * rows // sub, body, 0)
    both = mm(khi_out[...], wts[...], NN) + mm(klo_out[...], wts[...], NN)
    total = (both[:, :out] + both[:, out:]).reshape(src, 2, rows // 2, out)
    pred[...] = jnp.concatenate([total[:, 0], total[:, 1]], axis=2)


def residual_body(parts, targ, scale, resid, send, *, norm):
    value = scale[...] * jnp.sum(parts[...], axis=0) - targ[...]
    half, out = value.shape[0], value.shape[1] // 2
    resid[0:half, :] = value[:, :out]
    resid[half:, :] = value[:, out:]
    ready = value * scale[...] * norm
    for o in range(send.shape[0]):
        send[o] = ready


def grads_body(resid, khi, klo, centers, grads):
    src, half, wide = resid.shape
    out = wide // 2
    r = resid[...]
    r = jnp.concatenate([r[:, :, :out], r[:, :, out:]], axis=1).reshape(src * half * 2, out)
    r1, r2 = split2(r.T)
    rr = jnp.concatenate([r1, r2], axis=0)
    both = mm(rr, khi[...], NN) + mm(rr, klo[...], NN)
    b = centers[...]
    nb = full_nt(jnp.ones((8, b.shape[1]), F32), b * b)[0:1] * (1.0 / b.shape[1]) + EPS
    grads[...] = (both[:out] + both[out:]) * jnp.sqrt(nb)


def spread_of(recv, rows, total):
    peers = recv.shape[0]
    offs = recv[:, rows:, :].reshape(peers * CAP, 128)
    cols = lax.broadcasted_iota(jnp.int32, (peers * CAP, 128), 1).astype(F32)
    return jnp.concatenate(
        [(offs == cols + float(128 * k)).astype(BF) for k in range(total // 128)], axis=1
    )


def coeff_body(recv, grads, coeff):
    peers, height = recv.shape[0], recv.shape[1]
    q = coeff.shape[1]
    first = height - CAP * (q // 128 + 1)
    hot = spread_of(recv, height - CAP, grads.shape[1])
    g1, g2 = split2(pick(hot, grads[...], NT, flip=True))
    gg = jnp.concatenate([g1, g2], axis=0)
    out = grads.shape[0]
    for j in range(q // 128):
        block = recv[:, first + CAP * j : first + CAP * (j + 1), :].reshape(peers * CAP, 128)
        e1, e2 = split2(block)
        both = mm(gg, e1, NN) + mm(gg, e2, NN)
        coeff[:, 128 * j : 128 * (j + 1)] = both[:out] + both[out:]


def corr_body(recv, coeff, eig_scale, corr):
    peers, height = recv.shape[0], recv.shape[1]
    out, q = coeff.shape
    first = height - CAP * (q // 128 + 1)
    hot = spread_of(recv, height - CAP, corr.shape[1])
    total = jnp.zeros((2 * out, peers * CAP), F32)
    for j in range(q // 128):
        at = slice(128 * j, 128 * (j + 1))
        block = recv[:, first + CAP * j : first + CAP * (j + 1), :].reshape(peers * CAP, 128)
        e1, e2 = split2(block)
        c1, c2 = split2(coeff[:, at] * eig_scale[:, at])
        cc = jnp.concatenate([c1, c2], axis=0)
        total = total + mm(cc, e1, NT) + mm(cc, e2, NT)
    corr[...] = pick(hot, total[:out] + total[out:], NN, flip=True)


def finish_body(a, b, grads, update):
    update[...] = (a[...] + b[...] - grads[...]).T


def shape(*dims, dtype=F32):
    return jax.ShapeDtypeStruct(dims, dtype)


def params(mib=32):
    return pltpu.CompilerParams(vmem_limit_bytes=mib << 20)


def call(body, outs, *args, mib=32, **kw):
    many = isinstance(outs, (list, tuple))
    return pl.pallas_call(
        body,
        out_shape=outs,
        in_specs=[VMEM] * len(args),
        out_specs=[VMEM] * len(outs) if many else VMEM,
        compiler_params=params(mib),
        **kw,
    )(*args)


def shifts(axis):
    n = SIZES[axis]
    return [[(i, (i + s) % n) for i in range(n)] for s in range(1, n)]


def exchange(v, axes):
    sizes = [SIZES[a] for a in axes]
    spots = list(itertools.product(*[range(s) for s in sizes]))
    flat = {p: i for i, p in enumerate(spots)}
    total = v
    for off in spots[1:]:
        perm = [
            (flat[p], flat[tuple((i + o) % s for i, o, s in zip(p, off, sizes))]) for p in spots
        ]
        total = total + lax.ppermute(v, axes, perm)
    return total


def per_device(
    pool_features, pool_targets, batch_index, centers, weights,
    eig_vectors, eig_scale, nys_owner, nys_offset,
):
    rows, dim = batch_index.shape[0], pool_features.shape[1]
    peers = SIZES["x"] * SIZES["y"] * SIZES["zl"]
    cdev, out = weights.shape
    count, q = eig_vectors.shape
    half = rows // 2
    height = rows + CAP * (q // 128 + 1)
    norm = 1.0 / math.sqrt(rows * peers * SIZES["zh"] * SIZES["core"])

    send, targ, scale = call(
        prep_body,
        [shape(peers, height, dim), shape(half, 2 * out), shape(half, 2 * out)],
        pool_features, pool_targets, batch_index[:, None], eig_vectors,
        nys_owner.reshape(1, count), nys_owner, nys_offset[None, :],
    )
    recv = lax.all_to_all(send, CENTERS, split_axis=0, concat_axis=0, tiled=True)

    group = 8
    khi, klo, pred = pl.pallas_call(
        kernel_body,
        grid=(peers // group,),
        in_specs=[
            pl.BlockSpec((group, rows, dim), lambda i: (i, 0, 0)),
            pl.BlockSpec((cdev, dim), lambda i: (0, 0)),
            pl.BlockSpec((cdev, out), lambda i: (0, 0)),
        ],
        out_specs=[
            pl.BlockSpec((group * rows, cdev), lambda i: (i, 0)),
            pl.BlockSpec((group * rows, cdev), lambda i: (i, 0)),
            pl.BlockSpec((group, half, 2 * out), lambda i: (i, 0, 0)),
        ],
        out_shape=[
            shape(peers * rows, cdev, dtype=BF),
            shape(peers * rows, cdev, dtype=BF),
            shape(peers, half, 2 * out),
        ],
        scratch_shapes=[
            pltpu.VMEM((3, cdev, 2 * dim), BF),
            pltpu.VMEM((cdev, 2 * out), BF),
            pltpu.VMEM((group * rows, cdev), F32),
        ],
        compiler_params=params(),
    )(recv, centers, weights)

    parts = lax.all_to_all(pred, CENTERS, split_axis=0, concat_axis=0, tiled=True)
    resid, ready = call(
        lambda *refs: residual_body(*refs, norm=norm),
        [shape(rows, out), shape(peers, half, 2 * out)],
        parts, targ, scale,
    )
    every = lax.all_to_all(ready, CENTERS, split_axis=0, concat_axis=0, tiled=True)
    grads = call(grads_body, shape(out, cdev), every, khi, klo, centers)
    grads = exchange(grads, ("core",))
    grads = exchange(grads, ("zh",))
    coeff = call(coeff_body, shape(out, q), recv, grads)
    coeff = exchange(coeff, ("core",))
    me = lax.axis_index("core")
    mine = lax.dynamic_slice_in_dim(coeff, me * (out // 2), out // 2, 0)
    mine = exchange(mine, ("x",))
    mine = exchange(mine, ("y",))
    mine = exchange(mine, ("zh", "zl"))
    other = lax.ppermute(mine, "core", [(0, 1), (1, 0)])
    coeff = jnp.where(
        me == 0, jnp.concatenate([mine, other], 0), jnp.concatenate([other, mine], 0)
    )
    corr = call(corr_body, shape(out, cdev), recv, coeff, eig_scale[None, :])
    corr = exchange(corr, ("core",))
    far = lax.ppermute(corr, "zh", [(0, 1), (1, 0)])
    update = call(finish_body, shape(cdev, out), corr, far, grads)
    return resid, update


def solution(mesh):
    fine = Mesh(mesh.devices.reshape(tuple(SIZES[a] for a in ALL)), ALL)
    placed = (
        P(ALL, None),
        P(ALL, None),
        P(ALL),
        P(CENTERS, None),
        P(CENTERS, None),
        P(ALL, None),
        P(),
        P(ALL, None),
        P(ALL),
    )
    return jax.shard_map(
        per_device,
        mesh=fine,
        in_specs=placed,
        out_specs=(P(ALL, None), P(CENTERS, None)),
        check_vma=False,
    )
```

time: 952 us -> 154 us (0.16)
  waiting for transfers between devices: 756 us -> 59.9 us
  blocking collectives: 87.4 us -> 28.1 us
  matrix products: 50.3 us -> 0 us
  Pallas kernels: 0 us -> 25.6 us
  starting transfers between devices: 7.19 us -> 30.5 us
  local copies, waits for them, and re-layouts: 23.6 us -> 8.34 us
  between operations: 14.3 us -> 0.78 us
  other arithmetic: 12.7 us -> 0.21 us
    psum x4 -> x0, waiting for transfers between devices: 482 us -> none  [the longest x1 219 us: per_device(): prediction = lax.psum(partial_pred, 'centers')]
    reduce_scatter x1 -> x0, waiting for transfers between devices: 143 us -> none  [per_device(): lax.psum_scatter(spread, 'centers', scatter_dimension=0, tiled=True)]
    all_gather x1 -> x0, waiting for transfers between devices: 130 us -> none  [per_device(): lax.all_gather(local_rows, 'centers', axis=0, tiled=True)]
    all_gather x1 -> x0, blocking collectives: 73.5 us -> none  [per_device(): all_targets = lax.all_gather(local_targets, 'centers', axis=0, tiled=True)]
    dot_general x5 -> x0, matrix products: 50.3 us -> none  [the longest x1 37 us: kernel_rows(): lax.dot_general(row_block, center_block, (((1,), (1,)), ((), ())), precis...]
    ppermute x0 -> x15, waiting for transfers between devices: none -> 30.7 us  [the longest x13 24.7 us: exchange(): total = total + lax.ppermute(v, axes, perm)]
    all_to_all x1, waiting for transfers between devices: 0.01 us -> 29.2 us  [per_device(): lax.all_to_all(send, CENTERS, split_axis=0, concat_axis=0, tiled=True)]
    pallas_call x0 -> x7, Pallas kernels: none -> 25.6 us  [the longest x1 20.8 us: per_device(): pl.pallas_call(kernel_body, grid=(peers // group,), in_specs=[pl.BlockSpe...]
  transfers between devices with their start and end apart: 7 -> 16, of which waited for: 6 -> 15; matrix products, arithmetic and copies ran while one was open for 2% -> 0% of each run, Pallas kernels for 0% -> 0%
where the time goes in v1:
time: 154 us; the launch traced here: 153 us
  waiting for transfers between devices  59.9 us (39%)
  starting transfers between devices  30.5 us (20%)
  blocking collectives  28.1 us (18%)
  Pallas kernels  25.6 us (17%)
  local copies, waits for them, and re-layouts  8.34 us (5%)
    all_to_all x1, waiting for transfers between devices, per_device(): lax.all_to_all(send, CENTERS, split_axis=0, concat_axis=0, tiled=True)  29.2 us
    ppermute x13, waiting for transfers between devices, exchange(): total = total + lax.ppermute(v, axes, perm)  24.7 us
    pallas_call x1, Pallas kernels, per_device(): pl.pallas_call(kernel_body, grid=(peers // group,), in_specs=[pl.BlockSpe...  20.8 us
    ppermute x13, starting transfers between devices, exchange(): total = total + lax.ppermute(v, axes, perm)  17.1 us
    all_to_all x1, blocking collectives, per_device(): lax.all_to_all(pred, CENTERS, split_axis=0, concat_axis=0, tiled=True)  14.7 us
    all_to_all x1, blocking collectives, per_device(): lax.all_to_all(ready, CENTERS, split_axis=0, concat_axis=0, tiled=True)  13.4 us
    all_to_all x1, starting transfers between devices, per_device(): lax.all_to_all(send, CENTERS, split_axis=0, concat_axis=0, tiled=True)  9.36 us
    unnamed x20, local copies, waits for them, and re-layouts  7.6 us
  transfers between devices with their start and end apart: 16, of which 15 were waited for; matrix products, arithmetic and copies ran while one was open for 0% of the time, Pallas kernels for 0%

profile of v1, /device:TPU:1, one launch (start us, length us, event | category | flops | bytes accessed | tf_op | source)
XLA Modules:
  0.0 153.4 jit_solution(6841065520967302805)
XLA Ops:
  0.6 1.1 copy.11.pool_t
  3.3 1.0 copy-done.2
  4.3 1.0 copy-done.3
  7.6 1.4 copy-done
  9.0 9.4 %all-to-all-start = ((f32[32,136,128]{2,1,0:T(8,128)}), f32[32,136,128]{2,1,0:T(8,128)S(1)}, u32[]{:S(2)}, u32[]{:S(2)}) async-start(f32[32,136,128]{2,1,0:T(8,128)} %copy-done), calls=%async_computation | async-start | bytes 4456448 | tf_op jit(solution)/shard_map/all_to_all | solution.py:278
  18.5 29.2 %all-to-all-done.recv = f32[32,136,128]{2,1,0:T(8,128)S(1)} async-done(((f32[32,136,128]{2,1,0:T(8,128)}), f32[32,136,128]{2,1,0:T(8,128)S(1)}, u32[]{:S(2)}, u32[]{:S(2)}) %all-to-all-start) | async-done | bytes 2228256 | tf_op jit(solution)/shard_map/all_to_all | solution.py:278
  47.7 20.8 %shard_map.105 = (bf16[2048,512]{1,0:T(8,128)(2,1)S(1)}, bf16[2048,512]{1,0:T(8,128)(2,1)S(1)}, f32[32,32,128]{2,1,0:T(8,128)S(1)}) custom-call(f32[32,136,128]{2,1,0:T(8,128)S(1)} %all-to-all-done.recv, f32[512,128]{1,0:T(8,128)S(1)} %copy-done.1, f32[512,64]{1,0:T(8,128)S(1)} %copy.14.weights), custom_call_target="tpu_custom_call" | custom-call | tf_op jit(solution)/shard_map/pallas_call | solution.py:281
  68.5 14.7 %all_to_all.15.refs_0_ = f32[32,32,128]{2,1,0:T(8,128)S(1)} all-to-all(f32[32,32,128]{2,1,0:T(8,128)S(1)} %get-tuple-element.11), channel_id=1, replica_groups=mesh['zh'=2,'core'=2,'x'=4,'y'=4,'zl'=2] {'x','y','zl'}, dimensions={0} | all-to-all | bytes 1048576 | tf_op jit(solution)/shard_map/all_to_all | solution.py:307
  83.9 13.4 %all_to_all.16.resid = f32[32,32,128]{2,1,0:T(8,128)S(1)} all-to-all(f32[32,32,128]{2,1,0:T(8,128)S(1)} %get-tuple-element.15), channel_id=1, replica_groups=mesh['zh'=2,'core'=2,'x'=4,'y'=4,'zl'=2] {'x','y','zl'}, dimensions={0} | all-to-all | bytes 1048576 | tf_op jit(solution)/shard_map/all_to_all | solution.py:313
  97.3 1.1 shard_map.107
  98.4 3.7 %collective-permute-start = (f32[64,512]{1,0:T(8,128)S(1)}, f32[64,512]{1,0:T(8,128)S(1)}, u32[]{:S(2)}, u32[]{:S(2)}) collective-permute-start(f32[64,512]{1,0:T(8,128)S(1)} %shard_map.107), channel_id=1, source_target_pairs={{0,32},{32,0},{1,33},{33,1},{2,34},{34,2},{3,35},{35,3},{4,36},{36... | collective-permute-start | bytes 393224 | tf_op jit(solution)/shard_map/ppermute | solution.py:256
  102.1 1.0 collective-permute-done
  103.1 3.4 %collective-permute-start.1 = (f32[64,512]{1,0:T(8,128)S(1)}, f32[64,512]{1,0:T(8,128)S(1)}, u32[]{:S(2)}, u32[]{:S(2)}) collective-permute-start(f32[64,512]{1,0:T(8,128)S(1)} %add.42), channel_id=1, source_target_pairs={{0,64},{64,0},{1,65},{65,1},{2,66},{66,2},{3,67},{67,3},{4,68},{68... | collective-permute-start | bytes 393224 | tf_op jit(solution)/shard_map/ppermute | solution.py:256
  106.5 3.6 %collective-permute-done.1 = f32[64,512]{1,0:T(8,128)S(1)} collective-permute-done((f32[64,512]{1,0:T(8,128)S(1)}, f32[64,512]{1,0:T(8,128)S(1)}, u32[]{:S(2)}, u32[]{:S(2)}) %collective-permute-start.1) | collective-permute-done | bytes 131104 | tf_op jit(solution)/shard_map/ppermute | solution.py:256
  110.1 1.1 shard_map.108
  111.3 1.0 collective-permute-start.2
  112.3 1.2 collective-permute-done.2
  113.5 1.8 %collective-permute-start.4 = (f32[32,1024]{1,0:T(8,128)S(1)}, f32[32,1024]{1,0:T(8,128)S(1)}, u32[]{:S(2)}, u32[]{:S(2)}) collective-permute-start(f32[32,1024]{1,0:T(8,128)S(1)} %dynamic-slice_add_fusion), channel_id=1, source_target_pairs={{0,16},{8,24},{16,0},{24,8},{1,17},{9,25},{17,1},{25,9},{2,18},{10... | collective-permute-start | bytes 393224 | tf_op jit(solution)/shard_map/ppermute | solution.py:256
  116.2 4.0 %collective-permute-done.3 = f32[32,1024]{1,0:T(8,128)S(1)} collective-permute-done((f32[32,1024]{1,0:T(8,128)S(1)}, f32[32,1024]{1,0:T(8,128)S(1)}, u32[]{:S(2)}, u32[]{:S(2)}) %collective-permute-start.3) | collective-permute-done | bytes 131104 | tf_op jit(solution)/shard_map/ppermute | solution.py:256
  120.2 1.2 collective-permute-done.4
  121.4 1.2 collective-permute-done.5
  123.0 1.0 collective-permute-start.7
  124.0 1.4 collective-permute-start.8
  125.5 3.6 %collective-permute-done.6 = f32[32,1024]{1,0:T(8,128)S(1)} collective-permute-done((f32[32,1024]{1,0:T(8,128)S(1)}, f32[32,1024]{1,0:T(8,128)S(1)}, u32[]{:S(2)}, u32[]{:S(2)}) %collective-permute-start.6) | collective-permute-done | bytes 131104 | tf_op jit(solution)/shard_map/ppermute | solution.py:256
  130.7 3.0 %collective-permute-start.10 = (f32[32,1024]{1,0:T(8,128)S(1)}, f32[32,1024]{1,0:T(8,128)S(1)}, u32[]{:S(2)}, u32[]{:S(2)}) collective-permute-start(f32[32,1024]{1,0:T(8,128)S(1)} %add_add_fusion.1), channel_id=1, source_target_pairs={{0,64},{1,65},{64,0},{65,1},{2,66},{3,67},{66,2},{67,3},{4,68},{5,... | collective-permute-start | bytes 393224 | tf_op jit(solution)/shard_map/ppermute | solution.py:256
  133.7 2.4 %collective-permute-done.10 = f32[32,1024]{1,0:T(8,128)S(1)} collective-permute-done((f32[32,1024]{1,0:T(8,128)S(1)}, f32[32,1024]{1,0:T(8,128)S(1)}, u32[]{:S(2)}, u32[]{:S(2)}) %collective-permute-start.10) | collective-permute-done | bytes 131104 | tf_op jit(solution)/shard_map/ppermute | solution.py:256
  136.1 4.1 %collective-permute-done.11 = f32[32,1024]{1,0:T(8,128)S(1)} collective-permute-done((f32[32,1024]{1,0:T(8,128)S(1)}, f32[32,1024]{1,0:T(8,128)S(1)}, u32[]{:S(2)}, u32[]{:S(2)}) %collective-permute-start.11) | collective-permute-done | bytes 131104 | tf_op jit(solution)/shard_map/ppermute | solution.py:256
  140.2 2.7 %collective-permute-start.12 = (f32[32,1024]{1,0:T(8,128)S(1)}, f32[32,1024]{1,0:T(8,128)S(1)}, u32[]{:S(2)}, u32[]{:S(2)}) collective-permute-start(f32[32,1024]{1,0:T(8,128)S(1)} %add_add_fusion), channel_id=1, source_target_pairs={{0,32},{32,0},{1,33},{33,1},{2,34},{34,2},{3,35},{35,3},{4,36},{36... | collective-permute-start | bytes 393224 | tf_op jit(solution)/shard_map/ppermute | solution.py:324
  142.9 1.0 collective-permute-done.12
  145.2 1.0 collective-permute-done.13
  146.2 1.3 collective-permute-start.14
  147.5 5.0 %collective-permute-done.14.b = f32[64,512]{1,0:T(8,128)S(1)} collective-permute-done((f32[64,512]{1,0:T(8,128)S(1)}, f32[64,512]{1,0:T(8,128)S(1)}, u32[]{:S(2)}, u32[]{:S(2)}) %collective-permute-start.14) | collective-permute-done | bytes 131104 | tf_op jit(solution)/shard_map/ppermute | solution.py:330
  (38 shorter events, 9.9 us)
Async XLA Ops:
  3.3 1.0 copy-start.2
  4.3 1.0 copy-start.3
  5.4 0.7 copy-start.5
  6.0 0.7 copy-start.6
  7.6 1.4 copy-start
  9.0 9.4 %copy-start.7 = (f32[512,64]{0,1:T(8,128)S(1)}, f32[512,64]{0,1:T(8,128)}, u32[]{:S(2)}) copy-start(f32[512,64]{0,1:T(8,128)} %param.13) | copy-start | bytes 393220
  9.0 38.7 %copy-start.1 = (f32[512,128]{1,0:T(8,128)S(1)}, f32[512,128]{1,0:T(8,128)}, u32[]{:S(2)}) copy-start(f32[512,128]{1,0:T(8,128)} %centers.3) | copy-start | bytes 786436
  9.0 38.7 %all-to-all-start = ((f32[32,136,128]{2,1,0:T(8,128)}), f32[32,136,128]{2,1,0:T(8,128)S(1)}, u32[]{:S(2)}, u32[]{:S(2)}) async-start(f32[32,136,128]{2,1,0:T(8,128)} %copy-done), calls=%async_computation | async-start | bytes 4456448 | tf_op jit(solution)/shard_map/all_to_all | solution.py:278
  98.4 4.7 %collective-permute-start = (f32[64,512]{1,0:T(8,128)S(1)}, f32[64,512]{1,0:T(8,128)S(1)}, u32[]{:S(2)}, u32[]{:S(2)}) collective-permute-start(f32[64,512]{1,0:T(8,128)S(1)} %shard_map.107), channel_id=1, source_target_pairs={{0,32},{32,0},{1,33},{33,1},{2,34},{34,2},{3,35},{35,3},{4,36},{36... | collective-permute-start | bytes 393224 | tf_op jit(solution)/shard_map/ppermute | solution.py:256
  103.1 7.0 %collective-permute-start.1 = (f32[64,512]{1,0:T(8,128)S(1)}, f32[64,512]{1,0:T(8,128)S(1)}, u32[]{:S(2)}, u32[]{:S(2)}) collective-permute-start(f32[64,512]{1,0:T(8,128)S(1)} %add.42), channel_id=1, source_target_pairs={{0,64},{64,0},{1,65},{65,1},{2,66},{66,2},{3,67},{67,3},{4,68},{68... | collective-permute-start | bytes 393224 | tf_op jit(solution)/shard_map/ppermute | solution.py:256
  110.1 33.8 %copy-start.4 = (f32[1024]{0:T(1024)S(1)}, f32[1024]{0:T(1024)}, u32[]{:S(2)}) copy-start(f32[1024]{0:T(1024)} %param.15) | copy-start | bytes 12292
  111.3 2.1 %collective-permute-start.2 = (f32[64,1024]{1,0:T(8,128)S(1)}, f32[64,1024]{1,0:T(8,128)S(1)}, u32[]{:S(2)}, u32[]{:S(2)}) collective-permute-start(f32[64,1024]{1,0:T(8,128)S(1)} %shard_map.108), channel_id=1, source_target_pairs={{0,32},{32,0},{1,33},{33,1},{2,34},{34,2},{3,35},{35,3},{4,36},{36... | collective-permute-start | bytes 786440 | tf_op jit(solution)/shard_map/ppermute | solution.py:256
  113.4 6.8 %collective-permute-start.3 = (f32[32,1024]{1,0:T(8,128)S(1)}, f32[32,1024]{1,0:T(8,128)S(1)}, u32[]{:S(2)}, u32[]{:S(2)}) collective-permute-start(f32[32,1024]{1,0:T(8,128)S(1)} %dynamic-slice_add_fusion), channel_id=1, source_target_pairs={{0,8},{8,16},{16,24},{24,0},{1,9},{9,17},{17,25},{25,1},{2,10},{10... | collective-permute-start | bytes 393224 | tf_op jit(solution)/shard_map/ppermute | solution.py:256
  113.5 7.9 %collective-permute-start.4 = (f32[32,1024]{1,0:T(8,128)S(1)}, f32[32,1024]{1,0:T(8,128)S(1)}, u32[]{:S(2)}, u32[]{:S(2)}) collective-permute-start(f32[32,1024]{1,0:T(8,128)S(1)} %dynamic-slice_add_fusion), channel_id=1, source_target_pairs={{0,16},{8,24},{16,0},{24,8},{1,17},{9,25},{17,1},{25,9},{2,18},{10... | collective-permute-start | bytes 393224 | tf_op jit(solution)/shard_map/ppermute | solution.py:256
  115.3 7.3 %collective-permute-start.5 = (f32[32,1024]{1,0:T(8,128)S(1)}, f32[32,1024]{1,0:T(8,128)S(1)}, u32[]{:S(2)}, u32[]{:S(2)}) collective-permute-start(f32[32,1024]{1,0:T(8,128)S(1)} %dynamic-slice_add_fusion), channel_id=1, source_target_pairs={{0,24},{8,0},{16,8},{24,16},{1,25},{9,1},{17,9},{25,17},{2,26},{10... | collective-permute-start | bytes 393224 | tf_op jit(solution)/shard_map/ppermute | solution.py:256
  122.6 6.4 %collective-permute-start.6 = (f32[32,1024]{1,0:T(8,128)S(1)}, f32[32,1024]{1,0:T(8,128)S(1)}, u32[]{:S(2)}, u32[]{:S(2)}) collective-permute-start(f32[32,1024]{1,0:T(8,128)S(1)} %add_add_fusion.2), channel_id=1, source_target_pairs={{0,2},{2,4},{4,6},{6,0},{1,3},{3,5},{5,7},{7,1},{8,10},{10,12},{12... | collective-permute-start | bytes 393224 | tf_op jit(solution)/shard_map/ppermute | solution.py:256
  123.0 6.7 %collective-permute-start.7 = (f32[32,1024]{1,0:T(8,128)S(1)}, f32[32,1024]{1,0:T(8,128)S(1)}, u32[]{:S(2)}, u32[]{:S(2)}) collective-permute-start(f32[32,1024]{1,0:T(8,128)S(1)} %add_add_fusion.2), channel_id=1, source_target_pairs={{0,4},{2,6},{4,0},{6,2},{1,5},{3,7},{5,1},{7,3},{8,12},{10,14},{12... | collective-permute-start | bytes 393224 | tf_op jit(solution)/shard_map/ppermute | solution.py:256
  124.0 6.6 %collective-permute-start.8 = (f32[32,1024]{1,0:T(8,128)S(1)}, f32[32,1024]{1,0:T(8,128)S(1)}, u32[]{:S(2)}, u32[]{:S(2)}) collective-permute-start(f32[32,1024]{1,0:T(8,128)S(1)} %add_add_fusion.2), channel_id=1, source_target_pairs={{0,6},{2,0},{4,2},{6,4},{1,7},{3,1},{5,3},{7,5},{8,14},{10,8},{12,... | collective-permute-start | bytes 393224 | tf_op jit(solution)/shard_map/ppermute | solution.py:256
  130.7 5.4 %collective-permute-start.10 = (f32[32,1024]{1,0:T(8,128)S(1)}, f32[32,1024]{1,0:T(8,128)S(1)}, u32[]{:S(2)}, u32[]{:S(2)}) collective-permute-start(f32[32,1024]{1,0:T(8,128)S(1)} %add_add_fusion.1), channel_id=1, source_target_pairs={{0,64},{1,65},{64,0},{65,1},{2,66},{3,67},{66,2},{67,3},{4,68},{5,... | collective-permute-start | bytes 393224 | tf_op jit(solution)/shard_map/ppermute | solution.py:256
  133.7 6.4 %collective-permute-start.11 = (f32[32,1024]{1,0:T(8,128)S(1)}, f32[32,1024]{1,0:T(8,128)S(1)}, u32[]{:S(2)}, u32[]{:S(2)}) collective-permute-start(f32[32,1024]{1,0:T(8,128)S(1)} %add_add_fusion.1), channel_id=1, source_target_pairs={{0,65},{1,64},{64,1},{65,0},{2,67},{3,66},{66,3},{67,2},{4,69},{5,... | collective-permute-start | bytes 393224 | tf_op jit(solution)/shard_map/ppermute | solution.py:256
  133.7 6.4 %collective-permute-start.9 = (f32[32,1024]{1,0:T(8,128)S(1)}, f32[32,1024]{1,0:T(8,128)S(1)}, u32[]{:S(2)}, u32[]{:S(2)}) collective-permute-start(f32[32,1024]{1,0:T(8,128)S(1)} %add_add_fusion.1), channel_id=1, source_target_pairs={{0,1},{1,0},{64,65},{65,64},{2,3},{3,2},{66,67},{67,66},{4,5},{5,4... | collective-permute-start | bytes 393224 | tf_op jit(solution)/shard_map/ppermute | solution.py:256
  140.2 3.7 %collective-permute-start.12 = (f32[32,1024]{1,0:T(8,128)S(1)}, f32[32,1024]{1,0:T(8,128)S(1)}, u32[]{:S(2)}, u32[]{:S(2)}) collective-permute-start(f32[32,1024]{1,0:T(8,128)S(1)} %add_add_fusion), channel_id=1, source_target_pairs={{0,32},{32,0},{1,33},{33,1},{2,34},{34,2},{3,35},{35,3},{4,36},{36... | collective-permute-start | bytes 393224 | tf_op jit(solution)/shard_map/ppermute | solution.py:324
  144.8 1.4 collective-permute-start.13
  146.2 6.3 %collective-permute-start.14 = (f32[64,512]{1,0:T(8,128)S(1)}, f32[64,512]{1,0:T(8,128)S(1)}, u32[]{:S(2)}, u32[]{:S(2)}) collective-permute-start(f32[64,512]{1,0:T(8,128)S(1)} %add.55.a), channel_id=1, source_target_pairs={{0,64},{64,0},{1,65},{65,1},{2,66},{66,2},{3,67},{67,3},{4,68},{68... | collective-permute-start | bytes 393224 | tf_op jit(solution)/shard_map/ppermute | solution.py:330

commit v2 on v1

v2 whole, which is shorter than its diff:
```python
import functools
import itertools
import math

import jax
import jax.numpy as jnp
from jax import lax
from jax.experimental import pallas as pl
from jax.experimental.pallas import tpu as pltpu
from jax.sharding import Mesh, PartitionSpec as P

EPS = 1e-06
CAP = 8
BF = jnp.bfloat16
F32 = jnp.float32
SIZES = {"zh": 2, "core": 2, "x": 4, "y": 4, "zl": 2}
ALL = ("zh", "core", "x", "y", "zl")
CENTERS = ("x", "y", "zl")
VMEM = pl.BlockSpec(memory_space=pltpu.VMEM)

ACOS_FULL = (
    0.4999999701976776, -0.31830424070358276, 0.24984024465084076, -0.210431307554245,
    0.17730562388896942, -0.13514360785484314, 0.0806083083152771, -0.031184406951069832,
    0.005619336850941181,
)
ACOS_HIGH = (
    0.4999392330646515, -0.3173876106739044, 0.24387668073177338, -0.18864932656288147,
    0.12859871983528137, -0.06701970100402832, 0.02248113788664341, -0.003529248759150505,
)

NN = (((1,), (0,)), ((), ()))
NT = (((1,), (1,)), ((), ()))


def mm(a, b, dims):
    return lax.dot_general(a, b, dims, preferred_element_type=F32)


def split2(x):
    hi = x.astype(BF)
    return hi, (x - hi.astype(F32)).astype(BF)


def split3(x):
    hi = x.astype(BF)
    rest = x - hi.astype(F32)
    mid = rest.astype(BF)
    return hi, mid, (rest - mid.astype(F32)).astype(BF)


def pick(onehot, x, dims, flip=False):
    parts = split3(x)
    prods = [mm(p, onehot, dims) if flip else mm(onehot, p, dims) for p in parts]
    return prods[0] + prods[1] + prods[2]


def full_nt(a, b):
    a1, a2, a3 = split3(a)
    b1, b2, b3 = split3(b)
    return (
        mm(a1, b1, NT) + (mm(a1, b2, NT) + mm(a2, b1, NT))
        + (mm(a2, b2, NT) + mm(a1, b3, NT) + mm(a3, b1, NT))
    )


def horner(coefs, x):
    acc = coefs[-1] * x + coefs[-2]
    for c in coefs[-3::-1]:
        acc = acc * x + c
    return acc


def ntk_over_scale(c):
    inv_pi = 1.0 / math.pi
    ntk = c
    for layer in range(3):
        w = jnp.maximum(1.0 - c * c, 1e-30)
        root = w * lax.rsqrt(w)
        arg = jnp.abs(c) if layer == 0 else c
        angle = root * horner(ACOS_HIGH if layer == 2 else ACOS_FULL, arg)
        remain = jnp.where(c < 0.0, angle, 1.0 - angle) if layer == 0 else 1.0 - angle
        if layer == 2:
            return root * inv_pi + remain * (c + ntk)
        c = root * inv_pi + remain * c
        ntk = c + ntk * remain


def rows_hot(index, width):
    n = index.shape[1]
    col = jnp.broadcast_to(index.astype(F32), (128, n)).T
    lane = lax.broadcasted_iota(jnp.int32, (n, 128), 1).astype(F32)
    return jnp.concatenate(
        [(col == lane + float(128 * k)).astype(BF) for k in range(width // 128)], axis=1
    )


def features_body(pool_f, index, send, scale):
    rows = index.shape[1]
    feats = pick(rows_hot(index[...], pool_f.shape[0]), pool_f[...], NN)
    sa = jnp.sqrt(jnp.mean(feats * feats, axis=1, keepdims=True) + EPS)
    unit = feats / sa
    half, wide = scale.shape
    sa = jnp.broadcast_to(sa, (rows, wide // 2))
    scale[...] = jnp.concatenate([sa[:half], sa[half:]], axis=1)
    for o in range(send.shape[0]):
        send[o] = unit


def vectors_body(core, pool_t, index, eig, mate_eig, nys, mate_nys, send, targ, *, cdev):
    hot = rows_hot(index[...], pool_t.shape[1])
    targets = pick(hot, pool_t[...], NT, flip=True).T
    half = targets.shape[0] // 2
    targ[...] = jnp.concatenate([targets[:half], targets[half:]], axis=1)
    count, q = eig.shape
    part = q // 2
    peers = send.shape[0]
    blocks = part // 128
    mine = pl.ds(pl.multiple_of(core[0] * part, part), part)
    earlier = lax.broadcasted_iota(jnp.int32, (count, count), 0) < lax.broadcasted_iota(
        jnp.int32, (count, count), 1
    )
    for table, (vec, where) in enumerate(((eig, nys), (mate_eig, mate_nys))):
        owner = where[...] // cdev
        offset = where[...] - owner * cdev
        row = jnp.broadcast_to(owner.astype(F32), (count, count))
        same = jnp.where(row.T == row, 1.0, 0.0)
        rank = jnp.sum(jnp.where(earlier, same, 0.0), axis=0, keepdims=True).astype(jnp.int32)
        place = owner * CAP + rank == lax.broadcasted_iota(jnp.int32, (peers * CAP, count), 0)
        offs = jnp.sum(jnp.where(place, offset.astype(F32), 0.0), axis=1, keepdims=True)
        offs = jnp.broadcast_to(offs, (peers * CAP, 128))
        vectors = pick(place.astype(BF), vec[:, mine], NN)
        for o in range(peers):
            own = slice(o * CAP, (o + 1) * CAP)
            for j in range(blocks):
                at = CAP * (2 * j + table)
                send[o, at : at + CAP, :] = vectors[own, 128 * j : 128 * (j + 1)]
            at = CAP * (2 * blocks + table)
            send[o, at : at + CAP, :] = offs[own]


def kernel_body(recv, centers, weights, kern, pred, cen, wts, cos_a, cos_b, lhs, *, block, sub):
    src, rows, dim = recv.shape
    out, count = weights.shape
    b = centers[...]
    sb = jnp.sqrt(jnp.mean(b * b, axis=1, keepdims=True) + EPS)
    b1, b2, b3 = split3(b / sb * (1.0 / dim))
    cen[...] = jnp.concatenate([b1, b1, b2, b2, b3, b1], axis=1)
    w1, w2 = split2(weights[...].T * sb)
    w = jnp.concatenate([w1, w2], axis=1)
    wts[...] = jnp.concatenate([w, w], axis=0)
    blocks, group = src * rows // block, block // rows

    def stage(i):
        a1, a2, a3 = split3(recv[pl.ds(i * group, group)].reshape(block, dim))
        lhs[...] = jnp.concatenate([a1, a2, a1, a2, a1, a3], axis=1)

    def cosines(dst, n):
        at = slice(n * (count // 2), (n + 1) * (count // 2))
        dst[:, at] = mm(lhs[...], cen[at, :], NT)

    def elementwise(i, values, n):
        at = pl.ds(pl.multiple_of(i * block + n * sub, sub), sub)
        hi, lo = split2(ntk_over_scale(values[n * sub : (n + 1) * sub, :]))
        kern[at, :count] = hi
        kern[at, count:] = lo

    def predict(i):
        both = mm(kern[pl.ds(pl.multiple_of(i * block, block), block), :], wts[...], NN)
        total = (both[:, :out] + both[:, out:]).reshape(group, 2, rows // 2, out)
        pred[pl.ds(i * group, group)] = jnp.concatenate([total[:, 0], total[:, 1]], axis=2)

    def step(i, before, now, later):
        elems = [functools.partial(elementwise, i, now, n) for n in range(block // sub)]
        others = [
            functools.partial(cosines, later, 0),
            functools.partial(cosines, later, 1),
            functools.partial(predict, before),
        ]
        stage(jnp.minimum(i + 1, blocks - 1))
        every = len(elems) // len(others)
        for n, f in enumerate(elems):
            if n % every == 0 and others:
                others.pop(0)()
            f()

    stage(0)
    cosines(cos_a, 0)
    cosines(cos_a, 1)

    def pair(h, _):
        step(2 * h, jnp.maximum(2 * h - 1, 0), cos_a, cos_b)
        step(2 * h + 1, 2 * h, cos_b, cos_a)
        return 0

    lax.fori_loop(0, blocks // 2, pair, 0)
    predict(blocks - 1)


def residual_body(parts, targ, scale, resid, send, *, norm):
    value = scale[...] * jnp.sum(parts[...], axis=0) - targ[...]
    half, out = value.shape[0], value.shape[1] // 2
    resid[0:half, :] = value[:, :out]
    resid[half:, :] = value[:, out:]
    ready = value * scale[...] * norm
    for o in range(send.shape[0]):
        send[o] = ready


def grads_body(resid, kern, centers, grads):
    src, half, wide = resid.shape
    out, count = grads.shape
    r = resid[...]
    r = jnp.concatenate([r[:, :, :out], r[:, :, out:]], axis=1).reshape(src * half * 2, out)
    r1, r2 = split2(r.T)
    both = mm(jnp.concatenate([r1, r2], axis=0), kern[...], NN)
    both = both[:out] + both[out:]
    b = centers[...]
    nb = full_nt(jnp.ones((8, b.shape[1]), F32), b * b)[0:1] * (1.0 / b.shape[1]) + EPS
    grads[...] = (both[:, :count] + both[:, count:]) * jnp.sqrt(nb)


def unpack(recv, n):
    peers = recv.shape[0]
    return recv[:, 2 * CAP * n : 2 * CAP * (n + 1), :].reshape(peers * 2 * CAP, 128)


def points_hot(tables, blocks, width):
    offs = jnp.concatenate([unpack(t, blocks) for t in tables], axis=0)
    lane = lax.broadcasted_iota(jnp.int32, offs.shape, 1).astype(F32)
    return jnp.concatenate(
        [(offs == lane + float(128 * k)).astype(BF) for k in range(width // 128)], axis=1
    )


def coeff_body(near, far, grads, coeff):
    out, part = coeff.shape
    blocks = part // 128
    hot = points_hot((near, far), blocks, grads.shape[1])
    g1, g2 = split2(pick(hot, grads[...], NT, flip=True))
    gg = jnp.concatenate([g1, g2], axis=0)
    for j in range(blocks):
        e1, e2 = split2(jnp.concatenate([unpack(near, j), unpack(far, j)], axis=0))
        both = mm(gg, e1, NN) + mm(gg, e2, NN)
        coeff[:, 128 * j : 128 * (j + 1)] = both[:out] + both[out:]


def corr_body(core, near, far, coeff, eig_scale, corr):
    out, part = coeff.shape
    blocks = part // 128
    hot = points_hot((near, far), blocks, corr.shape[1])
    total = jnp.zeros((2 * out, hot.shape[0]), F32)
    for j in range(blocks):
        at = slice(128 * j, 128 * (j + 1))
        e1, e2 = split2(jnp.concatenate([unpack(near, j), unpack(far, j)], axis=0))
        scale = eig_scale[:, pl.ds(pl.multiple_of(core[0] * part + 128 * j, 128), 128)]
        c1, c2 = split2(coeff[:, at] * scale)
        cc = jnp.concatenate([c1, c2], axis=0)
        total = total + mm(cc, e1, NT) + mm(cc, e2, NT)
    corr[...] = pick(hot, total[:out] + total[out:], NN, flip=True)


def shape(*dims, dtype=F32):
    return jax.ShapeDtypeStruct(dims, dtype)


def params(mib=16):
    return pltpu.CompilerParams(vmem_limit_bytes=mib << 20)


def call(body, outs, *args, mib=16, scalars=0, **kw):
    many = isinstance(outs, (list, tuple))
    smem = pl.BlockSpec(memory_space=pltpu.SMEM)
    return pl.pallas_call(
        body,
        out_shape=outs,
        in_specs=[smem] * scalars + [VMEM] * (len(args) - scalars),
        out_specs=[VMEM] * len(outs) if many else VMEM,
        compiler_params=params(mib),
        **kw,
    )(*args)


def exchange(v, axes):
    sizes = [SIZES[a] for a in axes]
    spots = list(itertools.product(*[range(s) for s in sizes]))
    flat = {p: i for i, p in enumerate(spots)}
    total = v
    for off in spots[1:]:
        perm = [
            (flat[p], flat[tuple((i + o) % s for i, o, s in zip(p, off, sizes))]) for p in spots
        ]
        total = total + lax.ppermute(v, axes, perm)
    return total


def per_device(
    pool_features, pool_targets, batch_index, centers, weights,
    eig_vectors, eig_scale, nys_owner, nys_offset,
):
    rows, dim = batch_index.shape[0], pool_features.shape[1]
    peers = SIZES["x"] * SIZES["y"] * SIZES["zl"]
    cdev, out = weights.shape
    count, q = eig_vectors.shape
    half = rows // 2
    norm = 1.0 / math.sqrt(rows * peers * SIZES["zh"] * SIZES["core"])
    swap = [(0, 1), (1, 0)]
    core = lax.axis_index("core").astype(jnp.int32)[None]
    index = batch_index.reshape(1, rows)
    nys = (nys_owner.reshape(count) * cdev + nys_offset).reshape(1, count)

    send, scale = call(
        features_body,
        [shape(peers, rows, dim), shape(half, 2 * out)],
        pool_features, index,
    )
    recv = lax.all_to_all(send, CENTERS, split_axis=0, concat_axis=0, tiled=True)

    mate_eig = lax.ppermute(eig_vectors, "core", swap)
    mate_nys = lax.ppermute(nys, "core", swap)
    piece = 2 * CAP * (q // 256 + 1)
    points, targ = call(
        functools.partial(vectors_body, cdev=cdev),
        [shape(peers, piece, 128), shape(half, 2 * out)],
        core, pool_targets.T, index, eig_vectors, mate_eig, nys, mate_nys,
        scalars=1,
    )
    points, recv = lax.optimization_barrier((points, recv))
    near = lax.all_to_all(points, CENTERS, split_axis=0, concat_axis=0, tiled=True)

    block = 4 * rows
    kern, pred = call(
        functools.partial(kernel_body, block=block, sub=32),
        [shape(peers * rows, 2 * cdev, dtype=BF), shape(peers, half, 2 * out)],
        recv, centers, weights.T,
        scratch_shapes=[
            pltpu.VMEM((cdev, 6 * dim), BF),
            pltpu.VMEM((2 * cdev, 2 * out), BF),
            pltpu.VMEM((block, cdev), F32),
            pltpu.VMEM((block, cdev), F32),
            pltpu.VMEM((block, 6 * dim), BF),
        ],
        cost_estimate=pl.CostEstimate(
            flops=40_000_000_000, bytes_accessed=1 << 22, transcendentals=0
        ),
    )

    near, pred = lax.optimization_barrier((near, pred))
    far = lax.ppermute(near, "zh", swap)
    parts = lax.all_to_all(pred, CENTERS, split_axis=0, concat_axis=0, tiled=True)
    resid, ready = call(
        functools.partial(residual_body, norm=norm),
        [shape(rows, out), shape(peers, half, 2 * out)],
        parts, targ, scale,
    )
    every = lax.all_to_all(ready, CENTERS, split_axis=0, concat_axis=0, tiled=True)
    grads = call(grads_body, shape(out, cdev), every, kern, centers)
    grads = exchange(grads, ("core",))
    coeff = call(coeff_body, shape(out, q // 2), near, far, grads)
    coeff = exchange(coeff, ("x",))
    coeff = exchange(coeff, ("y",))
    coeff = exchange(coeff, ("zh", "zl"))
    corr = call(
        corr_body, shape(out, cdev), core, near, far, coeff, eig_scale[None, :], scalars=1
    )
    update = exchange(corr, ("core",)) - exchange(grads, ("zh",))
    return resid, update.T


def solution(mesh):
    fine = Mesh(mesh.devices.reshape(tuple(SIZES[a] for a in ALL)), ALL)
    placed = (
        P(ALL, None),
        P(ALL, None),
        P(ALL),
        P(CENTERS, None),
        P(CENTERS, None),
        P(ALL, None),
        P(),
        P(ALL, None),
        P(ALL),
    )
    return jax.shard_map(
        per_device,
        mesh=fine,
        in_specs=placed,
        out_specs=(P(ALL, None), P(CENTERS, None)),
        check_vma=False,
    )
```

time: 154 us -> 152 us (0.987)
  waiting for transfers between devices: 59.9 us -> 36.8 us
  blocking collectives: 28.1 us -> 49.8 us
  starting transfers between devices: 30.5 us -> 33.2 us
  local copies, waits for them, and re-layouts: 8.34 us -> 5.87 us
    all_to_all x1, blocking collectives: 14.7 us -> 32.6 us  [per_device(): lax.all_to_all(pred, CENTERS, split_axis=0, concat_axis=0, tiled=True)]
    all_to_all x1, waiting for transfers between devices: 29.2 us -> 11.7 us  [per_device(): lax.all_to_all(send, CENTERS, split_axis=0, concat_axis=0, tiled=True)]
    all_to_all x0 -> x1, starting transfers between devices: none -> 4.62 us  [per_device(): lax.all_to_all(points, CENTERS, split_axis=0, concat_axis=0, tiled=True)]
    ppermute x2 -> x3, waiting for transfers between devices: 6.03 us -> 1.42 us  [the longest x1 1.41 us: per_device(): mate_nys = lax.ppermute(nys, 'core', swap)]
    all_to_all x1, blocking collectives: 13.4 us -> 17.2 us  [per_device(): lax.all_to_all(ready, CENTERS, split_axis=0, concat_axis=0, tiled=True)]
    ppermute x13 -> x12, starting transfers between devices: 17.1 us -> 14.9 us  [exchange(): total = total + lax.ppermute(v, axes, perm)]
    unnamed x20 -> x24, local copies, waits for them, and re-layouts: 7.6 us -> 5.87 us
    ppermute x13 -> x12, waiting for transfers between devices: 24.7 us -> 23.6 us  [exchange(): total = total + lax.ppermute(v, axes, perm)]
  transfers between devices with their start and end apart: 16 -> 17, of which waited for: 15 -> 11; matrix products, arithmetic and copies ran while one was open for 0% -> 0% of each run, Pallas kernels for 0% -> 14%
where the time goes in v2:
time: 152 us
  blocking collectives  49.8 us (33%)
  waiting for transfers between devices  36.8 us (24%)
  starting transfers between devices  33.2 us (22%)
  Pallas kernels  24.5 us (16%)
  local copies, waits for them, and re-layouts  5.87 us (4%)
    all_to_all x1, blocking collectives, per_device(): lax.all_to_all(pred, CENTERS, split_axis=0, concat_axis=0, tiled=True)  32.6 us
    pallas_call x7, Pallas kernels, call(): pl.pallas_call(body, out_shape=outs, in_specs=[smem] * scalars + [VMEM] *...  24.5 us
    ppermute x12, waiting for transfers between devices, exchange(): total = total + lax.ppermute(v, axes, perm)  23.6 us
    all_to_all x1, blocking collectives, per_device(): lax.all_to_all(ready, CENTERS, split_axis=0, concat_axis=0, tiled=True)  17.2 us
    ppermute x12, starting transfers between devices, exchange(): total = total + lax.ppermute(v, axes, perm)  14.9 us
    all_to_all x1, waiting for transfers between devices, per_device(): lax.all_to_all(send, CENTERS, split_axis=0, concat_axis=0, tiled=True)  11.7 us
    all_to_all x1, starting transfers between devices, per_device(): lax.all_to_all(send, CENTERS, split_axis=0, concat_axis=0, tiled=True)  9.22 us
    unnamed x24, local copies, waits for them, and re-layouts  5.87 us
  transfers between devices with their start and end apart: 17, of which 11 were waited for; matrix products, arithmetic and copies ran while one was open for 0% of the time, Pallas kernels for 14%

profile of v2, /device:TPU:1, one launch (start us, length us, event | category | flops | bytes accessed | tf_op | source)
XLA Modules:
  0.0 151.9 jit_solution(8997922035496041310)
XLA Ops:
  0.6 1.0 copy-done.3
  2.4 1.5 %shard_map.105 = (f32[32,64,128]{2,1,0:T(8,128)}, f32[32,128]{1,0:T(8,128)S(1)}) custom-call(f32[1024,128]{1,0:T(8,128)S(1)} %copy-done.3, s32[1,64]{1,0:T(1,128)S(1)} %bitcast.15), custom_call_target="tpu_custom_call" | custom-call | tf_op jit(solution)/shard_map/pallas_call | solution.py:273
  3.9 9.2 %all-to-all-start = ((f32[32,64,128]{2,1,0:T(8,128)}), f32[32,64,128]{2,1,0:T(8,128)S(1)}, u32[]{:S(2)}, u32[]{:S(2)}) async-start(f32[32,64,128]{2,1,0:T(8,128)} %get-tuple-element.15), calls=%async_computation | async-start | bytes 2097152 | tf_op jit(solution)/shard_map/all_to_all | solution.py:316
  13.1 1.0 collective-permute-start
  14.3 1.4 collective-permute-done.1.mate_nys
  15.7 1.9 %shard_map.104 = (f32[32,80,128]{2,1,0:T(8,128)}, f32[32,128]{1,0:T(8,128)S(1)}) custom-call(s32[1]{0:T(128)} %bitcast.core, f32[64,1024]{1,0:T(8,128)S(1)} %bitcast.13, s32[1,64]{1,0:T(1,128)S(1)} %bitcast.16, f32[128,1024]{1,0:T(8,128)S(1)} %copy-done.2, f32[128,1024]{1,0:T(8,128)S(1)} %collective-permute-done.mate_eig, s32[1,128]{1,0:T(1,128)S(1)} %fusion.nys, ...), custom_call_target="tpu_custom_call" | custom-call | tf_op jit(solution)/shard_map/pallas_call | solution.py:273
  17.6 11.7 %all-to-all-done.recv = f32[32,64,128]{2,1,0:T(8,128)S(1)} async-done(((f32[32,64,128]{2,1,0:T(8,128)}), f32[32,64,128]{2,1,0:T(8,128)S(1)}, u32[]{:S(2)}, u32[]{:S(2)}) %all-to-all-start) | async-done | bytes 1048608 | tf_op jit(solution)/shard_map/all_to_all | solution.py:316
  29.3 4.6 %all-to-all-start.1 = ((f32[32,80,128]{2,1,0:T(8,128)}), f32[32,80,128]{2,1,0:T(8,128)S(1)}, u32[]{:S(2)}, u32[]{:S(2)}) async-start(f32[32,80,128]{2,1,0:T(8,128)} %get-tuple-element.16), calls=%async_computation.1 | async-start | bytes 2621440 | tf_op jit(solution)/shard_map/all_to_all | solution.py:328
  34.0 16.2 %shard_map.106 = (bf16[2048,1024]{1,0:T(8,128)(2,1)S(1)}, f32[32,32,128]{2,1,0:T(8,128)S(1)}) custom-call(f32[32,64,128]{2,1,0:T(8,128)S(1)} %all-to-all-done.recv, f32[512,128]{1,0:T(8,128)S(1)} %copy-done.5, f32[64,512]{1,0:T(8,128)S(1)} %bitcast.17), custom_call_target="tpu_custom_call" | custom-call | flops 40000000000 | bytes 4194304 | tf_op jit(solution)/shard_map/pallas_call | solution.py:273
  50.2 2.0 %copy-done = bf16[2048,1024]{1,0:T(8,128)(2,1)} copy-done((bf16[2048,1024]{1,0:T(8,128)(2,1)}, bf16[2048,1024]{1,0:T(8,128)(2,1)S(1)}, u32[]{:S(2)}) %copy-start) | copy-done | bytes 4194328
  52.1 3.3 %collective-permute-start.2 = (f32[32,80,128]{2,1,0:T(8,128)S(1)}, f32[32,80,128]{2,1,0:T(8,128)S(1)}, u32[]{:S(2)}, u32[]{:S(2)}) collective-permute-start(f32[32,80,128]{2,1,0:T(8,128)S(1)} %all-to-all-done.1.near), channel_id=1, source_target_pairs={{0,64},{64,0},{1,65},{65,1},{2,66},{66,2},{3,67},{67,3},{4,68},{68... | collective-permute-start | bytes 3932168 | tf_op jit(solution)/shard_map/ppermute | solution.py:348
  55.5 32.6 %all_to_all.20.parts = f32[32,32,128]{2,1,0:T(8,128)S(1)} all-to-all(f32[32,32,128]{2,1,0:T(8,128)S(1)} %get-tuple-element.19), channel_id=1, replica_groups=mesh['zh'=2,'core'=2,'x'=4,'y'=4,'zl'=2] {'x','y','zl'}, dimensions={0} | all-to-all | bytes 1048576 | tf_op jit(solution)/shard_map/all_to_all | solution.py:349
  88.1 0.7 shard_map.107
  88.8 17.2 %all_to_all.21.resid = f32[32,32,128]{2,1,0:T(8,128)S(1)} all-to-all(f32[32,32,128]{2,1,0:T(8,128)S(1)} %get-tuple-element.24), channel_id=1, replica_groups=mesh['zh'=2,'core'=2,'x'=4,'y'=4,'zl'=2] {'x','y','zl'}, dimensions={0} | all-to-all | bytes 1048576 | tf_op jit(solution)/shard_map/all_to_all | solution.py:355
  106.0 2.2 %copy-done.1 = bf16[2048,1024]{1,0:T(8,128)(2,1)S(1)} copy-done((bf16[2048,1024]{1,0:T(8,128)(2,1)S(1)}, bf16[2048,1024]{1,0:T(8,128)(2,1)}, u32[]{:S(2)}) %copy-start.1) | copy-done | bytes 4194328
  108.2 1.1 shard_map.108
  109.3 4.3 %collective-permute-start.3 = (f32[64,512]{1,0:T(8,128)S(1)}, f32[64,512]{1,0:T(8,128)S(1)}, u32[]{:S(2)}, u32[]{:S(2)}) collective-permute-start(f32[64,512]{1,0:T(8,128)S(1)} %shard_map.108), channel_id=1, source_target_pairs={{0,32},{32,0},{1,33},{33,1},{2,34},{34,2},{3,35},{35,3},{4,36},{36... | collective-permute-start | bytes 393224 | tf_op jit(solution)/shard_map/ppermute | solution.py:292
  113.6 1.0 collective-permute-done.3
  114.6 1.8 %shard_map.109 = f32[64,512]{1,0:T(8,128)S(1)} custom-call(f32[32,80,128]{2,1,0:T(8,128)S(1)} %all-to-all-done.1.near, f32[32,80,128]{2,1,0:T(8,128)S(1)} %collective-permute-done.2.far, f32[64,512]{1,0:T(8,128)S(1)} %add.40.grads), custom_call_target="tpu_custom_call" | custom-call | tf_op jit(solution)/shard_map/pallas_call | solution.py:273
  118.0 3.2 %collective-permute-done.6 = f32[64,512]{1,0:T(8,128)S(1)} collective-permute-done((f32[64,512]{1,0:T(8,128)S(1)}, f32[64,512]{1,0:T(8,128)S(1)}, u32[]{:S(2)}, u32[]{:S(2)}) %collective-permute-start.6) | collective-permute-done | bytes 131104 | tf_op jit(solution)/shard_map/ppermute | solution.py:292
  121.2 1.8 %collective-permute-done.5 = f32[64,512]{1,0:T(8,128)S(1)} collective-permute-done((f32[64,512]{1,0:T(8,128)S(1)}, f32[64,512]{1,0:T(8,128)S(1)}, u32[]{:S(2)}, u32[]{:S(2)}) %collective-permute-start.5) | collective-permute-done | bytes 131104 | tf_op jit(solution)/shard_map/ppermute | solution.py:292
  123.0 3.8 %collective-permute-done.4 = f32[64,512]{1,0:T(8,128)S(1)} collective-permute-done((f32[64,512]{1,0:T(8,128)S(1)}, f32[64,512]{1,0:T(8,128)S(1)}, u32[]{:S(2)}, u32[]{:S(2)}) %collective-permute-start.4) | collective-permute-done | bytes 131104 | tf_op jit(solution)/shard_map/ppermute | solution.py:292
  127.5 1.4 collective-permute-start.8
  128.9 2.6 %collective-permute-done.9 = f32[64,512]{1,0:T(8,128)S(1)} collective-permute-done((f32[64,512]{1,0:T(8,128)S(1)}, f32[64,512]{1,0:T(8,128)S(1)}, u32[]{:S(2)}, u32[]{:S(2)}) %collective-permute-start.9) | collective-permute-done | bytes 131104 | tf_op jit(solution)/shard_map/ppermute | solution.py:292
  131.5 1.3 collective-permute-done.8
  132.8 3.9 %collective-permute-done.7 = f32[64,512]{1,0:T(8,128)S(1)} collective-permute-done((f32[64,512]{1,0:T(8,128)S(1)}, f32[64,512]{1,0:T(8,128)S(1)}, u32[]{:S(2)}, u32[]{:S(2)}) %collective-permute-start.7) | collective-permute-done | bytes 131104 | tf_op jit(solution)/shard_map/ppermute | solution.py:292
  136.8 2.7 %collective-permute-start.11 = (f32[64,512]{1,0:T(8,128)S(1)}, f32[64,512]{1,0:T(8,128)S(1)}, u32[]{:S(2)}, u32[]{:S(2)}) collective-permute-start(f32[64,512]{1,0:T(8,128)S(1)} %add_add_fusion.1), channel_id=1, source_target_pairs={{0,64},{1,65},{64,0},{65,1},{2,66},{3,67},{66,2},{67,3},{4,68},{5,... | collective-permute-start | bytes 393224 | tf_op jit(solution)/shard_map/ppermute | solution.py:292
  140.0 1.3 collective-permute-start.14
  141.3 5.0 %collective-permute-done.12 = f32[64,512]{1,0:T(8,128)S(1)} collective-permute-done((f32[64,512]{1,0:T(8,128)S(1)}, f32[64,512]{1,0:T(8,128)S(1)}, u32[]{:S(2)}, u32[]{:S(2)}) %collective-permute-start.12) | collective-permute-done | bytes 131104 | tf_op jit(solution)/shard_map/ppermute | solution.py:292
  146.4 1.4 shard_map.110
  147.8 2.4 %collective-permute-start.13 = (f32[64,512]{1,0:T(8,128)S(1)}, f32[64,512]{1,0:T(8,128)S(1)}, u32[]{:S(2)}, u32[]{:S(2)}) collective-permute-start(f32[64,512]{1,0:T(8,128)S(1)} %shard_map.110), channel_id=1, source_target_pairs={{0,32},{32,0},{1,33},{33,1},{2,34},{34,2},{3,35},{35,3},{4,36},{36... | collective-permute-start | bytes 393224 | tf_op jit(solution)/shard_map/ppermute | solution.py:292
  150.2 1.0 collective-permute-done.13
  (41 shorter events, 4.5 us)
Async XLA Ops:
  0.6 1.0 copy-start.3
  1.7 0.7 copy-start.7
  2.3 10.8 %copy-start.2 = (f32[128,1024]{1,0:T(8,128)S(1)}, f32[128,1024]{1,0:T(8,128)}, u32[]{:S(2)}) copy-start(f32[128,1024]{1,0:T(8,128)} %eig.1) | copy-start | bytes 1572868
  2.3 11.8 %copy-start.10 = (s32[128]{0:T(128)S(1)}, s32[128]{0:T(128)}, u32[]{:S(2)}) copy-start(s32[128]{0:T(128)} %param.17) | copy-start | bytes 1540
  2.3 11.8 %copy-start.11 = (s32[128,1]{0,1:T(1,128)S(1)}, s32[128,1]{0,1:T(1,128)}, u32[]{:S(2)}) copy-start(s32[128,1]{0,1:T(1,128)} %param.16) | copy-start | bytes 1540
  2.3 13.3 %copy-start.4 = (f32[1024,64]{0,1:T(8,128)S(1)}, f32[1024,64]{0,1:T(8,128)}, u32[]{:S(2)}) copy-start(f32[1024,64]{0,1:T(8,128)} %param.10) | copy-start | bytes 786436
  2.3 13.3 %copy-start.8 = (s32[64]{0:T(128)S(1)}, s32[64]{0:T(128)}, u32[]{:S(2)}) copy-start(s32[64]{0:T(128)} %param.11) | copy-start | bytes 772
  3.9 25.5 %all-to-all-start = ((f32[32,64,128]{2,1,0:T(8,128)}), f32[32,64,128]{2,1,0:T(8,128)S(1)}, u32[]{:S(2)}, u32[]{:S(2)}) async-start(f32[32,64,128]{2,1,0:T(8,128)} %get-tuple-element.15), calls=%async_computation | async-start | bytes 2097152 | tf_op jit(solution)/shard_map/all_to_all | solution.py:316
  13.1 2.6 %collective-permute-start = (f32[128,1024]{1,0:T(8,128)S(1)}, f32[128,1024]{1,0:T(8,128)S(1)}, u32[]{:S(2)}, u32[]{:S(2)}) collective-permute-start(f32[128,1024]{1,0:T(8,128)S(1)} %copy-done.2), channel_id=1, source_target_pairs={{0,32},{32,0},{1,33},{33,1},{2,34},{34,2},{3,35},{35,3},{4,36},{36... | collective-permute-start | bytes 1572872 | tf_op jit(solution)/shard_map/ppermute | solution.py:318
  14.2 1.5 %collective-permute-start.1 = (s32[1,128]{1,0:T(1,128)S(1)}, s32[1,128]{1,0:T(1,128)S(1)}, u32[]{:S(2)}, u32[]{:S(2)}) collective-permute-start(s32[1,128]{1,0:T(1,128)S(1)} %fusion.nys), channel_id=1, source_target_pairs={{0,32},{32,0},{1,33},{33,1},{2,34},{34,2},{3,35},{35,3},{4,36},{36... | collective-permute-start | bytes 1544 | tf_op jit(solution)/shard_map/ppermute | solution.py:319
  29.3 4.6 %copy-start.5 = (f32[512,128]{1,0:T(8,128)S(1)}, f32[512,128]{1,0:T(8,128)}, u32[]{:S(2)}) copy-start(f32[512,128]{1,0:T(8,128)} %centers.3) | copy-start | bytes 786436
  29.3 4.6 %copy-start.9 = (f32[512,64]{0,1:T(8,128)S(1)}, f32[512,64]{0,1:T(8,128)}, u32[]{:S(2)}) copy-start(f32[512,64]{0,1:T(8,128)} %param.13) | copy-start | bytes 393220
  29.3 22.8 %all-to-all-start.1 = ((f32[32,80,128]{2,1,0:T(8,128)}), f32[32,80,128]{2,1,0:T(8,128)S(1)}, u32[]{:S(2)}, u32[]{:S(2)}) async-start(f32[32,80,128]{2,1,0:T(8,128)} %get-tuple-element.16), calls=%async_computation.1 | async-start | bytes 2621440 | tf_op jit(solution)/shard_map/all_to_all | solution.py:328
  50.1 2.0 %copy-start = (bf16[2048,1024]{1,0:T(8,128)(2,1)}, bf16[2048,1024]{1,0:T(8,128)(2,1)S(1)}, u32[]{:S(2)}) copy-start(bf16[2048,1024]{1,0:T(8,128)(2,1)S(1)} %get-tuple-element.25.kern) | copy-start | bytes 12582916
  52.1 62.5 %collective-permute-start.2 = (f32[32,80,128]{2,1,0:T(8,128)S(1)}, f32[32,80,128]{2,1,0:T(8,128)S(1)}, u32[]{:S(2)}, u32[]{:S(2)}) collective-permute-start(f32[32,80,128]{2,1,0:T(8,128)S(1)} %all-to-all-done.1.near), channel_id=1, source_target_pairs={{0,64},{64,0},{1,65},{65,1},{2,66},{66,2},{3,67},{67,3},{4,68},{68... | collective-permute-start | bytes 3932168 | tf_op jit(solution)/shard_map/ppermute | solution.py:348
  106.0 2.2 %copy-start.1 = (bf16[2048,1024]{1,0:T(8,128)(2,1)S(1)}, bf16[2048,1024]{1,0:T(8,128)(2,1)}, u32[]{:S(2)}) copy-start(bf16[2048,1024]{1,0:T(8,128)(2,1)} %copy-done) | copy-start | bytes 12582916
  109.3 5.3 %collective-permute-start.3 = (f32[64,512]{1,0:T(8,128)S(1)}, f32[64,512]{1,0:T(8,128)S(1)}, u32[]{:S(2)}, u32[]{:S(2)}) collective-permute-start(f32[64,512]{1,0:T(8,128)S(1)} %shard_map.108), channel_id=1, source_target_pairs={{0,32},{32,0},{1,33},{33,1},{2,34},{34,2},{3,35},{35,3},{4,36},{36... | collective-permute-start | bytes 393224 | tf_op jit(solution)/shard_map/ppermute | solution.py:292
  116.4 30.0 %copy-start.6 = (f32[1024]{0:T(1024)S(1)}, f32[1024]{0:T(1024)}, u32[]{:S(2)}) copy-start(f32[1024]{0:T(1024)} %param.15) | copy-start | bytes 12292
  116.4 4.8 %collective-permute-start.6 = (f32[64,512]{1,0:T(8,128)S(1)}, f32[64,512]{1,0:T(8,128)S(1)}, u32[]{:S(2)}, u32[]{:S(2)}) collective-permute-start(f32[64,512]{1,0:T(8,128)S(1)} %shard_map.109), channel_id=1, source_target_pairs={{0,24},{8,0},{16,8},{24,16},{1,25},{9,1},{17,9},{25,17},{2,26},{10... | collective-permute-start | bytes 393224 | tf_op jit(solution)/shard_map/ppermute | solution.py:292
  117.1 5.9 %collective-permute-start.5 = (f32[64,512]{1,0:T(8,128)S(1)}, f32[64,512]{1,0:T(8,128)S(1)}, u32[]{:S(2)}, u32[]{:S(2)}) collective-permute-start(f32[64,512]{1,0:T(8,128)S(1)} %shard_map.109), channel_id=1, source_target_pairs={{0,16},{8,24},{16,0},{24,8},{1,17},{9,25},{17,1},{25,9},{2,18},{10... | collective-permute-start | bytes 393224 | tf_op jit(solution)/shard_map/ppermute | solution.py:292
  117.4 9.4 %collective-permute-start.4 = (f32[64,512]{1,0:T(8,128)S(1)}, f32[64,512]{1,0:T(8,128)S(1)}, u32[]{:S(2)}, u32[]{:S(2)}) collective-permute-start(f32[64,512]{1,0:T(8,128)S(1)} %shard_map.109), channel_id=1, source_target_pairs={{0,8},{8,16},{16,24},{24,0},{1,9},{9,17},{17,25},{25,1},{2,10},{10... | collective-permute-start | bytes 393224 | tf_op jit(solution)/shard_map/ppermute | solution.py:292
  126.9 4.6 %collective-permute-start.9 = (f32[64,512]{1,0:T(8,128)S(1)}, f32[64,512]{1,0:T(8,128)S(1)}, u32[]{:S(2)}, u32[]{:S(2)}) collective-permute-start(f32[64,512]{1,0:T(8,128)S(1)} %add_add_fusion.2), channel_id=1, source_target_pairs={{0,6},{2,0},{4,2},{6,4},{1,7},{3,1},{5,3},{7,5},{8,14},{10,8},{12,... | collective-permute-start | bytes 393224 | tf_op jit(solution)/shard_map/ppermute | solution.py:292
  127.5 5.3 %collective-permute-start.8 = (f32[64,512]{1,0:T(8,128)S(1)}, f32[64,512]{1,0:T(8,128)S(1)}, u32[]{:S(2)}, u32[]{:S(2)}) collective-permute-start(f32[64,512]{1,0:T(8,128)S(1)} %add_add_fusion.2), channel_id=1, source_target_pairs={{0,4},{2,6},{4,0},{6,2},{1,5},{3,7},{5,1},{7,3},{8,12},{10,14},{12... | collective-permute-start | bytes 393224 | tf_op jit(solution)/shard_map/ppermute | solution.py:292
  128.9 7.8 %collective-permute-start.7 = (f32[64,512]{1,0:T(8,128)S(1)}, f32[64,512]{1,0:T(8,128)S(1)}, u32[]{:S(2)}, u32[]{:S(2)}) collective-permute-start(f32[64,512]{1,0:T(8,128)S(1)} %add_add_fusion.2), channel_id=1, source_target_pairs={{0,2},{2,4},{4,6},{6,0},{1,3},{3,5},{5,7},{7,1},{8,10},{10,12},{12... | collective-permute-start | bytes 393224 | tf_op jit(solution)/shard_map/ppermute | solution.py:292
  136.7 9.6 %collective-permute-start.12 = (f32[64,512]{1,0:T(8,128)S(1)}, f32[64,512]{1,0:T(8,128)S(1)}, u32[]{:S(2)}, u32[]{:S(2)}) collective-permute-start(f32[64,512]{1,0:T(8,128)S(1)} %add_add_fusion.1), channel_id=1, source_target_pairs={{0,65},{1,64},{64,1},{65,0},{2,67},{3,66},{66,3},{67,2},{4,69},{5,... | collective-permute-start | bytes 393224 | tf_op jit(solution)/shard_map/ppermute | solution.py:292
  136.8 9.5 %collective-permute-start.11 = (f32[64,512]{1,0:T(8,128)S(1)}, f32[64,512]{1,0:T(8,128)S(1)}, u32[]{:S(2)}, u32[]{:S(2)}) collective-permute-start(f32[64,512]{1,0:T(8,128)S(1)} %add_add_fusion.1), channel_id=1, source_target_pairs={{0,64},{1,65},{64,0},{65,1},{2,66},{3,67},{66,2},{67,3},{4,68},{5,... | collective-permute-start | bytes 393224 | tf_op jit(solution)/shard_map/ppermute | solution.py:292
  139.5 6.9 %collective-permute-start.10 = (f32[64,512]{1,0:T(8,128)S(1)}, f32[64,512]{1,0:T(8,128)S(1)}, u32[]{:S(2)}, u32[]{:S(2)}) collective-permute-start(f32[64,512]{1,0:T(8,128)S(1)} %add_add_fusion.1), channel_id=1, source_target_pairs={{0,1},{1,0},{64,65},{65,64},{2,3},{3,2},{66,67},{67,66},{4,5},{5,4... | collective-permute-start | bytes 393224 | tf_op jit(solution)/shard_map/ppermute | solution.py:292
  140.0 10.2 %collective-permute-start.14 = (f32[64,512]{1,0:T(8,128)S(1)}, f32[64,512]{1,0:T(8,128)S(1)}, u32[]{:S(2)}, u32[]{:S(2)}) collective-permute-start(f32[64,512]{1,0:T(8,128)S(1)} %add.40.grads), channel_id=1, source_target_pairs={{0,64},{64,0},{1,65},{65,1},{2,66},{66,2},{3,67},{67,3},{4,68},{68... | collective-permute-start | bytes 393224 | tf_op jit(solution)/shard_map/ppermute | solution.py:292
  147.8 3.4 %collective-permute-start.13 = (f32[64,512]{1,0:T(8,128)S(1)}, f32[64,512]{1,0:T(8,128)S(1)}, u32[]{:S(2)}, u32[]{:S(2)}) collective-permute-start(f32[64,512]{1,0:T(8,128)S(1)} %shard_map.110), channel_id=1, source_target_pairs={{0,32},{32,0},{1,33},{33,1},{2,34},{34,2},{3,35},{35,3},{4,36},{36... | collective-permute-start | bytes 393224 | tf_op jit(solution)/shard_map/ppermute | solution.py:292

commit v3 on v2

--- a/solution.py
+++ b/solution.py
@@ -16,6 +16,7 @@
 SIZES = {"zh": 2, "core": 2, "x": 4, "y": 4, "zl": 2}
 ALL = ("zh", "core", "x", "y", "zl")
 CENTERS = ("x", "y", "zl")
+GROUP = ("zh", "core")
 VMEM = pl.BlockSpec(memory_space=pltpu.VMEM)
 
 ACOS_FULL = (
@@ -106,39 +107,52 @@
         send[o] = unit
 
 
-def vectors_body(core, pool_t, index, eig, mate_eig, nys, mate_nys, send, targ, *, cdev):
+def quarters_body(member, eig, nys, *outs):
+    count, q = eig.shape
+    part = q // len(outs)
+    row = jnp.broadcast_to(nys[...].astype(F32), (8, count))
+    row = jnp.concatenate([row] * (part // count), axis=1)
+    for o, out in enumerate(outs):
+        mate = member[0] ^ o
+        out[0:count, :] = eig[:, pl.ds(pl.multiple_of(mate * part, part), part)]
+        out[count:, :] = row
+
+
+def vectors_body(pool_t, index, *refs, cdev):
+    tables, (send, targ) = refs[:-2], refs[-2:]
     hot = rows_hot(index[...], pool_t.shape[1])
     targets = pick(hot, pool_t[...], NT, flip=True).T
     half = targets.shape[0] // 2
     targ[...] = jnp.concatenate([targets[:half], targets[half:]], axis=1)
-    count, q = eig.shape
-    part = q // 2
+    count, part = tables[0].shape[0] - 8, tables[0].shape[1]
     peers = send.shape[0]
-    blocks = part // 128
-    mine = pl.ds(pl.multiple_of(core[0] * part, part), part)
+    blocks, group, lanes = part // 128, CAP * len(tables), 128 // len(tables)
     earlier = lax.broadcasted_iota(jnp.int32, (count, count), 0) < lax.broadcasted_iota(
         jnp.int32, (count, count), 1
     )
-    for table, (vec, where) in enumerate(((eig, nys), (mate_eig, mate_nys))):
-        owner = where[...] // cdev
-        offset = where[...] - owner * cdev
+    shared = []
+    for t, table in enumerate(tables):
+        nys = table[count : count + 1, 0:count].astype(jnp.int32)
+        owner = nys // cdev
+        offset = nys - owner * cdev
         row = jnp.broadcast_to(owner.astype(F32), (count, count))
         same = jnp.where(row.T == row, 1.0, 0.0)
         rank = jnp.sum(jnp.where(earlier, same, 0.0), axis=0, keepdims=True).astype(jnp.int32)
         place = owner * CAP + rank == lax.broadcasted_iota(jnp.int32, (peers * CAP, count), 0)
         offs = jnp.sum(jnp.where(place, offset.astype(F32), 0.0), axis=1, keepdims=True)
-        offs = jnp.broadcast_to(offs, (peers * CAP, 128))
-        vectors = pick(place.astype(BF), vec[:, mine], NN)
+        shared.append(jnp.broadcast_to(offs, (peers * CAP, lanes)))
+        vectors = pick(place.astype(BF), table[0:count, :], NN)
         for o in range(peers):
             own = slice(o * CAP, (o + 1) * CAP)
             for j in range(blocks):
-                at = CAP * (2 * j + table)
+                at = group * j + CAP * t
                 send[o, at : at + CAP, :] = vectors[own, 128 * j : 128 * (j + 1)]
-            at = CAP * (2 * blocks + table)
-            send[o, at : at + CAP, :] = offs[own]
-
-
-def kernel_body(recv, centers, weights, kern, pred, cen, wts, cos_a, cos_b, lhs, *, block, sub):
+    shared = jnp.concatenate(shared, axis=1)
+    for o in range(peers):
+        send[o, group * blocks :, :] = shared[o * CAP : (o + 1) * CAP]
+
+
+def kernel_body(recv, centers, weights, khi, klo, pred, cen, wts, cos_a, cos_b, lhs, *, block, sub):
     src, rows, dim = recv.shape
     out, count = weights.shape
     b = centers[...]
@@ -147,7 +161,7 @@
     cen[...] = jnp.concatenate([b1, b1, b2, b2, b3, b1], axis=1)
     w1, w2 = split2(weights[...].T * sb)
     w = jnp.concatenate([w1, w2], axis=1)
-    wts[...] = jnp.concatenate([w, w], axis=0)
+    wts[...] = w
     blocks, group = src * rows // block, block // rows
 
     def stage(i):
@@ -161,11 +175,12 @@
     def elementwise(i, values, n):
         at = pl.ds(pl.multiple_of(i * block + n * sub, sub), sub)
         hi, lo = split2(ntk_over_scale(values[n * sub : (n + 1) * sub, :]))
-        kern[at, :count] = hi
-        kern[at, count:] = lo
+        khi[at, :] = hi
+        klo[at, :] = lo
 
     def predict(i):
-        both = mm(kern[pl.ds(pl.multiple_of(i * block, block), block), :], wts[...], NN)
+        at = pl.ds(pl.multiple_of(i * block, block), block)
+        both = mm(khi[at, :], wts[...], NN) + mm(klo[at, :], wts[...], NN)
         total = (both[:, :out] + both[:, out:]).reshape(group, 2, rows // 2, out)
         pred[pl.ds(i * group, group)] = jnp.concatenate([total[:, 0], total[:, 1]], axis=2)
 
@@ -206,53 +221,61 @@
         send[o] = ready
 
 
-def grads_body(resid, kern, centers, grads):
+def grads_body(resid, khi, klo, centers, grads):
     src, half, wide = resid.shape
-    out, count = grads.shape
+    out = grads.shape[0]
     r = resid[...]
     r = jnp.concatenate([r[:, :, :out], r[:, :, out:]], axis=1).reshape(src * half * 2, out)
     r1, r2 = split2(r.T)
-    both = mm(jnp.concatenate([r1, r2], axis=0), kern[...], NN)
-    both = both[:out] + both[out:]
+    rr = jnp.concatenate([r1, r2], axis=0)
+    both = mm(rr, khi[...], NN) + mm(rr, klo[...], NN)
     b = centers[...]
     nb = full_nt(jnp.ones((8, b.shape[1]), F32), b * b)[0:1] * (1.0 / b.shape[1]) + EPS
-    grads[...] = (both[:, :count] + both[:, count:]) * jnp.sqrt(nb)
-
-
-def unpack(recv, n):
-    peers = recv.shape[0]
-    return recv[:, 2 * CAP * n : 2 * CAP * (n + 1), :].reshape(peers * 2 * CAP, 128)
-
-
-def points_hot(tables, blocks, width):
-    offs = jnp.concatenate([unpack(t, blocks) for t in tables], axis=0)
+    grads[...] = (both[:out] + both[out:]) * jnp.sqrt(nb)
+
+
+def block_of(points, j, tables):
+    peers, group = points.shape[0], CAP * tables
+    return points[:, group * j : group * (j + 1), :].reshape(peers * group, 128)
+
+
+def points_hot(points, blocks, tables, width):
+    peers, lanes = points.shape[0], 128 // tables
+    offs = points[:, CAP * tables * blocks :, :]
+    offs = jnp.concatenate(
+        [
+            jnp.broadcast_to(offs[:, :, lanes * t : lanes * t + 1], (peers, CAP, 128))
+            for t in range(tables)
+        ],
+        axis=1,
+    ).reshape(peers * CAP * tables, 128)
     lane = lax.broadcasted_iota(jnp.int32, offs.shape, 1).astype(F32)
     return jnp.concatenate(
         [(offs == lane + float(128 * k)).astype(BF) for k in range(width // 128)], axis=1
     )
 
 
-def coeff_body(near, far, grads, coeff):
+def coeff_body(points, grads, coeff, *, tables):
     out, part = coeff.shape
     blocks = part // 128
-    hot = points_hot((near, far), blocks, grads.shape[1])
+    hot = points_hot(points, blocks, tables, grads.shape[1])
     g1, g2 = split2(pick(hot, grads[...], NT, flip=True))
     gg = jnp.concatenate([g1, g2], axis=0)
     for j in range(blocks):
-        e1, e2 = split2(jnp.concatenate([unpack(near, j), unpack(far, j)], axis=0))
+        e1, e2 = split2(block_of(points, j, tables))
         both = mm(gg, e1, NN) + mm(gg, e2, NN)
         coeff[:, 128 * j : 128 * (j + 1)] = both[:out] + both[out:]
 
 
-def corr_body(core, near, far, coeff, eig_scale, corr):
+def corr_body(member, points, coeff, eig_scale, corr, *, tables):
     out, part = coeff.shape
     blocks = part // 128
-    hot = points_hot((near, far), blocks, corr.shape[1])
+    hot = points_hot(points, blocks, tables, corr.shape[1])
     total = jnp.zeros((2 * out, hot.shape[0]), F32)
     for j in range(blocks):
         at = slice(128 * j, 128 * (j + 1))
-        e1, e2 = split2(jnp.concatenate([unpack(near, j), unpack(far, j)], axis=0))
-        scale = eig_scale[:, pl.ds(pl.multiple_of(core[0] * part + 128 * j, 128), 128)]
+        e1, e2 = split2(block_of(points, j, tables))
+        scale = eig_scale[:, pl.ds(pl.multiple_of(member[0] * part + 128 * j, 128), 128)]
         c1, c2 = split2(coeff[:, at] * scale)
         cc = jnp.concatenate([c1, c2], axis=0)
         total = total + mm(cc, e1, NT) + mm(cc, e2, NT)
@@ -303,10 +326,10 @@
     count, q = eig_vectors.shape
     half = rows // 2
     norm = 1.0 / math.sqrt(rows * peers * SIZES["zh"] * SIZES["core"])
-    swap = [(0, 1), (1, 0)]
-    core = lax.axis_index("core").astype(jnp.int32)[None]
     index = batch_index.reshape(1, rows)
     nys = (nys_owner.reshape(count) * cdev + nys_offset).reshape(1, count)
+    tables = SIZES[GROUP[0]] * SIZES[GROUP[1]]
+    member = lax.axis_index(GROUP).astype(jnp.int32)[None]
 
     send, scale = call(
         features_body,
@@ -315,26 +338,31 @@
     )
     recv = lax.all_to_all(send, CENTERS, split_axis=0, concat_axis=0, tiled=True)
 
-    mate_eig = lax.ppermute(eig_vectors, "core", swap)
-    mate_nys = lax.ppermute(nys, "core", swap)
-    piece = 2 * CAP * (q // 256 + 1)
+    parted = call(
+        quarters_body, [shape(count + 8, q // tables)] * tables,
+        member, eig_vectors, nys, scalars=1,
+    )
+    parted = [parted[0]] + [
+        lax.ppermute(part, GROUP, [(i, i ^ o) for i in range(tables)])
+        for o, part in enumerate(parted) if o
+    ]
+    piece = CAP * (tables * (q // tables // 128) + 1)
     points, targ = call(
         functools.partial(vectors_body, cdev=cdev),
         [shape(peers, piece, 128), shape(half, 2 * out)],
-        core, pool_targets.T, index, eig_vectors, mate_eig, nys, mate_nys,
-        scalars=1,
+        pool_targets.T, index, *parted,
     )
     points, recv = lax.optimization_barrier((points, recv))
-    near = lax.all_to_all(points, CENTERS, split_axis=0, concat_axis=0, tiled=True)
+    points = lax.all_to_all(points, CENTERS, split_axis=0, concat_axis=0, tiled=True)
 
     block = 4 * rows
-    kern, pred = call(
+    khi, klo, pred = call(
         functools.partial(kernel_body, block=block, sub=32),
-        [shape(peers * rows, 2 * cdev, dtype=BF), shape(peers, half, 2 * out)],
+        [shape(peers * rows, cdev, dtype=BF)] * 2 + [shape(peers, half, 2 * out)],
         recv, centers, weights.T,
         scratch_shapes=[
             pltpu.VMEM((cdev, 6 * dim), BF),
-            pltpu.VMEM((2 * cdev, 2 * out), BF),
+            pltpu.VMEM((cdev, 2 * out), BF),
             pltpu.VMEM((block, cdev), F32),
             pltpu.VMEM((block, cdev), F32),
             pltpu.VMEM((block, 6 * dim), BF),
@@ -344,8 +372,7 @@
         ),
     )
 
-    near, pred = lax.optimization_barrier((near, pred))
-    far = lax.ppermute(near, "zh", swap)
+    points, pred = lax.optimization_barrier((points, pred))
     parts = lax.all_to_all(pred, CENTERS, split_axis=0, concat_axis=0, tiled=True)
     resid, ready = call(
         functools.partial(residual_body, norm=norm),
@@ -353,17 +380,22 @@
         parts, targ, scale,
     )
     every = lax.all_to_all(ready, CENTERS, split_axis=0, concat_axis=0, tiled=True)
-    grads = call(grads_body, shape(out, cdev), every, kern, centers)
-    grads = exchange(grads, ("core",))
-    coeff = call(coeff_body, shape(out, q // 2), near, far, grads)
-    coeff = exchange(coeff, ("x",))
-    coeff = exchange(coeff, ("y",))
-    coeff = exchange(coeff, ("zh", "zl"))
+    grads = call(grads_body, shape(out, cdev), every, khi, klo, centers)
+    for axis in GROUP[::-1]:
+        grads = exchange(grads, (axis,))
+    coeff = call(
+        functools.partial(coeff_body, tables=tables), shape(out, q // tables), points, grads
+    )
+    for axis in CENTERS:
+        coeff = exchange(coeff, (axis,))
     corr = call(
-        corr_body, shape(out, cdev), core, near, far, coeff, eig_scale[None, :], scalars=1
-    )
-    update = exchange(corr, ("core",)) - exchange(grads, ("zh",))
-    return resid, update.T
+        functools.partial(corr_body, tables=tables),
+        shape(out, cdev), member, points, coeff, eig_scale[None, :],
+        scalars=1,
+    )
+    for axis in GROUP[::-1]:
+        corr = exchange(corr, (axis,))
+    return resid, (corr - grads).T
 
 
 def solution(mesh):

time: 152 us -> 144 us (0.947)
  blocking collectives: 49.8 us -> 32.1 us
  waiting for transfers between devices: 36.8 us -> 41 us
  starting transfers between devices: 33.2 us -> 36.2 us
  local copies, waits for them, and re-layouts: 5.87 us -> 8.3 us
    ppermute x3, waiting for transfers between devices: 1.42 us -> 17.7 us  [per_device(): lax.ppermute(part, GROUP, [(i, i ^ o) for i in range(tables)])]
    all_to_all x1, blocking collectives: 32.6 us -> 18.4 us  [per_device(): lax.all_to_all(pred, CENTERS, split_axis=0, concat_axis=0, tiled=True)]
    all_to_all x1, waiting for transfers between devices: 11.7 us -> 0.01 us  [per_device(): lax.all_to_all(send, CENTERS, split_axis=0, concat_axis=0, tiled=True)]
    all_to_all x1, blocking collectives: 17.2 us -> 13.7 us  [per_device(): lax.all_to_all(ready, CENTERS, split_axis=0, concat_axis=0, tiled=True)]
    unnamed x24 -> x32, local copies, waits for them, and re-layouts: 5.87 us -> 8.3 us
    all_to_all x1, starting transfers between devices: 4.62 us -> 6.52 us  [per_device(): lax.all_to_all(points, CENTERS, split_axis=0, concat_axis=0, tiled=True)]
    ppermute x12 -> x11, starting transfers between devices: 14.9 us -> 16 us  [exchange(): total = total + lax.ppermute(v, axes, perm)]
    pallas_call x7 -> x8, Pallas kernels: 24.5 us -> 23.9 us  [call(): pl.pallas_call(body, out_shape=outs, in_specs=[smem] * scalars + [VMEM] *...]
  transfers between devices with their start and end apart: 17 -> 16, of which waited for: 11 -> 13; matrix products, arithmetic and copies ran while one was open for 0% -> 0% of each run, Pallas kernels for 14% -> 13%
where the time goes in v3:
time: 144 us; the launch traced here: 143 us
  waiting for transfers between devices  41 us (28%)
  starting transfers between devices  36.2 us (25%)
  blocking collectives  32.1 us (22%)
  Pallas kernels  23.9 us (17%)
  local copies, waits for them, and re-layouts  8.3 us (6%)
    pallas_call x8, Pallas kernels, call(): pl.pallas_call(body, out_shape=outs, in_specs=[smem] * scalars + [VMEM] *...  23.9 us
    ppermute x11, waiting for transfers between devices, exchange(): total = total + lax.ppermute(v, axes, perm)  23.3 us
    all_to_all x1, blocking collectives, per_device(): lax.all_to_all(pred, CENTERS, split_axis=0, concat_axis=0, tiled=True)  18.4 us
    ppermute x3, waiting for transfers between devices, per_device(): lax.ppermute(part, GROUP, [(i, i ^ o) for i in range(tables)])  17.7 us
    ppermute x11, starting transfers between devices, exchange(): total = total + lax.ppermute(v, axes, perm)  16 us
    all_to_all x1, blocking collectives, per_device(): lax.all_to_all(ready, CENTERS, split_axis=0, concat_axis=0, tiled=True)  13.7 us
    all_to_all x1, starting transfers between devices, per_device(): lax.all_to_all(send, CENTERS, split_axis=0, concat_axis=0, tiled=True)  9.23 us
    unnamed x32, local copies, waits for them, and re-layouts  8.3 us
  transfers between devices with their start and end apart: 16, of which 13 were waited for; matrix products, arithmetic and copies ran while one was open for 0% of the time, Pallas kernels for 13%

profile of v3, /device:TPU:1, one launch (start us, length us, event | category | flops | bytes accessed | tf_op | source)
XLA Modules:
  0.0 143.1 jit_solution(14925382327144284749)
XLA Ops:
  0.7 1.0 copy-done.4
  2.4 1.5 %shard_map.106 = (f32[32,64,128]{2,1,0:T(8,128)}, f32[32,128]{1,0:T(8,128)S(1)}) custom-call(f32[1024,128]{1,0:T(8,128)S(1)} %copy-done.4, s32[1,64]{1,0:T(1,128)S(1)} %bitcast.15), custom_call_target="tpu_custom_call" | custom-call | tf_op jit(solution)/shard_map/pallas_call | solution.py:296
  3.9 9.2 %all-to-all-start = ((f32[32,64,128]{2,1,0:T(8,128)}), f32[32,64,128]{2,1,0:T(8,128)S(1)}, u32[]{:S(2)}, u32[]{:S(2)}) async-start(f32[32,64,128]{2,1,0:T(8,128)} %get-tuple-element.24), calls=%async_computation | async-start | bytes 2097152 | tf_op jit(solution)/shard_map/all_to_all | solution.py:339
  13.2 1.0 collective-permute-start
  14.2 3.3 %collective-permute-start.1 = (f32[136,256]{1,0:T(8,128)S(1)}, f32[136,256]{1,0:T(8,128)S(1)}, u32[]{:S(2)}, u32[]{:S(2)}) collective-permute-start(f32[136,256]{1,0:T(8,128)S(1)} %get-tuple-element.21), channel_id=1, source_target_pairs={{0,64},{32,96},{64,0},{96,32},{1,65},{33,97},{65,1},{97,33},{2,66}... | collective-permute-start | bytes 417800 | tf_op jit(solution)/shard_map/ppermute | solution.py:346
  17.6 11.4 %collective-permute-done.1.refs_2_ = f32[136,256]{1,0:T(8,128)S(1)} collective-permute-done((f32[136,256]{1,0:T(8,128)S(1)}, f32[136,256]{1,0:T(8,128)S(1)}, u32[]{:S(2)}, u32[]{:S(2)}) %collective-permute-start.1) | collective-permute-done | bytes 139296 | tf_op jit(solution)/shard_map/ppermute | solution.py:346
  29.0 6.3 %collective-permute-done.2.refs_3_ = f32[136,256]{1,0:T(8,128)S(1)} collective-permute-done((f32[136,256]{1,0:T(8,128)S(1)}, f32[136,256]{1,0:T(8,128)S(1)}, u32[]{:S(2)}, u32[]{:S(2)}) %collective-permute-start.2) | collective-permute-done | bytes 139296 | tf_op jit(solution)/shard_map/ppermute | solution.py:346
  35.3 1.8 %shard_map.105 = (f32[32,72,128]{2,1,0:T(8,128)}, f32[32,128]{1,0:T(8,128)S(1)}) custom-call(f32[64,1024]{1,0:T(8,128)S(1)} %bitcast.13, s32[1,64]{1,0:T(1,128)S(1)} %bitcast.16, f32[136,256]{1,0:T(8,128)S(1)} %get-tuple-element.19.refs_0_, f32[136,256]{1,0:T(8,128)S(1)} %collective-permute-done.refs_1_, f32[136,256]{1,0:T(8,128)S(1)} %collective-permute-done.1.refs_2_, ...), custom_call_target="tpu_custom_call" | custom-call | tf_op jit(solution)/shard_map/pallas_call | solution.py:296
  38.8 6.5 %all-to-all-start.1 = ((f32[32,72,128]{2,1,0:T(8,128)}), f32[32,72,128]{2,1,0:T(8,128)S(1)}, u32[]{:S(2)}, u32[]{:S(2)}) async-start(f32[32,72,128]{2,1,0:T(8,128)} %get-tuple-element.25), calls=%async_computation.1 | async-start | bytes 2359296 | tf_op jit(solution)/shard_map/all_to_all | solution.py:356
  45.3 1.2 copy-done.3
  47.4 16.0 %shard_map.107 = (bf16[2048,512]{1,0:T(8,128)(2,1)S(1)}, bf16[2048,512]{1,0:T(8,128)(2,1)S(1)}, f32[32,32,128]{2,1,0:T(8,128)S(1)}) custom-call(f32[32,64,128]{2,1,0:T(8,128)S(1)} %copy-done.3, f32[512,128]{1,0:T(8,128)S(1)} %copy-done.7, f32[64,512]{1,0:T(8,128)S(1)} %bitcast.17), custom_call_target="tpu_custom_call" | custom-call | flops 40000000000 | bytes 4194304 | tf_op jit(solution)/shard_map/pallas_call | solution.py:296
  63.5 1.4 copy-done
  65.6 18.4 %all_to_all.20.parts = f32[32,32,128]{2,1,0:T(8,128)S(1)} all-to-all(f32[32,32,128]{2,1,0:T(8,128)} %copy-done.6), channel_id=1, replica_groups=mesh['zh'=2,'core'=2,'x'=4,'y'=4,'zl'=2] {'x','y','zl'}, dimensions={0} | all-to-all | bytes 1048576 | tf_op jit(solution)/shard_map/all_to_all | solution.py:376
  85.5 13.7 %all_to_all.21.resid = f32[32,32,128]{2,1,0:T(8,128)S(1)} all-to-all(f32[32,32,128]{2,1,0:T(8,128)S(1)} %get-tuple-element.33), channel_id=1, replica_groups=mesh['zh'=2,'core'=2,'x'=4,'y'=4,'zl'=2] {'x','y','zl'}, dimensions={0} | all-to-all | bytes 1048576 | tf_op jit(solution)/shard_map/all_to_all | solution.py:382
  99.2 1.1 shard_map.109
  100.3 3.2 %collective-permute-start.3 = (f32[64,512]{1,0:T(8,128)S(1)}, f32[64,512]{1,0:T(8,128)S(1)}, u32[]{:S(2)}, u32[]{:S(2)}) collective-permute-start(f32[64,512]{1,0:T(8,128)S(1)} %shard_map.109), channel_id=1, source_target_pairs={{0,32},{32,0},{1,33},{33,1},{2,34},{34,2},{3,35},{35,3},{4,36},{36... | collective-permute-start | bytes 393224 | tf_op jit(solution)/shard_map/ppermute | solution.py:315
  103.5 1.0 collective-permute-done.3
  104.5 1.0 collective-permute-start.4
  105.5 5.3 %collective-permute-done.4 = f32[64,512]{1,0:T(8,128)S(1)} collective-permute-done((f32[64,512]{1,0:T(8,128)S(1)}, f32[64,512]{1,0:T(8,128)S(1)}, u32[]{:S(2)}, u32[]{:S(2)}) %collective-permute-start.4) | collective-permute-done | bytes 131104 | tf_op jit(solution)/shard_map/ppermute | solution.py:315
  110.8 1.6 %shard_map.110 = f32[64,256]{1,0:T(8,128)S(1)} custom-call(f32[32,72,128]{2,1,0:T(8,128)S(1)} %all-to-all-done.1.points, f32[64,512]{1,0:T(8,128)S(1)} %add.42.grads), custom_call_target="tpu_custom_call" | custom-call | tf_op jit(solution)/shard_map/pallas_call | solution.py:296
  114.0 1.6 %collective-permute-done.7 = f32[64,256]{1,0:T(8,128)S(1)} collective-permute-done((f32[64,256]{1,0:T(8,128)S(1)}, f32[64,256]{1,0:T(8,128)S(1)}, u32[]{:S(2)}, u32[]{:S(2)}) %collective-permute-start.7) | collective-permute-done | bytes 65568 | tf_op jit(solution)/shard_map/ppermute | solution.py:315
  115.6 2.2 %collective-permute-done.6 = f32[64,256]{1,0:T(8,128)S(1)} collective-permute-done((f32[64,256]{1,0:T(8,128)S(1)}, f32[64,256]{1,0:T(8,128)S(1)}, u32[]{:S(2)}, u32[]{:S(2)}) %collective-permute-start.6) | collective-permute-done | bytes 65568 | tf_op jit(solution)/shard_map/ppermute | solution.py:315
  119.2 1.3 collective-permute-start.9
  121.6 2.2 %collective-permute-done.9 = f32[64,256]{1,0:T(8,128)S(1)} collective-permute-done((f32[64,256]{1,0:T(8,128)S(1)}, f32[64,256]{1,0:T(8,128)S(1)}, u32[]{:S(2)}, u32[]{:S(2)}) %collective-permute-start.9) | collective-permute-done | bytes 65568 | tf_op jit(solution)/shard_map/ppermute | solution.py:315
  123.8 1.0 collective-permute-done.8
  124.8 1.0 collective-permute-start.11
  125.9 2.2 %collective-permute-done.11 = f32[64,256]{1,0:T(8,128)S(1)} collective-permute-done((f32[64,256]{1,0:T(8,128)S(1)}, f32[64,256]{1,0:T(8,128)S(1)}, u32[]{:S(2)}, u32[]{:S(2)}) %collective-permute-start.11) | collective-permute-done | bytes 65568 | tf_op jit(solution)/shard_map/ppermute | solution.py:315
  128.1 1.1 shard_map.111
  129.2 5.9 %collective-permute-start.12 = (f32[64,512]{1,0:T(8,128)S(1)}, f32[64,512]{1,0:T(8,128)S(1)}, u32[]{:S(2)}, u32[]{:S(2)}) collective-permute-start(f32[64,512]{1,0:T(8,128)S(1)} %shard_map.111), channel_id=1, source_target_pairs={{0,32},{32,0},{1,33},{33,1},{2,34},{34,2},{3,35},{35,3},{4,36},{36... | collective-permute-start | bytes 393224 | tf_op jit(solution)/shard_map/ppermute | solution.py:315
  135.1 1.0 collective-permute-done.12
  136.1 1.0 collective-permute-start.13
  137.0 5.3 %collective-permute-done.13 = f32[64,512]{1,0:T(8,128)S(1)} collective-permute-done((f32[64,512]{1,0:T(8,128)S(1)}, f32[64,512]{1,0:T(8,128)S(1)}, u32[]{:S(2)}, u32[]{:S(2)}) %collective-permute-start.13) | collective-permute-done | bytes 131104 | tf_op jit(solution)/shard_map/ppermute | solution.py:315
  (50 shorter events, 10.4 us)
Async XLA Ops:
  0.6 12.5 %copy-start.14 = (s32[128]{0:T(128)S(1)}, s32[128]{0:T(128)}, u32[]{:S(2)}) copy-start(s32[128]{0:T(128)} %param.17) | copy-start | bytes 1540
  0.6 12.5 %copy-start.15 = (s32[128,1]{0,1:T(1,128)S(1)}, s32[128,1]{0,1:T(1,128)}, u32[]{:S(2)}) copy-start(s32[128,1]{0,1:T(1,128)} %param.16) | copy-start | bytes 1540
  0.7 1.1 copy-start.4
  1.7 0.7 copy-start.12
  2.4 10.8 %copy-start.5 = (f32[128,1024]{1,0:T(8,128)S(1)}, f32[128,1024]{1,0:T(8,128)}, u32[]{:S(2)}) copy-start(f32[128,1024]{1,0:T(8,128)} %eig.1) | copy-start | bytes 1572868
  2.4 33.0 %copy-start.8 = (f32[1024,64]{0,1:T(8,128)S(1)}, f32[1024,64]{0,1:T(8,128)}, u32[]{:S(2)}) copy-start(f32[1024,64]{0,1:T(8,128)} %param.10) | copy-start | bytes 786436
  3.9 33.9 %all-to-all-start = ((f32[32,64,128]{2,1,0:T(8,128)}), f32[32,64,128]{2,1,0:T(8,128)S(1)}, u32[]{:S(2)}, u32[]{:S(2)}) async-start(f32[32,64,128]{2,1,0:T(8,128)} %get-tuple-element.24), calls=%async_computation | async-start | bytes 2097152 | tf_op jit(solution)/shard_map/all_to_all | solution.py:339
  13.1 32.2 %copy-start.7 = (f32[512,128]{1,0:T(8,128)S(1)}, f32[512,128]{1,0:T(8,128)}, u32[]{:S(2)}) copy-start(f32[512,128]{1,0:T(8,128)} %centers.3) | copy-start | bytes 786436
  13.2 4.4 %collective-permute-start = (f32[136,256]{1,0:T(8,128)S(1)}, f32[136,256]{1,0:T(8,128)S(1)}, u32[]{:S(2)}, u32[]{:S(2)}) collective-permute-start(f32[136,256]{1,0:T(8,128)S(1)} %get-tuple-element.20), channel_id=1, source_target_pairs={{0,32},{32,0},{64,96},{96,64},{1,33},{33,1},{65,97},{97,65},{2,34}... | collective-permute-start | bytes 417800 | tf_op jit(solution)/shard_map/ppermute | solution.py:346
  14.2 14.8 %collective-permute-start.1 = (f32[136,256]{1,0:T(8,128)S(1)}, f32[136,256]{1,0:T(8,128)S(1)}, u32[]{:S(2)}, u32[]{:S(2)}) collective-permute-start(f32[136,256]{1,0:T(8,128)S(1)} %get-tuple-element.21), channel_id=1, source_target_pairs={{0,64},{32,96},{64,0},{96,32},{1,65},{33,97},{65,1},{97,33},{2,66}... | collective-permute-start | bytes 417800 | tf_op jit(solution)/shard_map/ppermute | solution.py:346
  17.6 17.8 %collective-permute-start.2 = (f32[136,256]{1,0:T(8,128)S(1)}, f32[136,256]{1,0:T(8,128)S(1)}, u32[]{:S(2)}, u32[]{:S(2)}) collective-permute-start(f32[136,256]{1,0:T(8,128)S(1)} %get-tuple-element.22), channel_id=1, source_target_pairs={{0,96},{32,64},{64,32},{96,0},{1,97},{33,65},{65,33},{97,1},{2,98}... | collective-permute-start | bytes 417800 | tf_op jit(solution)/shard_map/ppermute | solution.py:346
  37.2 0.6 copy-start.9
  37.8 1.0 copy-start.2
  38.8 26.9 %all-to-all-start.1 = ((f32[32,72,128]{2,1,0:T(8,128)}), f32[32,72,128]{2,1,0:T(8,128)S(1)}, u32[]{:S(2)}, u32[]{:S(2)}) async-start(f32[32,72,128]{2,1,0:T(8,128)} %get-tuple-element.25), calls=%async_computation.1 | async-start | bytes 2359296 | tf_op jit(solution)/shard_map/all_to_all | solution.py:356
  45.3 1.2 copy-start.3
  46.5 0.9 copy-start.13
  63.5 1.4 copy-start
  64.8 0.8 copy-start.6
  65.6 33.6 %copy-start.1 = (bf16[2048,512]{1,0:T(8,128)(2,1)S(1)}, bf16[2048,512]{1,0:T(8,128)(2,1)}, u32[]{:S(2)}) copy-start(bf16[2048,512]{1,0:T(8,128)(2,1)} %copy-done) | copy-start | bytes 6291460
  84.0 0.7 copy-start.10
  100.3 27.8 %copy-start.11 = (f32[1024]{0:T(1024)S(1)}, f32[1024]{0:T(1024)}, u32[]{:S(2)}) copy-start(f32[1024]{0:T(1024)} %param.15) | copy-start | bytes 12292
  100.3 4.2 %collective-permute-start.3 = (f32[64,512]{1,0:T(8,128)S(1)}, f32[64,512]{1,0:T(8,128)S(1)}, u32[]{:S(2)}, u32[]{:S(2)}) collective-permute-start(f32[64,512]{1,0:T(8,128)S(1)} %shard_map.109), channel_id=1, source_target_pairs={{0,32},{32,0},{1,33},{33,1},{2,34},{34,2},{3,35},{35,3},{4,36},{36... | collective-permute-start | bytes 393224 | tf_op jit(solution)/shard_map/ppermute | solution.py:315
  104.5 6.3 %collective-permute-start.4 = (f32[64,512]{1,0:T(8,128)S(1)}, f32[64,512]{1,0:T(8,128)S(1)}, u32[]{:S(2)}, u32[]{:S(2)}) collective-permute-start(f32[64,512]{1,0:T(8,128)S(1)} %add.41), channel_id=1, source_target_pairs={{0,64},{64,0},{1,65},{65,1},{2,66},{66,2},{3,67},{67,3},{4,68},{68... | collective-permute-start | bytes 393224 | tf_op jit(solution)/shard_map/ppermute | solution.py:315
  112.4 3.2 %collective-permute-start.7 = (f32[64,256]{1,0:T(8,128)S(1)}, f32[64,256]{1,0:T(8,128)S(1)}, u32[]{:S(2)}, u32[]{:S(2)}) collective-permute-start(f32[64,256]{1,0:T(8,128)S(1)} %shard_map.110), channel_id=1, source_target_pairs={{0,24},{8,0},{16,8},{24,16},{1,25},{9,1},{17,9},{25,17},{2,26},{10... | collective-permute-start | bytes 196616 | tf_op jit(solution)/shard_map/ppermute | solution.py:315
  113.1 4.7 %collective-permute-start.6 = (f32[64,256]{1,0:T(8,128)S(1)}, f32[64,256]{1,0:T(8,128)S(1)}, u32[]{:S(2)}, u32[]{:S(2)}) collective-permute-start(f32[64,256]{1,0:T(8,128)S(1)} %shard_map.110), channel_id=1, source_target_pairs={{0,16},{8,24},{16,0},{24,8},{1,17},{9,25},{17,1},{25,9},{2,18},{10... | collective-permute-start | bytes 196616 | tf_op jit(solution)/shard_map/ppermute | solution.py:315
  113.4 5.0 %collective-permute-start.5 = (f32[64,256]{1,0:T(8,128)S(1)}, f32[64,256]{1,0:T(8,128)S(1)}, u32[]{:S(2)}, u32[]{:S(2)}) collective-permute-start(f32[64,256]{1,0:T(8,128)S(1)} %shard_map.110), channel_id=1, source_target_pairs={{0,8},{8,16},{16,24},{24,0},{1,9},{9,17},{17,25},{25,1},{2,10},{10... | collective-permute-start | bytes 196616 | tf_op jit(solution)/shard_map/ppermute | solution.py:315
  118.4 3.2 %collective-permute-start.10 = (f32[64,256]{1,0:T(8,128)S(1)}, f32[64,256]{1,0:T(8,128)S(1)}, u32[]{:S(2)}, u32[]{:S(2)}) collective-permute-start(f32[64,256]{1,0:T(8,128)S(1)} %add_add_fusion.1), channel_id=1, source_target_pairs={{0,6},{2,0},{4,2},{6,4},{1,7},{3,1},{5,3},{7,5},{8,14},{10,8},{12,... | collective-permute-start | bytes 196616 | tf_op jit(solution)/shard_map/ppermute | solution.py:315
  119.2 4.6 %collective-permute-start.9 = (f32[64,256]{1,0:T(8,128)S(1)}, f32[64,256]{1,0:T(8,128)S(1)}, u32[]{:S(2)}, u32[]{:S(2)}) collective-permute-start(f32[64,256]{1,0:T(8,128)S(1)} %add_add_fusion.1), channel_id=1, source_target_pairs={{0,4},{2,6},{4,0},{6,2},{1,5},{3,7},{5,1},{7,3},{8,12},{10,14},{12... | collective-permute-start | bytes 196616 | tf_op jit(solution)/shard_map/ppermute | solution.py:315
  120.5 4.3 %collective-permute-start.8 = (f32[64,256]{1,0:T(8,128)S(1)}, f32[64,256]{1,0:T(8,128)S(1)}, u32[]{:S(2)}, u32[]{:S(2)}) collective-permute-start(f32[64,256]{1,0:T(8,128)S(1)} %add_add_fusion.1), channel_id=1, source_target_pairs={{0,2},{2,4},{4,6},{6,0},{1,3},{3,5},{5,7},{7,1},{8,10},{10,12},{12... | collective-permute-start | bytes 196616 | tf_op jit(solution)/shard_map/ppermute | solution.py:315
  124.8 3.2 %collective-permute-start.11 = (f32[64,256]{1,0:T(8,128)S(1)}, f32[64,256]{1,0:T(8,128)S(1)}, u32[]{:S(2)}, u32[]{:S(2)}) collective-permute-start(f32[64,256]{1,0:T(8,128)S(1)} %add_add_fusion), channel_id=1, source_target_pairs={{0,1},{1,0},{2,3},{3,2},{4,5},{5,4},{6,7},{7,6},{8,9},{9,8},{10,11... | collective-permute-start | bytes 196616 | tf_op jit(solution)/shard_map/ppermute | solution.py:315
  129.2 6.9 %collective-permute-start.12 = (f32[64,512]{1,0:T(8,128)S(1)}, f32[64,512]{1,0:T(8,128)S(1)}, u32[]{:S(2)}, u32[]{:S(2)}) collective-permute-start(f32[64,512]{1,0:T(8,128)S(1)} %shard_map.111), channel_id=1, source_target_pairs={{0,32},{32,0},{1,33},{33,1},{2,34},{34,2},{3,35},{35,3},{4,36},{36... | collective-permute-start | bytes 393224 | tf_op jit(solution)/shard_map/ppermute | solution.py:315
  136.1 6.3 %collective-permute-start.13 = (f32[64,512]{1,0:T(8,128)S(1)}, f32[64,512]{1,0:T(8,128)S(1)}, u32[]{:S(2)}, u32[]{:S(2)}) collective-permute-start(f32[64,512]{1,0:T(8,128)S(1)} %add.50), channel_id=1, source_target_pairs={{0,64},{64,0},{1,65},{65,1},{2,66},{66,2},{3,67},{67,3},{4,68},{68... | collective-permute-start | bytes 393224 | tf_op jit(solution)/shard_map/ppermute | solution.py:315

commit v4 on v3

--- a/solution.py
+++ b/solution.py
@@ -1,5 +1,4 @@
 import functools
-import itertools
 import math
 
 import jax
@@ -16,7 +15,8 @@
 SIZES = {"zh": 2, "core": 2, "x": 4, "y": 4, "zl": 2}
 ALL = ("zh", "core", "x", "y", "zl")
 CENTERS = ("x", "y", "zl")
-GROUP = ("zh", "core")
+PLANES = ("zh", "zl")
+OWNERS = ("x", "y", "core")
 VMEM = pl.BlockSpec(memory_space=pltpu.VMEM)
 
 ACOS_FULL = (
@@ -95,16 +95,33 @@
     )
 
 
-def features_body(pool_f, index, send, scale):
+def packed(x):
+    half = x.shape[0] // 2
+    return jnp.concatenate([x[:half], x[half:]], axis=1)
+
+
+def unpacked(x):
+    wide = x.shape[-1] // 2
+    return jnp.concatenate([x[..., :wide], x[..., wide:]], axis=-2)
+
+
+def features_body(pool_f, pool_t, index, drawn):
     rows = index.shape[1]
-    feats = pick(rows_hot(index[...], pool_f.shape[0]), pool_f[...], NN)
-    sa = jnp.sqrt(jnp.mean(feats * feats, axis=1, keepdims=True) + EPS)
-    unit = feats / sa
-    half, wide = scale.shape
-    sa = jnp.broadcast_to(sa, (rows, wide // 2))
-    scale[...] = jnp.concatenate([sa[:half], sa[half:]], axis=1)
-    for o in range(send.shape[0]):
-        send[o] = unit
+    hot = rows_hot(index[...], pool_f.shape[0])
+    drawn[0:rows, :] = pick(hot, pool_f[...], NN)
+    drawn[rows:, :] = packed(pick(hot, pool_t[...], NT, flip=True).T)
+
+
+def centers_body(centers, weights, pack):
+    count = centers.shape[0]
+    pack[0:count, :] = centers[...]
+    pack[count:, :] = packed(weights[...].T)
+
+
+def order_body(x, *refs):
+    parts, out = refs[:-1], refs[-1]
+    for o, part in enumerate(parts):
+        out[x[0] ^ o] = part[...]
 
 
 def quarters_body(member, eig, nys, *outs):
@@ -118,12 +135,8 @@
         out[count:, :] = row
 
 
-def vectors_body(pool_t, index, *refs, cdev):
-    tables, (send, targ) = refs[:-2], refs[-2:]
-    hot = rows_hot(index[...], pool_t.shape[1])
-    targets = pick(hot, pool_t[...], NT, flip=True).T
-    half = targets.shape[0] // 2
-    targ[...] = jnp.concatenate([targets[:half], targets[half:]], axis=1)
+def vectors_body(*refs, cdev):
+    tables, send = refs[:-1], refs[-1]
     count, part = tables[0].shape[0] - 8, tables[0].shape[1]
     peers = send.shape[0]
     blocks, group, lanes = part // 128, CAP * len(tables), 128 // len(tables)
@@ -152,86 +165,100 @@
         send[o, group * blocks :, :] = shared[o * CAP : (o + 1) * CAP]
 
 
-def kernel_body(recv, centers, weights, khi, klo, pred, cen, wts, cos_a, cos_b, lhs, *, block, sub):
-    src, rows, dim = recv.shape
-    out, count = weights.shape
-    b = centers[...]
-    sb = jnp.sqrt(jnp.mean(b * b, axis=1, keepdims=True) + EPS)
-    b1, b2, b3 = split3(b / sb * (1.0 / dim))
-    cen[...] = jnp.concatenate([b1, b1, b2, b2, b3, b1], axis=1)
-    w1, w2 = split2(weights[...].T * sb)
-    w = jnp.concatenate([w1, w2], axis=1)
-    wts[...] = w
-    blocks, group = src * rows // block, block // rows
-
-    def stage(i):
-        a1, a2, a3 = split3(recv[pl.ds(i * group, group)].reshape(block, dim))
-        lhs[...] = jnp.concatenate([a1, a2, a1, a2, a1, a3], axis=1)
-
-    def cosines(dst, n):
+def kernel_body(*refs, nb, rows, sub, extra):
+    own, mate = refs[0:2]
+    packs = refs[2 : 2 + nb]
+    khi, klo, keep, send = refs[2 + nb : 6 + nb]
+    lhs, cen, wts, cos_a, cos_b, acc = refs[-6:]
+    dim, count = own.shape[2], khi.shape[2]
+    block = own.shape[0] * rows
+    out = dim // 2
+    for h, part in enumerate((own, mate)):
+        f = part[:, 0:rows, :].reshape(block, dim)
+        sa = jnp.sqrt(jnp.mean(f * f, axis=1, keepdims=True) + EPS)
+        a1, a2, a3 = split3(f / sa)
+        lhs[h] = jnp.concatenate([a1, a2, a1, a2, a1, a3], axis=1)
+        if extra and h == 0:
+            wide = jnp.broadcast_to(sa, (block, out)).reshape(own.shape[0], rows, out)
+            half = rows // 2
+            refs[6 + nb][...] = jnp.concatenate([wide[:, :half], wide[:, half:]], axis=2)
+    for j, pack in enumerate(packs):
+        b = pack[0:count, :]
+        sb = jnp.sqrt(jnp.mean(b * b, axis=1, keepdims=True) + EPS)
+        b1, b2, b3 = split3(b / sb * (1.0 / dim))
+        cen[j] = jnp.concatenate([b1, b1, b2, b2, b3, b1], axis=1)
+        w1, w2 = split2(unpacked(pack[count:, :]) * sb)
+        wts[j] = jnp.concatenate([w1, w2], axis=1)
+        if extra:
+            nb_row = full_nt(jnp.ones((8, dim), F32), b * b) * (1.0 / dim) + EPS
+            refs[7 + nb][...] = jnp.sqrt(nb_row)
+    acc[...] = jnp.zeros(acc.shape, F32)
+
+    def cosines(dst, j, h, n):
         at = slice(n * (count // 2), (n + 1) * (count // 2))
-        dst[:, at] = mm(lhs[...], cen[at, :], NT)
-
-    def elementwise(i, values, n):
-        at = pl.ds(pl.multiple_of(i * block + n * sub, sub), sub)
+        dst[:, at] = mm(lhs[h], cen[j, at, :], NT)
+
+    def elementwise(values, j, h, n):
+        at = slice(h * block + n * sub, h * block + (n + 1) * sub)
         hi, lo = split2(ntk_over_scale(values[n * sub : (n + 1) * sub, :]))
-        khi[at, :] = hi
-        klo[at, :] = lo
-
-    def predict(i):
-        at = pl.ds(pl.multiple_of(i * block, block), block)
-        both = mm(khi[at, :], wts[...], NN) + mm(klo[at, :], wts[...], NN)
-        total = (both[:, :out] + both[:, out:]).reshape(group, 2, rows // 2, out)
-        pred[pl.ds(i * group, group)] = jnp.concatenate([total[:, 0], total[:, 1]], axis=2)
-
-    def step(i, before, now, later):
-        elems = [functools.partial(elementwise, i, now, n) for n in range(block // sub)]
-        others = [
-            functools.partial(cosines, later, 0),
-            functools.partial(cosines, later, 1),
-            functools.partial(predict, before),
-        ]
-        stage(jnp.minimum(i + 1, blocks - 1))
-        every = len(elems) // len(others)
+        khi[j, at, :] = hi
+        klo[j, at, :] = lo
+
+    def predict(j, h):
+        at = slice(h * block, (h + 1) * block)
+        both = mm(khi[j, at, :], wts[j], NN) + mm(klo[j, at, :], wts[j], NN)
+        acc[at, :] = acc[at, :] + both
+
+    def step(j, h, now, later, after):
+        elems = [functools.partial(elementwise, now, j, h, n) for n in range(block // sub)]
+        others = [functools.partial(cosines, later, *after, n) for n in range(2)] if after else []
+        if h == 1:
+            others.append(functools.partial(predict, j, 0))
+        every = len(elems) // 3
         for n, f in enumerate(elems):
             if n % every == 0 and others:
                 others.pop(0)()
             f()
 
-    stage(0)
-    cosines(cos_a, 0)
-    cosines(cos_a, 1)
-
-    def pair(h, _):
-        step(2 * h, jnp.maximum(2 * h - 1, 0), cos_a, cos_b)
-        step(2 * h + 1, 2 * h, cos_b, cos_a)
-        return 0
-
-    lax.fori_loop(0, blocks // 2, pair, 0)
-    predict(blocks - 1)
-
-
-def residual_body(parts, targ, scale, resid, send, *, norm):
-    value = scale[...] * jnp.sum(parts[...], axis=0) - targ[...]
-    half, out = value.shape[0], value.shape[1] // 2
-    resid[0:half, :] = value[:, :out]
-    resid[half:, :] = value[:, out:]
-    ready = value * scale[...] * norm
-    for o in range(send.shape[0]):
-        send[o] = ready
-
-
-def grads_body(resid, khi, klo, centers, grads):
-    src, half, wide = resid.shape
-    out = grads.shape[0]
-    r = resid[...]
-    r = jnp.concatenate([r[:, :, :out], r[:, :, out:]], axis=1).reshape(src * half * 2, out)
-    r1, r2 = split2(r.T)
+    for n in range(2):
+        cosines(cos_a, 0, 0, n)
+    if nb == 1:
+        step(0, 0, cos_a, cos_b, (0, 1))
+        step(0, 1, cos_b, cos_a, None)
+        predict(0, 1)
+    else:
+
+        def pair(j, _):
+            step(j, 0, cos_a, cos_b, (j, 1))
+            step(j, 1, cos_b, cos_a, (jnp.minimum(j + 1, nb - 1), 0))
+            predict(j, 1)
+            return 0
+
+        lax.fori_loop(0, nb, pair, 0)
+    for h, dst in enumerate((keep, send)):
+        total = acc[h * block : (h + 1) * block, :]
+        total = (total[:, :out] + total[:, out:]).reshape(own.shape[0], 2, rows // 2, out)
+        dst[...] = jnp.concatenate([total[:, 0], total[:, 1]], axis=2)
+
+
+def residual_body(x, total, own, scale, resid, ready, value, *, rows, norm):
+    value[...] = scale[...] * total[...] - own[:, rows:, :]
+    resid[...] = unpacked(value[x[0]])
+    ready[...] = value[...] * scale[...] * norm
+
+
+def grads_body(own, mate, *refs):
+    outs = refs[-4:]
+    r = jnp.concatenate([unpacked(own[...]), unpacked(mate[...])], axis=0)
+    out = r.shape[2]
+    r1, r2 = split2(r.reshape(-1, out).T)
     rr = jnp.concatenate([r1, r2], axis=0)
-    both = mm(rr, khi[...], NN) + mm(rr, klo[...], NN)
-    b = centers[...]
-    nb = full_nt(jnp.ones((8, b.shape[1]), F32), b * b)[0:1] * (1.0 / b.shape[1]) + EPS
-    grads[...] = (both[:out] + both[out:]) * jnp.sqrt(nb)
+    place = 0
+    for khi, klo in zip(refs[0:-4:2], refs[1:-4:2]):
+        for j in range(khi.shape[0]):
+            both = mm(rr, khi[j], NN) + mm(rr, klo[j], NN)
+            outs[place][...] = both[:out] + both[out:]
+            place += 1
 
 
 def block_of(points, j, tables):
@@ -304,16 +331,18 @@
 
 
 def exchange(v, axes):
-    sizes = [SIZES[a] for a in axes]
-    spots = list(itertools.product(*[range(s) for s in sizes]))
-    flat = {p: i for i, p in enumerate(spots)}
-    total = v
-    for off in spots[1:]:
-        perm = [
-            (flat[p], flat[tuple((i + o) % s for i, o, s in zip(p, off, sizes))]) for p in spots
-        ]
-        total = total + lax.ppermute(v, axes, perm)
-    return total
+    return functools.reduce(jnp.add, [v] + mates([v] * math.prod(SIZES[a] for a in axes), axes))
+
+
+def mates(parts, axes):
+    n = math.prod(SIZES[a] for a in axes)
+    return [
+        lax.ppermute(parts[o], axes, [(i, i ^ o) for i in range(n)]) for o in range(1, n)
+    ]
+
+
+def together(*arrays):
+    return lax.optimization_barrier(arrays)
 
 
 def per_device(
@@ -321,81 +350,98 @@
     eig_vectors, eig_scale, nys_owner, nys_offset,
 ):
     rows, dim = batch_index.shape[0], pool_features.shape[1]
-    peers = SIZES["x"] * SIZES["y"] * SIZES["zl"]
+    nx, ny, half = SIZES["x"], SIZES["y"], rows // 2
     cdev, out = weights.shape
     count, q = eig_vectors.shape
-    half = rows // 2
-    norm = 1.0 / math.sqrt(rows * peers * SIZES["zh"] * SIZES["core"])
-    index = batch_index.reshape(1, rows)
+    tables = math.prod(SIZES[a] for a in PLANES)
+    peers = math.prod(SIZES[a] for a in OWNERS)
+    norm = 1.0 / math.sqrt(rows * math.prod(SIZES[a] for a in ALL))
+    x = lax.axis_index("x").astype(jnp.int32)[None]
+    member = lax.axis_index(PLANES).astype(jnp.int32)[None]
+    straight = lax.axis_index("core") == lax.axis_index("zl")
+    wide = 2 * out
+
+    pack = call(centers_body, shape(cdev + cdev // 2, dim), centers, weights.T)
+    moved = lax.ppermute(pack, ("core", "zl"), [(0, 1), (3, 2)])
+    tile = jnp.where(straight, pack, moved)
+
+    drawn = call(
+        features_body, shape(rows + half, dim),
+        pool_features, pool_targets.T, batch_index.reshape(1, rows),
+    )
+    tile, *gathered = together(tile, drawn, *mates([drawn] * nx, ("x",)))
+    own = call(order_body, shape(nx, rows + half, dim), x, *gathered, scalars=1)
+    others = mates([tile] * ny, ("y",))
+    (mate,) = mates([own] * 2, ("core",))
+    eig_vectors, own = together(eig_vectors, own)
+
+    def kernel(packs, extra):
+        nb = len(packs)
+        outs = [shape(nb, 2 * nx * rows, cdev, dtype=BF)] * 2 + [shape(nx, half, wide)] * 2
+        if extra:
+            outs = outs + [shape(nx, half, wide), shape(8, cdev)]
+        return call(
+            functools.partial(kernel_body, nb=nb, rows=rows, sub=32, extra=extra),
+            outs, own, mate, *packs,
+            scratch_shapes=[
+                pltpu.VMEM((2, nx * rows, 6 * dim), BF),
+                pltpu.VMEM((nb, cdev, 6 * dim), BF),
+                pltpu.VMEM((nb, cdev, wide), BF),
+                pltpu.VMEM((nx * rows, cdev), F32),
+                pltpu.VMEM((nx * rows, cdev), F32),
+                pltpu.VMEM((2 * nx * rows, wide), F32),
+            ],
+            cost_estimate=pl.CostEstimate(
+                flops=10_000_000_000 * nb, bytes_accessed=1 << 20, transcendentals=0
+            ),
+        )
+
+    khi_a, klo_a, keep_a, send_a, scale, sb = kernel([tile], True)
+
     nys = (nys_owner.reshape(count) * cdev + nys_offset).reshape(1, count)
-    tables = SIZES[GROUP[0]] * SIZES[GROUP[1]]
-    member = lax.axis_index(GROUP).astype(jnp.int32)[None]
-
-    send, scale = call(
-        features_body,
-        [shape(peers, rows, dim), shape(half, 2 * out)],
-        pool_features, index,
-    )
-    recv = lax.all_to_all(send, CENTERS, split_axis=0, concat_axis=0, tiled=True)
-
     parted = call(
         quarters_body, [shape(count + 8, q // tables)] * tables,
         member, eig_vectors, nys, scalars=1,
     )
-    parted = [parted[0]] + [
-        lax.ppermute(part, GROUP, [(i, i ^ o) for i in range(tables)])
-        for o, part in enumerate(parted) if o
-    ]
-    piece = CAP * (tables * (q // tables // 128) + 1)
-    points, targ = call(
+    keep_a, *parted = together(keep_a, parted[0], *mates(parted, PLANES))
+    points = call(
         functools.partial(vectors_body, cdev=cdev),
-        [shape(peers, piece, 128), shape(half, 2 * out)],
-        pool_targets.T, index, *parted,
-    )
-    points, recv = lax.optimization_barrier((points, recv))
-    points = lax.all_to_all(points, CENTERS, split_axis=0, concat_axis=0, tiled=True)
-
-    block = 4 * rows
-    khi, klo, pred = call(
-        functools.partial(kernel_body, block=block, sub=32),
-        [shape(peers * rows, cdev, dtype=BF)] * 2 + [shape(peers, half, 2 * out)],
-        recv, centers, weights.T,
-        scratch_shapes=[
-            pltpu.VMEM((cdev, 6 * dim), BF),
-            pltpu.VMEM((cdev, 2 * out), BF),
-            pltpu.VMEM((block, cdev), F32),
-            pltpu.VMEM((block, cdev), F32),
-            pltpu.VMEM((block, 6 * dim), BF),
-        ],
-        cost_estimate=pl.CostEstimate(
-            flops=40_000_000_000, bytes_accessed=1 << 22, transcendentals=0
-        ),
-    )
-
-    points, pred = lax.optimization_barrier((points, pred))
-    parts = lax.all_to_all(pred, CENTERS, split_axis=0, concat_axis=0, tiled=True)
+        shape(peers, CAP * (tables * (q // tables // 128) + 1), 128),
+        *parted,
+    )
+    points = lax.all_to_all(points, OWNERS, split_axis=0, concat_axis=0, tiled=True)
+
+    khi_b, klo_b, keep_b, send_b = kernel(others, False)
+
+    (got,) = mates([send_a + send_b] * 2, ("core",))
+    total = exchange(keep_a + keep_b + got, ("x",))
     resid, ready = call(
-        functools.partial(residual_body, norm=norm),
-        [shape(rows, out), shape(peers, half, 2 * out)],
-        parts, targ, scale,
-    )
-    every = lax.all_to_all(ready, CENTERS, split_axis=0, concat_axis=0, tiled=True)
-    grads = call(grads_body, shape(out, cdev), every, khi, klo, centers)
-    for axis in GROUP[::-1]:
-        grads = exchange(grads, (axis,))
+        functools.partial(residual_body, rows=rows, norm=norm),
+        [shape(rows, out), shape(nx, half, wide)],
+        x, total, own, scale,
+        scalars=1, scratch_shapes=[pltpu.VMEM((nx, half, wide), F32)],
+    )
+    (ready_mate,) = mates([ready] * 2, ("core",))
+
+    parts = call(
+        grads_body, [shape(out, cdev)] * 4, ready, ready_mate, khi_a, klo_a, khi_b, klo_b
+    )
+    grads = functools.reduce(jnp.add, mates(parts, ("y",)), parts[0]) * sb[0:1]
+    points, grads = together(points, grads)
+    grads = exchange(grads, PLANES)
     coeff = call(
         functools.partial(coeff_body, tables=tables), shape(out, q // tables), points, grads
     )
-    for axis in CENTERS:
+    for axis in OWNERS[::-1]:
         coeff = exchange(coeff, (axis,))
     corr = call(
         functools.partial(corr_body, tables=tables),
         shape(out, cdev), member, points, coeff, eig_scale[None, :],
         scalars=1,
     )
-    for axis in GROUP[::-1]:
-        corr = exchange(corr, (axis,))
-    return resid, (corr - grads).T
+    update = exchange(corr, PLANES) - grads
+    (swapped,) = mates([update] * 2, ("core",))
+    return resid, jnp.where(straight, update, swapped).T
 
 
 def solution(mesh):

time: 144 us -> 128 us (0.89)
  blocking collectives: 32.1 us -> 0 us
  starting transfers between devices: 36.2 us -> 56.1 us
  local copies, waits for them, and re-layouts: 8.3 us -> 5.43 us
    all_to_all x2 -> x0, blocking collectives: 32.1 us -> none  [the longest x1 18.4 us: per_device(): lax.all_to_all(pred, CENTERS, split_axis=0, concat_axis=0, tiled=True)]
    ppermute x14 -> x33, starting transfers between devices: 20.4 us -> 49.8 us  [the longest x32 48.5 us: mates(): lax.ppermute(parts[o], axes, [(i, i ^ o) for i in range(n)])]
    all_to_all x2 -> x1, starting transfers between devices: 15.8 us -> 6.35 us  [per_device(): lax.all_to_all(points, OWNERS, split_axis=0, concat_axis=0, tiled=True)]
    unnamed x32 -> x22, local copies, waits for them, and re-layouts: 8.3 us -> 5.43 us
    ppermute x14 -> x33, waiting for transfers between devices: 41 us -> 39.7 us  [the longest x32 39.7 us: mates(): lax.ppermute(parts[o], axes, [(i, i ^ o) for i in range(n)])]
    pallas_call x8 -> x11, Pallas kernels: 23.9 us -> 24.2 us  [call(): pl.pallas_call(body, out_shape=outs, in_specs=[smem] * scalars + [VMEM] *...]
  transfers between devices with their start and end apart: 16 -> 34, of which waited for: 13 -> 21; matrix products, arithmetic and copies ran while one was open for 0% -> 0% of each run, Pallas kernels for 13% -> 17%
where the time goes in v4:
time: 128 us; the launch traced here: 127 us
  starting transfers between devices  56.1 us (44%)
  waiting for transfers between devices  39.7 us (31%)
  Pallas kernels  24.2 us (19%)
  local copies, waits for them, and re-layouts  5.43 us (4%)
    ppermute x32, starting transfers between devices, mates(): lax.ppermute(parts[o], axes, [(i, i ^ o) for i in range(n)])  48.5 us
    ppermute x32, waiting for transfers between devices, mates(): lax.ppermute(parts[o], axes, [(i, i ^ o) for i in range(n)])  39.7 us
    pallas_call x11, Pallas kernels, call(): pl.pallas_call(body, out_shape=outs, in_specs=[smem] * scalars + [VMEM] *...  24.2 us
    all_to_all x1, starting transfers between devices, per_device(): lax.all_to_all(points, OWNERS, split_axis=0, concat_axis=0, tiled=True)  6.35 us
    unnamed x22, local copies, waits for them, and re-layouts  5.43 us
  transfers between devices with their start and end apart: 34, of which 21 were waited for; matrix products, arithmetic and copies ran while one was open for 0% of the time, Pallas kernels for 17%

profile of v4, /device:TPU:1, one launch (start us, length us, event | category | flops | bytes accessed | tf_op | source)
XLA Modules:
  0.0 127.3 jit_solution(1826216867597087769)
XLA Ops:
  7.2 2.1 %collective-permute-start.1 = (f32[96,128]{1,0:T(8,128)S(1)}, f32[96,128]{1,0:T(8,128)S(1)}, u32[]{:S(2)}, u32[]{:S(2)}) collective-permute-start(f32[96,128]{1,0:T(8,128)S(1)} %shard_map.105.refs_0_), channel_id=1, source_target_pairs={{0,8},{8,0},{16,24},{24,16},{1,9},{9,1},{17,25},{25,17},{2,10},{10... | collective-permute-start | bytes 147464 | tf_op jit(solution)/shard_map/ppermute | solution.py:340
  9.3 2.5 %collective-permute-start.2 = (f32[96,128]{1,0:T(8,128)S(1)}, f32[96,128]{1,0:T(8,128)S(1)}, u32[]{:S(2)}, u32[]{:S(2)}) collective-permute-start(f32[96,128]{1,0:T(8,128)S(1)} %shard_map.105.refs_0_), channel_id=1, source_target_pairs={{0,16},{8,24},{16,0},{24,8},{1,17},{9,25},{17,1},{25,9},{2,18},{10... | collective-permute-start | bytes 147464 | tf_op jit(solution)/shard_map/ppermute | solution.py:340
  11.8 1.9 %collective-permute-done.2.refs_2_ = f32[96,128]{1,0:T(8,128)S(1)} collective-permute-done((f32[96,128]{1,0:T(8,128)S(1)}, f32[96,128]{1,0:T(8,128)S(1)}, u32[]{:S(2)}, u32[]{:S(2)}) %collective-permute-start.2) | collective-permute-done | bytes 49184 | tf_op jit(solution)/shard_map/ppermute | solution.py:340
  13.7 2.1 %collective-permute-done.3.refs_3_ = f32[96,128]{1,0:T(8,128)S(1)} collective-permute-done((f32[96,128]{1,0:T(8,128)S(1)}, f32[96,128]{1,0:T(8,128)S(1)}, u32[]{:S(2)}, u32[]{:S(2)}) %collective-permute-start.3) | collective-permute-done | bytes 49184 | tf_op jit(solution)/shard_map/ppermute | solution.py:340
  15.9 5.0 %collective-permute-start.4 = (f32[4,96,128]{2,1,0:T(8,128)S(1)}, f32[4,96,128]{2,1,0:T(8,128)S(1)}, u32[]{:S(2)}, u32[]{:S(2)}) collective-permute-start(f32[4,96,128]{2,1,0:T(8,128)S(1)} %shard_map.106.refs_0_.own), channel_id=1, source_target_pairs={{0,32},{32,0},{1,33},{33,1},{2,34},{34,2},{3,35},{35,3},{4,36},{36... | collective-permute-start | bytes 589832 | tf_op jit(solution)/shard_map/ppermute | solution.py:340
  21.1 2.8 %collective-permute-start.10 = (f32[768,128]{1,0:T(8,128)S(1)}, f32[768,128]{1,0:T(8,128)S(1)}, u32[]{:S(2)}, u32[]{:S(2)}) collective-permute-start(f32[768,128]{1,0:T(8,128)S(1)} %broadcast_select_fusion.refs_2_), channel_id=1, source_target_pairs={{0,6},{2,4},{4,2},{6,0},{1,7},{3,5},{5,3},{7,1},{8,14},{10,12},{12... | collective-permute-start | bytes 1179656 | tf_op jit(solution)/shard_map/ppermute | solution.py:340
  26.3 3.3 %collective-permute-start.6 = (f32[136,256]{1,0:T(8,128)S(1)}, f32[136,256]{1,0:T(8,128)S(1)}, u32[]{:S(2)}, u32[]{:S(2)}) collective-permute-start(f32[136,256]{1,0:T(8,128)S(1)} %get-tuple-element.46), channel_id=1, source_target_pairs={{0,64},{1,65},{64,0},{65,1},{2,66},{3,67},{66,2},{67,3},{4,68},{5,... | collective-permute-start | bytes 417800 | tf_op jit(solution)/shard_map/ppermute | solution.py:340
  29.7 4.1 %shard_map.107 = (bf16[1,512,512]{2,1,0:T(8,128)(2,1)S(1)}, bf16[1,512,512]{2,1,0:T(8,128)(2,1)S(1)}, f32[4,32,128]{2,1,0:T(8,128)S(1)}, f32[4,32,128]{2,1,0:T(8...) custom-call(f32[4,96,128]{2,1,0:T(8,128)S(1)} %shard_map.106.refs_0_.own, ...), custom_call_target="tpu_custom_call" | custom-call | flops 10000000000 | bytes 1048576 | tf_op jit(solution)/shard_map/pallas_call | solution.py:323
  33.7 1.9 %collective-permute-done.7.refs_3_ = f32[136,256]{1,0:T(8,128)S(1)} collective-permute-done((f32[136,256]{1,0:T(8,128)S(1)}, f32[136,256]{1,0:T(8,128)S(1)}, u32[]{:S(2)}, u32[]{:S(2)}) %collective-permute-start.7) | collective-permute-done | bytes 139296 | tf_op jit(solution)/shard_map/ppermute | solution.py:340
  35.6 1.8 %shard_map.111 = f32[32,72,128]{2,1,0:T(8,128)} custom-call(f32[136,256]{1,0:T(8,128)S(1)} %get-tuple-element.54.refs_0_, f32[136,256]{1,0:T(8,128)S(1)} %collective-permute-done.5.refs_1_, f32[136,256]{1,0:T(8,128)S(1)} %collective-permute-done.6.refs_2_, f32[136,256]{1,0:T(8,128)S(1)} %collective-permute-done.7.refs_3_), custom_call_target="tpu_custom_call" | custom-call | tf_op jit(solution)/shard_map/pallas_call | solution.py:323
  37.4 6.4 %all-to-all-start = ((f32[32,72,128]{2,1,0:T(8,128)}), f32[32,72,128]{2,1,0:T(8,128)S(1)}, u32[]{:S(2)}, u32[]{:S(2)}) async-start(f32[32,72,128]{2,1,0:T(8,128)} %shard_map.111), calls=%async_computation | async-start | bytes 2359296 | tf_op jit(solution)/shard_map/all_to_all | solution.py:412
  44.7 13.4 %shard_map.109 = (bf16[3,512,512]{2,1,0:T(8,128)(2,1)S(1)}, bf16[3,512,512]{2,1,0:T(8,128)(2,1)S(1)}, f32[4,32,128]{2,1,0:T(8,128)S(1)}, f32[4,32,128]{2,1,0:T(8,128)S(1)}) custom-call(f32[4,96,128]{2,1,0:T(8,128)S(1)} %shard_map.106.refs_0_.own, f32[4,96,128]{2,1,0:T(8,128)S(1)} %copy-done.8, f32[768,128]{1,0:T(8,128)} %collective-permute-done.8.refs_2_, ...), custom_call_target="tpu_custom_call" | custom-call | flops 30000001024 | bytes 1048576 | tf_op jit(solution)/shard_map/pallas_call | solution.py:323
  61.0 2.4 %collective-permute-start.13 = (f32[4,32,128]{2,1,0:T(8,128)S(1)}, f32[4,32,128]{2,1,0:T(8,128)S(1)}, u32[]{:S(2)}, u32[]{:S(2)}) collective-permute-start(f32[4,32,128]{2,1,0:T(8,128)S(1)} %add_add_fusion.4), channel_id=1, source_target_pairs={{0,16},{8,24},{16,0},{24,8},{1,17},{9,25},{17,1},{25,9},{2,18},{10... | collective-permute-start | bytes 196616 | tf_op jit(solution)/shard_map/ppermute | solution.py:340
  63.5 2.9 %collective-permute-done.13 = f32[4,32,128]{2,1,0:T(8,128)S(1)} collective-permute-done((f32[4,32,128]{2,1,0:T(8,128)S(1)}, f32[4,32,128]{2,1,0:T(8,128)S(1)}, u32[]{:S(2)}, u32[]{:S(2)}) %collective-permute-start.13) | collective-permute-done | bytes 65568 | tf_op jit(solution)/shard_map/ppermute | solution.py:340
  66.4 1.5 %collective-permute-done.14 = f32[4,32,128]{2,1,0:T(8,128)S(1)} collective-permute-done((f32[4,32,128]{2,1,0:T(8,128)S(1)}, f32[4,32,128]{2,1,0:T(8,128)S(1)}, u32[]{:S(2)}, u32[]{:S(2)}) %collective-permute-start.14) | collective-permute-done | bytes 65568 | tf_op jit(solution)/shard_map/ppermute | solution.py:340
  68.6 1.9 %collective-permute-start.15 = (f32[4,32,128]{2,1,0:T(8,128)S(1)}, f32[4,32,128]{2,1,0:T(8,128)S(1)}, u32[]{:S(2)}, u32[]{:S(2)}) collective-permute-start(f32[4,32,128]{2,1,0:T(8,128)S(1)} %get-tuple-element.58.own), channel_id=1, source_target_pairs={{0,32},{32,0},{1,33},{33,1},{2,34},{34,2},{3,35},{35,3},{4,36},{36... | collective-permute-start | bytes 196616 | tf_op jit(solution)/shard_map/ppermute | solution.py:340
  73.5 2.4 %collective-permute-start.17 = (f32[64,512]{1,0:T(8,128)S(1)}, f32[64,512]{1,0:T(8,128)S(1)}, u32[]{:S(2)}, u32[]{:S(2)}) collective-permute-start(f32[64,512]{1,0:T(8,128)S(1)} %get-tuple-element.65), channel_id=1, source_target_pairs={{0,4},{2,6},{4,0},{6,2},{1,5},{3,7},{5,1},{7,3},{8,12},{10,14},{12... | collective-permute-start | bytes 393224 | tf_op jit(solution)/shard_map/ppermute | solution.py:340
  77.1 5.0 %collective-permute-done.17 = f32[64,512]{1,0:T(8,128)S(1)} collective-permute-done((f32[64,512]{1,0:T(8,128)S(1)}, f32[64,512]{1,0:T(8,128)S(1)}, u32[]{:S(2)}, u32[]{:S(2)}) %collective-permute-start.17) | collective-permute-done | bytes 131104 | tf_op jit(solution)/shard_map/ppermute | solution.py:340
  82.1 2.5 %collective-permute-done.18 = f32[64,512]{1,0:T(8,128)S(1)} collective-permute-done((f32[64,512]{1,0:T(8,128)S(1)}, f32[64,512]{1,0:T(8,128)S(1)}, u32[]{:S(2)}, u32[]{:S(2)}) %collective-permute-start.18) | collective-permute-done | bytes 131104 | tf_op jit(solution)/shard_map/ppermute | solution.py:340
  84.7 3.2 %collective-permute-start.20 = (f32[64,512]{1,0:T(8,128)S(1)}, f32[64,512]{1,0:T(8,128)S(1)}, u32[]{:S(2)}, u32[]{:S(2)}) collective-permute-start(f32[64,512]{1,0:T(8,128)S(1)} %add_multiply_fusion), channel_id=1, source_target_pairs={{0,64},{1,65},{64,0},{65,1},{2,66},{3,67},{66,2},{67,3},{4,68},{5,... | collective-permute-start | bytes 393224 | tf_op jit(solution)/shard_map/ppermute | solution.py:340
  88.6 4.4 %collective-permute-done.20 = f32[64,512]{1,0:T(8,128)S(1)} collective-permute-done((f32[64,512]{1,0:T(8,128)S(1)}, f32[64,512]{1,0:T(8,128)S(1)}, u32[]{:S(2)}, u32[]{:S(2)}) %collective-permute-start.20) | collective-permute-done | bytes 131104 | tf_op jit(solution)/shard_map/ppermute | solution.py:340
  92.9 2.8 %collective-permute-done.21 = f32[64,512]{1,0:T(8,128)S(1)} collective-permute-done((f32[64,512]{1,0:T(8,128)S(1)}, f32[64,512]{1,0:T(8,128)S(1)}, u32[]{:S(2)}, u32[]{:S(2)}) %collective-permute-start.21) | collective-permute-done | bytes 131104 | tf_op jit(solution)/shard_map/ppermute | solution.py:340
  95.8 1.6 %shard_map.113 = f32[64,256]{1,0:T(8,128)S(1)} custom-call(f32[32,72,128]{2,1,0:T(8,128)S(1)} %all-to-all-done.points, f32[64,512]{1,0:T(8,128)S(1)} %add_add_fusion.grads), custom_call_target="tpu_custom_call" | custom-call | tf_op jit(solution)/shard_map/pallas_call | solution.py:323
  97.3 1.5 %collective-permute-start.22 = (f32[64,256]{1,0:T(8,128)S(1)}, f32[64,256]{1,0:T(8,128)S(1)}, u32[]{:S(2)}, u32[]{:S(2)}) collective-permute-start(f32[64,256]{1,0:T(8,128)S(1)} %shard_map.113), channel_id=1, source_target_pairs={{0,32},{32,0},{1,33},{33,1},{2,34},{34,2},{3,35},{35,3},{4,36},{36... | collective-permute-start | bytes 196616 | tf_op jit(solution)/shard_map/ppermute | solution.py:340
  99.8 1.6 %collective-permute-start.24 = (f32[64,256]{1,0:T(8,128)S(1)}, f32[64,256]{1,0:T(8,128)S(1)}, u32[]{:S(2)}, u32[]{:S(2)}) collective-permute-start(f32[64,256]{1,0:T(8,128)S(1)} %add.86), channel_id=1, source_target_pairs={{0,4},{2,6},{4,0},{6,2},{1,5},{3,7},{5,1},{7,3},{8,12},{10,14},{12... | collective-permute-start | bytes 196616 | tf_op jit(solution)/shard_map/ppermute | solution.py:340
  101.4 2.3 %collective-permute-start.25 = (f32[64,256]{1,0:T(8,128)S(1)}, f32[64,256]{1,0:T(8,128)S(1)}, u32[]{:S(2)}, u32[]{:S(2)}) collective-permute-start(f32[64,256]{1,0:T(8,128)S(1)} %add.86), channel_id=1, source_target_pairs={{0,6},{2,4},{4,2},{6,0},{1,7},{3,5},{5,3},{7,1},{8,14},{10,12},{12... | collective-permute-start | bytes 196616 | tf_op jit(solution)/shard_map/ppermute | solution.py:340
  106.1 2.5 %collective-permute-start.27 = (f32[64,256]{1,0:T(8,128)S(1)}, f32[64,256]{1,0:T(8,128)S(1)}, u32[]{:S(2)}, u32[]{:S(2)}) collective-permute-start(f32[64,256]{1,0:T(8,128)S(1)} %add_add_fusion.2), channel_id=1, source_target_pairs={{0,16},{8,24},{16,0},{24,8},{1,17},{9,25},{17,1},{25,9},{2,18},{10... | collective-permute-start | bytes 196616 | tf_op jit(solution)/shard_map/ppermute | solution.py:340
  111.0 2.7 %collective-permute-done.28 = f32[64,256]{1,0:T(8,128)S(1)} collective-permute-done((f32[64,256]{1,0:T(8,128)S(1)}, f32[64,256]{1,0:T(8,128)S(1)}, u32[]{:S(2)}, u32[]{:S(2)}) %collective-permute-start.28) | collective-permute-done | bytes 65568 | tf_op jit(solution)/shard_map/ppermute | solution.py:340
  114.9 1.5 %collective-permute-start.30 = (f32[64,512]{1,0:T(8,128)S(1)}, f32[64,512]{1,0:T(8,128)S(1)}, u32[]{:S(2)}, u32[]{:S(2)}) collective-permute-start(f32[64,512]{1,0:T(8,128)S(1)} %shard_map.114), channel_id=1, source_target_pairs={{0,64},{1,65},{64,0},{65,1},{2,66},{3,67},{66,2},{67,3},{4,68},{5,... | collective-permute-start | bytes 393224 | tf_op jit(solution)/shard_map/ppermute | solution.py:340
  116.4 2.3 %collective-permute-start.31 = (f32[64,512]{1,0:T(8,128)S(1)}, f32[64,512]{1,0:T(8,128)S(1)}, u32[]{:S(2)}, u32[]{:S(2)}) collective-permute-start(f32[64,512]{1,0:T(8,128)S(1)} %shard_map.114), channel_id=1, source_target_pairs={{0,65},{1,64},{64,1},{65,0},{2,67},{3,66},{66,3},{67,2},{4,69},{5,... | collective-permute-start | bytes 393224 | tf_op jit(solution)/shard_map/ppermute | solution.py:340
  118.7 1.6 %collective-permute-done.30 = f32[64,512]{1,0:T(8,128)S(1)} collective-permute-done((f32[64,512]{1,0:T(8,128)S(1)}, f32[64,512]{1,0:T(8,128)S(1)}, u32[]{:S(2)}, u32[]{:S(2)}) %collective-permute-start.30) | collective-permute-done | bytes 131104 | tf_op jit(solution)/shard_map/ppermute | solution.py:340
  121.8 3.9 %collective-permute-start.32 = (f32[64,512]{1,0:T(8,128)S(1)}, f32[64,512]{1,0:T(8,128)S(1)}, u32[]{:S(2)}, u32[]{:S(2)}) collective-permute-start(f32[64,512]{1,0:T(8,128)S(1)} %add_subtract_fusion), channel_id=1, source_target_pairs={{0,32},{32,0},{1,33},{33,1},{2,34},{34,2},{3,35},{35,3},{4,36},{36... | collective-permute-start | bytes 393224 | tf_op jit(solution)/shard_map/ppermute | solution.py:340
  (82 shorter events, 28.8 us)
Async XLA Ops:
  2.7 9.1 %collective-permute-start = (f32[768,128]{1,0:T(8,128)S(1)}, f32[768,128]{1,0:T(8,128)S(1)}, u32[]{:S(2)}, u32[]{:S(2)}) collective-permute-start(f32[768,128]{1,0:T(8,128)S(1)} %shard_map.104), channel_id=1, source_target_pairs={{0,1},{33,32},{2,3},{35,34},{4,5},{37,36},{6,7},{39,38},{8,9},{41,... | collective-permute-start | bytes 1179656 | tf_op jit(solution)/shard_map/ppermute | solution.py:365
  7.2 4.7 %collective-permute-start.1 = (f32[96,128]{1,0:T(8,128)S(1)}, f32[96,128]{1,0:T(8,128)S(1)}, u32[]{:S(2)}, u32[]{:S(2)}) collective-permute-start(f32[96,128]{1,0:T(8,128)S(1)} %shard_map.105.refs_0_), channel_id=1, source_target_pairs={{0,8},{8,0},{16,24},{24,16},{1,9},{9,1},{17,25},{25,17},{2,10},{10... | collective-permute-start | bytes 147464 | tf_op jit(solution)/shard_map/ppermute | solution.py:340
  9.3 4.5 %collective-permute-start.2 = (f32[96,128]{1,0:T(8,128)S(1)}, f32[96,128]{1,0:T(8,128)S(1)}, u32[]{:S(2)}, u32[]{:S(2)}) collective-permute-start(f32[96,128]{1,0:T(8,128)S(1)} %shard_map.105.refs_0_), channel_id=1, source_target_pairs={{0,16},{8,24},{16,0},{24,8},{1,17},{9,25},{17,1},{25,9},{2,18},{10... | collective-permute-start | bytes 147464 | tf_op jit(solution)/shard_map/ppermute | solution.py:340
  11.7 4.2 %collective-permute-start.3 = (f32[96,128]{1,0:T(8,128)S(1)}, f32[96,128]{1,0:T(8,128)S(1)}, u32[]{:S(2)}, u32[]{:S(2)}) collective-permute-start(f32[96,128]{1,0:T(8,128)S(1)} %shard_map.105.refs_0_), channel_id=1, source_target_pairs={{0,24},{8,16},{16,8},{24,0},{1,25},{9,17},{17,9},{25,1},{2,26},{10... | collective-permute-start | bytes 147464 | tf_op jit(solution)/shard_map/ppermute | solution.py:340
  15.9 13.8 %collective-permute-start.4 = (f32[4,96,128]{2,1,0:T(8,128)S(1)}, f32[4,96,128]{2,1,0:T(8,128)S(1)}, u32[]{:S(2)}, u32[]{:S(2)}) collective-permute-start(f32[4,96,128]{2,1,0:T(8,128)S(1)} %shard_map.106.refs_0_.own), channel_id=1, source_target_pairs={{0,32},{32,0},{1,33},{33,1},{2,34},{34,2},{3,35},{35,3},{4,36},{36... | collective-permute-start | bytes 589832 | tf_op jit(solution)/shard_map/ppermute | solution.py:340
  21.0 5.3 %collective-permute-start.5 = (f32[136,256]{1,0:T(8,128)S(1)}, f32[136,256]{1,0:T(8,128)S(1)}, u32[]{:S(2)}, u32[]{:S(2)}) collective-permute-start(f32[136,256]{1,0:T(8,128)S(1)} %get-tuple-element.45), channel_id=1, source_target_pairs={{0,1},{1,0},{64,65},{65,64},{2,3},{3,2},{66,67},{67,66},{4,5},{5,4... | collective-permute-start | bytes 417800 | tf_op jit(solution)/shard_map/ppermute | solution.py:340
  21.1 22.7 %collective-permute-start.10 = (f32[768,128]{1,0:T(8,128)S(1)}, f32[768,128]{1,0:T(8,128)S(1)}, u32[]{:S(2)}, u32[]{:S(2)}) collective-permute-start(f32[768,128]{1,0:T(8,128)S(1)} %broadcast_select_fusion.refs_2_), channel_id=1, source_target_pairs={{0,6},{2,4},{4,2},{6,0},{1,7},{3,5},{5,3},{7,1},{8,14},{10,12},{12... | collective-permute-start | bytes 1179656 | tf_op jit(solution)/shard_map/ppermute | solution.py:340
  23.9 19.9 %collective-permute-start.8 = (f32[768,128]{1,0:T(8,128)S(1)}, f32[768,128]{1,0:T(8,128)}, u32[]{:S(2)}, u32[]{:S(2)}) collective-permute-start(f32[768,128]{1,0:T(8,128)S(1)} %broadcast_select_fusion.refs_2_), channel_id=1, source_target_pairs={{0,2},{2,0},{4,6},{6,4},{1,3},{3,1},{5,7},{7,5},{8,10},{10,8},{12,... | collective-permute-start | bytes 1179656 | tf_op jit(solution)/shard_map/ppermute | solution.py:340
  23.9 19.9 %collective-permute-start.9 = (f32[768,128]{1,0:T(8,128)S(1)}, f32[768,128]{1,0:T(8,128)}, u32[]{:S(2)}, u32[]{:S(2)}) collective-permute-start(f32[768,128]{1,0:T(8,128)S(1)} %broadcast_select_fusion.refs_2_), channel_id=1, source_target_pairs={{0,4},{2,6},{4,0},{6,2},{1,5},{3,7},{5,1},{7,3},{8,12},{10,14},{12... | collective-permute-start | bytes 1179656 | tf_op jit(solution)/shard_map/ppermute | solution.py:340
  26.3 7.4 %collective-permute-start.6 = (f32[136,256]{1,0:T(8,128)S(1)}, f32[136,256]{1,0:T(8,128)S(1)}, u32[]{:S(2)}, u32[]{:S(2)}) collective-permute-start(f32[136,256]{1,0:T(8,128)S(1)} %get-tuple-element.46), channel_id=1, source_target_pairs={{0,64},{1,65},{64,0},{65,1},{2,66},{3,67},{66,2},{67,3},{4,68},{5,... | collective-permute-start | bytes 417800 | tf_op jit(solution)/shard_map/ppermute | solution.py:340
  29.7 6.0 %collective-permute-start.7 = (f32[136,256]{1,0:T(8,128)S(1)}, f32[136,256]{1,0:T(8,128)S(1)}, u32[]{:S(2)}, u32[]{:S(2)}) collective-permute-start(f32[136,256]{1,0:T(8,128)S(1)} %get-tuple-element.47), channel_id=1, source_target_pairs={{0,65},{1,64},{64,1},{65,0},{2,67},{3,66},{66,3},{67,2},{4,69},{5,... | collective-permute-start | bytes 417800 | tf_op jit(solution)/shard_map/ppermute | solution.py:340
  37.4 47.2 %all-to-all-start = ((f32[32,72,128]{2,1,0:T(8,128)}), f32[32,72,128]{2,1,0:T(8,128)S(1)}, u32[]{:S(2)}, u32[]{:S(2)}) async-start(f32[32,72,128]{2,1,0:T(8,128)} %shard_map.111), calls=%async_computation | async-start | bytes 2359296 | tf_op jit(solution)/shard_map/all_to_all | solution.py:412
  59.6 3.9 %collective-permute-start.12 = (f32[4,32,128]{2,1,0:T(8,128)S(1)}, f32[4,32,128]{2,1,0:T(8,128)S(1)}, u32[]{:S(2)}, u32[]{:S(2)}) collective-permute-start(f32[4,32,128]{2,1,0:T(8,128)S(1)} %add_add_fusion.4), channel_id=1, source_target_pairs={{0,8},{8,0},{16,24},{24,16},{1,9},{9,1},{17,25},{25,17},{2,10},{10... | collective-permute-start | bytes 196616 | tf_op jit(solution)/shard_map/ppermute | solution.py:340
  61.0 5.4 %collective-permute-start.13 = (f32[4,32,128]{2,1,0:T(8,128)S(1)}, f32[4,32,128]{2,1,0:T(8,128)S(1)}, u32[]{:S(2)}, u32[]{:S(2)}) collective-permute-start(f32[4,32,128]{2,1,0:T(8,128)S(1)} %add_add_fusion.4), channel_id=1, source_target_pairs={{0,16},{8,24},{16,0},{24,8},{1,17},{9,25},{17,1},{25,9},{2,18},{10... | collective-permute-start | bytes 196616 | tf_op jit(solution)/shard_map/ppermute | solution.py:340
  63.4 4.5 %collective-permute-start.14 = (f32[4,32,128]{2,1,0:T(8,128)S(1)}, f32[4,32,128]{2,1,0:T(8,128)S(1)}, u32[]{:S(2)}, u32[]{:S(2)}) collective-permute-start(f32[4,32,128]{2,1,0:T(8,128)S(1)} %add_add_fusion.4), channel_id=1, source_target_pairs={{0,24},{8,16},{16,8},{24,0},{1,25},{9,17},{17,9},{25,1},{2,26},{10... | collective-permute-start | bytes 196616 | tf_op jit(solution)/shard_map/ppermute | solution.py:340
  68.6 2.8 %collective-permute-start.15 = (f32[4,32,128]{2,1,0:T(8,128)S(1)}, f32[4,32,128]{2,1,0:T(8,128)S(1)}, u32[]{:S(2)}, u32[]{:S(2)}) collective-permute-start(f32[4,32,128]{2,1,0:T(8,128)S(1)} %get-tuple-element.58.own), channel_id=1, source_target_pairs={{0,32},{32,0},{1,33},{33,1},{2,34},{34,2},{3,35},{35,3},{4,36},{36... | collective-permute-start | bytes 196616 | tf_op jit(solution)/shard_map/ppermute | solution.py:340
  72.3 4.8 %collective-permute-start.16 = (f32[64,512]{1,0:T(8,128)S(1)}, f32[64,512]{1,0:T(8,128)S(1)}, u32[]{:S(2)}, u32[]{:S(2)}) collective-permute-start(f32[64,512]{1,0:T(8,128)S(1)} %get-tuple-element.64), channel_id=1, source_target_pairs={{0,2},{2,0},{4,6},{6,4},{1,3},{3,1},{5,7},{7,5},{8,10},{10,8},{12,... | collective-permute-start | bytes 393224 | tf_op jit(solution)/shard_map/ppermute | solution.py:340
  73.5 8.5 %collective-permute-start.17 = (f32[64,512]{1,0:T(8,128)S(1)}, f32[64,512]{1,0:T(8,128)S(1)}, u32[]{:S(2)}, u32[]{:S(2)}) collective-permute-start(f32[64,512]{1,0:T(8,128)S(1)} %get-tuple-element.65), channel_id=1, source_target_pairs={{0,4},{2,6},{4,0},{6,2},{1,5},{3,7},{5,1},{7,3},{8,12},{10,14},{12... | collective-permute-start | bytes 393224 | tf_op jit(solution)/shard_map/ppermute | solution.py:340
  76.0 8.6 %collective-permute-start.18 = (f32[64,512]{1,0:T(8,128)S(1)}, f32[64,512]{1,0:T(8,128)S(1)}, u32[]{:S(2)}, u32[]{:S(2)}) collective-permute-start(f32[64,512]{1,0:T(8,128)S(1)} %get-tuple-element.66), channel_id=1, source_target_pairs={{0,6},{2,4},{4,2},{6,0},{1,7},{3,5},{5,3},{7,1},{8,14},{10,12},{12... | collective-permute-start | bytes 393224 | tf_op jit(solution)/shard_map/ppermute | solution.py:340
  84.6 3.9 %collective-permute-start.19 = (f32[64,512]{1,0:T(8,128)S(1)}, f32[64,512]{1,0:T(8,128)S(1)}, u32[]{:S(2)}, u32[]{:S(2)}) collective-permute-start(f32[64,512]{1,0:T(8,128)S(1)} %add_multiply_fusion), channel_id=1, source_target_pairs={{0,1},{1,0},{64,65},{65,64},{2,3},{3,2},{66,67},{67,66},{4,5},{5,4... | collective-permute-start | bytes 393224 | tf_op jit(solution)/shard_map/ppermute | solution.py:340
  84.7 8.2 %collective-permute-start.20 = (f32[64,512]{1,0:T(8,128)S(1)}, f32[64,512]{1,0:T(8,128)S(1)}, u32[]{:S(2)}, u32[]{:S(2)}) collective-permute-start(f32[64,512]{1,0:T(8,128)S(1)} %add_multiply_fusion), channel_id=1, source_target_pairs={{0,64},{1,65},{64,0},{65,1},{2,66},{3,67},{66,2},{67,3},{4,68},{5,... | collective-permute-start | bytes 393224 | tf_op jit(solution)/shard_map/ppermute | solution.py:340
  87.9 7.8 %collective-permute-start.21 = (f32[64,512]{1,0:T(8,128)S(1)}, f32[64,512]{1,0:T(8,128)S(1)}, u32[]{:S(2)}, u32[]{:S(2)}) collective-permute-start(f32[64,512]{1,0:T(8,128)S(1)} %add_multiply_fusion), channel_id=1, source_target_pairs={{0,65},{1,64},{64,1},{65,0},{2,67},{3,66},{66,3},{67,2},{4,69},{5,... | collective-permute-start | bytes 393224 | tf_op jit(solution)/shard_map/ppermute | solution.py:340
  99.7 3.9 %collective-permute-start.23 = (f32[64,256]{1,0:T(8,128)S(1)}, f32[64,256]{1,0:T(8,128)S(1)}, u32[]{:S(2)}, u32[]{:S(2)}) collective-permute-start(f32[64,256]{1,0:T(8,128)S(1)} %add.86), channel_id=1, source_target_pairs={{0,2},{2,0},{4,6},{6,4},{1,3},{3,1},{5,7},{7,5},{8,10},{10,8},{12,... | collective-permute-start | bytes 196616 | tf_op jit(solution)/shard_map/ppermute | solution.py:340
  99.8 4.8 %collective-permute-start.24 = (f32[64,256]{1,0:T(8,128)S(1)}, f32[64,256]{1,0:T(8,128)S(1)}, u32[]{:S(2)}, u32[]{:S(2)}) collective-permute-start(f32[64,256]{1,0:T(8,128)S(1)} %add.86), channel_id=1, source_target_pairs={{0,4},{2,6},{4,0},{6,2},{1,5},{3,7},{5,1},{7,3},{8,12},{10,14},{12... | collective-permute-start | bytes 196616 | tf_op jit(solution)/shard_map/ppermute | solution.py:340
  101.4 4.6 %collective-permute-start.25 = (f32[64,256]{1,0:T(8,128)S(1)}, f32[64,256]{1,0:T(8,128)S(1)}, u32[]{:S(2)}, u32[]{:S(2)}) collective-permute-start(f32[64,256]{1,0:T(8,128)S(1)} %add.86), channel_id=1, source_target_pairs={{0,6},{2,4},{4,2},{6,0},{1,7},{3,5},{5,3},{7,1},{8,14},{10,12},{12... | collective-permute-start | bytes 196616 | tf_op jit(solution)/shard_map/ppermute | solution.py:340
  106.1 3.9 %collective-permute-start.26 = (f32[64,256]{1,0:T(8,128)S(1)}, f32[64,256]{1,0:T(8,128)S(1)}, u32[]{:S(2)}, u32[]{:S(2)}) collective-permute-start(f32[64,256]{1,0:T(8,128)S(1)} %add_add_fusion.2), channel_id=1, source_target_pairs={{0,8},{8,0},{16,24},{24,16},{1,9},{9,1},{17,25},{25,17},{2,10},{10... | collective-permute-start | bytes 196616 | tf_op jit(solution)/shard_map/ppermute | solution.py:340
  106.1 4.8 %collective-permute-start.27 = (f32[64,256]{1,0:T(8,128)S(1)}, f32[64,256]{1,0:T(8,128)S(1)}, u32[]{:S(2)}, u32[]{:S(2)}) collective-permute-start(f32[64,256]{1,0:T(8,128)S(1)} %add_add_fusion.2), channel_id=1, source_target_pairs={{0,16},{8,24},{16,0},{24,8},{1,17},{9,25},{17,1},{25,9},{2,18},{10... | collective-permute-start | bytes 196616 | tf_op jit(solution)/shard_map/ppermute | solution.py:340
  108.6 5.0 %collective-permute-start.28 = (f32[64,256]{1,0:T(8,128)S(1)}, f32[64,256]{1,0:T(8,128)S(1)}, u32[]{:S(2)}, u32[]{:S(2)}) collective-permute-start(f32[64,256]{1,0:T(8,128)S(1)} %add_add_fusion.2), channel_id=1, source_target_pairs={{0,24},{8,16},{16,8},{24,0},{1,25},{9,17},{17,9},{25,1},{2,26},{10... | collective-permute-start | bytes 196616 | tf_op jit(solution)/shard_map/ppermute | solution.py:340
  114.8 3.9 %collective-permute-start.29 = (f32[64,512]{1,0:T(8,128)S(1)}, f32[64,512]{1,0:T(8,128)S(1)}, u32[]{:S(2)}, u32[]{:S(2)}) collective-permute-start(f32[64,512]{1,0:T(8,128)S(1)} %shard_map.114), channel_id=1, source_target_pairs={{0,1},{1,0},{64,65},{65,64},{2,3},{3,2},{66,67},{67,66},{4,5},{5,4... | collective-permute-start | bytes 393224 | tf_op jit(solution)/shard_map/ppermute | solution.py:340
  114.9 5.5 %collective-permute-start.30 = (f32[64,512]{1,0:T(8,128)S(1)}, f32[64,512]{1,0:T(8,128)S(1)}, u32[]{:S(2)}, u32[]{:S(2)}) collective-permute-start(f32[64,512]{1,0:T(8,128)S(1)} %shard_map.114), channel_id=1, source_target_pairs={{0,64},{1,65},{64,0},{65,1},{2,66},{3,67},{66,2},{67,3},{4,68},{5,... | collective-permute-start | bytes 393224 | tf_op jit(solution)/shard_map/ppermute | solution.py:340
  116.4 5.3 %collective-permute-start.31 = (f32[64,512]{1,0:T(8,128)S(1)}, f32[64,512]{1,0:T(8,128)S(1)}, u32[]{:S(2)}, u32[]{:S(2)}) collective-permute-start(f32[64,512]{1,0:T(8,128)S(1)} %shard_map.114), channel_id=1, source_target_pairs={{0,65},{1,64},{64,1},{65,0},{2,67},{3,66},{66,3},{67,2},{4,69},{5,... | collective-permute-start | bytes 393224 | tf_op jit(solution)/shard_map/ppermute | solution.py:340
  121.8 4.9 %collective-permute-start.32 = (f32[64,512]{1,0:T(8,128)S(1)}, f32[64,512]{1,0:T(8,128)S(1)}, u32[]{:S(2)}, u32[]{:S(2)}) collective-permute-start(f32[64,512]{1,0:T(8,128)S(1)} %add_subtract_fusion), channel_id=1, source_target_pairs={{0,32},{32,0},{1,33},{33,1},{2,34},{34,2},{3,35},{35,3},{4,36},{36... | collective-permute-start | bytes 393224 | tf_op jit(solution)/shard_map/ppermute | solution.py:340
  (13 other events, 97.7 us)

commit v5 on v4

--- a/solution.py
+++ b/solution.py
@@ -105,17 +105,25 @@
     return jnp.concatenate([x[..., :wide], x[..., wide:]], axis=-2)
 
 
-def features_body(pool_f, pool_t, index, drawn):
+def front_body(index, pool_f, pool_t, centers, weights, drawn, pack, feats, targs, wts, sems):
+    count = centers.shape[0]
+    copies = [
+        pltpu.make_async_copy(src, dst, sems.at[n])
+        for n, (src, dst) in enumerate(
+            ((pool_f, feats), (pool_t, targs), (weights, wts), (centers, pack.at[0:count, :]))
+        )
+    ]
+    for copy in copies:
+        copy.start()
     rows = index.shape[1]
-    hot = rows_hot(index[...], pool_f.shape[0])
-    drawn[0:rows, :] = pick(hot, pool_f[...], NN)
-    drawn[rows:, :] = packed(pick(hot, pool_t[...], NT, flip=True).T)
-
-
-def centers_body(centers, weights, pack):
-    count = centers.shape[0]
-    pack[0:count, :] = centers[...]
-    pack[count:, :] = packed(weights[...].T)
+    hot = rows_hot(index[...], feats.shape[0])
+    copies[0].wait()
+    drawn[0:rows, :] = pick(hot, feats[...], NN)
+    copies[1].wait()
+    drawn[rows:, :] = packed(pick(hot, targs[...], NT, flip=True).T)
+    copies[2].wait()
+    pack[count:, :] = packed(wts[...].T)
+    copies[3].wait()
 
 
 def order_body(x, *refs):
@@ -341,6 +349,15 @@
     ]
 
 
+def tile_from(pack, o):
+    ny = SIZES["y"]
+    perm = [
+        ((c * ny + y) * 2 + z, (z * ny + (y ^ o)) * 2 + c)
+        for c in range(2) for y in range(ny) for z in range(2)
+    ]
+    return lax.ppermute(pack, ("core", "y", "zl"), perm)
+
+
 def together(*arrays):
     return lax.optimization_barrier(arrays)
 
@@ -361,17 +378,25 @@
     straight = lax.axis_index("core") == lax.axis_index("zl")
     wide = 2 * out
 
-    pack = call(centers_body, shape(cdev + cdev // 2, dim), centers, weights.T)
-    moved = lax.ppermute(pack, ("core", "zl"), [(0, 1), (3, 2)])
-    tile = jnp.where(straight, pack, moved)
-
-    drawn = call(
-        features_body, shape(rows + half, dim),
-        pool_features, pool_targets.T, batch_index.reshape(1, rows),
-    )
-    tile, *gathered = together(tile, drawn, *mates([drawn] * nx, ("x",)))
-    own = call(order_body, shape(nx, rows + half, dim), x, *gathered, scalars=1)
-    others = mates([tile] * ny, ("y",))
+    drawn, pack = pl.pallas_call(
+        front_body,
+        out_shape=[shape(rows + half, dim), shape(cdev + cdev // 2, dim)],
+        in_specs=[VMEM] + [pl.BlockSpec(memory_space=pltpu.HBM)] * 4,
+        out_specs=[VMEM] * 2,
+        scratch_shapes=[
+            pltpu.VMEM(pool_features.shape, F32),
+            pltpu.VMEM(pool_targets.shape[::-1], F32),
+            pltpu.VMEM((out, cdev), F32),
+            pltpu.SemaphoreType.DMA((4,)),
+        ],
+        compiler_params=params(60),
+    )(batch_index.reshape(1, rows), pool_features, pool_targets.T, centers, weights.T)
+
+    gathered = mates([drawn] * nx, ("x",))
+    tile = tile_from(pack, 0)
+    tile, drawn, *gathered = together(tile, drawn, *gathered)
+    own = call(order_body, shape(nx, rows + half, dim), x, drawn, *gathered, scalars=1)
+    others = [tile_from(pack, o) for o in range(1, ny)]
     (mate,) = mates([own] * 2, ("core",))
     eig_vectors, own = together(eig_vectors, own)
 
@@ -392,7 +417,7 @@
                 pltpu.VMEM((2 * nx * rows, wide), F32),
             ],
             cost_estimate=pl.CostEstimate(
-                flops=10_000_000_000 * nb, bytes_accessed=1 << 20, transcendentals=0
+                flops=100_000_000 if extra else 10_000_000_000 * nb, bytes_accessed=1 << 16, transcendentals=0
             ),
         )
 

time: 128 us -> 136 us (1.062)
  waiting for transfers between devices: 39.7 us -> 47.9 us
  local copies, waits for them, and re-layouts: 5.43 us -> 0.82 us
  Pallas kernels: 24.2 us -> 27.1 us
  starting transfers between devices: 56.1 us -> 57.8 us
    ppermute x1 -> x4, starting transfers between devices: 1.29 us -> 11 us  [tile_from(): return lax.ppermute(pack, ('core', 'y', 'zl'), perm)]
    ppermute x32 -> x29, waiting for transfers between devices: 39.7 us -> 47.9 us  [mates(): lax.ppermute(parts[o], axes, [(i, i ^ o) for i in range(n)])]
    ppermute x32 -> x29, starting transfers between devices: 48.5 us -> 40.5 us  [mates(): lax.ppermute(parts[o], axes, [(i, i ^ o) for i in range(n)])]
    unnamed x22 -> x10, local copies, waits for them, and re-layouts: 5.43 us -> 0.82 us
    pallas_call x0 -> x1, Pallas kernels: none -> 3.61 us  [per_device(): pl.pallas_call(front_body, out_shape=[shape(rows + half, dim), shape(cdev...]
    pallas_call x11 -> x9, Pallas kernels: 24.2 us -> 23.4 us  [call(): pl.pallas_call(body, out_shape=outs, in_specs=[smem] * scalars + [VMEM] *...]
  transfers between devices with their start and end apart: 34 -> 34, of which waited for: 21 -> 19; matrix products, arithmetic and copies ran while one was open for 0% -> 0% of each run, Pallas kernels for 17% -> 15%
where the time goes in v5:
time: 136 us; the launch traced here: 135 us
  starting transfers between devices  57.8 us (42%)
  waiting for transfers between devices  47.9 us (35%)
  Pallas kernels  27.1 us (20%)
    ppermute x29, waiting for transfers between devices, mates(): lax.ppermute(parts[o], axes, [(i, i ^ o) for i in range(n)])  47.9 us
    ppermute x29, starting transfers between devices, mates(): lax.ppermute(parts[o], axes, [(i, i ^ o) for i in range(n)])  40.5 us
    pallas_call x9, Pallas kernels, call(): pl.pallas_call(body, out_shape=outs, in_specs=[smem] * scalars + [VMEM] *...  23.4 us
    ppermute x4, starting transfers between devices, tile_from(): return lax.ppermute(pack, ('core', 'y', 'zl'), perm)  11 us
    all_to_all x1, starting transfers between devices, per_device(): lax.all_to_all(points, OWNERS, split_axis=0, concat_axis=0, tiled=True)  6.27 us
    pallas_call x1, Pallas kernels, per_device(): pl.pallas_call(front_body, out_shape=[shape(rows + half, dim), shape(cdev...  3.61 us
  transfers between devices with their start and end apart: 34, of which 19 were waited for; matrix products, arithmetic and copies ran while one was open for 0% of the time, Pallas kernels for 15%

profile of v5, /device:TPU:1, one launch (start us, length us, event | category | flops | bytes accessed | tf_op | source)
XLA Modules:
  0.0 135.4 jit_solution(1381976543115103888)
XLA Ops:
  0.7 3.6 %shard_map.104 = (f32[96,128]{1,0:T(8,128)}, f32[768,128]{1,0:T(8,128)}) custom-call(s32[1,64]{1,0:T(1,128)} %bitcast.19, f32[1024,128]{1,0:T(8,128)} %pool_f.1, f32[64,1024]{1,0:T(8,128)} %bitcast.16, f32[512,128]{1,0:T(8,128)} %centers.1, f32[64,512]{1,0:T(8,128)} %bitcast.17), custom_call_target="tpu_custom_call" | custom-call | tf_op jit(solution)/shard_map/pallas_call | solution.py:381
  4.3 4.9 %collective-permute-start = (f32[768,128]{1,0:T(8,128)}, f32[768,128]{1,0:T(8,128)S(1)}, u32[]{:S(2)}, u32[]{:S(2)}) collective-permute-start(f32[768,128]{1,0:T(8,128)} %get-tuple-element.38), channel_id=1, source_target_pairs={{0,0},{1,32},{2,2},{3,34},{4,4},{5,36},{6,6},{7,38},{32,1},{33,33}... | collective-permute-start | bytes 1179656 | tf_op jit(solution)/shard_map/ppermute | solution.py:358
  10.5 2.5 %collective-permute-start.2 = (f32[96,128]{1,0:T(8,128)}, f32[96,128]{1,0:T(8,128)S(1)}, u32[]{:S(2)}, u32[]{:S(2)}) collective-permute-start(f32[96,128]{1,0:T(8,128)} %get-tuple-element.40.refs_0_), channel_id=1, source_target_pairs={{0,16},{8,24},{16,0},{24,8},{1,17},{9,25},{17,1},{25,9},{2,18},{10... | collective-permute-start | bytes 147464 | tf_op jit(solution)/shard_map/ppermute | solution.py:348
  13.2 3.3 %collective-permute-start.10 = (f32[768,128]{1,0:T(8,128)}, f32[768,128]{1,0:T(8,128)S(1)}, u32[]{:S(2)}, u32[]{:S(2)}) collective-permute-start(f32[768,128]{1,0:T(8,128)} %get-tuple-element.38), channel_id=1, source_target_pairs={{0,6},{1,38},{2,4},{3,36},{4,2},{5,34},{6,0},{7,32},{32,7},{33,39}... | collective-permute-start | bytes 1179656 | tf_op jit(solution)/shard_map/ppermute | solution.py:358
  16.9 2.3 %collective-permute-start.9 = (f32[768,128]{1,0:T(8,128)}, f32[768,128]{1,0:T(8,128)}, u32[]{:S(2)}, u32[]{:S(2)}) collective-permute-start(f32[768,128]{1,0:T(8,128)} %get-tuple-element.38), channel_id=1, source_target_pairs={{0,4},{1,36},{2,6},{3,38},{4,0},{5,32},{6,2},{7,34},{32,5},{33,37}... | collective-permute-start | bytes 1179656 | tf_op jit(solution)/shard_map/ppermute | solution.py:358
  20.9 14.6 %collective-permute-done.5.refs_1_ = f32[136,256]{1,0:T(8,128)S(1)} collective-permute-done((f32[136,256]{1,0:T(8,128)S(1)}, f32[136,256]{1,0:T(8,128)S(1)}, u32[]{:S(2)}, u32[]{:S(2)}) %collective-permute-start.5) | collective-permute-done | bytes 139296 | tf_op jit(solution)/shard_map/ppermute | solution.py:348
  35.4 3.3 %collective-permute-start.6 = (f32[136,256]{1,0:T(8,128)S(1)}, f32[136,256]{1,0:T(8,128)S(1)}, u32[]{:S(2)}, u32[]{:S(2)}) collective-permute-start(f32[136,256]{1,0:T(8,128)S(1)} %get-tuple-element.50), channel_id=1, source_target_pairs={{0,64},{1,65},{64,0},{65,1},{2,66},{3,67},{66,2},{67,3},{4,68},{5,... | collective-permute-start | bytes 417800 | tf_op jit(solution)/shard_map/ppermute | solution.py:348
  38.7 4.1 %shard_map.106 = (bf16[1,512,512]{2,1,0:T(8,128)(2,1)S(1)}, bf16[1,512,512]{2,1,0:T(8,128)(2,1)S(1)}, f32[4,32,128]{2,1,0:T(8,128)S(1)}, f32[4,32,128]{2,1,0:T(8...) custom-call(f32[4,96,128]{2,1,0:T(8,128)S(1)} %shard_map.105.refs_0_.own, ...), custom_call_target="tpu_custom_call" | custom-call | flops 100000000 | bytes 65536 | tf_op jit(solution)/shard_map/pallas_call | solution.py:331
  42.8 2.2 %collective-permute-done.7.refs_3_ = f32[136,256]{1,0:T(8,128)S(1)} collective-permute-done((f32[136,256]{1,0:T(8,128)S(1)}, f32[136,256]{1,0:T(8,128)S(1)}, u32[]{:S(2)}, u32[]{:S(2)}) %collective-permute-start.7) | collective-permute-done | bytes 139296 | tf_op jit(solution)/shard_map/ppermute | solution.py:348
  45.0 1.7 %shard_map.110 = f32[32,72,128]{2,1,0:T(8,128)} custom-call(f32[136,256]{1,0:T(8,128)S(1)} %get-tuple-element.58.refs_0_, f32[136,256]{1,0:T(8,128)S(1)} %collective-permute-done.5.refs_1_, f32[136,256]{1,0:T(8,128)S(1)} %collective-permute-done.6.refs_2_, f32[136,256]{1,0:T(8,128)S(1)} %collective-permute-done.7.refs_3_), custom_call_target="tpu_custom_call" | custom-call | tf_op jit(solution)/shard_map/pallas_call | solution.py:331
  46.7 6.3 %all-to-all-start = ((f32[32,72,128]{2,1,0:T(8,128)}), f32[32,72,128]{2,1,0:T(8,128)S(1)}, u32[]{:S(2)}, u32[]{:S(2)}) async-start(f32[32,72,128]{2,1,0:T(8,128)} %shard_map.110), calls=%async_computation | async-start | bytes 2359296 | tf_op jit(solution)/shard_map/all_to_all | solution.py:437
  53.0 13.4 %shard_map.108 = (bf16[3,512,512]{2,1,0:T(8,128)(2,1)S(1)}, bf16[3,512,512]{2,1,0:T(8,128)(2,1)S(1)}, f32[4,32,128]{2,1,0:T(8,128)S(1)}, f32[4,32,128]{2,1,0:T(8,128)S(1)}) custom-call(f32[4,96,128]{2,1,0:T(8,128)S(1)} %shard_map.105.refs_0_.own, f32[4,96,128]{2,1,0:T(8,128)S(1)} %collective-permute-done.4.refs_1_, ...), custom_call_target="tpu_custom_call" | custom-call | flops 30000001024 | bytes 65536 | tf_op jit(solution)/shard_map/pallas_call | solution.py:331
  69.3 2.4 %collective-permute-start.13 = (f32[4,32,128]{2,1,0:T(8,128)S(1)}, f32[4,32,128]{2,1,0:T(8,128)S(1)}, u32[]{:S(2)}, u32[]{:S(2)}) collective-permute-start(f32[4,32,128]{2,1,0:T(8,128)S(1)} %add_add_fusion.4), channel_id=1, source_target_pairs={{0,16},{8,24},{16,0},{24,8},{1,17},{9,25},{17,1},{25,9},{2,18},{10... | collective-permute-start | bytes 196616 | tf_op jit(solution)/shard_map/ppermute | solution.py:348
  71.8 2.9 %collective-permute-done.13 = f32[4,32,128]{2,1,0:T(8,128)S(1)} collective-permute-done((f32[4,32,128]{2,1,0:T(8,128)S(1)}, f32[4,32,128]{2,1,0:T(8,128)S(1)}, u32[]{:S(2)}, u32[]{:S(2)}) %collective-permute-start.13) | collective-permute-done | bytes 65568 | tf_op jit(solution)/shard_map/ppermute | solution.py:348
  74.7 1.5 %collective-permute-done.14 = f32[4,32,128]{2,1,0:T(8,128)S(1)} collective-permute-done((f32[4,32,128]{2,1,0:T(8,128)S(1)}, f32[4,32,128]{2,1,0:T(8,128)S(1)}, u32[]{:S(2)}, u32[]{:S(2)}) %collective-permute-start.14) | collective-permute-done | bytes 65568 | tf_op jit(solution)/shard_map/ppermute | solution.py:348
  76.9 1.9 %collective-permute-start.15 = (f32[4,32,128]{2,1,0:T(8,128)S(1)}, f32[4,32,128]{2,1,0:T(8,128)S(1)}, u32[]{:S(2)}, u32[]{:S(2)}) collective-permute-start(f32[4,32,128]{2,1,0:T(8,128)S(1)} %get-tuple-element.62.own), channel_id=1, source_target_pairs={{0,32},{32,0},{1,33},{33,1},{2,34},{34,2},{3,35},{35,3},{4,36},{36... | collective-permute-start | bytes 196616 | tf_op jit(solution)/shard_map/ppermute | solution.py:348
  81.9 2.4 %collective-permute-start.17 = (f32[64,512]{1,0:T(8,128)S(1)}, f32[64,512]{1,0:T(8,128)S(1)}, u32[]{:S(2)}, u32[]{:S(2)}) collective-permute-start(f32[64,512]{1,0:T(8,128)S(1)} %get-tuple-element.69), channel_id=1, source_target_pairs={{0,4},{2,6},{4,0},{6,2},{1,5},{3,7},{5,1},{7,3},{8,12},{10,14},{12... | collective-permute-start | bytes 393224 | tf_op jit(solution)/shard_map/ppermute | solution.py:348
  85.4 5.0 %collective-permute-done.17 = f32[64,512]{1,0:T(8,128)S(1)} collective-permute-done((f32[64,512]{1,0:T(8,128)S(1)}, f32[64,512]{1,0:T(8,128)S(1)}, u32[]{:S(2)}, u32[]{:S(2)}) %collective-permute-start.17) | collective-permute-done | bytes 131104 | tf_op jit(solution)/shard_map/ppermute | solution.py:348
  90.4 2.5 %collective-permute-done.18 = f32[64,512]{1,0:T(8,128)S(1)} collective-permute-done((f32[64,512]{1,0:T(8,128)S(1)}, f32[64,512]{1,0:T(8,128)S(1)}, u32[]{:S(2)}, u32[]{:S(2)}) %collective-permute-start.18) | collective-permute-done | bytes 131104 | tf_op jit(solution)/shard_map/ppermute | solution.py:348
  93.0 1.7 %collective-permute-start.20 = (f32[64,512]{1,0:T(8,128)S(1)}, f32[64,512]{1,0:T(8,128)S(1)}, u32[]{:S(2)}, u32[]{:S(2)}) collective-permute-start(f32[64,512]{1,0:T(8,128)S(1)} %add_multiply_fusion), channel_id=1, source_target_pairs={{0,64},{1,65},{64,0},{65,1},{2,66},{3,67},{66,2},{67,3},{4,68},{5,... | collective-permute-start | bytes 393224 | tf_op jit(solution)/shard_map/ppermute | solution.py:348
  94.7 2.1 %collective-permute-start.21 = (f32[64,512]{1,0:T(8,128)S(1)}, f32[64,512]{1,0:T(8,128)S(1)}, u32[]{:S(2)}, u32[]{:S(2)}) collective-permute-start(f32[64,512]{1,0:T(8,128)S(1)} %add_multiply_fusion), channel_id=1, source_target_pairs={{0,65},{1,64},{64,1},{65,0},{2,67},{3,66},{66,3},{67,2},{4,69},{5,... | collective-permute-start | bytes 393224 | tf_op jit(solution)/shard_map/ppermute | solution.py:348
  96.9 2.9 %collective-permute-done.20 = f32[64,512]{1,0:T(8,128)S(1)} collective-permute-done((f32[64,512]{1,0:T(8,128)S(1)}, f32[64,512]{1,0:T(8,128)S(1)}, u32[]{:S(2)}, u32[]{:S(2)}) %collective-permute-start.20) | collective-permute-done | bytes 131104 | tf_op jit(solution)/shard_map/ppermute | solution.py:348
  99.8 2.8 %collective-permute-done.21 = f32[64,512]{1,0:T(8,128)S(1)} collective-permute-done((f32[64,512]{1,0:T(8,128)S(1)}, f32[64,512]{1,0:T(8,128)S(1)}, u32[]{:S(2)}, u32[]{:S(2)}) %collective-permute-start.21) | collective-permute-done | bytes 131104 | tf_op jit(solution)/shard_map/ppermute | solution.py:348
  102.6 1.6 %shard_map.112 = f32[64,256]{1,0:T(8,128)S(1)} custom-call(f32[32,72,128]{2,1,0:T(8,128)S(1)} %all-to-all-done.points, f32[64,512]{1,0:T(8,128)S(1)} %add_add_fusion.grads), custom_call_target="tpu_custom_call" | custom-call | tf_op jit(solution)/shard_map/pallas_call | solution.py:331
  106.7 1.6 %collective-permute-start.24 = (f32[64,256]{1,0:T(8,128)S(1)}, f32[64,256]{1,0:T(8,128)S(1)}, u32[]{:S(2)}, u32[]{:S(2)}) collective-permute-start(f32[64,256]{1,0:T(8,128)S(1)} %add.86), channel_id=1, source_target_pairs={{0,4},{2,6},{4,0},{6,2},{1,5},{3,7},{5,1},{7,3},{8,12},{10,14},{12... | collective-permute-start | bytes 196616 | tf_op jit(solution)/shard_map/ppermute | solution.py:348
  108.3 2.3 %collective-permute-start.25 = (f32[64,256]{1,0:T(8,128)S(1)}, f32[64,256]{1,0:T(8,128)S(1)}, u32[]{:S(2)}, u32[]{:S(2)}) collective-permute-start(f32[64,256]{1,0:T(8,128)S(1)} %add.86), channel_id=1, source_target_pairs={{0,6},{2,4},{4,2},{6,0},{1,7},{3,5},{5,3},{7,1},{8,14},{10,12},{12... | collective-permute-start | bytes 196616 | tf_op jit(solution)/shard_map/ppermute | solution.py:348
  111.4 1.5 %collective-permute-done.25 = f32[64,256]{1,0:T(8,128)S(1)} collective-permute-done((f32[64,256]{1,0:T(8,128)S(1)}, f32[64,256]{1,0:T(8,128)S(1)}, u32[]{:S(2)}, u32[]{:S(2)}) %collective-permute-start.25) | collective-permute-done | bytes 65568 | tf_op jit(solution)/shard_map/ppermute | solution.py:348
  113.0 1.5 %collective-permute-start.27 = (f32[64,256]{1,0:T(8,128)S(1)}, f32[64,256]{1,0:T(8,128)S(1)}, u32[]{:S(2)}, u32[]{:S(2)}) collective-permute-start(f32[64,256]{1,0:T(8,128)S(1)} %add_add_fusion.2), channel_id=1, source_target_pairs={{0,16},{8,24},{16,0},{24,8},{1,17},{9,25},{17,1},{25,9},{2,18},{10... | collective-permute-start | bytes 196616 | tf_op jit(solution)/shard_map/ppermute | solution.py:348
  114.6 2.3 %collective-permute-start.28 = (f32[64,256]{1,0:T(8,128)S(1)}, f32[64,256]{1,0:T(8,128)S(1)}, u32[]{:S(2)}, u32[]{:S(2)}) collective-permute-start(f32[64,256]{1,0:T(8,128)S(1)} %add_add_fusion.2), channel_id=1, source_target_pairs={{0,24},{8,16},{16,8},{24,0},{1,25},{9,17},{17,9},{25,1},{2,26},{10... | collective-permute-start | bytes 196616 | tf_op jit(solution)/shard_map/ppermute | solution.py:348
  120.2 3.2 %collective-permute-start.30 = (f32[64,512]{1,0:T(8,128)S(1)}, f32[64,512]{1,0:T(8,128)S(1)}, u32[]{:S(2)}, u32[]{:S(2)}) collective-permute-start(f32[64,512]{1,0:T(8,128)S(1)} %shard_map.113), channel_id=1, source_target_pairs={{0,64},{1,65},{64,0},{65,1},{2,66},{3,67},{66,2},{67,3},{4,68},{5,... | collective-permute-start | bytes 393224 | tf_op jit(solution)/shard_map/ppermute | solution.py:348
  124.0 3.2 %collective-permute-done.30 = f32[64,512]{1,0:T(8,128)S(1)} collective-permute-done((f32[64,512]{1,0:T(8,128)S(1)}, f32[64,512]{1,0:T(8,128)S(1)}, u32[]{:S(2)}, u32[]{:S(2)}) %collective-permute-start.30) | collective-permute-done | bytes 131104 | tf_op jit(solution)/shard_map/ppermute | solution.py:348
  128.6 5.1 %collective-permute-start.32 = (f32[64,512]{1,0:T(8,128)S(1)}, f32[64,512]{1,0:T(8,128)S(1)}, u32[]{:S(2)}, u32[]{:S(2)}) collective-permute-start(f32[64,512]{1,0:T(8,128)S(1)} %add_subtract_fusion), channel_id=1, source_target_pairs={{0,32},{32,0},{1,33},{33,1},{2,34},{34,2},{3,35},{35,3},{4,36},{36... | collective-permute-start | bytes 393224 | tf_op jit(solution)/shard_map/ppermute | solution.py:348
  (68 shorter events, 21.9 us)
Async XLA Ops:
  4.3 15.0 %collective-permute-start = (f32[768,128]{1,0:T(8,128)}, f32[768,128]{1,0:T(8,128)S(1)}, u32[]{:S(2)}, u32[]{:S(2)}) collective-permute-start(f32[768,128]{1,0:T(8,128)} %get-tuple-element.38), channel_id=1, source_target_pairs={{0,0},{1,32},{2,2},{3,34},{4,4},{5,36},{6,6},{7,38},{32,1},{33,33}... | collective-permute-start | bytes 1179656 | tf_op jit(solution)/shard_map/ppermute | solution.py:358
  9.2 7.2 %collective-permute-start.1 = (f32[96,128]{1,0:T(8,128)}, f32[96,128]{1,0:T(8,128)S(1)}, u32[]{:S(2)}, u32[]{:S(2)}) collective-permute-start(f32[96,128]{1,0:T(8,128)} %get-tuple-element.40.refs_0_), channel_id=1, source_target_pairs={{0,8},{8,0},{16,24},{24,16},{1,9},{9,1},{17,25},{25,17},{2,10},{10... | collective-permute-start | bytes 147464 | tf_op jit(solution)/shard_map/ppermute | solution.py:348
  10.5 6.4 %collective-permute-start.2 = (f32[96,128]{1,0:T(8,128)}, f32[96,128]{1,0:T(8,128)S(1)}, u32[]{:S(2)}, u32[]{:S(2)}) collective-permute-start(f32[96,128]{1,0:T(8,128)} %get-tuple-element.40.refs_0_), channel_id=1, source_target_pairs={{0,16},{8,24},{16,0},{24,8},{1,17},{9,25},{17,1},{25,9},{2,18},{10... | collective-permute-start | bytes 147464 | tf_op jit(solution)/shard_map/ppermute | solution.py:348
  13.0 6.3 %collective-permute-start.3 = (f32[96,128]{1,0:T(8,128)}, f32[96,128]{1,0:T(8,128)S(1)}, u32[]{:S(2)}, u32[]{:S(2)}) collective-permute-start(f32[96,128]{1,0:T(8,128)} %get-tuple-element.40.refs_0_), channel_id=1, source_target_pairs={{0,24},{8,16},{16,8},{24,0},{1,25},{9,17},{17,9},{25,1},{2,26},{10... | collective-permute-start | bytes 147464 | tf_op jit(solution)/shard_map/ppermute | solution.py:348
  13.2 39.8 %collective-permute-start.10 = (f32[768,128]{1,0:T(8,128)}, f32[768,128]{1,0:T(8,128)S(1)}, u32[]{:S(2)}, u32[]{:S(2)}) collective-permute-start(f32[768,128]{1,0:T(8,128)} %get-tuple-element.38), channel_id=1, source_target_pairs={{0,6},{1,38},{2,4},{3,36},{4,2},{5,34},{6,0},{7,32},{32,7},{33,39}... | collective-permute-start | bytes 1179656 | tf_op jit(solution)/shard_map/ppermute | solution.py:358
  16.5 36.5 %collective-permute-start.8 = (f32[768,128]{1,0:T(8,128)}, f32[768,128]{1,0:T(8,128)}, u32[]{:S(2)}, u32[]{:S(2)}) collective-permute-start(f32[768,128]{1,0:T(8,128)} %get-tuple-element.38), channel_id=1, source_target_pairs={{0,2},{1,34},{2,0},{3,32},{4,6},{5,38},{6,4},{7,36},{32,3},{33,35}... | collective-permute-start | bytes 1179656 | tf_op jit(solution)/shard_map/ppermute | solution.py:358
  16.9 36.1 %collective-permute-start.9 = (f32[768,128]{1,0:T(8,128)}, f32[768,128]{1,0:T(8,128)}, u32[]{:S(2)}, u32[]{:S(2)}) collective-permute-start(f32[768,128]{1,0:T(8,128)} %get-tuple-element.38), channel_id=1, source_target_pairs={{0,4},{1,36},{2,6},{3,38},{4,0},{5,32},{6,2},{7,34},{32,5},{33,37}... | collective-permute-start | bytes 1179656 | tf_op jit(solution)/shard_map/ppermute | solution.py:358
  20.1 18.6 %collective-permute-start.4 = (f32[4,96,128]{2,1,0:T(8,128)S(1)}, f32[4,96,128]{2,1,0:T(8,128)S(1)}, u32[]{:S(2)}, u32[]{:S(2)}) collective-permute-start(f32[4,96,128]{2,1,0:T(8,128)S(1)} %shard_map.105.refs_0_.own), channel_id=1, source_target_pairs={{0,32},{32,0},{1,33},{33,1},{2,34},{34,2},{3,35},{35,3},{4,36},{36... | collective-permute-start | bytes 589832 | tf_op jit(solution)/shard_map/ppermute | solution.py:348
  20.3 15.1 %collective-permute-start.5 = (f32[136,256]{1,0:T(8,128)S(1)}, f32[136,256]{1,0:T(8,128)S(1)}, u32[]{:S(2)}, u32[]{:S(2)}) collective-permute-start(f32[136,256]{1,0:T(8,128)S(1)} %get-tuple-element.49), channel_id=1, source_target_pairs={{0,1},{1,0},{64,65},{65,64},{2,3},{3,2},{66,67},{67,66},{4,5},{5,4... | collective-permute-start | bytes 417800 | tf_op jit(solution)/shard_map/ppermute | solution.py:348
  35.4 7.4 %collective-permute-start.6 = (f32[136,256]{1,0:T(8,128)S(1)}, f32[136,256]{1,0:T(8,128)S(1)}, u32[]{:S(2)}, u32[]{:S(2)}) collective-permute-start(f32[136,256]{1,0:T(8,128)S(1)} %get-tuple-element.50), channel_id=1, source_target_pairs={{0,64},{1,65},{64,0},{65,1},{2,66},{3,67},{66,2},{67,3},{4,68},{5,... | collective-permute-start | bytes 417800 | tf_op jit(solution)/shard_map/ppermute | solution.py:348
  38.7 6.3 %collective-permute-start.7 = (f32[136,256]{1,0:T(8,128)S(1)}, f32[136,256]{1,0:T(8,128)S(1)}, u32[]{:S(2)}, u32[]{:S(2)}) collective-permute-start(f32[136,256]{1,0:T(8,128)S(1)} %get-tuple-element.51), channel_id=1, source_target_pairs={{0,65},{1,64},{64,1},{65,0},{2,67},{3,66},{66,3},{67,2},{4,69},{5,... | collective-permute-start | bytes 417800 | tf_op jit(solution)/shard_map/ppermute | solution.py:348
  46.7 46.2 %all-to-all-start = ((f32[32,72,128]{2,1,0:T(8,128)}), f32[32,72,128]{2,1,0:T(8,128)S(1)}, u32[]{:S(2)}, u32[]{:S(2)}) async-start(f32[32,72,128]{2,1,0:T(8,128)} %shard_map.110), calls=%async_computation | async-start | bytes 2359296 | tf_op jit(solution)/shard_map/all_to_all | solution.py:437
  67.9 3.9 %collective-permute-start.12 = (f32[4,32,128]{2,1,0:T(8,128)S(1)}, f32[4,32,128]{2,1,0:T(8,128)S(1)}, u32[]{:S(2)}, u32[]{:S(2)}) collective-permute-start(f32[4,32,128]{2,1,0:T(8,128)S(1)} %add_add_fusion.4), channel_id=1, source_target_pairs={{0,8},{8,0},{16,24},{24,16},{1,9},{9,1},{17,25},{25,17},{2,10},{10... | collective-permute-start | bytes 196616 | tf_op jit(solution)/shard_map/ppermute | solution.py:348
  69.3 5.4 %collective-permute-start.13 = (f32[4,32,128]{2,1,0:T(8,128)S(1)}, f32[4,32,128]{2,1,0:T(8,128)S(1)}, u32[]{:S(2)}, u32[]{:S(2)}) collective-permute-start(f32[4,32,128]{2,1,0:T(8,128)S(1)} %add_add_fusion.4), channel_id=1, source_target_pairs={{0,16},{8,24},{16,0},{24,8},{1,17},{9,25},{17,1},{25,9},{2,18},{10... | collective-permute-start | bytes 196616 | tf_op jit(solution)/shard_map/ppermute | solution.py:348
  71.7 4.5 %collective-permute-start.14 = (f32[4,32,128]{2,1,0:T(8,128)S(1)}, f32[4,32,128]{2,1,0:T(8,128)S(1)}, u32[]{:S(2)}, u32[]{:S(2)}) collective-permute-start(f32[4,32,128]{2,1,0:T(8,128)S(1)} %add_add_fusion.4), channel_id=1, source_target_pairs={{0,24},{8,16},{16,8},{24,0},{1,25},{9,17},{17,9},{25,1},{2,26},{10... | collective-permute-start | bytes 196616 | tf_op jit(solution)/shard_map/ppermute | solution.py:348
  76.9 2.8 %collective-permute-start.15 = (f32[4,32,128]{2,1,0:T(8,128)S(1)}, f32[4,32,128]{2,1,0:T(8,128)S(1)}, u32[]{:S(2)}, u32[]{:S(2)}) collective-permute-start(f32[4,32,128]{2,1,0:T(8,128)S(1)} %get-tuple-element.62.own), channel_id=1, source_target_pairs={{0,32},{32,0},{1,33},{33,1},{2,34},{34,2},{3,35},{35,3},{4,36},{36... | collective-permute-start | bytes 196616 | tf_op jit(solution)/shard_map/ppermute | solution.py:348
  80.6 4.8 %collective-permute-start.16 = (f32[64,512]{1,0:T(8,128)S(1)}, f32[64,512]{1,0:T(8,128)S(1)}, u32[]{:S(2)}, u32[]{:S(2)}) collective-permute-start(f32[64,512]{1,0:T(8,128)S(1)} %get-tuple-element.68), channel_id=1, source_target_pairs={{0,2},{2,0},{4,6},{6,4},{1,3},{3,1},{5,7},{7,5},{8,10},{10,8},{12,... | collective-permute-start | bytes 393224 | tf_op jit(solution)/shard_map/ppermute | solution.py:348
  81.9 8.5 %collective-permute-start.17 = (f32[64,512]{1,0:T(8,128)S(1)}, f32[64,512]{1,0:T(8,128)S(1)}, u32[]{:S(2)}, u32[]{:S(2)}) collective-permute-start(f32[64,512]{1,0:T(8,128)S(1)} %get-tuple-element.69), channel_id=1, source_target_pairs={{0,4},{2,6},{4,0},{6,2},{1,5},{3,7},{5,1},{7,3},{8,12},{10,14},{12... | collective-permute-start | bytes 393224 | tf_op jit(solution)/shard_map/ppermute | solution.py:348
  84.3 8.6 %collective-permute-start.18 = (f32[64,512]{1,0:T(8,128)S(1)}, f32[64,512]{1,0:T(8,128)S(1)}, u32[]{:S(2)}, u32[]{:S(2)}) collective-permute-start(f32[64,512]{1,0:T(8,128)S(1)} %get-tuple-element.70), channel_id=1, source_target_pairs={{0,6},{2,4},{4,2},{6,0},{1,7},{3,5},{5,3},{7,1},{8,14},{10,12},{12... | collective-permute-start | bytes 393224 | tf_op jit(solution)/shard_map/ppermute | solution.py:348
  92.9 3.9 %collective-permute-start.19 = (f32[64,512]{1,0:T(8,128)S(1)}, f32[64,512]{1,0:T(8,128)S(1)}, u32[]{:S(2)}, u32[]{:S(2)}) collective-permute-start(f32[64,512]{1,0:T(8,128)S(1)} %add_multiply_fusion), channel_id=1, source_target_pairs={{0,1},{1,0},{64,65},{65,64},{2,3},{3,2},{66,67},{67,66},{4,5},{5,4... | collective-permute-start | bytes 393224 | tf_op jit(solution)/shard_map/ppermute | solution.py:348
  93.0 6.7 %collective-permute-start.20 = (f32[64,512]{1,0:T(8,128)S(1)}, f32[64,512]{1,0:T(8,128)S(1)}, u32[]{:S(2)}, u32[]{:S(2)}) collective-permute-start(f32[64,512]{1,0:T(8,128)S(1)} %add_multiply_fusion), channel_id=1, source_target_pairs={{0,64},{1,65},{64,0},{65,1},{2,66},{3,67},{66,2},{67,3},{4,68},{5,... | collective-permute-start | bytes 393224 | tf_op jit(solution)/shard_map/ppermute | solution.py:348
  94.7 7.8 %collective-permute-start.21 = (f32[64,512]{1,0:T(8,128)S(1)}, f32[64,512]{1,0:T(8,128)S(1)}, u32[]{:S(2)}, u32[]{:S(2)}) collective-permute-start(f32[64,512]{1,0:T(8,128)S(1)} %add_multiply_fusion), channel_id=1, source_target_pairs={{0,65},{1,64},{64,1},{65,0},{2,67},{3,66},{66,3},{67,2},{4,69},{5,... | collective-permute-start | bytes 393224 | tf_op jit(solution)/shard_map/ppermute | solution.py:348
  106.6 3.9 %collective-permute-start.23 = (f32[64,256]{1,0:T(8,128)S(1)}, f32[64,256]{1,0:T(8,128)S(1)}, u32[]{:S(2)}, u32[]{:S(2)}) collective-permute-start(f32[64,256]{1,0:T(8,128)S(1)} %add.86), channel_id=1, source_target_pairs={{0,2},{2,0},{4,6},{6,4},{1,3},{3,1},{5,7},{7,5},{8,10},{10,8},{12,... | collective-permute-start | bytes 196616 | tf_op jit(solution)/shard_map/ppermute | solution.py:348
  106.7 4.7 %collective-permute-start.24 = (f32[64,256]{1,0:T(8,128)S(1)}, f32[64,256]{1,0:T(8,128)S(1)}, u32[]{:S(2)}, u32[]{:S(2)}) collective-permute-start(f32[64,256]{1,0:T(8,128)S(1)} %add.86), channel_id=1, source_target_pairs={{0,4},{2,6},{4,0},{6,2},{1,5},{3,7},{5,1},{7,3},{8,12},{10,14},{12... | collective-permute-start | bytes 196616 | tf_op jit(solution)/shard_map/ppermute | solution.py:348
  108.3 4.6 %collective-permute-start.25 = (f32[64,256]{1,0:T(8,128)S(1)}, f32[64,256]{1,0:T(8,128)S(1)}, u32[]{:S(2)}, u32[]{:S(2)}) collective-permute-start(f32[64,256]{1,0:T(8,128)S(1)} %add.86), channel_id=1, source_target_pairs={{0,6},{2,4},{4,2},{6,0},{1,7},{3,5},{5,3},{7,1},{8,14},{10,12},{12... | collective-permute-start | bytes 196616 | tf_op jit(solution)/shard_map/ppermute | solution.py:348
  112.9 3.9 %collective-permute-start.26 = (f32[64,256]{1,0:T(8,128)S(1)}, f32[64,256]{1,0:T(8,128)S(1)}, u32[]{:S(2)}, u32[]{:S(2)}) collective-permute-start(f32[64,256]{1,0:T(8,128)S(1)} %add_add_fusion.2), channel_id=1, source_target_pairs={{0,8},{8,0},{16,24},{24,16},{1,9},{9,1},{17,25},{25,17},{2,10},{10... | collective-permute-start | bytes 196616 | tf_op jit(solution)/shard_map/ppermute | solution.py:348
  113.0 4.7 %collective-permute-start.27 = (f32[64,256]{1,0:T(8,128)S(1)}, f32[64,256]{1,0:T(8,128)S(1)}, u32[]{:S(2)}, u32[]{:S(2)}) collective-permute-start(f32[64,256]{1,0:T(8,128)S(1)} %add_add_fusion.2), channel_id=1, source_target_pairs={{0,16},{8,24},{16,0},{24,8},{1,17},{9,25},{17,1},{25,9},{2,18},{10... | collective-permute-start | bytes 196616 | tf_op jit(solution)/shard_map/ppermute | solution.py:348
  114.6 4.3 %collective-permute-start.28 = (f32[64,256]{1,0:T(8,128)S(1)}, f32[64,256]{1,0:T(8,128)S(1)}, u32[]{:S(2)}, u32[]{:S(2)}) collective-permute-start(f32[64,256]{1,0:T(8,128)S(1)} %add_add_fusion.2), channel_id=1, source_target_pairs={{0,24},{8,16},{16,8},{24,0},{1,25},{9,17},{17,9},{25,1},{2,26},{10... | collective-permute-start | bytes 196616 | tf_op jit(solution)/shard_map/ppermute | solution.py:348
  120.0 3.9 %collective-permute-start.29 = (f32[64,512]{1,0:T(8,128)S(1)}, f32[64,512]{1,0:T(8,128)S(1)}, u32[]{:S(2)}, u32[]{:S(2)}) collective-permute-start(f32[64,512]{1,0:T(8,128)S(1)} %shard_map.113), channel_id=1, source_target_pairs={{0,1},{1,0},{64,65},{65,64},{2,3},{3,2},{66,67},{67,66},{4,5},{5,4... | collective-permute-start | bytes 393224 | tf_op jit(solution)/shard_map/ppermute | solution.py:348
  120.2 7.0 %collective-permute-start.30 = (f32[64,512]{1,0:T(8,128)S(1)}, f32[64,512]{1,0:T(8,128)S(1)}, u32[]{:S(2)}, u32[]{:S(2)}) collective-permute-start(f32[64,512]{1,0:T(8,128)S(1)} %shard_map.113), channel_id=1, source_target_pairs={{0,64},{1,65},{64,0},{65,1},{2,66},{3,67},{66,2},{67,3},{4,68},{5,... | collective-permute-start | bytes 393224 | tf_op jit(solution)/shard_map/ppermute | solution.py:348
  123.4 5.2 %collective-permute-start.31 = (f32[64,512]{1,0:T(8,128)S(1)}, f32[64,512]{1,0:T(8,128)S(1)}, u32[]{:S(2)}, u32[]{:S(2)}) collective-permute-start(f32[64,512]{1,0:T(8,128)S(1)} %shard_map.113), channel_id=1, source_target_pairs={{0,65},{1,64},{64,1},{65,0},{2,67},{3,66},{66,3},{67,2},{4,69},{5,... | collective-permute-start | bytes 393224 | tf_op jit(solution)/shard_map/ppermute | solution.py:348
  128.6 6.1 %collective-permute-start.32 = (f32[64,512]{1,0:T(8,128)S(1)}, f32[64,512]{1,0:T(8,128)S(1)}, u32[]{:S(2)}, u32[]{:S(2)}) collective-permute-start(f32[64,512]{1,0:T(8,128)S(1)} %add_subtract_fusion), channel_id=1, source_target_pairs={{0,32},{32,0},{1,33},{33,1},{2,34},{34,2},{3,35},{35,3},{4,36},{36... | collective-permute-start | bytes 393224 | tf_op jit(solution)/shard_map/ppermute | solution.py:348
  (7 other events, 89.2 us)

commit v6 on v5

--- a/solution.py
+++ b/solution.py
@@ -349,15 +349,6 @@
     ]
 
 
-def tile_from(pack, o):
-    ny = SIZES["y"]
-    perm = [
-        ((c * ny + y) * 2 + z, (z * ny + (y ^ o)) * 2 + c)
-        for c in range(2) for y in range(ny) for z in range(2)
-    ]
-    return lax.ppermute(pack, ("core", "y", "zl"), perm)
-
-
 def together(*arrays):
     return lax.optimization_barrier(arrays)
 
@@ -393,10 +384,10 @@
     )(batch_index.reshape(1, rows), pool_features, pool_targets.T, centers, weights.T)
 
     gathered = mates([drawn] * nx, ("x",))
-    tile = tile_from(pack, 0)
+    tile = lax.ppermute(pack, ("core", "zl"), [(0, 0), (2, 1), (1, 2), (3, 3)])
     tile, drawn, *gathered = together(tile, drawn, *gathered)
     own = call(order_body, shape(nx, rows + half, dim), x, drawn, *gathered, scalars=1)
-    others = [tile_from(pack, o) for o in range(1, ny)]
+    others = mates([tile] * ny, ("y",))
     (mate,) = mates([own] * 2, ("core",))
     eig_vectors, own = together(eig_vectors, own)
 

time: 136 us -> 130 us (0.956)
  waiting for transfers between devices: 47.9 us -> 42.2 us
    ppermute x29 -> x32, starting transfers between devices: 40.5 us -> 46.7 us  [mates(): lax.ppermute(parts[o], axes, [(i, i ^ o) for i in range(n)])]
    ppermute x4 -> x1, starting transfers between devices: 11 us -> 4.94 us  [per_device(): tile = lax.ppermute(pack, ('core', 'zl'), [(0, 0), (2, 1), (1, 2), (3, 3)])]
    ppermute x29 -> x32, waiting for transfers between devices: 47.9 us -> 42.2 us  [mates(): lax.ppermute(parts[o], axes, [(i, i ^ o) for i in range(n)])]
  transfers between devices with their start and end apart: 34 -> 34, of which waited for: 19 -> 21; matrix products, arithmetic and copies ran while one was open for 0% -> 0% of each run, Pallas kernels for 15% -> 16%
where the time goes in v6:
time: 130 us; the launch traced here: 129 us
  starting transfers between devices  57.3 us (44%)
  waiting for transfers between devices  42.2 us (32%)
  Pallas kernels  27.2 us (21%)
    ppermute x32, starting transfers between devices, mates(): lax.ppermute(parts[o], axes, [(i, i ^ o) for i in range(n)])  46.7 us
    ppermute x32, waiting for transfers between devices, mates(): lax.ppermute(parts[o], axes, [(i, i ^ o) for i in range(n)])  42.2 us
    pallas_call x9, Pallas kernels, call(): pl.pallas_call(body, out_shape=outs, in_specs=[smem] * scalars + [VMEM] *...  23.6 us
    all_to_all x1, starting transfers between devices, per_device(): lax.all_to_all(points, OWNERS, split_axis=0, concat_axis=0, tiled=True)  5.76 us
    ppermute x1, starting transfers between devices, per_device(): tile = lax.ppermute(pack, ('core', 'zl'), [(0, 0), (2, 1), (1, 2), (3, 3)])  4.94 us
    pallas_call x1, Pallas kernels, per_device(): pl.pallas_call(front_body, out_shape=[shape(rows + half, dim), shape(cdev...  3.59 us
  transfers between devices with their start and end apart: 34, of which 21 were waited for; matrix products, arithmetic and copies ran while one was open for 0% of the time, Pallas kernels for 16%

profile of v6, /device:TPU:1, one launch (start us, length us, event | category | flops | bytes accessed | tf_op | source)
XLA Modules:
  0.0 129.3 jit_solution(2466758036929320501)
XLA Ops:
  0.7 3.6 %shard_map.104 = (f32[96,128]{1,0:T(8,128)}, f32[768,128]{1,0:T(8,128)}) custom-call(s32[1,64]{1,0:T(1,128)} %bitcast.19, f32[1024,128]{1,0:T(8,128)} %pool_f.1, f32[64,1024]{1,0:T(8,128)} %bitcast.16, f32[512,128]{1,0:T(8,128)} %centers.1, f32[64,512]{1,0:T(8,128)} %bitcast.17), custom_call_target="tpu_custom_call" | custom-call | tf_op jit(solution)/shard_map/pallas_call | solution.py:372
  4.3 4.9 %collective-permute-start = (f32[768,128]{1,0:T(8,128)}, f32[768,128]{1,0:T(8,128)S(1)}, u32[]{:S(2)}, u32[]{:S(2)}) collective-permute-start(f32[768,128]{1,0:T(8,128)} %get-tuple-element.38), channel_id=1, source_target_pairs={{0,0},{32,1},{1,32},{33,33},{2,2},{34,3},{3,34},{35,35},{4,4},{36,... | collective-permute-start | bytes 1179656 | tf_op jit(solution)/shard_map/ppermute | solution.py:387
  10.5 2.5 %collective-permute-start.2 = (f32[96,128]{1,0:T(8,128)}, f32[96,128]{1,0:T(8,128)S(1)}, u32[]{:S(2)}, u32[]{:S(2)}) collective-permute-start(f32[96,128]{1,0:T(8,128)} %get-tuple-element.40.refs_0_), channel_id=1, source_target_pairs={{0,16},{8,24},{16,0},{24,8},{1,17},{9,25},{17,1},{25,9},{2,18},{10... | collective-permute-start | bytes 147464 | tf_op jit(solution)/shard_map/ppermute | solution.py:348
  13.1 2.0 %collective-permute-done.2.refs_2_ = f32[96,128]{1,0:T(8,128)S(1)} collective-permute-done((f32[96,128]{1,0:T(8,128)}, f32[96,128]{1,0:T(8,128)S(1)}, u32[]{:S(2)}, u32[]{:S(2)}) %collective-permute-start.2) | collective-permute-done | bytes 49184 | tf_op jit(solution)/shard_map/ppermute | solution.py:348
  15.2 2.1 %collective-permute-done.3.refs_3_ = f32[96,128]{1,0:T(8,128)S(1)} collective-permute-done((f32[96,128]{1,0:T(8,128)}, f32[96,128]{1,0:T(8,128)S(1)}, u32[]{:S(2)}, u32[]{:S(2)}) %collective-permute-start.3) | collective-permute-done | bytes 49184 | tf_op jit(solution)/shard_map/ppermute | solution.py:348
  17.3 2.7 %collective-permute-start.10 = (f32[768,128]{1,0:T(8,128)S(1)}, f32[768,128]{1,0:T(8,128)}, u32[]{:S(2)}, u32[]{:S(2)}) collective-permute-start(f32[768,128]{1,0:T(8,128)S(1)} %collective-permute-done.refs_2_), channel_id=1, source_target_pairs={{0,6},{2,4},{4,2},{6,0},{1,7},{3,5},{5,3},{7,1},{8,14},{10,12},{12... | collective-permute-start | bytes 1179656 | tf_op jit(solution)/shard_map/ppermute | solution.py:348
  22.8 2.1 %collective-permute-start.5 = (f32[136,256]{1,0:T(8,128)S(1)}, f32[136,256]{1,0:T(8,128)S(1)}, u32[]{:S(2)}, u32[]{:S(2)}) collective-permute-start(f32[136,256]{1,0:T(8,128)S(1)} %get-tuple-element.49), channel_id=1, source_target_pairs={{0,1},{1,0},{64,65},{65,64},{2,3},{3,2},{66,67},{67,66},{4,5},{5,4... | collective-permute-start | bytes 417800 | tf_op jit(solution)/shard_map/ppermute | solution.py:348
  24.9 4.1 %collective-permute-done.5.refs_1_ = f32[136,256]{1,0:T(8,128)S(1)} collective-permute-done((f32[136,256]{1,0:T(8,128)S(1)}, f32[136,256]{1,0:T(8,128)S(1)}, u32[]{:S(2)}, u32[]{:S(2)}) %collective-permute-start.5) | collective-permute-done | bytes 139296 | tf_op jit(solution)/shard_map/ppermute | solution.py:348
  29.0 3.2 %collective-permute-start.6 = (f32[136,256]{1,0:T(8,128)S(1)}, f32[136,256]{1,0:T(8,128)S(1)}, u32[]{:S(2)}, u32[]{:S(2)}) collective-permute-start(f32[136,256]{1,0:T(8,128)S(1)} %get-tuple-element.50), channel_id=1, source_target_pairs={{0,64},{1,65},{64,0},{65,1},{2,66},{3,67},{66,2},{67,3},{4,68},{5,... | collective-permute-start | bytes 417800 | tf_op jit(solution)/shard_map/ppermute | solution.py:348
  32.7 4.1 %shard_map.106 = (bf16[1,512,512]{2,1,0:T(8,128)(2,1)S(1)}, bf16[1,512,512]{2,1,0:T(8,128)(2,1)S(1)}, f32[4,32,128]{2,1,0:T(8,128)S(1)}, f32[4,32,128]{2,1,0:T(8...) custom-call(f32[4,96,128]{2,1,0:T(8,128)S(1)} %shard_map.105.refs_0_.own, ...), custom_call_target="tpu_custom_call" | custom-call | flops 100000000 | bytes 65536 | tf_op jit(solution)/shard_map/pallas_call | solution.py:331
  36.7 2.3 %collective-permute-done.7.refs_3_ = f32[136,256]{1,0:T(8,128)S(1)} collective-permute-done((f32[136,256]{1,0:T(8,128)S(1)}, f32[136,256]{1,0:T(8,128)S(1)}, u32[]{:S(2)}, u32[]{:S(2)}) %collective-permute-start.7) | collective-permute-done | bytes 139296 | tf_op jit(solution)/shard_map/ppermute | solution.py:348
  39.0 1.7 %shard_map.110 = f32[32,72,128]{2,1,0:T(8,128)} custom-call(f32[136,256]{1,0:T(8,128)S(1)} %get-tuple-element.58.refs_0_, f32[136,256]{1,0:T(8,128)S(1)} %collective-permute-done.5.refs_1_, f32[136,256]{1,0:T(8,128)S(1)} %collective-permute-done.6.refs_2_, f32[136,256]{1,0:T(8,128)S(1)} %collective-permute-done.7.refs_3_), custom_call_target="tpu_custom_call" | custom-call | tf_op jit(solution)/shard_map/pallas_call | solution.py:331
  40.8 5.8 %all-to-all-start = ((f32[32,72,128]{2,1,0:T(8,128)}), f32[32,72,128]{2,1,0:T(8,128)S(1)}, u32[]{:S(2)}, u32[]{:S(2)}) async-start(f32[32,72,128]{2,1,0:T(8,128)} %shard_map.110), calls=%async_computation | async-start | bytes 2359296 | tf_op jit(solution)/shard_map/all_to_all | solution.py:428
  46.6 13.5 %shard_map.108 = (bf16[3,512,512]{2,1,0:T(8,128)(2,1)S(1)}, bf16[3,512,512]{2,1,0:T(8,128)(2,1)S(1)}, f32[4,32,128]{2,1,0:T(8,128)S(1)}, f32[4,32,128]{2,1,0:T(8,128)S(1)}) custom-call(f32[4,96,128]{2,1,0:T(8,128)S(1)} %shard_map.105.refs_0_.own, f32[4,96,128]{2,1,0:T(8,128)S(1)} %collective-permute-done.4.refs_1_, ...), custom_call_target="tpu_custom_call" | custom-call | flops 30000001024 | bytes 65536 | tf_op jit(solution)/shard_map/pallas_call | solution.py:331
  63.0 2.4 %collective-permute-start.13 = (f32[4,32,128]{2,1,0:T(8,128)S(1)}, f32[4,32,128]{2,1,0:T(8,128)S(1)}, u32[]{:S(2)}, u32[]{:S(2)}) collective-permute-start(f32[4,32,128]{2,1,0:T(8,128)S(1)} %add_add_fusion.4), channel_id=1, source_target_pairs={{0,16},{8,24},{16,0},{24,8},{1,17},{9,25},{17,1},{25,9},{2,18},{10... | collective-permute-start | bytes 196616 | tf_op jit(solution)/shard_map/ppermute | solution.py:348
  65.5 2.9 %collective-permute-done.13 = f32[4,32,128]{2,1,0:T(8,128)S(1)} collective-permute-done((f32[4,32,128]{2,1,0:T(8,128)S(1)}, f32[4,32,128]{2,1,0:T(8,128)S(1)}, u32[]{:S(2)}, u32[]{:S(2)}) %collective-permute-start.13) | collective-permute-done | bytes 65568 | tf_op jit(solution)/shard_map/ppermute | solution.py:348
  68.4 1.5 %collective-permute-done.14 = f32[4,32,128]{2,1,0:T(8,128)S(1)} collective-permute-done((f32[4,32,128]{2,1,0:T(8,128)S(1)}, f32[4,32,128]{2,1,0:T(8,128)S(1)}, u32[]{:S(2)}, u32[]{:S(2)}) %collective-permute-start.14) | collective-permute-done | bytes 65568 | tf_op jit(solution)/shard_map/ppermute | solution.py:348
  70.6 1.9 %collective-permute-start.15 = (f32[4,32,128]{2,1,0:T(8,128)S(1)}, f32[4,32,128]{2,1,0:T(8,128)S(1)}, u32[]{:S(2)}, u32[]{:S(2)}) collective-permute-start(f32[4,32,128]{2,1,0:T(8,128)S(1)} %get-tuple-element.62.own), channel_id=1, source_target_pairs={{0,32},{32,0},{1,33},{33,1},{2,34},{34,2},{3,35},{35,3},{4,36},{36... | collective-permute-start | bytes 196616 | tf_op jit(solution)/shard_map/ppermute | solution.py:348
  75.5 2.4 %collective-permute-start.17 = (f32[64,512]{1,0:T(8,128)S(1)}, f32[64,512]{1,0:T(8,128)S(1)}, u32[]{:S(2)}, u32[]{:S(2)}) collective-permute-start(f32[64,512]{1,0:T(8,128)S(1)} %get-tuple-element.69), channel_id=1, source_target_pairs={{0,4},{2,6},{4,0},{6,2},{1,5},{3,7},{5,1},{7,3},{8,12},{10,14},{12... | collective-permute-start | bytes 393224 | tf_op jit(solution)/shard_map/ppermute | solution.py:348
  79.0 5.0 %collective-permute-done.17 = f32[64,512]{1,0:T(8,128)S(1)} collective-permute-done((f32[64,512]{1,0:T(8,128)S(1)}, f32[64,512]{1,0:T(8,128)S(1)}, u32[]{:S(2)}, u32[]{:S(2)}) %collective-permute-start.17) | collective-permute-done | bytes 131104 | tf_op jit(solution)/shard_map/ppermute | solution.py:348
  84.0 2.5 %collective-permute-done.18 = f32[64,512]{1,0:T(8,128)S(1)} collective-permute-done((f32[64,512]{1,0:T(8,128)S(1)}, f32[64,512]{1,0:T(8,128)S(1)}, u32[]{:S(2)}, u32[]{:S(2)}) %collective-permute-start.18) | collective-permute-done | bytes 131104 | tf_op jit(solution)/shard_map/ppermute | solution.py:348
  87.2 3.3 %collective-permute-start.20 = (f32[64,512]{1,0:T(8,128)S(1)}, f32[64,512]{1,0:T(8,128)S(1)}, u32[]{:S(2)}, u32[]{:S(2)}) collective-permute-start(f32[64,512]{1,0:T(8,128)S(1)} %add_multiply_fusion), channel_id=1, source_target_pairs={{0,64},{1,65},{64,0},{65,1},{2,66},{3,67},{66,2},{67,3},{4,68},{5,... | collective-permute-start | bytes 393224 | tf_op jit(solution)/shard_map/ppermute | solution.py:348
  90.5 5.0 %collective-permute-done.20 = f32[64,512]{1,0:T(8,128)S(1)} collective-permute-done((f32[64,512]{1,0:T(8,128)S(1)}, f32[64,512]{1,0:T(8,128)S(1)}, u32[]{:S(2)}, u32[]{:S(2)}) %collective-permute-start.20) | collective-permute-done | bytes 131104 | tf_op jit(solution)/shard_map/ppermute | solution.py:348
  95.5 2.8 %collective-permute-done.21 = f32[64,512]{1,0:T(8,128)S(1)} collective-permute-done((f32[64,512]{1,0:T(8,128)S(1)}, f32[64,512]{1,0:T(8,128)S(1)}, u32[]{:S(2)}, u32[]{:S(2)}) %collective-permute-start.21) | collective-permute-done | bytes 131104 | tf_op jit(solution)/shard_map/ppermute | solution.py:348
  98.4 1.6 %shard_map.112 = f32[64,256]{1,0:T(8,128)S(1)} custom-call(f32[32,72,128]{2,1,0:T(8,128)S(1)} %all-to-all-done.points, f32[64,512]{1,0:T(8,128)S(1)} %add_add_fusion.grads), custom_call_target="tpu_custom_call" | custom-call | tf_op jit(solution)/shard_map/pallas_call | solution.py:331
  102.4 1.6 %collective-permute-start.24 = (f32[64,256]{1,0:T(8,128)S(1)}, f32[64,256]{1,0:T(8,128)S(1)}, u32[]{:S(2)}, u32[]{:S(2)}) collective-permute-start(f32[64,256]{1,0:T(8,128)S(1)} %add.86), channel_id=1, source_target_pairs={{0,4},{2,6},{4,0},{6,2},{1,5},{3,7},{5,1},{7,3},{8,12},{10,14},{12... | collective-permute-start | bytes 196616 | tf_op jit(solution)/shard_map/ppermute | solution.py:348
  104.0 2.3 %collective-permute-start.25 = (f32[64,256]{1,0:T(8,128)S(1)}, f32[64,256]{1,0:T(8,128)S(1)}, u32[]{:S(2)}, u32[]{:S(2)}) collective-permute-start(f32[64,256]{1,0:T(8,128)S(1)} %add.86), channel_id=1, source_target_pairs={{0,6},{2,4},{4,2},{6,0},{1,7},{3,5},{5,3},{7,1},{8,14},{10,12},{12... | collective-permute-start | bytes 196616 | tf_op jit(solution)/shard_map/ppermute | solution.py:348
  108.8 1.5 %collective-permute-start.27 = (f32[64,256]{1,0:T(8,128)S(1)}, f32[64,256]{1,0:T(8,128)S(1)}, u32[]{:S(2)}, u32[]{:S(2)}) collective-permute-start(f32[64,256]{1,0:T(8,128)S(1)} %add_add_fusion.2), channel_id=1, source_target_pairs={{0,16},{8,24},{16,0},{24,8},{1,17},{9,25},{17,1},{25,9},{2,18},{10... | collective-permute-start | bytes 196616 | tf_op jit(solution)/shard_map/ppermute | solution.py:348
  110.3 2.3 %collective-permute-start.28 = (f32[64,256]{1,0:T(8,128)S(1)}, f32[64,256]{1,0:T(8,128)S(1)}, u32[]{:S(2)}, u32[]{:S(2)}) collective-permute-start(f32[64,256]{1,0:T(8,128)S(1)} %add_add_fusion.2), channel_id=1, source_target_pairs={{0,24},{8,16},{16,8},{24,0},{1,25},{9,17},{17,9},{25,1},{2,26},{10... | collective-permute-start | bytes 196616 | tf_op jit(solution)/shard_map/ppermute | solution.py:348
  117.3 2.4 %collective-permute-start.31 = (f32[64,512]{1,0:T(8,128)S(1)}, f32[64,512]{1,0:T(8,128)S(1)}, u32[]{:S(2)}, u32[]{:S(2)}) collective-permute-start(f32[64,512]{1,0:T(8,128)S(1)} %shard_map.113), channel_id=1, source_target_pairs={{0,65},{1,64},{64,1},{65,0},{2,67},{3,66},{66,3},{67,2},{4,69},{5,... | collective-permute-start | bytes 393224 | tf_op jit(solution)/shard_map/ppermute | solution.py:348
  119.7 1.6 %collective-permute-done.30 = f32[64,512]{1,0:T(8,128)S(1)} collective-permute-done((f32[64,512]{1,0:T(8,128)S(1)}, f32[64,512]{1,0:T(8,128)S(1)}, u32[]{:S(2)}, u32[]{:S(2)}) %collective-permute-start.30) | collective-permute-done | bytes 131104 | tf_op jit(solution)/shard_map/ppermute | solution.py:348
  122.7 4.9 %collective-permute-start.32 = (f32[64,512]{1,0:T(8,128)S(1)}, f32[64,512]{1,0:T(8,128)S(1)}, u32[]{:S(2)}, u32[]{:S(2)}) collective-permute-start(f32[64,512]{1,0:T(8,128)S(1)} %add_subtract_fusion), channel_id=1, source_target_pairs={{0,32},{32,0},{1,33},{33,1},{2,34},{34,2},{3,35},{35,3},{4,36},{36... | collective-permute-start | bytes 393224 | tf_op jit(solution)/shard_map/ppermute | solution.py:348
  (68 shorter events, 25.8 us)
Async XLA Ops:
  4.3 13.0 %collective-permute-start = (f32[768,128]{1,0:T(8,128)}, f32[768,128]{1,0:T(8,128)S(1)}, u32[]{:S(2)}, u32[]{:S(2)}) collective-permute-start(f32[768,128]{1,0:T(8,128)} %get-tuple-element.38), channel_id=1, source_target_pairs={{0,0},{32,1},{1,32},{33,33},{2,2},{34,3},{3,34},{35,35},{4,4},{36,... | collective-permute-start | bytes 1179656 | tf_op jit(solution)/shard_map/ppermute | solution.py:387
  9.2 3.9 %collective-permute-start.1 = (f32[96,128]{1,0:T(8,128)}, f32[96,128]{1,0:T(8,128)S(1)}, u32[]{:S(2)}, u32[]{:S(2)}) collective-permute-start(f32[96,128]{1,0:T(8,128)} %get-tuple-element.40.refs_0_), channel_id=1, source_target_pairs={{0,8},{8,0},{16,24},{24,16},{1,9},{9,1},{17,25},{25,17},{2,10},{10... | collective-permute-start | bytes 147464 | tf_op jit(solution)/shard_map/ppermute | solution.py:348
  10.5 4.7 %collective-permute-start.2 = (f32[96,128]{1,0:T(8,128)}, f32[96,128]{1,0:T(8,128)S(1)}, u32[]{:S(2)}, u32[]{:S(2)}) collective-permute-start(f32[96,128]{1,0:T(8,128)} %get-tuple-element.40.refs_0_), channel_id=1, source_target_pairs={{0,16},{8,24},{16,0},{24,8},{1,17},{9,25},{17,1},{25,9},{2,18},{10... | collective-permute-start | bytes 147464 | tf_op jit(solution)/shard_map/ppermute | solution.py:348
  12.9 4.4 %collective-permute-start.3 = (f32[96,128]{1,0:T(8,128)}, f32[96,128]{1,0:T(8,128)S(1)}, u32[]{:S(2)}, u32[]{:S(2)}) collective-permute-start(f32[96,128]{1,0:T(8,128)} %get-tuple-element.40.refs_0_), channel_id=1, source_target_pairs={{0,24},{8,16},{16,8},{24,0},{1,25},{9,17},{17,9},{25,1},{2,26},{10... | collective-permute-start | bytes 147464 | tf_op jit(solution)/shard_map/ppermute | solution.py:348
  17.3 29.2 %collective-permute-start.10 = (f32[768,128]{1,0:T(8,128)S(1)}, f32[768,128]{1,0:T(8,128)}, u32[]{:S(2)}, u32[]{:S(2)}) collective-permute-start(f32[768,128]{1,0:T(8,128)S(1)} %collective-permute-done.refs_2_), channel_id=1, source_target_pairs={{0,6},{2,4},{4,2},{6,0},{1,7},{3,5},{5,3},{7,1},{8,14},{10,12},{12... | collective-permute-start | bytes 1179656 | tf_op jit(solution)/shard_map/ppermute | solution.py:348
  20.0 26.5 %collective-permute-start.8 = (f32[768,128]{1,0:T(8,128)S(1)}, f32[768,128]{1,0:T(8,128)}, u32[]{:S(2)}, u32[]{:S(2)}) collective-permute-start(f32[768,128]{1,0:T(8,128)S(1)} %collective-permute-done.refs_2_), channel_id=1, source_target_pairs={{0,2},{2,0},{4,6},{6,4},{1,3},{3,1},{5,7},{7,5},{8,10},{10,8},{12,... | collective-permute-start | bytes 1179656 | tf_op jit(solution)/shard_map/ppermute | solution.py:348
  20.1 26.5 %collective-permute-start.9 = (f32[768,128]{1,0:T(8,128)S(1)}, f32[768,128]{1,0:T(8,128)}, u32[]{:S(2)}, u32[]{:S(2)}) collective-permute-start(f32[768,128]{1,0:T(8,128)S(1)} %collective-permute-done.refs_2_), channel_id=1, source_target_pairs={{0,4},{2,6},{4,0},{6,2},{1,5},{3,7},{5,1},{7,3},{8,12},{10,14},{12... | collective-permute-start | bytes 1179656 | tf_op jit(solution)/shard_map/ppermute | solution.py:348
  22.1 10.2 %collective-permute-start.4 = (f32[4,96,128]{2,1,0:T(8,128)S(1)}, f32[4,96,128]{2,1,0:T(8,128)S(1)}, u32[]{:S(2)}, u32[]{:S(2)}) collective-permute-start(f32[4,96,128]{2,1,0:T(8,128)S(1)} %shard_map.105.refs_0_.own), channel_id=1, source_target_pairs={{0,32},{32,0},{1,33},{33,1},{2,34},{34,2},{3,35},{35,3},{4,36},{36... | collective-permute-start | bytes 589832 | tf_op jit(solution)/shard_map/ppermute | solution.py:348
  22.8 6.2 %collective-permute-start.5 = (f32[136,256]{1,0:T(8,128)S(1)}, f32[136,256]{1,0:T(8,128)S(1)}, u32[]{:S(2)}, u32[]{:S(2)}) collective-permute-start(f32[136,256]{1,0:T(8,128)S(1)} %get-tuple-element.49), channel_id=1, source_target_pairs={{0,1},{1,0},{64,65},{65,64},{2,3},{3,2},{66,67},{67,66},{4,5},{5,4... | collective-permute-start | bytes 417800 | tf_op jit(solution)/shard_map/ppermute | solution.py:348
  29.0 7.7 %collective-permute-start.6 = (f32[136,256]{1,0:T(8,128)S(1)}, f32[136,256]{1,0:T(8,128)S(1)}, u32[]{:S(2)}, u32[]{:S(2)}) collective-permute-start(f32[136,256]{1,0:T(8,128)S(1)} %get-tuple-element.50), channel_id=1, source_target_pairs={{0,64},{1,65},{64,0},{65,1},{2,66},{3,67},{66,2},{67,3},{4,68},{5,... | collective-permute-start | bytes 417800 | tf_op jit(solution)/shard_map/ppermute | solution.py:348
  32.3 6.8 %collective-permute-start.7 = (f32[136,256]{1,0:T(8,128)S(1)}, f32[136,256]{1,0:T(8,128)S(1)}, u32[]{:S(2)}, u32[]{:S(2)}) collective-permute-start(f32[136,256]{1,0:T(8,128)S(1)} %get-tuple-element.51), channel_id=1, source_target_pairs={{0,65},{1,64},{64,1},{65,0},{2,67},{3,66},{66,3},{67,2},{4,69},{5,... | collective-permute-start | bytes 417800 | tf_op jit(solution)/shard_map/ppermute | solution.py:348
  40.8 45.8 %all-to-all-start = ((f32[32,72,128]{2,1,0:T(8,128)}), f32[32,72,128]{2,1,0:T(8,128)S(1)}, u32[]{:S(2)}, u32[]{:S(2)}) async-start(f32[32,72,128]{2,1,0:T(8,128)} %shard_map.110), calls=%async_computation | async-start | bytes 2359296 | tf_op jit(solution)/shard_map/all_to_all | solution.py:428
  61.5 3.9 %collective-permute-start.12 = (f32[4,32,128]{2,1,0:T(8,128)S(1)}, f32[4,32,128]{2,1,0:T(8,128)S(1)}, u32[]{:S(2)}, u32[]{:S(2)}) collective-permute-start(f32[4,32,128]{2,1,0:T(8,128)S(1)} %add_add_fusion.4), channel_id=1, source_target_pairs={{0,8},{8,0},{16,24},{24,16},{1,9},{9,1},{17,25},{25,17},{2,10},{10... | collective-permute-start | bytes 196616 | tf_op jit(solution)/shard_map/ppermute | solution.py:348
  63.0 5.4 %collective-permute-start.13 = (f32[4,32,128]{2,1,0:T(8,128)S(1)}, f32[4,32,128]{2,1,0:T(8,128)S(1)}, u32[]{:S(2)}, u32[]{:S(2)}) collective-permute-start(f32[4,32,128]{2,1,0:T(8,128)S(1)} %add_add_fusion.4), channel_id=1, source_target_pairs={{0,16},{8,24},{16,0},{24,8},{1,17},{9,25},{17,1},{25,9},{2,18},{10... | collective-permute-start | bytes 196616 | tf_op jit(solution)/shard_map/ppermute | solution.py:348
  65.4 4.5 %collective-permute-start.14 = (f32[4,32,128]{2,1,0:T(8,128)S(1)}, f32[4,32,128]{2,1,0:T(8,128)S(1)}, u32[]{:S(2)}, u32[]{:S(2)}) collective-permute-start(f32[4,32,128]{2,1,0:T(8,128)S(1)} %add_add_fusion.4), channel_id=1, source_target_pairs={{0,24},{8,16},{16,8},{24,0},{1,25},{9,17},{17,9},{25,1},{2,26},{10... | collective-permute-start | bytes 196616 | tf_op jit(solution)/shard_map/ppermute | solution.py:348
  70.6 2.8 %collective-permute-start.15 = (f32[4,32,128]{2,1,0:T(8,128)S(1)}, f32[4,32,128]{2,1,0:T(8,128)S(1)}, u32[]{:S(2)}, u32[]{:S(2)}) collective-permute-start(f32[4,32,128]{2,1,0:T(8,128)S(1)} %get-tuple-element.62.own), channel_id=1, source_target_pairs={{0,32},{32,0},{1,33},{33,1},{2,34},{34,2},{3,35},{35,3},{4,36},{36... | collective-permute-start | bytes 196616 | tf_op jit(solution)/shard_map/ppermute | solution.py:348
  74.2 4.8 %collective-permute-start.16 = (f32[64,512]{1,0:T(8,128)S(1)}, f32[64,512]{1,0:T(8,128)S(1)}, u32[]{:S(2)}, u32[]{:S(2)}) collective-permute-start(f32[64,512]{1,0:T(8,128)S(1)} %get-tuple-element.68), channel_id=1, source_target_pairs={{0,2},{2,0},{4,6},{6,4},{1,3},{3,1},{5,7},{7,5},{8,10},{10,8},{12,... | collective-permute-start | bytes 393224 | tf_op jit(solution)/shard_map/ppermute | solution.py:348
  75.5 8.5 %collective-permute-start.17 = (f32[64,512]{1,0:T(8,128)S(1)}, f32[64,512]{1,0:T(8,128)S(1)}, u32[]{:S(2)}, u32[]{:S(2)}) collective-permute-start(f32[64,512]{1,0:T(8,128)S(1)} %get-tuple-element.69), channel_id=1, source_target_pairs={{0,4},{2,6},{4,0},{6,2},{1,5},{3,7},{5,1},{7,3},{8,12},{10,14},{12... | collective-permute-start | bytes 393224 | tf_op jit(solution)/shard_map/ppermute | solution.py:348
  77.9 8.6 %collective-permute-start.18 = (f32[64,512]{1,0:T(8,128)S(1)}, f32[64,512]{1,0:T(8,128)S(1)}, u32[]{:S(2)}, u32[]{:S(2)}) collective-permute-start(f32[64,512]{1,0:T(8,128)S(1)} %get-tuple-element.70), channel_id=1, source_target_pairs={{0,6},{2,4},{4,2},{6,0},{1,7},{3,5},{5,3},{7,1},{8,14},{10,12},{12... | collective-permute-start | bytes 393224 | tf_op jit(solution)/shard_map/ppermute | solution.py:348
  86.6 3.9 %collective-permute-start.19 = (f32[64,512]{1,0:T(8,128)S(1)}, f32[64,512]{1,0:T(8,128)S(1)}, u32[]{:S(2)}, u32[]{:S(2)}) collective-permute-start(f32[64,512]{1,0:T(8,128)S(1)} %add_multiply_fusion), channel_id=1, source_target_pairs={{0,1},{1,0},{64,65},{65,64},{2,3},{3,2},{66,67},{67,66},{4,5},{5,4... | collective-permute-start | bytes 393224 | tf_op jit(solution)/shard_map/ppermute | solution.py:348
  87.2 8.3 %collective-permute-start.20 = (f32[64,512]{1,0:T(8,128)S(1)}, f32[64,512]{1,0:T(8,128)S(1)}, u32[]{:S(2)}, u32[]{:S(2)}) collective-permute-start(f32[64,512]{1,0:T(8,128)S(1)} %add_multiply_fusion), channel_id=1, source_target_pairs={{0,64},{1,65},{64,0},{65,1},{2,66},{3,67},{66,2},{67,3},{4,68},{5,... | collective-permute-start | bytes 393224 | tf_op jit(solution)/shard_map/ppermute | solution.py:348
  90.5 7.8 %collective-permute-start.21 = (f32[64,512]{1,0:T(8,128)S(1)}, f32[64,512]{1,0:T(8,128)S(1)}, u32[]{:S(2)}, u32[]{:S(2)}) collective-permute-start(f32[64,512]{1,0:T(8,128)S(1)} %add_multiply_fusion), channel_id=1, source_target_pairs={{0,65},{1,64},{64,1},{65,0},{2,67},{3,66},{66,3},{67,2},{4,69},{5,... | collective-permute-start | bytes 393224 | tf_op jit(solution)/shard_map/ppermute | solution.py:348
  102.3 3.9 %collective-permute-start.23 = (f32[64,256]{1,0:T(8,128)S(1)}, f32[64,256]{1,0:T(8,128)S(1)}, u32[]{:S(2)}, u32[]{:S(2)}) collective-permute-start(f32[64,256]{1,0:T(8,128)S(1)} %add.86), channel_id=1, source_target_pairs={{0,2},{2,0},{4,6},{6,4},{1,3},{3,1},{5,7},{7,5},{8,10},{10,8},{12,... | collective-permute-start | bytes 196616 | tf_op jit(solution)/shard_map/ppermute | solution.py:348
  102.4 4.7 %collective-permute-start.24 = (f32[64,256]{1,0:T(8,128)S(1)}, f32[64,256]{1,0:T(8,128)S(1)}, u32[]{:S(2)}, u32[]{:S(2)}) collective-permute-start(f32[64,256]{1,0:T(8,128)S(1)} %add.86), channel_id=1, source_target_pairs={{0,4},{2,6},{4,0},{6,2},{1,5},{3,7},{5,1},{7,3},{8,12},{10,14},{12... | collective-permute-start | bytes 196616 | tf_op jit(solution)/shard_map/ppermute | solution.py:348
  104.0 4.6 %collective-permute-start.25 = (f32[64,256]{1,0:T(8,128)S(1)}, f32[64,256]{1,0:T(8,128)S(1)}, u32[]{:S(2)}, u32[]{:S(2)}) collective-permute-start(f32[64,256]{1,0:T(8,128)S(1)} %add.86), channel_id=1, source_target_pairs={{0,6},{2,4},{4,2},{6,0},{1,7},{3,5},{5,3},{7,1},{8,14},{10,12},{12... | collective-permute-start | bytes 196616 | tf_op jit(solution)/shard_map/ppermute | solution.py:348
  108.7 3.9 %collective-permute-start.26 = (f32[64,256]{1,0:T(8,128)S(1)}, f32[64,256]{1,0:T(8,128)S(1)}, u32[]{:S(2)}, u32[]{:S(2)}) collective-permute-start(f32[64,256]{1,0:T(8,128)S(1)} %add_add_fusion.2), channel_id=1, source_target_pairs={{0,8},{8,0},{16,24},{24,16},{1,9},{9,1},{17,25},{25,17},{2,10},{10... | collective-permute-start | bytes 196616 | tf_op jit(solution)/shard_map/ppermute | solution.py:348
  108.8 4.8 %collective-permute-start.27 = (f32[64,256]{1,0:T(8,128)S(1)}, f32[64,256]{1,0:T(8,128)S(1)}, u32[]{:S(2)}, u32[]{:S(2)}) collective-permute-start(f32[64,256]{1,0:T(8,128)S(1)} %add_add_fusion.2), channel_id=1, source_target_pairs={{0,16},{8,24},{16,0},{24,8},{1,17},{9,25},{17,1},{25,9},{2,18},{10... | collective-permute-start | bytes 196616 | tf_op jit(solution)/shard_map/ppermute | solution.py:348
  110.3 4.3 %collective-permute-start.28 = (f32[64,256]{1,0:T(8,128)S(1)}, f32[64,256]{1,0:T(8,128)S(1)}, u32[]{:S(2)}, u32[]{:S(2)}) collective-permute-start(f32[64,256]{1,0:T(8,128)S(1)} %add_add_fusion.2), channel_id=1, source_target_pairs={{0,24},{8,16},{16,8},{24,0},{1,25},{9,17},{17,9},{25,1},{2,26},{10... | collective-permute-start | bytes 196616 | tf_op jit(solution)/shard_map/ppermute | solution.py:348
  115.8 3.9 %collective-permute-start.29 = (f32[64,512]{1,0:T(8,128)S(1)}, f32[64,512]{1,0:T(8,128)S(1)}, u32[]{:S(2)}, u32[]{:S(2)}) collective-permute-start(f32[64,512]{1,0:T(8,128)S(1)} %shard_map.113), channel_id=1, source_target_pairs={{0,1},{1,0},{64,65},{65,64},{2,3},{3,2},{66,67},{67,66},{4,5},{5,4... | collective-permute-start | bytes 393224 | tf_op jit(solution)/shard_map/ppermute | solution.py:348
  115.8 5.4 %collective-permute-start.30 = (f32[64,512]{1,0:T(8,128)S(1)}, f32[64,512]{1,0:T(8,128)S(1)}, u32[]{:S(2)}, u32[]{:S(2)}) collective-permute-start(f32[64,512]{1,0:T(8,128)S(1)} %shard_map.113), channel_id=1, source_target_pairs={{0,64},{1,65},{64,0},{65,1},{2,66},{3,67},{66,2},{67,3},{4,68},{5,... | collective-permute-start | bytes 393224 | tf_op jit(solution)/shard_map/ppermute | solution.py:348
  117.3 5.4 %collective-permute-start.31 = (f32[64,512]{1,0:T(8,128)S(1)}, f32[64,512]{1,0:T(8,128)S(1)}, u32[]{:S(2)}, u32[]{:S(2)}) collective-permute-start(f32[64,512]{1,0:T(8,128)S(1)} %shard_map.113), channel_id=1, source_target_pairs={{0,65},{1,64},{64,1},{65,0},{2,67},{3,66},{66,3},{67,2},{4,69},{5,... | collective-permute-start | bytes 393224 | tf_op jit(solution)/shard_map/ppermute | solution.py:348
  122.7 5.9 %collective-permute-start.32 = (f32[64,512]{1,0:T(8,128)S(1)}, f32[64,512]{1,0:T(8,128)S(1)}, u32[]{:S(2)}, u32[]{:S(2)}) collective-permute-start(f32[64,512]{1,0:T(8,128)S(1)} %add_subtract_fusion), channel_id=1, source_target_pairs={{0,32},{32,0},{1,33},{33,1},{2,34},{34,2},{3,35},{35,3},{4,36},{36... | collective-permute-start | bytes 393224 | tf_op jit(solution)/shard_map/ppermute | solution.py:348
  (7 other events, 99.0 us)

commit v7 on v6

--- a/solution.py
+++ b/solution.py
@@ -105,42 +105,48 @@
     return jnp.concatenate([x[..., :wide], x[..., wide:]], axis=-2)
 
 
-def front_body(index, pool_f, pool_t, centers, weights, drawn, pack, feats, targs, wts, sems):
-    count = centers.shape[0]
+def front_body(member, *refs, tables):
+    index_h, pool_f, pool_t, weights_h, centers, eig_h, owner_h, offset_h = refs[0:8]
+    drawn, pack = refs[8:10]
+    parts = refs[10 : 10 + tables]
+    index, feats, targs, wts, eig, owner, offset, sems = refs[10 + tables :]
+    cdev = centers.shape[0]
     copies = [
         pltpu.make_async_copy(src, dst, sems.at[n])
         for n, (src, dst) in enumerate(
-            ((pool_f, feats), (pool_t, targs), (weights, wts), (centers, pack.at[0:count, :]))
+            (
+                (index_h, index), (pool_f, feats), (pool_t, targs), (weights_h, wts),
+                (centers, pack.at[0:cdev, :]), (eig_h, eig), (owner_h, owner), (offset_h, offset),
+            )
         )
     ]
     for copy in copies:
         copy.start()
     rows = index.shape[1]
+    copies[0].wait()
     hot = rows_hot(index[...], feats.shape[0])
-    copies[0].wait()
+    copies[1].wait()
     drawn[0:rows, :] = pick(hot, feats[...], NN)
-    copies[1].wait()
+    copies[2].wait()
     drawn[rows:, :] = packed(pick(hot, targs[...], NT, flip=True).T)
-    copies[2].wait()
-    pack[count:, :] = packed(wts[...].T)
     copies[3].wait()
+    pack[cdev:, :] = packed(wts[...].T)
+    for copy in copies[4:]:
+        copy.wait()
+    count, q = eig.shape
+    part = q // tables
+    row = jnp.broadcast_to((owner[...] * cdev + offset[...]).astype(F32), (8, count))
+    row = jnp.concatenate([row] * (part // count), axis=1)
+    for o, out in enumerate(parts):
+        mate = member[0] ^ o
+        out[0:count, :] = eig[:, pl.ds(pl.multiple_of(mate * part, part), part)]
+        out[count:, :] = row
 
 
 def order_body(x, *refs):
     parts, out = refs[:-1], refs[-1]
     for o, part in enumerate(parts):
         out[x[0] ^ o] = part[...]
-
-
-def quarters_body(member, eig, nys, *outs):
-    count, q = eig.shape
-    part = q // len(outs)
-    row = jnp.broadcast_to(nys[...].astype(F32), (8, count))
-    row = jnp.concatenate([row] * (part // count), axis=1)
-    for o, out in enumerate(outs):
-        mate = member[0] ^ o
-        out[0:count, :] = eig[:, pl.ds(pl.multiple_of(mate * part, part), part)]
-        out[count:, :] = row
 
 
 def vectors_body(*refs, cdev):
@@ -343,10 +349,12 @@
 
 
 def mates(parts, axes):
+    return [mate_of(parts[o], axes, o) for o in range(1, len(parts))]
+
+
+def mate_of(v, axes, o):
     n = math.prod(SIZES[a] for a in axes)
-    return [
-        lax.ppermute(parts[o], axes, [(i, i ^ o) for i in range(n)]) for o in range(1, n)
-    ]
+    return lax.ppermute(v, axes, [(i, i ^ o) for i in range(n)])
 
 
 def together(*arrays):
@@ -369,27 +377,38 @@
     straight = lax.axis_index("core") == lax.axis_index("zl")
     wide = 2 * out
 
-    drawn, pack = pl.pallas_call(
-        front_body,
-        out_shape=[shape(rows + half, dim), shape(cdev + cdev // 2, dim)],
-        in_specs=[VMEM] + [pl.BlockSpec(memory_space=pltpu.HBM)] * 4,
-        out_specs=[VMEM] * 2,
+    hbm = pl.BlockSpec(memory_space=pltpu.HBM)
+    drawn, pack, *parted = pl.pallas_call(
+        functools.partial(front_body, tables=tables),
+        out_shape=[shape(rows + half, dim), shape(cdev + cdev // 2, dim)]
+        + [shape(count + 8, q // tables)] * tables,
+        in_specs=[pl.BlockSpec(memory_space=pltpu.SMEM)] + [hbm] * 8,
+        out_specs=[VMEM] * (2 + tables),
         scratch_shapes=[
+            pltpu.VMEM((1, rows), jnp.int32),
             pltpu.VMEM(pool_features.shape, F32),
             pltpu.VMEM(pool_targets.shape[::-1], F32),
             pltpu.VMEM((out, cdev), F32),
-            pltpu.SemaphoreType.DMA((4,)),
+            pltpu.VMEM(eig_vectors.shape, F32),
+            pltpu.VMEM((1, count), jnp.int32),
+            pltpu.VMEM((1, count), jnp.int32),
+            pltpu.SemaphoreType.DMA((8,)),
         ],
         compiler_params=params(60),
-    )(batch_index.reshape(1, rows), pool_features, pool_targets.T, centers, weights.T)
+    )(
+        member, batch_index.reshape(1, rows), pool_features, pool_targets.T, weights.T, centers,
+        eig_vectors, nys_owner.reshape(1, count), nys_offset.reshape(1, count),
+    )
 
     gathered = mates([drawn] * nx, ("x",))
     tile = lax.ppermute(pack, ("core", "zl"), [(0, 0), (2, 1), (1, 2), (3, 3)])
-    tile, drawn, *gathered = together(tile, drawn, *gathered)
+    first = mate_of(parted[2], PLANES, 2)
+    tile, first, drawn, *gathered = together(tile, first, drawn, *gathered)
     own = call(order_body, shape(nx, rows + half, dim), x, drawn, *gathered, scalars=1)
     others = mates([tile] * ny, ("y",))
-    (mate,) = mates([own] * 2, ("core",))
-    eig_vectors, own = together(eig_vectors, own)
+    mate = mate_of(own, ("core",), 1)
+    mate, second, third = together(mate, parted[1], parted[3])
+    parted = [parted[0], first, mate_of(second, PLANES, 1), mate_of(third, PLANES, 3)]
 
     def kernel(packs, extra):
         nb = len(packs)
@@ -414,12 +433,7 @@
 
     khi_a, klo_a, keep_a, send_a, scale, sb = kernel([tile], True)
 
-    nys = (nys_owner.reshape(count) * cdev + nys_offset).reshape(1, count)
-    parted = call(
-        quarters_body, [shape(count + 8, q // tables)] * tables,
-        member, eig_vectors, nys, scalars=1,
-    )
-    keep_a, *parted = together(keep_a, parted[0], *mates(parted, PLANES))
+    keep_a, *parted = together(keep_a, *parted)
     points = call(
         functools.partial(vectors_body, cdev=cdev),
         shape(peers, CAP * (tables * (q // tables // 128) + 1), 128),

time: 130 us -> 127 us (0.977)
  waiting for transfers between devices: 42.2 us -> 38.6 us
    ppermute x32, waiting for transfers between devices: 42.2 us -> 38.6 us  [mate_of(): return lax.ppermute(v, axes, [(i, i ^ o) for i in range(n)])]
    pallas_call x9 -> x8, Pallas kernels: 23.6 us -> 23.5 us  [call(): pl.pallas_call(body, out_shape=outs, in_specs=[smem] * scalars + [VMEM] *...]
  transfers between devices with their start and end apart: 34 -> 34, of which waited for: 21 -> 22; matrix products, arithmetic and copies ran while one was open for 0% -> 0% of each run, Pallas kernels for 16% -> 17%
where the time goes in v7:
time: 127 us; the launch traced here: 126 us
  starting transfers between devices  57.5 us (45%)
  waiting for transfers between devices  38.6 us (30%)
  Pallas kernels  26.7 us (21%)
  local copies, waits for them, and re-layouts  1.71 us (1%)
    ppermute x32, starting transfers between devices, mate_of(): return lax.ppermute(v, axes, [(i, i ^ o) for i in range(n)])  45.8 us
    ppermute x32, waiting for transfers between devices, mate_of(): return lax.ppermute(v, axes, [(i, i ^ o) for i in range(n)])  38.6 us
    pallas_call x8, Pallas kernels, call(): pl.pallas_call(body, out_shape=outs, in_specs=[smem] * scalars + [VMEM] *...  23.5 us
    all_to_all x1, starting transfers between devices, per_device(): lax.all_to_all(points, OWNERS, split_axis=0, concat_axis=0, tiled=True)  6.7 us
    ppermute x1, starting transfers between devices, per_device(): tile = lax.ppermute(pack, ('core', 'zl'), [(0, 0), (2, 1), (1, 2), (3, 3)])  4.93 us
    pallas_call x1, Pallas kernels, per_device(): pl.pallas_call(functools.partial(front_body, tables=tables), out_shape=[s...  3.17 us
  transfers between devices with their start and end apart: 34, of which 22 were waited for; matrix products, arithmetic and copies ran while one was open for 0% of the time, Pallas kernels for 17%

profile of v7, /device:TPU:1, one launch (start us, length us, event | category | flops | bytes accessed | tf_op | source)
XLA Modules:
  0.0 126.2 jit_solution(15497429459488781709)
XLA Ops:
  0.6 3.2 %shard_map.104 = (f32[96,128]{1,0:T(8,128)}, f32[768,128]{1,0:T(8,128)}, f32[136,256]{1,0:T(8,128)}, f32[136,256]{1,0:T(8,128)}, f32[136,256]{1,0:T(8,128)}, /*index=5*/f32[136,256]{1,0:T(8,128)}) custom-call(s32[1]{0:T(128)} %bitcast.1.member, s32[1,64]{1,0:T(1,128)} %bitcast.15, f32[1024,128]{1,0:T(8,128)} %refs_1_.1, f32[64,1024]{1,0:T(8,128)} %bitcast.12, ...), custom_call_target="tpu_custom_call" | custom-call | tf_op jit(solution)/shard_map/pallas_call | solution.py:381
  3.8 4.9 %collective-permute-start = (f32[768,128]{1,0:T(8,128)}, f32[768,128]{1,0:T(8,128)S(1)}, u32[]{:S(2)}, u32[]{:S(2)}) collective-permute-start(f32[768,128]{1,0:T(8,128)} %get-tuple-element.40), channel_id=1, source_target_pairs={{0,0},{32,1},{1,32},{33,33},{2,2},{34,3},{3,34},{35,35},{4,4},{36,... | collective-permute-start | bytes 1179656 | tf_op jit(solution)/shard_map/ppermute | solution.py:404
  8.8 3.4 %collective-permute-start.1 = (f32[136,256]{1,0:T(8,128)}, f32[136,256]{1,0:T(8,128)S(1)}, u32[]{:S(2)}, u32[]{:S(2)}) collective-permute-start(f32[136,256]{1,0:T(8,128)} %get-tuple-element.41), channel_id=1, source_target_pairs={{0,64},{1,65},{64,0},{65,1},{2,66},{3,67},{66,2},{67,3},{4,68},{5,... | collective-permute-start | bytes 417800 | tf_op jit(solution)/shard_map/ppermute | solution.py:357
  13.4 2.4 %collective-permute-start.3 = (f32[96,128]{1,0:T(8,128)}, f32[96,128]{1,0:T(8,128)S(1)}, u32[]{:S(2)}, u32[]{:S(2)}) collective-permute-start(f32[96,128]{1,0:T(8,128)} %get-tuple-element.43.refs_0_), channel_id=1, source_target_pairs={{0,16},{8,24},{16,0},{24,8},{1,17},{9,25},{17,1},{25,9},{2,18},{10... | collective-permute-start | bytes 147464 | tf_op jit(solution)/shard_map/ppermute | solution.py:357
  16.0 2.5 %collective-permute-done.3.refs_2_ = f32[96,128]{1,0:T(8,128)S(1)} collective-permute-done((f32[96,128]{1,0:T(8,128)}, f32[96,128]{1,0:T(8,128)S(1)}, u32[]{:S(2)}, u32[]{:S(2)}) %collective-permute-start.3) | collective-permute-done | bytes 49184 | tf_op jit(solution)/shard_map/ppermute | solution.py:357
  18.5 1.9 %collective-permute-done.4.refs_3_ = f32[96,128]{1,0:T(8,128)S(1)} collective-permute-done((f32[96,128]{1,0:T(8,128)}, f32[96,128]{1,0:T(8,128)S(1)}, u32[]{:S(2)}, u32[]{:S(2)}) %collective-permute-start.4) | collective-permute-done | bytes 49184 | tf_op jit(solution)/shard_map/ppermute | solution.py:357
  20.4 2.7 %collective-permute-start.10 = (f32[768,128]{1,0:T(8,128)S(1)}, f32[768,128]{1,0:T(8,128)}, u32[]{:S(2)}, u32[]{:S(2)}) collective-permute-start(f32[768,128]{1,0:T(8,128)S(1)} %collective-permute-done.refs_2_), channel_id=1, source_target_pairs={{0,6},{2,4},{4,2},{6,0},{1,7},{3,5},{5,3},{7,1},{8,14},{10,12},{12... | collective-permute-start | bytes 1179656 | tf_op jit(solution)/shard_map/ppermute | solution.py:357
  28.4 4.1 %shard_map.106 = (bf16[1,512,512]{2,1,0:T(8,128)(2,1)S(1)}, bf16[1,512,512]{2,1,0:T(8,128)(2,1)S(1)}, f32[4,32,128]{2,1,0:T(8,128)S(1)}, f32[4,32,128]{2,1,0:T(8...) custom-call(f32[4,96,128]{2,1,0:T(8,128)S(1)} %shard_map.105.refs_0_.own, ...), custom_call_target="tpu_custom_call" | custom-call | flops 100000000 | bytes 65536 | tf_op jit(solution)/shard_map/pallas_call | solution.py:337
  32.7 1.6 %collective-permute-done.7.refs_3_ = f32[136,256]{1,0:T(8,128)S(1)} collective-permute-done((f32[136,256]{1,0:T(8,128)}, f32[136,256]{1,0:T(8,128)S(1)}, u32[]{:S(2)}, u32[]{:S(2)}) %collective-permute-start.7) | collective-permute-done | bytes 139296 | tf_op jit(solution)/shard_map/ppermute | solution.py:357
  35.2 1.7 %shard_map.109 = f32[32,72,128]{2,1,0:T(8,128)} custom-call(f32[136,256]{1,0:T(8,128)S(1)} %copy-done, f32[136,256]{1,0:T(8,128)S(1)} %collective-permute-done.1.refs_1_, f32[136,256]{1,0:T(8,128)S(1)} %collective-permute-done.6.refs_2_, f32[136,256]{1,0:T(8,128)S(1)} %collective-permute-done.7.refs_3_), custom_call_target="tpu_custom_call" | custom-call | tf_op jit(solution)/shard_map/pallas_call | solution.py:337
  37.0 6.7 %all-to-all-start = ((f32[32,72,128]{2,1,0:T(8,128)}), f32[32,72,128]{2,1,0:T(8,128)S(1)}, u32[]{:S(2)}, u32[]{:S(2)}) async-start(f32[32,72,128]{2,1,0:T(8,128)} %shard_map.109), calls=%async_computation | async-start | bytes 2359296 | tf_op jit(solution)/shard_map/all_to_all | solution.py:442
  43.7 13.5 %shard_map.107 = (bf16[3,512,512]{2,1,0:T(8,128)(2,1)S(1)}, bf16[3,512,512]{2,1,0:T(8,128)(2,1)S(1)}, f32[4,32,128]{2,1,0:T(8,128)S(1)}, f32[4,32,128]{2,1,0:T(8,128)S(1)}) custom-call(f32[4,96,128]{2,1,0:T(8,128)S(1)} %shard_map.105.refs_0_.own, f32[4,96,128]{2,1,0:T(8,128)S(1)} %collective-permute-done.5.refs_1_, ...), custom_call_target="tpu_custom_call" | custom-call | flops 30000001024 | bytes 65536 | tf_op jit(solution)/shard_map/pallas_call | solution.py:337
  60.1 2.4 %collective-permute-start.13 = (f32[4,32,128]{2,1,0:T(8,128)S(1)}, f32[4,32,128]{2,1,0:T(8,128)S(1)}, u32[]{:S(2)}, u32[]{:S(2)}) collective-permute-start(f32[4,32,128]{2,1,0:T(8,128)S(1)} %add_add_fusion.4), channel_id=1, source_target_pairs={{0,16},{8,24},{16,0},{24,8},{1,17},{9,25},{17,1},{25,9},{2,18},{10... | collective-permute-start | bytes 196616 | tf_op jit(solution)/shard_map/ppermute | solution.py:357
  62.6 2.9 %collective-permute-done.13 = f32[4,32,128]{2,1,0:T(8,128)S(1)} collective-permute-done((f32[4,32,128]{2,1,0:T(8,128)S(1)}, f32[4,32,128]{2,1,0:T(8,128)S(1)}, u32[]{:S(2)}, u32[]{:S(2)}) %collective-permute-start.13) | collective-permute-done | bytes 65568 | tf_op jit(solution)/shard_map/ppermute | solution.py:357
  65.5 1.5 %collective-permute-done.14 = f32[4,32,128]{2,1,0:T(8,128)S(1)} collective-permute-done((f32[4,32,128]{2,1,0:T(8,128)S(1)}, f32[4,32,128]{2,1,0:T(8,128)S(1)}, u32[]{:S(2)}, u32[]{:S(2)}) %collective-permute-start.14) | collective-permute-done | bytes 65568 | tf_op jit(solution)/shard_map/ppermute | solution.py:357
  67.7 1.9 %collective-permute-start.15 = (f32[4,32,128]{2,1,0:T(8,128)S(1)}, f32[4,32,128]{2,1,0:T(8,128)S(1)}, u32[]{:S(2)}, u32[]{:S(2)}) collective-permute-start(f32[4,32,128]{2,1,0:T(8,128)S(1)} %get-tuple-element.66.own), channel_id=1, source_target_pairs={{0,32},{32,0},{1,33},{33,1},{2,34},{34,2},{3,35},{35,3},{4,36},{36... | collective-permute-start | bytes 196616 | tf_op jit(solution)/shard_map/ppermute | solution.py:357
  72.7 2.4 %collective-permute-start.17 = (f32[64,512]{1,0:T(8,128)S(1)}, f32[64,512]{1,0:T(8,128)S(1)}, u32[]{:S(2)}, u32[]{:S(2)}) collective-permute-start(f32[64,512]{1,0:T(8,128)S(1)} %get-tuple-element.73), channel_id=1, source_target_pairs={{0,4},{2,6},{4,0},{6,2},{1,5},{3,7},{5,1},{7,3},{8,12},{10,14},{12... | collective-permute-start | bytes 393224 | tf_op jit(solution)/shard_map/ppermute | solution.py:357
  76.2 5.0 %collective-permute-done.17 = f32[64,512]{1,0:T(8,128)S(1)} collective-permute-done((f32[64,512]{1,0:T(8,128)S(1)}, f32[64,512]{1,0:T(8,128)S(1)}, u32[]{:S(2)}, u32[]{:S(2)}) %collective-permute-start.17) | collective-permute-done | bytes 131104 | tf_op jit(solution)/shard_map/ppermute | solution.py:357
  81.2 2.5 %collective-permute-done.18 = f32[64,512]{1,0:T(8,128)S(1)} collective-permute-done((f32[64,512]{1,0:T(8,128)S(1)}, f32[64,512]{1,0:T(8,128)S(1)}, u32[]{:S(2)}, u32[]{:S(2)}) %collective-permute-start.18) | collective-permute-done | bytes 131104 | tf_op jit(solution)/shard_map/ppermute | solution.py:357
  83.9 1.7 %collective-permute-start.20 = (f32[64,512]{1,0:T(8,128)S(1)}, f32[64,512]{1,0:T(8,128)S(1)}, u32[]{:S(2)}, u32[]{:S(2)}) collective-permute-start(f32[64,512]{1,0:T(8,128)S(1)} %add_multiply_fusion), channel_id=1, source_target_pairs={{0,64},{1,65},{64,0},{65,1},{2,66},{3,67},{66,2},{67,3},{4,68},{5,... | collective-permute-start | bytes 393224 | tf_op jit(solution)/shard_map/ppermute | solution.py:357
  85.5 2.2 %collective-permute-start.21 = (f32[64,512]{1,0:T(8,128)S(1)}, f32[64,512]{1,0:T(8,128)S(1)}, u32[]{:S(2)}, u32[]{:S(2)}) collective-permute-start(f32[64,512]{1,0:T(8,128)S(1)} %add_multiply_fusion), channel_id=1, source_target_pairs={{0,65},{1,64},{64,1},{65,0},{2,67},{3,66},{66,3},{67,2},{4,69},{5,... | collective-permute-start | bytes 393224 | tf_op jit(solution)/shard_map/ppermute | solution.py:357
  87.7 2.9 %collective-permute-done.20 = f32[64,512]{1,0:T(8,128)S(1)} collective-permute-done((f32[64,512]{1,0:T(8,128)S(1)}, f32[64,512]{1,0:T(8,128)S(1)}, u32[]{:S(2)}, u32[]{:S(2)}) %collective-permute-start.20) | collective-permute-done | bytes 131104 | tf_op jit(solution)/shard_map/ppermute | solution.py:357
  90.6 2.8 %collective-permute-done.21 = f32[64,512]{1,0:T(8,128)S(1)} collective-permute-done((f32[64,512]{1,0:T(8,128)S(1)}, f32[64,512]{1,0:T(8,128)S(1)}, u32[]{:S(2)}, u32[]{:S(2)}) %collective-permute-start.21) | collective-permute-done | bytes 131104 | tf_op jit(solution)/shard_map/ppermute | solution.py:357
  93.4 1.6 %shard_map.111 = f32[64,256]{1,0:T(8,128)S(1)} custom-call(f32[32,72,128]{2,1,0:T(8,128)S(1)} %all-to-all-done.points, f32[64,512]{1,0:T(8,128)S(1)} %add_add_fusion.grads), custom_call_target="tpu_custom_call" | custom-call | tf_op jit(solution)/shard_map/pallas_call | solution.py:337
  97.5 1.6 %collective-permute-start.24 = (f32[64,256]{1,0:T(8,128)S(1)}, f32[64,256]{1,0:T(8,128)S(1)}, u32[]{:S(2)}, u32[]{:S(2)}) collective-permute-start(f32[64,256]{1,0:T(8,128)S(1)} %add.82), channel_id=1, source_target_pairs={{0,4},{2,6},{4,0},{6,2},{1,5},{3,7},{5,1},{7,3},{8,12},{10,14},{12... | collective-permute-start | bytes 196616 | tf_op jit(solution)/shard_map/ppermute | solution.py:357
  99.1 2.3 %collective-permute-start.25 = (f32[64,256]{1,0:T(8,128)S(1)}, f32[64,256]{1,0:T(8,128)S(1)}, u32[]{:S(2)}, u32[]{:S(2)}) collective-permute-start(f32[64,256]{1,0:T(8,128)S(1)} %add.82), channel_id=1, source_target_pairs={{0,6},{2,4},{4,2},{6,0},{1,7},{3,5},{5,3},{7,1},{8,14},{10,12},{12... | collective-permute-start | bytes 196616 | tf_op jit(solution)/shard_map/ppermute | solution.py:357
  102.2 1.5 %collective-permute-done.25 = f32[64,256]{1,0:T(8,128)S(1)} collective-permute-done((f32[64,256]{1,0:T(8,128)S(1)}, f32[64,256]{1,0:T(8,128)S(1)}, u32[]{:S(2)}, u32[]{:S(2)}) %collective-permute-start.25) | collective-permute-done | bytes 65568 | tf_op jit(solution)/shard_map/ppermute | solution.py:357
  103.8 1.6 %collective-permute-start.27 = (f32[64,256]{1,0:T(8,128)S(1)}, f32[64,256]{1,0:T(8,128)S(1)}, u32[]{:S(2)}, u32[]{:S(2)}) collective-permute-start(f32[64,256]{1,0:T(8,128)S(1)} %add_add_fusion.2), channel_id=1, source_target_pairs={{0,16},{8,24},{16,0},{24,8},{1,17},{9,25},{17,1},{25,9},{2,18},{10... | collective-permute-start | bytes 196616 | tf_op jit(solution)/shard_map/ppermute | solution.py:357
  105.4 2.3 %collective-permute-start.28 = (f32[64,256]{1,0:T(8,128)S(1)}, f32[64,256]{1,0:T(8,128)S(1)}, u32[]{:S(2)}, u32[]{:S(2)}) collective-permute-start(f32[64,256]{1,0:T(8,128)S(1)} %add_add_fusion.2), channel_id=1, source_target_pairs={{0,24},{8,16},{16,8},{24,0},{1,25},{9,17},{17,9},{25,1},{2,26},{10... | collective-permute-start | bytes 196616 | tf_op jit(solution)/shard_map/ppermute | solution.py:357
  110.9 3.3 %collective-permute-start.30 = (f32[64,512]{1,0:T(8,128)S(1)}, f32[64,512]{1,0:T(8,128)S(1)}, u32[]{:S(2)}, u32[]{:S(2)}) collective-permute-start(f32[64,512]{1,0:T(8,128)S(1)} %shard_map.112), channel_id=1, source_target_pairs={{0,64},{1,65},{64,0},{65,1},{2,66},{3,67},{66,2},{67,3},{4,68},{5,... | collective-permute-start | bytes 393224 | tf_op jit(solution)/shard_map/ppermute | solution.py:357
  114.8 3.2 %collective-permute-done.30 = f32[64,512]{1,0:T(8,128)S(1)} collective-permute-done((f32[64,512]{1,0:T(8,128)S(1)}, f32[64,512]{1,0:T(8,128)S(1)}, u32[]{:S(2)}, u32[]{:S(2)}) %collective-permute-start.30) | collective-permute-done | bytes 131104 | tf_op jit(solution)/shard_map/ppermute | solution.py:357
  119.4 5.1 %collective-permute-start.32 = (f32[64,512]{1,0:T(8,128)S(1)}, f32[64,512]{1,0:T(8,128)S(1)}, u32[]{:S(2)}, u32[]{:S(2)}) collective-permute-start(f32[64,512]{1,0:T(8,128)S(1)} %add_subtract_fusion), channel_id=1, source_target_pairs={{0,32},{32,0},{1,33},{33,1},{2,34},{34,2},{3,35},{35,3},{4,36},{36... | collective-permute-start | bytes 393224 | tf_op jit(solution)/shard_map/ppermute | solution.py:357
  (62 shorter events, 26.1 us)
Async XLA Ops:
  3.8 16.6 %collective-permute-start = (f32[768,128]{1,0:T(8,128)}, f32[768,128]{1,0:T(8,128)S(1)}, u32[]{:S(2)}, u32[]{:S(2)}) collective-permute-start(f32[768,128]{1,0:T(8,128)} %get-tuple-element.40), channel_id=1, source_target_pairs={{0,0},{32,1},{1,32},{33,33},{2,2},{34,3},{3,34},{35,35},{4,4},{36,... | collective-permute-start | bytes 1179656 | tf_op jit(solution)/shard_map/ppermute | solution.py:404
  8.8 11.7 %collective-permute-start.1 = (f32[136,256]{1,0:T(8,128)}, f32[136,256]{1,0:T(8,128)S(1)}, u32[]{:S(2)}, u32[]{:S(2)}) collective-permute-start(f32[136,256]{1,0:T(8,128)} %get-tuple-element.41), channel_id=1, source_target_pairs={{0,64},{1,65},{64,0},{65,1},{2,66},{3,67},{66,2},{67,3},{4,68},{5,... | collective-permute-start | bytes 417800 | tf_op jit(solution)/shard_map/ppermute | solution.py:357
  12.1 3.9 %collective-permute-start.2 = (f32[96,128]{1,0:T(8,128)}, f32[96,128]{1,0:T(8,128)S(1)}, u32[]{:S(2)}, u32[]{:S(2)}) collective-permute-start(f32[96,128]{1,0:T(8,128)} %get-tuple-element.43.refs_0_), channel_id=1, source_target_pairs={{0,8},{8,0},{16,24},{24,16},{1,9},{9,1},{17,25},{25,17},{2,10},{10... | collective-permute-start | bytes 147464 | tf_op jit(solution)/shard_map/ppermute | solution.py:357
  13.4 5.2 %collective-permute-start.3 = (f32[96,128]{1,0:T(8,128)}, f32[96,128]{1,0:T(8,128)S(1)}, u32[]{:S(2)}, u32[]{:S(2)}) collective-permute-start(f32[96,128]{1,0:T(8,128)} %get-tuple-element.43.refs_0_), channel_id=1, source_target_pairs={{0,16},{8,24},{16,0},{24,8},{1,17},{9,25},{17,1},{25,9},{2,18},{10... | collective-permute-start | bytes 147464 | tf_op jit(solution)/shard_map/ppermute | solution.py:357
  15.8 4.6 %collective-permute-start.4 = (f32[96,128]{1,0:T(8,128)}, f32[96,128]{1,0:T(8,128)S(1)}, u32[]{:S(2)}, u32[]{:S(2)}) collective-permute-start(f32[96,128]{1,0:T(8,128)} %get-tuple-element.43.refs_0_), channel_id=1, source_target_pairs={{0,24},{8,16},{16,8},{24,0},{1,25},{9,17},{17,9},{25,1},{2,26},{10... | collective-permute-start | bytes 147464 | tf_op jit(solution)/shard_map/ppermute | solution.py:357
  20.4 23.2 %collective-permute-start.10 = (f32[768,128]{1,0:T(8,128)S(1)}, f32[768,128]{1,0:T(8,128)}, u32[]{:S(2)}, u32[]{:S(2)}) collective-permute-start(f32[768,128]{1,0:T(8,128)S(1)} %collective-permute-done.refs_2_), channel_id=1, source_target_pairs={{0,6},{2,4},{4,2},{6,0},{1,7},{3,5},{5,3},{7,1},{8,14},{10,12},{12... | collective-permute-start | bytes 1179656 | tf_op jit(solution)/shard_map/ppermute | solution.py:357
  23.2 20.5 %collective-permute-start.8 = (f32[768,128]{1,0:T(8,128)S(1)}, f32[768,128]{1,0:T(8,128)}, u32[]{:S(2)}, u32[]{:S(2)}) collective-permute-start(f32[768,128]{1,0:T(8,128)S(1)} %collective-permute-done.refs_2_), channel_id=1, source_target_pairs={{0,2},{2,0},{4,6},{6,4},{1,3},{3,1},{5,7},{7,5},{8,10},{10,8},{12,... | collective-permute-start | bytes 1179656 | tf_op jit(solution)/shard_map/ppermute | solution.py:357
  23.2 20.5 %collective-permute-start.9 = (f32[768,128]{1,0:T(8,128)S(1)}, f32[768,128]{1,0:T(8,128)}, u32[]{:S(2)}, u32[]{:S(2)}) collective-permute-start(f32[768,128]{1,0:T(8,128)S(1)} %collective-permute-done.refs_2_), channel_id=1, source_target_pairs={{0,4},{2,6},{4,0},{6,2},{1,5},{3,7},{5,1},{7,3},{8,12},{10,14},{12... | collective-permute-start | bytes 1179656 | tf_op jit(solution)/shard_map/ppermute | solution.py:357
  27.5 5.2 %collective-permute-start.6 = (f32[136,256]{1,0:T(8,128)}, f32[136,256]{1,0:T(8,128)S(1)}, u32[]{:S(2)}, u32[]{:S(2)}) collective-permute-start(f32[136,256]{1,0:T(8,128)} %get-tuple-element.54), channel_id=1, source_target_pairs={{0,1},{1,0},{64,65},{65,64},{2,3},{3,2},{66,67},{67,66},{4,5},{5,4... | collective-permute-start | bytes 417800 | tf_op jit(solution)/shard_map/ppermute | solution.py:357
  28.4 6.0 %collective-permute-start.7 = (f32[136,256]{1,0:T(8,128)}, f32[136,256]{1,0:T(8,128)S(1)}, u32[]{:S(2)}, u32[]{:S(2)}) collective-permute-start(f32[136,256]{1,0:T(8,128)} %get-tuple-element.55), channel_id=1, source_target_pairs={{0,65},{1,64},{64,1},{65,0},{2,67},{3,66},{66,3},{67,2},{4,69},{5,... | collective-permute-start | bytes 417800 | tf_op jit(solution)/shard_map/ppermute | solution.py:357
  37.0 46.8 %all-to-all-start = ((f32[32,72,128]{2,1,0:T(8,128)}), f32[32,72,128]{2,1,0:T(8,128)S(1)}, u32[]{:S(2)}, u32[]{:S(2)}) async-start(f32[32,72,128]{2,1,0:T(8,128)} %shard_map.109), calls=%async_computation | async-start | bytes 2359296 | tf_op jit(solution)/shard_map/all_to_all | solution.py:442
  58.7 3.9 %collective-permute-start.12 = (f32[4,32,128]{2,1,0:T(8,128)S(1)}, f32[4,32,128]{2,1,0:T(8,128)S(1)}, u32[]{:S(2)}, u32[]{:S(2)}) collective-permute-start(f32[4,32,128]{2,1,0:T(8,128)S(1)} %add_add_fusion.4), channel_id=1, source_target_pairs={{0,8},{8,0},{16,24},{24,16},{1,9},{9,1},{17,25},{25,17},{2,10},{10... | collective-permute-start | bytes 196616 | tf_op jit(solution)/shard_map/ppermute | solution.py:357
  60.1 5.4 %collective-permute-start.13 = (f32[4,32,128]{2,1,0:T(8,128)S(1)}, f32[4,32,128]{2,1,0:T(8,128)S(1)}, u32[]{:S(2)}, u32[]{:S(2)}) collective-permute-start(f32[4,32,128]{2,1,0:T(8,128)S(1)} %add_add_fusion.4), channel_id=1, source_target_pairs={{0,16},{8,24},{16,0},{24,8},{1,17},{9,25},{17,1},{25,9},{2,18},{10... | collective-permute-start | bytes 196616 | tf_op jit(solution)/shard_map/ppermute | solution.py:357
  62.6 4.5 %collective-permute-start.14 = (f32[4,32,128]{2,1,0:T(8,128)S(1)}, f32[4,32,128]{2,1,0:T(8,128)S(1)}, u32[]{:S(2)}, u32[]{:S(2)}) collective-permute-start(f32[4,32,128]{2,1,0:T(8,128)S(1)} %add_add_fusion.4), channel_id=1, source_target_pairs={{0,24},{8,16},{16,8},{24,0},{1,25},{9,17},{17,9},{25,1},{2,26},{10... | collective-permute-start | bytes 196616 | tf_op jit(solution)/shard_map/ppermute | solution.py:357
  67.7 2.8 %collective-permute-start.15 = (f32[4,32,128]{2,1,0:T(8,128)S(1)}, f32[4,32,128]{2,1,0:T(8,128)S(1)}, u32[]{:S(2)}, u32[]{:S(2)}) collective-permute-start(f32[4,32,128]{2,1,0:T(8,128)S(1)} %get-tuple-element.66.own), channel_id=1, source_target_pairs={{0,32},{32,0},{1,33},{33,1},{2,34},{34,2},{3,35},{35,3},{4,36},{36... | collective-permute-start | bytes 196616 | tf_op jit(solution)/shard_map/ppermute | solution.py:357
  71.4 4.8 %collective-permute-start.16 = (f32[64,512]{1,0:T(8,128)S(1)}, f32[64,512]{1,0:T(8,128)S(1)}, u32[]{:S(2)}, u32[]{:S(2)}) collective-permute-start(f32[64,512]{1,0:T(8,128)S(1)} %get-tuple-element.72), channel_id=1, source_target_pairs={{0,2},{2,0},{4,6},{6,4},{1,3},{3,1},{5,7},{7,5},{8,10},{10,8},{12,... | collective-permute-start | bytes 393224 | tf_op jit(solution)/shard_map/ppermute | solution.py:357
  72.7 8.5 %collective-permute-start.17 = (f32[64,512]{1,0:T(8,128)S(1)}, f32[64,512]{1,0:T(8,128)S(1)}, u32[]{:S(2)}, u32[]{:S(2)}) collective-permute-start(f32[64,512]{1,0:T(8,128)S(1)} %get-tuple-element.73), channel_id=1, source_target_pairs={{0,4},{2,6},{4,0},{6,2},{1,5},{3,7},{5,1},{7,3},{8,12},{10,14},{12... | collective-permute-start | bytes 393224 | tf_op jit(solution)/shard_map/ppermute | solution.py:357
  75.1 8.6 %collective-permute-start.18 = (f32[64,512]{1,0:T(8,128)S(1)}, f32[64,512]{1,0:T(8,128)S(1)}, u32[]{:S(2)}, u32[]{:S(2)}) collective-permute-start(f32[64,512]{1,0:T(8,128)S(1)} %get-tuple-element.74), channel_id=1, source_target_pairs={{0,6},{2,4},{4,2},{6,0},{1,7},{3,5},{5,3},{7,1},{8,14},{10,12},{12... | collective-permute-start | bytes 393224 | tf_op jit(solution)/shard_map/ppermute | solution.py:357
  83.8 3.9 %collective-permute-start.19 = (f32[64,512]{1,0:T(8,128)S(1)}, f32[64,512]{1,0:T(8,128)S(1)}, u32[]{:S(2)}, u32[]{:S(2)}) collective-permute-start(f32[64,512]{1,0:T(8,128)S(1)} %add_multiply_fusion), channel_id=1, source_target_pairs={{0,1},{1,0},{64,65},{65,64},{2,3},{3,2},{66,67},{67,66},{4,5},{5,4... | collective-permute-start | bytes 393224 | tf_op jit(solution)/shard_map/ppermute | solution.py:357
  83.9 6.7 %collective-permute-start.20 = (f32[64,512]{1,0:T(8,128)S(1)}, f32[64,512]{1,0:T(8,128)S(1)}, u32[]{:S(2)}, u32[]{:S(2)}) collective-permute-start(f32[64,512]{1,0:T(8,128)S(1)} %add_multiply_fusion), channel_id=1, source_target_pairs={{0,64},{1,65},{64,0},{65,1},{2,66},{3,67},{66,2},{67,3},{4,68},{5,... | collective-permute-start | bytes 393224 | tf_op jit(solution)/shard_map/ppermute | solution.py:357
  85.5 7.8 %collective-permute-start.21 = (f32[64,512]{1,0:T(8,128)S(1)}, f32[64,512]{1,0:T(8,128)S(1)}, u32[]{:S(2)}, u32[]{:S(2)}) collective-permute-start(f32[64,512]{1,0:T(8,128)S(1)} %add_multiply_fusion), channel_id=1, source_target_pairs={{0,65},{1,64},{64,1},{65,0},{2,67},{3,66},{66,3},{67,2},{4,69},{5,... | collective-permute-start | bytes 393224 | tf_op jit(solution)/shard_map/ppermute | solution.py:357
  95.0 2.4 %collective-permute-start.22 = (f32[64,256]{1,0:T(8,128)S(1)}, f32[64,256]{1,0:T(8,128)S(1)}, u32[]{:S(2)}, u32[]{:S(2)}) collective-permute-start(f32[64,256]{1,0:T(8,128)S(1)} %shard_map.111), channel_id=1, source_target_pairs={{0,32},{32,0},{1,33},{33,1},{2,34},{34,2},{3,35},{35,3},{4,36},{36... | collective-permute-start | bytes 196616 | tf_op jit(solution)/shard_map/ppermute | solution.py:357
  97.4 3.9 %collective-permute-start.23 = (f32[64,256]{1,0:T(8,128)S(1)}, f32[64,256]{1,0:T(8,128)S(1)}, u32[]{:S(2)}, u32[]{:S(2)}) collective-permute-start(f32[64,256]{1,0:T(8,128)S(1)} %add.82), channel_id=1, source_target_pairs={{0,2},{2,0},{4,6},{6,4},{1,3},{3,1},{5,7},{7,5},{8,10},{10,8},{12,... | collective-permute-start | bytes 196616 | tf_op jit(solution)/shard_map/ppermute | solution.py:357
  97.5 4.7 %collective-permute-start.24 = (f32[64,256]{1,0:T(8,128)S(1)}, f32[64,256]{1,0:T(8,128)S(1)}, u32[]{:S(2)}, u32[]{:S(2)}) collective-permute-start(f32[64,256]{1,0:T(8,128)S(1)} %add.82), channel_id=1, source_target_pairs={{0,4},{2,6},{4,0},{6,2},{1,5},{3,7},{5,1},{7,3},{8,12},{10,14},{12... | collective-permute-start | bytes 196616 | tf_op jit(solution)/shard_map/ppermute | solution.py:357
  99.1 4.6 %collective-permute-start.25 = (f32[64,256]{1,0:T(8,128)S(1)}, f32[64,256]{1,0:T(8,128)S(1)}, u32[]{:S(2)}, u32[]{:S(2)}) collective-permute-start(f32[64,256]{1,0:T(8,128)S(1)} %add.82), channel_id=1, source_target_pairs={{0,6},{2,4},{4,2},{6,0},{1,7},{3,5},{5,3},{7,1},{8,14},{10,12},{12... | collective-permute-start | bytes 196616 | tf_op jit(solution)/shard_map/ppermute | solution.py:357
  103.7 3.9 %collective-permute-start.26 = (f32[64,256]{1,0:T(8,128)S(1)}, f32[64,256]{1,0:T(8,128)S(1)}, u32[]{:S(2)}, u32[]{:S(2)}) collective-permute-start(f32[64,256]{1,0:T(8,128)S(1)} %add_add_fusion.2), channel_id=1, source_target_pairs={{0,8},{8,0},{16,24},{24,16},{1,9},{9,1},{17,25},{25,17},{2,10},{10... | collective-permute-start | bytes 196616 | tf_op jit(solution)/shard_map/ppermute | solution.py:357
  103.8 4.8 %collective-permute-start.27 = (f32[64,256]{1,0:T(8,128)S(1)}, f32[64,256]{1,0:T(8,128)S(1)}, u32[]{:S(2)}, u32[]{:S(2)}) collective-permute-start(f32[64,256]{1,0:T(8,128)S(1)} %add_add_fusion.2), channel_id=1, source_target_pairs={{0,16},{8,24},{16,0},{24,8},{1,17},{9,25},{17,1},{25,9},{2,18},{10... | collective-permute-start | bytes 196616 | tf_op jit(solution)/shard_map/ppermute | solution.py:357
  105.4 4.3 %collective-permute-start.28 = (f32[64,256]{1,0:T(8,128)S(1)}, f32[64,256]{1,0:T(8,128)S(1)}, u32[]{:S(2)}, u32[]{:S(2)}) collective-permute-start(f32[64,256]{1,0:T(8,128)S(1)} %add_add_fusion.2), channel_id=1, source_target_pairs={{0,24},{8,16},{16,8},{24,0},{1,25},{9,17},{17,9},{25,1},{2,26},{10... | collective-permute-start | bytes 196616 | tf_op jit(solution)/shard_map/ppermute | solution.py:357
  110.8 3.9 %collective-permute-start.29 = (f32[64,512]{1,0:T(8,128)S(1)}, f32[64,512]{1,0:T(8,128)S(1)}, u32[]{:S(2)}, u32[]{:S(2)}) collective-permute-start(f32[64,512]{1,0:T(8,128)S(1)} %shard_map.112), channel_id=1, source_target_pairs={{0,1},{1,0},{64,65},{65,64},{2,3},{3,2},{66,67},{67,66},{4,5},{5,4... | collective-permute-start | bytes 393224 | tf_op jit(solution)/shard_map/ppermute | solution.py:357
  110.9 7.1 %collective-permute-start.30 = (f32[64,512]{1,0:T(8,128)S(1)}, f32[64,512]{1,0:T(8,128)S(1)}, u32[]{:S(2)}, u32[]{:S(2)}) collective-permute-start(f32[64,512]{1,0:T(8,128)S(1)} %shard_map.112), channel_id=1, source_target_pairs={{0,64},{1,65},{64,0},{65,1},{2,66},{3,67},{66,2},{67,3},{4,68},{5,... | collective-permute-start | bytes 393224 | tf_op jit(solution)/shard_map/ppermute | solution.py:357
  114.2 5.2 %collective-permute-start.31 = (f32[64,512]{1,0:T(8,128)S(1)}, f32[64,512]{1,0:T(8,128)S(1)}, u32[]{:S(2)}, u32[]{:S(2)}) collective-permute-start(f32[64,512]{1,0:T(8,128)S(1)} %shard_map.112), channel_id=1, source_target_pairs={{0,65},{1,64},{64,1},{65,0},{2,67},{3,66},{66,3},{67,2},{4,69},{5,... | collective-permute-start | bytes 393224 | tf_op jit(solution)/shard_map/ppermute | solution.py:357
  119.4 6.1 %collective-permute-start.32 = (f32[64,512]{1,0:T(8,128)S(1)}, f32[64,512]{1,0:T(8,128)S(1)}, u32[]{:S(2)}, u32[]{:S(2)}) collective-permute-start(f32[64,512]{1,0:T(8,128)S(1)} %add_subtract_fusion), channel_id=1, source_target_pairs={{0,32},{32,0},{1,33},{33,1},{2,34},{34,2},{3,35},{35,3},{4,36},{36... | collective-permute-start | bytes 393224 | tf_op jit(solution)/shard_map/ppermute | solution.py:357
  (5 other events, 31.3 us)

commit v8 on v7

--- a/solution.py
+++ b/solution.py
@@ -105,18 +105,14 @@
     return jnp.concatenate([x[..., :wide], x[..., wide:]], axis=-2)
 
 
-def front_body(member, *refs, tables):
-    index_h, pool_f, pool_t, weights_h, centers, eig_h, owner_h, offset_h = refs[0:8]
-    drawn, pack = refs[8:10]
-    parts = refs[10 : 10 + tables]
-    index, feats, targs, wts, eig, owner, offset, sems = refs[10 + tables :]
+def front_body(index_h, pool_f, pool_t, weights_h, centers, drawn, pack, index, feats, targs, wts, sems):
     cdev = centers.shape[0]
     copies = [
         pltpu.make_async_copy(src, dst, sems.at[n])
         for n, (src, dst) in enumerate(
             (
                 (index_h, index), (pool_f, feats), (pool_t, targs), (weights_h, wts),
-                (centers, pack.at[0:cdev, :]), (eig_h, eig), (owner_h, owner), (offset_h, offset),
+                (centers, pack.at[0:cdev, :]),
             )
         )
     ]
@@ -131,16 +127,7 @@
     drawn[rows:, :] = packed(pick(hot, targs[...], NT, flip=True).T)
     copies[3].wait()
     pack[cdev:, :] = packed(wts[...].T)
-    for copy in copies[4:]:
-        copy.wait()
-    count, q = eig.shape
-    part = q // tables
-    row = jnp.broadcast_to((owner[...] * cdev + offset[...]).astype(F32), (8, count))
-    row = jnp.concatenate([row] * (part // count), axis=1)
-    for o, out in enumerate(parts):
-        mate = member[0] ^ o
-        out[0:count, :] = eig[:, pl.ds(pl.multiple_of(mate * part, part), part)]
-        out[count:, :] = row
+    copies[4].wait()
 
 
 def order_body(x, *refs):
@@ -149,34 +136,30 @@
         out[x[0] ^ o] = part[...]
 
 
-def vectors_body(*refs, cdev):
-    tables, send = refs[:-1], refs[-1]
-    count, part = tables[0].shape[0] - 8, tables[0].shape[1]
-    peers = send.shape[0]
-    blocks, group, lanes = part // 128, CAP * len(tables), 128 // len(tables)
+def vectors_body(eig, owner_row, offset_row, send, *, planes):
+    count, q = eig.shape
+    peers = send.shape[0] // planes
+    blocks = q // planes // 128
+    owner = owner_row[...]
     earlier = lax.broadcasted_iota(jnp.int32, (count, count), 0) < lax.broadcasted_iota(
         jnp.int32, (count, count), 1
     )
-    shared = []
-    for t, table in enumerate(tables):
-        nys = table[count : count + 1, 0:count].astype(jnp.int32)
-        owner = nys // cdev
-        offset = nys - owner * cdev
-        row = jnp.broadcast_to(owner.astype(F32), (count, count))
-        same = jnp.where(row.T == row, 1.0, 0.0)
-        rank = jnp.sum(jnp.where(earlier, same, 0.0), axis=0, keepdims=True).astype(jnp.int32)
-        place = owner * CAP + rank == lax.broadcasted_iota(jnp.int32, (peers * CAP, count), 0)
-        offs = jnp.sum(jnp.where(place, offset.astype(F32), 0.0), axis=1, keepdims=True)
-        shared.append(jnp.broadcast_to(offs, (peers * CAP, lanes)))
-        vectors = pick(place.astype(BF), table[0:count, :], NN)
-        for o in range(peers):
-            own = slice(o * CAP, (o + 1) * CAP)
+    row = jnp.broadcast_to(owner.astype(F32), (count, count))
+    same = jnp.where(row.T == row, 1.0, 0.0)
+    rank = jnp.sum(jnp.where(earlier, same, 0.0), axis=0, keepdims=True).astype(jnp.int32)
+    place = owner * CAP + rank == lax.broadcasted_iota(jnp.int32, (peers * CAP, count), 0)
+    offs = jnp.sum(
+        jnp.where(place, offset_row[...].astype(F32), 0.0), axis=1, keepdims=True
+    )
+    offs = jnp.broadcast_to(offs, (peers * CAP, 128))
+    vectors = pick(place.astype(BF), eig[...], NN)
+    for o in range(peers):
+        own = slice(o * CAP, (o + 1) * CAP)
+        for p in range(planes):
             for j in range(blocks):
-                at = group * j + CAP * t
-                send[o, at : at + CAP, :] = vectors[own, 128 * j : 128 * (j + 1)]
-    shared = jnp.concatenate(shared, axis=1)
-    for o in range(peers):
-        send[o, group * blocks :, :] = shared[o * CAP : (o + 1) * CAP]
+                at = 128 * (p * blocks + j)
+                send[o * planes + p, CAP * j : CAP * (j + 1), :] = vectors[own, at : at + 128]
+            send[o * planes + p, CAP * blocks :, :] = offs[own]
 
 
 def kernel_body(*refs, nb, rows, sub, extra):
@@ -275,47 +258,38 @@
             place += 1
 
 
-def block_of(points, j, tables):
-    peers, group = points.shape[0], CAP * tables
-    return points[:, group * j : group * (j + 1), :].reshape(peers * group, 128)
-
-
-def points_hot(points, blocks, tables, width):
-    peers, lanes = points.shape[0], 128 // tables
-    offs = points[:, CAP * tables * blocks :, :]
-    offs = jnp.concatenate(
-        [
-            jnp.broadcast_to(offs[:, :, lanes * t : lanes * t + 1], (peers, CAP, 128))
-            for t in range(tables)
-        ],
-        axis=1,
-    ).reshape(peers * CAP * tables, 128)
+def block_of(points, j):
+    return points[:, CAP * j : CAP * (j + 1), :].reshape(-1, 128)
+
+
+def points_hot(points, blocks, width):
+    offs = block_of(points, blocks)
     lane = lax.broadcasted_iota(jnp.int32, offs.shape, 1).astype(F32)
     return jnp.concatenate(
         [(offs == lane + float(128 * k)).astype(BF) for k in range(width // 128)], axis=1
     )
 
 
-def coeff_body(points, grads, coeff, *, tables):
+def coeff_body(points, grads, coeff):
     out, part = coeff.shape
     blocks = part // 128
-    hot = points_hot(points, blocks, tables, grads.shape[1])
+    hot = points_hot(points, blocks, grads.shape[1])
     g1, g2 = split2(pick(hot, grads[...], NT, flip=True))
     gg = jnp.concatenate([g1, g2], axis=0)
     for j in range(blocks):
-        e1, e2 = split2(block_of(points, j, tables))
+        e1, e2 = split2(block_of(points, j))
         both = mm(gg, e1, NN) + mm(gg, e2, NN)
         coeff[:, 128 * j : 128 * (j + 1)] = both[:out] + both[out:]
 
 
-def corr_body(member, points, coeff, eig_scale, corr, *, tables):
+def corr_body(member, points, coeff, eig_scale, corr):
     out, part = coeff.shape
     blocks = part // 128
-    hot = points_hot(points, blocks, tables, corr.shape[1])
+    hot = points_hot(points, blocks, corr.shape[1])
     total = jnp.zeros((2 * out, hot.shape[0]), F32)
     for j in range(blocks):
         at = slice(128 * j, 128 * (j + 1))
-        e1, e2 = split2(block_of(points, j, tables))
+        e1, e2 = split2(block_of(points, j))
         scale = eig_scale[:, pl.ds(pl.multiple_of(member[0] * part + 128 * j, 128), 128)]
         c1, c2 = split2(coeff[:, at] * scale)
         cc = jnp.concatenate([c1, c2], axis=0)
@@ -369,7 +343,7 @@
     nx, ny, half = SIZES["x"], SIZES["y"], rows // 2
     cdev, out = weights.shape
     count, q = eig_vectors.shape
-    tables = math.prod(SIZES[a] for a in PLANES)
+    planes = math.prod(SIZES[a] for a in PLANES)
     peers = math.prod(SIZES[a] for a in OWNERS)
     norm = 1.0 / math.sqrt(rows * math.prod(SIZES[a] for a in ALL))
     x = lax.axis_index("x").astype(jnp.int32)[None]
@@ -378,37 +352,35 @@
     wide = 2 * out
 
     hbm = pl.BlockSpec(memory_space=pltpu.HBM)
-    drawn, pack, *parted = pl.pallas_call(
-        functools.partial(front_body, tables=tables),
-        out_shape=[shape(rows + half, dim), shape(cdev + cdev // 2, dim)]
-        + [shape(count + 8, q // tables)] * tables,
-        in_specs=[pl.BlockSpec(memory_space=pltpu.SMEM)] + [hbm] * 8,
-        out_specs=[VMEM] * (2 + tables),
+    drawn, pack = pl.pallas_call(
+        front_body,
+        out_shape=[shape(rows + half, dim), shape(cdev + cdev // 2, dim)],
+        in_specs=[hbm] * 5,
+        out_specs=[VMEM] * 2,
         scratch_shapes=[
             pltpu.VMEM((1, rows), jnp.int32),
             pltpu.VMEM(pool_features.shape, F32),
             pltpu.VMEM(pool_targets.shape[::-1], F32),
             pltpu.VMEM((out, cdev), F32),
-            pltpu.VMEM(eig_vectors.shape, F32),
-            pltpu.VMEM((1, count), jnp.int32),
-            pltpu.VMEM((1, count), jnp.int32),
-            pltpu.SemaphoreType.DMA((8,)),
+            pltpu.SemaphoreType.DMA((5,)),
         ],
         compiler_params=params(60),
-    )(
-        member, batch_index.reshape(1, rows), pool_features, pool_targets.T, weights.T, centers,
-        eig_vectors, nys_owner.reshape(1, count), nys_offset.reshape(1, count),
-    )
+    )(batch_index.reshape(1, rows), pool_features, pool_targets.T, weights.T, centers)
 
     gathered = mates([drawn] * nx, ("x",))
     tile = lax.ppermute(pack, ("core", "zl"), [(0, 0), (2, 1), (1, 2), (3, 3)])
-    first = mate_of(parted[2], PLANES, 2)
-    tile, first, drawn, *gathered = together(tile, first, drawn, *gathered)
+    tile, drawn, *gathered = together(tile, drawn, *gathered)
     own = call(order_body, shape(nx, rows + half, dim), x, drawn, *gathered, scalars=1)
     others = mates([tile] * ny, ("y",))
     mate = mate_of(own, ("core",), 1)
-    mate, second, third = together(mate, parted[1], parted[3])
-    parted = [parted[0], first, mate_of(second, PLANES, 1), mate_of(third, PLANES, 3)]
+
+    points = call(
+        functools.partial(vectors_body, planes=planes),
+        shape(peers * planes, CAP * (q // planes // 128 + 1), 128),
+        eig_vectors, nys_owner.reshape(1, count), nys_offset.reshape(1, count),
+    )
+    points, mate = together(points, mate)
+    points = lax.all_to_all(points, OWNERS + PLANES, split_axis=0, concat_axis=0, tiled=True)
 
     def kernel(packs, extra):
         nb = len(packs)
@@ -433,14 +405,6 @@
 
     khi_a, klo_a, keep_a, send_a, scale, sb = kernel([tile], True)
 
-    keep_a, *parted = together(keep_a, *parted)
-    points = call(
-        functools.partial(vectors_body, cdev=cdev),
-        shape(peers, CAP * (tables * (q // tables // 128) + 1), 128),
-        *parted,
-    )
-    points = lax.all_to_all(points, OWNERS, split_axis=0, concat_axis=0, tiled=True)
-
     khi_b, klo_b, keep_b, send_b = kernel(others, False)
 
     (got,) = mates([send_a + send_b] * 2, ("core",))
@@ -459,14 +423,11 @@
     grads = functools.reduce(jnp.add, mates(parts, ("y",)), parts[0]) * sb[0:1]
     points, grads = together(points, grads)
     grads = exchange(grads, PLANES)
-    coeff = call(
-        functools.partial(coeff_body, tables=tables), shape(out, q // tables), points, grads
-    )
+    coeff = call(coeff_body, shape(out, q // planes), points, grads)
     for axis in OWNERS[::-1]:
         coeff = exchange(coeff, (axis,))
     corr = call(
-        functools.partial(corr_body, tables=tables),
-        shape(out, cdev), member, points, coeff, eig_scale[None, :],
+        corr_body, shape(out, cdev), member, points, coeff, eig_scale[None, :],
         scalars=1,
     )
     update = exchange(corr, PLANES) - grads

time: 127 us -> 137 us (1.079)
  waiting for transfers between devices: 38.6 us -> 54.1 us
  starting transfers between devices: 57.5 us -> 54.4 us
  Pallas kernels: 26.7 us -> 25.3 us
    ppermute x32 -> x29, waiting for transfers between devices: 38.6 us -> 54.1 us  [mate_of(): return lax.ppermute(v, axes, [(i, i ^ o) for i in range(n)])]
    ppermute x32 -> x29, starting transfers between devices: 45.8 us -> 41.4 us  [mate_of(): return lax.ppermute(v, axes, [(i, i ^ o) for i in range(n)])]
    all_to_all x1, starting transfers between devices: 6.7 us -> 8.15 us  [per_device(): lax.all_to_all(points, OWNERS + PLANES, split_axis=0, concat_axis=0, tile...]
  transfers between devices with their start and end apart: 34 -> 31, of which waited for: 22 -> 21; matrix products, arithmetic and copies ran while one was open for 0% -> 0% of each run, Pallas kernels for 17% -> 14%
where the time goes in v8:
time: 137 us; the launch traced here: 136 us
  starting transfers between devices  54.4 us (40%)
  waiting for transfers between devices  54.1 us (39%)
  Pallas kernels  25.3 us (18%)
    ppermute x29, waiting for transfers between devices, mate_of(): return lax.ppermute(v, axes, [(i, i ^ o) for i in range(n)])  54.1 us
    ppermute x29, starting transfers between devices, mate_of(): return lax.ppermute(v, axes, [(i, i ^ o) for i in range(n)])  41.4 us
    pallas_call x8, Pallas kernels, call(): pl.pallas_call(body, out_shape=outs, in_specs=[smem] * scalars + [VMEM] *...  22.4 us
    all_to_all x1, starting transfers between devices, per_device(): lax.all_to_all(points, OWNERS + PLANES, split_axis=0, concat_axis=0, tile...  8.15 us
    ppermute x1, starting transfers between devices, per_device(): tile = lax.ppermute(pack, ('core', 'zl'), [(0, 0), (2, 1), (1, 2), (3, 3)])  4.94 us
    pallas_call x1, Pallas kernels, per_device(): pl.pallas_call(front_body, out_shape=[shape(rows + half, dim), shape(cdev...  2.97 us
  transfers between devices with their start and end apart: 31, of which 21 were waited for; matrix products, arithmetic and copies ran while one was open for 0% of the time, Pallas kernels for 14%

profile of v8, /device:TPU:1, one launch (start us, length us, event | category | flops | bytes accessed | tf_op | source)
XLA Modules:
  0.0 136.4 jit_solution(15306636636617826355)
XLA Ops:
  0.7 3.0 %shard_map.104 = (f32[96,128]{1,0:T(8,128)}, f32[768,128]{1,0:T(8,128)}) custom-call(s32[1,64]{1,0:T(1,128)} %bitcast.17, f32[1024,128]{1,0:T(8,128)} %pool_f.1, f32[64,1024]{1,0:T(8,128)} %bitcast.14, f32[64,512]{1,0:T(8,128)} %bitcast.15, f32[512,128]{1,0:T(8,128)} %centers.1), custom_call_target="tpu_custom_call" | custom-call | tf_op jit(solution)/shard_map/pallas_call | solution.py:355
  3.6 4.9 %collective-permute-start = (f32[768,128]{1,0:T(8,128)}, f32[768,128]{1,0:T(8,128)S(1)}, u32[]{:S(2)}, u32[]{:S(2)}) collective-permute-start(f32[768,128]{1,0:T(8,128)} %get-tuple-element.29), channel_id=1, source_target_pairs={{0,0},{32,1},{1,32},{33,33},{2,2},{34,3},{3,34},{35,35},{4,4},{36,... | collective-permute-start | bytes 1179656 | tf_op jit(solution)/shard_map/ppermute | solution.py:371
  9.9 2.5 %collective-permute-start.2 = (f32[96,128]{1,0:T(8,128)}, f32[96,128]{1,0:T(8,128)S(1)}, u32[]{:S(2)}, u32[]{:S(2)}) collective-permute-start(f32[96,128]{1,0:T(8,128)} %get-tuple-element.31.refs_0_), channel_id=1, source_target_pairs={{0,16},{8,24},{16,0},{24,8},{1,17},{9,25},{17,1},{25,9},{2,18},{10... | collective-permute-start | bytes 147464 | tf_op jit(solution)/shard_map/ppermute | solution.py:331
  12.5 2.0 %collective-permute-done.2.refs_2_ = f32[96,128]{1,0:T(8,128)S(1)} collective-permute-done((f32[96,128]{1,0:T(8,128)}, f32[96,128]{1,0:T(8,128)S(1)}, u32[]{:S(2)}, u32[]{:S(2)}) %collective-permute-start.2) | collective-permute-done | bytes 49184 | tf_op jit(solution)/shard_map/ppermute | solution.py:331
  14.5 2.1 %collective-permute-done.3.refs_3_ = f32[96,128]{1,0:T(8,128)S(1)} collective-permute-done((f32[96,128]{1,0:T(8,128)}, f32[96,128]{1,0:T(8,128)S(1)}, u32[]{:S(2)}, u32[]{:S(2)}) %collective-permute-start.3) | collective-permute-done | bytes 49184 | tf_op jit(solution)/shard_map/ppermute | solution.py:331
  18.0 2.6 %collective-permute-start.6 = (f32[768,128]{1,0:T(8,128)S(1)}, f32[768,128]{1,0:T(8,128)S(1)}, u32[]{:S(2)}, u32[]{:S(2)}) collective-permute-start(f32[768,128]{1,0:T(8,128)S(1)} %collective-permute-done.refs_2_), channel_id=1, source_target_pairs={{0,4},{2,6},{4,0},{6,2},{1,5},{3,7},{5,1},{7,3},{8,12},{10,14},{12... | collective-permute-start | bytes 1179656 | tf_op jit(solution)/shard_map/ppermute | solution.py:331
  22.2 1.9 %shard_map.106 = f32[128,24,128]{2,1,0:T(8,128)} custom-call(f32[128,1024]{1,0:T(8,128)S(1)} %copy-done, s32[1,128]{1,0:T(1,128)S(1)} %bitcast.12, s32[1,128]{1,0:T(1,128)S(1)} %bitcast.13), custom_call_target="tpu_custom_call" | custom-call | tf_op jit(solution)/shard_map/pallas_call | solution.py:311
  24.0 8.1 %all-to-all-start = ((f32[128,24,128]{2,1,0:T(8,128)}), f32[128,24,128]{2,1,0:T(8,128)S(1)}, u32[]{:S(2)}, u32[]{:S(2)}) async-start(f32[128,24,128]{2,1,0:T(8,128)} %shard_map.106), calls=%async_computation | async-start | bytes 3145728 | tf_op jit(solution)/shard_map/all_to_all | solution.py:383
  32.2 4.1 %shard_map.107 = (bf16[1,512,512]{2,1,0:T(8,128)(2,1)S(1)}, bf16[1,512,512]{2,1,0:T(8,128)(2,1)S(1)}, f32[4,32,128]{2,1,0:T(8,128)S(1)}, f32[4,32,128]{2,1,0:T(8...) custom-call(f32[4,96,128]{2,1,0:T(8,128)S(1)} %shard_map.105.refs_0_.own, ...), custom_call_target="tpu_custom_call" | custom-call | flops 100000000 | bytes 65536 | tf_op jit(solution)/shard_map/pallas_call | solution.py:311
  36.3 5.7 %collective-permute-done.6.refs_3_ = f32[768,128]{1,0:T(8,128)S(1)} collective-permute-done((f32[768,128]{1,0:T(8,128)S(1)}, f32[768,128]{1,0:T(8,128)S(1)}, u32[]{:S(2)}, u32[]{:S(2)}) %collective-permute-start.6) | collective-permute-done | bytes 393248 | tf_op jit(solution)/shard_map/ppermute | solution.py:331
  42.0 12.3 %collective-permute-done.7.refs_4_ = f32[768,128]{1,0:T(8,128)S(1)} collective-permute-done((f32[768,128]{1,0:T(8,128)S(1)}, f32[768,128]{1,0:T(8,128)S(1)}, u32[]{:S(2)}, u32[]{:S(2)}) %collective-permute-start.7) | collective-permute-done | bytes 393248 | tf_op jit(solution)/shard_map/ppermute | solution.py:331
  54.3 12.3 %shard_map.108 = (bf16[3,512,512]{2,1,0:T(8,128)(2,1)S(1)}, bf16[3,512,512]{2,1,0:T(8,128)(2,1)S(1)}, f32[4,32,128]{2,1,0:T(8,128)S(1)}, f32[4,32,128]{2,1,0:T(8,128)S(1)}) custom-call(f32[4,96,128]{2,1,0:T(8,128)S(1)} %shard_map.105.refs_0_.own, f32[4,96,128]{2,1,0:T(8,128)S(1)} %collective-permute-done.4.refs_1_, ...), custom_call_target="tpu_custom_call" | custom-call | flops 30000001024 | bytes 65536 | tf_op jit(solution)/shard_map/pallas_call | solution.py:311
  66.6 3.2 %collective-permute-start.8 = (f32[4,32,128]{2,1,0:T(8,128)S(1)}, f32[4,32,128]{2,1,0:T(8,128)S(1)}, u32[]{:S(2)}, u32[]{:S(2)}) collective-permute-start(f32[4,32,128]{2,1,0:T(8,128)S(1)} %add.70), channel_id=1, source_target_pairs={{0,32},{32,0},{1,33},{33,1},{2,34},{34,2},{3,35},{35,3},{4,36},{36... | collective-permute-start | bytes 196616 | tf_op jit(solution)/shard_map/ppermute | solution.py:331
  70.8 1.5 %collective-permute-start.11 = (f32[4,32,128]{2,1,0:T(8,128)S(1)}, f32[4,32,128]{2,1,0:T(8,128)S(1)}, u32[]{:S(2)}, u32[]{:S(2)}) collective-permute-start(f32[4,32,128]{2,1,0:T(8,128)S(1)} %add_add_fusion.4), channel_id=1, source_target_pairs={{0,24},{8,16},{16,8},{24,0},{1,25},{9,17},{17,9},{25,1},{2,26},{10... | collective-permute-start | bytes 196616 | tf_op jit(solution)/shard_map/ppermute | solution.py:331
  73.5 2.1 %collective-permute-done.10 = f32[4,32,128]{2,1,0:T(8,128)S(1)} collective-permute-done((f32[4,32,128]{2,1,0:T(8,128)S(1)}, f32[4,32,128]{2,1,0:T(8,128)S(1)}, u32[]{:S(2)}, u32[]{:S(2)}) %collective-permute-start.10) | collective-permute-done | bytes 65568 | tf_op jit(solution)/shard_map/ppermute | solution.py:331
  75.5 1.8 %collective-permute-done.11 = f32[4,32,128]{2,1,0:T(8,128)S(1)} collective-permute-done((f32[4,32,128]{2,1,0:T(8,128)S(1)}, f32[4,32,128]{2,1,0:T(8,128)S(1)}, u32[]{:S(2)}, u32[]{:S(2)}) %collective-permute-start.11) | collective-permute-done | bytes 65568 | tf_op jit(solution)/shard_map/ppermute | solution.py:331
  81.7 2.8 %collective-permute-start.15 = (f32[64,512]{1,0:T(8,128)S(1)}, f32[64,512]{1,0:T(8,128)S(1)}, u32[]{:S(2)}, u32[]{:S(2)}) collective-permute-start(f32[64,512]{1,0:T(8,128)S(1)} %get-tuple-element.52), channel_id=1, source_target_pairs={{0,6},{2,4},{4,2},{6,0},{1,7},{3,5},{5,3},{7,1},{8,14},{10,12},{12... | collective-permute-start | bytes 393224 | tf_op jit(solution)/shard_map/ppermute | solution.py:331
  85.3 2.5 %collective-permute-done.14 = f32[64,512]{1,0:T(8,128)S(1)} collective-permute-done((f32[64,512]{1,0:T(8,128)S(1)}, f32[64,512]{1,0:T(8,128)S(1)}, u32[]{:S(2)}, u32[]{:S(2)}) %collective-permute-start.14) | collective-permute-done | bytes 131104 | tf_op jit(solution)/shard_map/ppermute | solution.py:331
  87.8 2.6 %collective-permute-done.15 = f32[64,512]{1,0:T(8,128)S(1)} collective-permute-done((f32[64,512]{1,0:T(8,128)S(1)}, f32[64,512]{1,0:T(8,128)S(1)}, u32[]{:S(2)}, u32[]{:S(2)}) %collective-permute-start.15) | collective-permute-done | bytes 131104 | tf_op jit(solution)/shard_map/ppermute | solution.py:331
  90.5 3.9 %collective-permute-start.17 = (f32[64,512]{1,0:T(8,128)S(1)}, f32[64,512]{1,0:T(8,128)S(1)}, u32[]{:S(2)}, u32[]{:S(2)}) collective-permute-start(f32[64,512]{1,0:T(8,128)S(1)} %add_multiply_fusion), channel_id=1, source_target_pairs={{0,64},{1,65},{64,0},{65,1},{2,66},{3,67},{66,2},{67,3},{4,68},{5,... | collective-permute-start | bytes 393224 | tf_op jit(solution)/shard_map/ppermute | solution.py:331
  94.4 5.4 %collective-permute-done.17 = f32[64,512]{1,0:T(8,128)S(1)} collective-permute-done((f32[64,512]{1,0:T(8,128)S(1)}, f32[64,512]{1,0:T(8,128)S(1)}, u32[]{:S(2)}, u32[]{:S(2)}) %collective-permute-start.17) | collective-permute-done | bytes 131104 | tf_op jit(solution)/shard_map/ppermute | solution.py:331
  99.8 2.8 %collective-permute-done.18 = f32[64,512]{1,0:T(8,128)S(1)} collective-permute-done((f32[64,512]{1,0:T(8,128)S(1)}, f32[64,512]{1,0:T(8,128)S(1)}, u32[]{:S(2)}, u32[]{:S(2)}) %collective-permute-start.18) | collective-permute-done | bytes 131104 | tf_op jit(solution)/shard_map/ppermute | solution.py:331
  102.7 1.5 %shard_map.111 = f32[64,256]{1,0:T(8,128)S(1)} custom-call(f32[128,24,128]{2,1,0:T(8,128)S(1)} %all-to-all-done.points, f32[64,512]{1,0:T(8,128)S(1)} %add_add_fusion.grads), custom_call_target="tpu_custom_call" | custom-call | tf_op jit(solution)/shard_map/pallas_call | solution.py:311
  106.3 3.8 %collective-permute-start.21 = (f32[64,256]{1,0:T(8,128)S(1)}, f32[64,256]{1,0:T(8,128)S(1)}, u32[]{:S(2)}, u32[]{:S(2)}) collective-permute-start(f32[64,256]{1,0:T(8,128)S(1)} %add.82), channel_id=1, source_target_pairs={{0,4},{2,6},{4,0},{6,2},{1,5},{3,7},{5,1},{7,3},{8,12},{10,14},{12... | collective-permute-start | bytes 196616 | tf_op jit(solution)/shard_map/ppermute | solution.py:331
  110.2 2.9 %collective-permute-done.21 = f32[64,256]{1,0:T(8,128)S(1)} collective-permute-done((f32[64,256]{1,0:T(8,128)S(1)}, f32[64,256]{1,0:T(8,128)S(1)}, u32[]{:S(2)}, u32[]{:S(2)}) %collective-permute-start.21) | collective-permute-done | bytes 65568 | tf_op jit(solution)/shard_map/ppermute | solution.py:331
  113.1 1.5 %collective-permute-done.22 = f32[64,256]{1,0:T(8,128)S(1)} collective-permute-done((f32[64,256]{1,0:T(8,128)S(1)}, f32[64,256]{1,0:T(8,128)S(1)}, u32[]{:S(2)}, u32[]{:S(2)}) %collective-permute-start.22) | collective-permute-done | bytes 65568 | tf_op jit(solution)/shard_map/ppermute | solution.py:331
  115.2 1.7 %collective-permute-start.24 = (f32[64,256]{1,0:T(8,128)S(1)}, f32[64,256]{1,0:T(8,128)S(1)}, u32[]{:S(2)}, u32[]{:S(2)}) collective-permute-start(f32[64,256]{1,0:T(8,128)S(1)} %add_add_fusion.2), channel_id=1, source_target_pairs={{0,16},{8,24},{16,0},{24,8},{1,17},{9,25},{17,1},{25,9},{2,18},{10... | collective-permute-start | bytes 196616 | tf_op jit(solution)/shard_map/ppermute | solution.py:331
  116.8 1.7 %collective-permute-start.25 = (f32[64,256]{1,0:T(8,128)S(1)}, f32[64,256]{1,0:T(8,128)S(1)}, u32[]{:S(2)}, u32[]{:S(2)}) collective-permute-start(f32[64,256]{1,0:T(8,128)S(1)} %add_add_fusion.2), channel_id=1, source_target_pairs={{0,24},{8,16},{16,8},{24,0},{1,25},{9,17},{17,9},{25,1},{2,26},{10... | collective-permute-start | bytes 196616 | tf_op jit(solution)/shard_map/ppermute | solution.py:331
  122.4 1.9 %collective-permute-start.27 = (f32[64,512]{1,0:T(8,128)S(1)}, f32[64,512]{1,0:T(8,128)S(1)}, u32[]{:S(2)}, u32[]{:S(2)}) collective-permute-start(f32[64,512]{1,0:T(8,128)S(1)} %shard_map.112), channel_id=1, source_target_pairs={{0,64},{1,65},{64,0},{65,1},{2,66},{3,67},{66,2},{67,3},{4,68},{5,... | collective-permute-start | bytes 393224 | tf_op jit(solution)/shard_map/ppermute | solution.py:331
  124.2 2.0 %collective-permute-start.28 = (f32[64,512]{1,0:T(8,128)S(1)}, f32[64,512]{1,0:T(8,128)S(1)}, u32[]{:S(2)}, u32[]{:S(2)}) collective-permute-start(f32[64,512]{1,0:T(8,128)S(1)} %shard_map.112), channel_id=1, source_target_pairs={{0,65},{1,64},{64,1},{65,0},{2,67},{3,66},{66,3},{67,2},{4,69},{5,... | collective-permute-start | bytes 393224 | tf_op jit(solution)/shard_map/ppermute | solution.py:331
  126.2 1.8 %collective-permute-done.27 = f32[64,512]{1,0:T(8,128)S(1)} collective-permute-done((f32[64,512]{1,0:T(8,128)S(1)}, f32[64,512]{1,0:T(8,128)S(1)}, u32[]{:S(2)}, u32[]{:S(2)}) %collective-permute-start.27) | collective-permute-done | bytes 131104 | tf_op jit(solution)/shard_map/ppermute | solution.py:331
  129.4 5.3 %collective-permute-start.29 = (f32[64,512]{1,0:T(8,128)S(1)}, f32[64,512]{1,0:T(8,128)S(1)}, u32[]{:S(2)}, u32[]{:S(2)}) collective-permute-start(f32[64,512]{1,0:T(8,128)S(1)} %add_subtract_fusion), channel_id=1, source_target_pairs={{0,32},{32,0},{1,33},{33,1},{2,34},{34,2},{3,35},{35,3},{4,36},{36... | collective-permute-start | bytes 393224 | tf_op jit(solution)/shard_map/ppermute | solution.py:331
  (60 shorter events, 21.5 us)
Async XLA Ops:
  3.6 13.0 %collective-permute-start = (f32[768,128]{1,0:T(8,128)}, f32[768,128]{1,0:T(8,128)S(1)}, u32[]{:S(2)}, u32[]{:S(2)}) collective-permute-start(f32[768,128]{1,0:T(8,128)} %get-tuple-element.29), channel_id=1, source_target_pairs={{0,0},{32,1},{1,32},{33,33},{2,2},{34,3},{3,34},{35,35},{4,4},{36,... | collective-permute-start | bytes 1179656 | tf_op jit(solution)/shard_map/ppermute | solution.py:371
  8.6 3.9 %collective-permute-start.1 = (f32[96,128]{1,0:T(8,128)}, f32[96,128]{1,0:T(8,128)S(1)}, u32[]{:S(2)}, u32[]{:S(2)}) collective-permute-start(f32[96,128]{1,0:T(8,128)} %get-tuple-element.31.refs_0_), channel_id=1, source_target_pairs={{0,8},{8,0},{16,24},{24,16},{1,9},{9,1},{17,25},{25,17},{2,10},{10... | collective-permute-start | bytes 147464 | tf_op jit(solution)/shard_map/ppermute | solution.py:331
  9.9 4.7 %collective-permute-start.2 = (f32[96,128]{1,0:T(8,128)}, f32[96,128]{1,0:T(8,128)S(1)}, u32[]{:S(2)}, u32[]{:S(2)}) collective-permute-start(f32[96,128]{1,0:T(8,128)} %get-tuple-element.31.refs_0_), channel_id=1, source_target_pairs={{0,16},{8,24},{16,0},{24,8},{1,17},{9,25},{17,1},{25,9},{2,18},{10... | collective-permute-start | bytes 147464 | tf_op jit(solution)/shard_map/ppermute | solution.py:331
  12.3 4.4 %collective-permute-start.3 = (f32[96,128]{1,0:T(8,128)}, f32[96,128]{1,0:T(8,128)S(1)}, u32[]{:S(2)}, u32[]{:S(2)}) collective-permute-start(f32[96,128]{1,0:T(8,128)} %get-tuple-element.31.refs_0_), channel_id=1, source_target_pairs={{0,24},{8,16},{16,8},{24,0},{1,25},{9,17},{17,9},{25,1},{2,26},{10... | collective-permute-start | bytes 147464 | tf_op jit(solution)/shard_map/ppermute | solution.py:331
  16.7 19.6 %collective-permute-start.5 = (f32[768,128]{1,0:T(8,128)S(1)}, f32[768,128]{1,0:T(8,128)S(1)}, u32[]{:S(2)}, u32[]{:S(2)}) collective-permute-start(f32[768,128]{1,0:T(8,128)S(1)} %collective-permute-done.refs_2_), channel_id=1, source_target_pairs={{0,2},{2,0},{4,6},{6,4},{1,3},{3,1},{5,7},{7,5},{8,10},{10,8},{12,... | collective-permute-start | bytes 1179656 | tf_op jit(solution)/shard_map/ppermute | solution.py:331
  18.0 24.0 %collective-permute-start.6 = (f32[768,128]{1,0:T(8,128)S(1)}, f32[768,128]{1,0:T(8,128)S(1)}, u32[]{:S(2)}, u32[]{:S(2)}) collective-permute-start(f32[768,128]{1,0:T(8,128)S(1)} %collective-permute-done.refs_2_), channel_id=1, source_target_pairs={{0,4},{2,6},{4,0},{6,2},{1,5},{3,7},{5,1},{7,3},{8,12},{10,14},{12... | collective-permute-start | bytes 1179656 | tf_op jit(solution)/shard_map/ppermute | solution.py:331
  20.6 33.7 %collective-permute-start.7 = (f32[768,128]{1,0:T(8,128)S(1)}, f32[768,128]{1,0:T(8,128)S(1)}, u32[]{:S(2)}, u32[]{:S(2)}) collective-permute-start(f32[768,128]{1,0:T(8,128)S(1)} %collective-permute-done.refs_2_), channel_id=1, source_target_pairs={{0,6},{2,4},{4,2},{6,0},{1,7},{3,5},{5,3},{7,1},{8,14},{10,12},{12... | collective-permute-start | bytes 1179656 | tf_op jit(solution)/shard_map/ppermute | solution.py:331
  21.4 2.6 %collective-permute-start.4 = (f32[4,96,128]{2,1,0:T(8,128)S(1)}, f32[4,96,128]{2,1,0:T(8,128)S(1)}, u32[]{:S(2)}, u32[]{:S(2)}) collective-permute-start(f32[4,96,128]{2,1,0:T(8,128)S(1)} %shard_map.105.refs_0_.own), channel_id=1, source_target_pairs={{0,32},{32,0},{1,33},{33,1},{2,34},{34,2},{3,35},{35,3},{4,36},{36... | collective-permute-start | bytes 589832 | tf_op jit(solution)/shard_map/ppermute | solution.py:331
  24.0 66.4 %all-to-all-start = ((f32[128,24,128]{2,1,0:T(8,128)}), f32[128,24,128]{2,1,0:T(8,128)S(1)}, u32[]{:S(2)}, u32[]{:S(2)}) async-start(f32[128,24,128]{2,1,0:T(8,128)} %shard_map.106), calls=%async_computation | async-start | bytes 3145728 | tf_op jit(solution)/shard_map/all_to_all | solution.py:383
  66.6 4.1 %collective-permute-start.8 = (f32[4,32,128]{2,1,0:T(8,128)S(1)}, f32[4,32,128]{2,1,0:T(8,128)S(1)}, u32[]{:S(2)}, u32[]{:S(2)}) collective-permute-start(f32[4,32,128]{2,1,0:T(8,128)S(1)} %add.70), channel_id=1, source_target_pairs={{0,32},{32,0},{1,33},{33,1},{2,34},{34,2},{3,35},{35,3},{4,36},{36... | collective-permute-start | bytes 196616 | tf_op jit(solution)/shard_map/ppermute | solution.py:331
  70.7 4.8 %collective-permute-start.10 = (f32[4,32,128]{2,1,0:T(8,128)S(1)}, f32[4,32,128]{2,1,0:T(8,128)S(1)}, u32[]{:S(2)}, u32[]{:S(2)}) collective-permute-start(f32[4,32,128]{2,1,0:T(8,128)S(1)} %add_add_fusion.4), channel_id=1, source_target_pairs={{0,16},{8,24},{16,0},{24,8},{1,17},{9,25},{17,1},{25,9},{2,18},{10... | collective-permute-start | bytes 196616 | tf_op jit(solution)/shard_map/ppermute | solution.py:331
  70.8 6.5 %collective-permute-start.11 = (f32[4,32,128]{2,1,0:T(8,128)S(1)}, f32[4,32,128]{2,1,0:T(8,128)S(1)}, u32[]{:S(2)}, u32[]{:S(2)}) collective-permute-start(f32[4,32,128]{2,1,0:T(8,128)S(1)} %add_add_fusion.4), channel_id=1, source_target_pairs={{0,24},{8,16},{16,8},{24,0},{1,25},{9,17},{17,9},{25,1},{2,26},{10... | collective-permute-start | bytes 196616 | tf_op jit(solution)/shard_map/ppermute | solution.py:331
  72.3 5.0 %collective-permute-start.9 = (f32[4,32,128]{2,1,0:T(8,128)S(1)}, f32[4,32,128]{2,1,0:T(8,128)S(1)}, u32[]{:S(2)}, u32[]{:S(2)}) collective-permute-start(f32[4,32,128]{2,1,0:T(8,128)S(1)} %add_add_fusion.4), channel_id=1, source_target_pairs={{0,8},{8,0},{16,24},{24,16},{1,9},{9,1},{17,25},{25,17},{2,10},{10... | collective-permute-start | bytes 196616 | tf_op jit(solution)/shard_map/ppermute | solution.py:331
  78.1 1.6 %collective-permute-start.12 = (f32[4,32,128]{2,1,0:T(8,128)S(1)}, f32[4,32,128]{2,1,0:T(8,128)S(1)}, u32[]{:S(2)}, u32[]{:S(2)}) collective-permute-start(f32[4,32,128]{2,1,0:T(8,128)S(1)} %get-tuple-element.44.own), channel_id=1, source_target_pairs={{0,32},{32,0},{1,33},{33,1},{2,34},{34,2},{3,35},{35,3},{4,36},{36... | collective-permute-start | bytes 196616 | tf_op jit(solution)/shard_map/ppermute | solution.py:331
  80.5 4.8 %collective-permute-start.13 = (f32[64,512]{1,0:T(8,128)S(1)}, f32[64,512]{1,0:T(8,128)S(1)}, u32[]{:S(2)}, u32[]{:S(2)}) collective-permute-start(f32[64,512]{1,0:T(8,128)S(1)} %get-tuple-element.50), channel_id=1, source_target_pairs={{0,2},{2,0},{4,6},{6,4},{1,3},{3,1},{5,7},{7,5},{8,10},{10,8},{12,... | collective-permute-start | bytes 393224 | tf_op jit(solution)/shard_map/ppermute | solution.py:331
  80.6 7.2 %collective-permute-start.14 = (f32[64,512]{1,0:T(8,128)S(1)}, f32[64,512]{1,0:T(8,128)S(1)}, u32[]{:S(2)}, u32[]{:S(2)}) collective-permute-start(f32[64,512]{1,0:T(8,128)S(1)} %get-tuple-element.51), channel_id=1, source_target_pairs={{0,4},{2,6},{4,0},{6,2},{1,5},{3,7},{5,1},{7,3},{8,12},{10,14},{12... | collective-permute-start | bytes 393224 | tf_op jit(solution)/shard_map/ppermute | solution.py:331
  81.7 8.7 %collective-permute-start.15 = (f32[64,512]{1,0:T(8,128)S(1)}, f32[64,512]{1,0:T(8,128)S(1)}, u32[]{:S(2)}, u32[]{:S(2)}) collective-permute-start(f32[64,512]{1,0:T(8,128)S(1)} %get-tuple-element.52), channel_id=1, source_target_pairs={{0,6},{2,4},{4,2},{6,0},{1,7},{3,5},{5,3},{7,1},{8,14},{10,12},{12... | collective-permute-start | bytes 393224 | tf_op jit(solution)/shard_map/ppermute | solution.py:331
  90.4 30.8 %copy-start.2 = (f32[1024]{0:T(1024)S(1)}, f32[1024]{0:T(1024)}, u32[]{:S(2)}) copy-start(f32[1024]{0:T(1024)} %param.15) | copy-start | bytes 12292
  90.4 4.0 %collective-permute-start.16 = (f32[64,512]{1,0:T(8,128)S(1)}, f32[64,512]{1,0:T(8,128)S(1)}, u32[]{:S(2)}, u32[]{:S(2)}) collective-permute-start(f32[64,512]{1,0:T(8,128)S(1)} %add_multiply_fusion), channel_id=1, source_target_pairs={{0,1},{1,0},{64,65},{65,64},{2,3},{3,2},{66,67},{67,66},{4,5},{5,4... | collective-permute-start | bytes 393224 | tf_op jit(solution)/shard_map/ppermute | solution.py:331
  90.5 9.3 %collective-permute-start.17 = (f32[64,512]{1,0:T(8,128)S(1)}, f32[64,512]{1,0:T(8,128)S(1)}, u32[]{:S(2)}, u32[]{:S(2)}) collective-permute-start(f32[64,512]{1,0:T(8,128)S(1)} %add_multiply_fusion), channel_id=1, source_target_pairs={{0,64},{1,65},{64,0},{65,1},{2,66},{3,67},{66,2},{67,3},{4,68},{5,... | collective-permute-start | bytes 393224 | tf_op jit(solution)/shard_map/ppermute | solution.py:331
  94.4 8.2 %collective-permute-start.18 = (f32[64,512]{1,0:T(8,128)S(1)}, f32[64,512]{1,0:T(8,128)S(1)}, u32[]{:S(2)}, u32[]{:S(2)}) collective-permute-start(f32[64,512]{1,0:T(8,128)S(1)} %add_multiply_fusion), channel_id=1, source_target_pairs={{0,65},{1,64},{64,1},{65,0},{2,67},{3,66},{66,3},{67,2},{4,69},{5,... | collective-permute-start | bytes 393224 | tf_op jit(solution)/shard_map/ppermute | solution.py:331
  104.2 2.0 %collective-permute-start.19 = (f32[64,256]{1,0:T(8,128)S(1)}, f32[64,256]{1,0:T(8,128)S(1)}, u32[]{:S(2)}, u32[]{:S(2)}) collective-permute-start(f32[64,256]{1,0:T(8,128)S(1)} %shard_map.111), channel_id=1, source_target_pairs={{0,32},{32,0},{1,33},{33,1},{2,34},{34,2},{3,35},{35,3},{4,36},{36... | collective-permute-start | bytes 196616 | tf_op jit(solution)/shard_map/ppermute | solution.py:331
  106.2 3.9 %collective-permute-start.20 = (f32[64,256]{1,0:T(8,128)S(1)}, f32[64,256]{1,0:T(8,128)S(1)}, u32[]{:S(2)}, u32[]{:S(2)}) collective-permute-start(f32[64,256]{1,0:T(8,128)S(1)} %add.82), channel_id=1, source_target_pairs={{0,2},{2,0},{4,6},{6,4},{1,3},{3,1},{5,7},{7,5},{8,10},{10,8},{12,... | collective-permute-start | bytes 196616 | tf_op jit(solution)/shard_map/ppermute | solution.py:331
  106.3 6.8 %collective-permute-start.21 = (f32[64,256]{1,0:T(8,128)S(1)}, f32[64,256]{1,0:T(8,128)S(1)}, u32[]{:S(2)}, u32[]{:S(2)}) collective-permute-start(f32[64,256]{1,0:T(8,128)S(1)} %add.82), channel_id=1, source_target_pairs={{0,4},{2,6},{4,0},{6,2},{1,5},{3,7},{5,1},{7,3},{8,12},{10,14},{12... | collective-permute-start | bytes 196616 | tf_op jit(solution)/shard_map/ppermute | solution.py:331
  110.1 4.5 %collective-permute-start.22 = (f32[64,256]{1,0:T(8,128)S(1)}, f32[64,256]{1,0:T(8,128)S(1)}, u32[]{:S(2)}, u32[]{:S(2)}) collective-permute-start(f32[64,256]{1,0:T(8,128)S(1)} %add.82), channel_id=1, source_target_pairs={{0,6},{2,4},{4,2},{6,0},{1,7},{3,5},{5,3},{7,1},{8,14},{10,12},{12... | collective-permute-start | bytes 196616 | tf_op jit(solution)/shard_map/ppermute | solution.py:331
  114.6 3.9 %collective-permute-start.23 = (f32[64,256]{1,0:T(8,128)S(1)}, f32[64,256]{1,0:T(8,128)S(1)}, u32[]{:S(2)}, u32[]{:S(2)}) collective-permute-start(f32[64,256]{1,0:T(8,128)S(1)} %add_add_fusion.2), channel_id=1, source_target_pairs={{0,8},{8,0},{16,24},{24,16},{1,9},{9,1},{17,25},{25,17},{2,10},{10... | collective-permute-start | bytes 196616 | tf_op jit(solution)/shard_map/ppermute | solution.py:331
  115.2 4.6 %collective-permute-start.24 = (f32[64,256]{1,0:T(8,128)S(1)}, f32[64,256]{1,0:T(8,128)S(1)}, u32[]{:S(2)}, u32[]{:S(2)}) collective-permute-start(f32[64,256]{1,0:T(8,128)S(1)} %add_add_fusion.2), channel_id=1, source_target_pairs={{0,16},{8,24},{16,0},{24,8},{1,17},{9,25},{17,1},{25,9},{2,18},{10... | collective-permute-start | bytes 196616 | tf_op jit(solution)/shard_map/ppermute | solution.py:331
  116.8 4.3 %collective-permute-start.25 = (f32[64,256]{1,0:T(8,128)S(1)}, f32[64,256]{1,0:T(8,128)S(1)}, u32[]{:S(2)}, u32[]{:S(2)}) collective-permute-start(f32[64,256]{1,0:T(8,128)S(1)} %add_add_fusion.2), channel_id=1, source_target_pairs={{0,24},{8,16},{16,8},{24,0},{1,25},{9,17},{17,9},{25,1},{2,26},{10... | collective-permute-start | bytes 196616 | tf_op jit(solution)/shard_map/ppermute | solution.py:331
  122.3 3.9 %collective-permute-start.26 = (f32[64,512]{1,0:T(8,128)S(1)}, f32[64,512]{1,0:T(8,128)S(1)}, u32[]{:S(2)}, u32[]{:S(2)}) collective-permute-start(f32[64,512]{1,0:T(8,128)S(1)} %shard_map.112), channel_id=1, source_target_pairs={{0,1},{1,0},{64,65},{65,64},{2,3},{3,2},{66,67},{67,66},{4,5},{5,4... | collective-permute-start | bytes 393224 | tf_op jit(solution)/shard_map/ppermute | solution.py:331
  122.4 5.6 %collective-permute-start.27 = (f32[64,512]{1,0:T(8,128)S(1)}, f32[64,512]{1,0:T(8,128)S(1)}, u32[]{:S(2)}, u32[]{:S(2)}) collective-permute-start(f32[64,512]{1,0:T(8,128)S(1)} %shard_map.112), channel_id=1, source_target_pairs={{0,64},{1,65},{64,0},{65,1},{2,66},{3,67},{66,2},{67,3},{4,68},{5,... | collective-permute-start | bytes 393224 | tf_op jit(solution)/shard_map/ppermute | solution.py:331
  124.2 5.2 %collective-permute-start.28 = (f32[64,512]{1,0:T(8,128)S(1)}, f32[64,512]{1,0:T(8,128)S(1)}, u32[]{:S(2)}, u32[]{:S(2)}) collective-permute-start(f32[64,512]{1,0:T(8,128)S(1)} %shard_map.112), channel_id=1, source_target_pairs={{0,65},{1,64},{64,1},{65,0},{2,67},{3,66},{66,3},{67,2},{4,69},{5,... | collective-permute-start | bytes 393224 | tf_op jit(solution)/shard_map/ppermute | solution.py:331
  129.4 6.3 %collective-permute-start.29 = (f32[64,512]{1,0:T(8,128)S(1)}, f32[64,512]{1,0:T(8,128)S(1)}, u32[]{:S(2)}, u32[]{:S(2)}) collective-permute-start(f32[64,512]{1,0:T(8,128)S(1)} %add_subtract_fusion), channel_id=1, source_target_pairs={{0,32},{32,0},{1,33},{33,1},{2,34},{34,2},{3,35},{35,3},{4,36},{36... | collective-permute-start | bytes 393224 | tf_op jit(solution)/shard_map/ppermute | solution.py:331
  (4 other events, 65.3 us)

commit v9 on v8

--- a/solution.py
+++ b/solution.py
@@ -374,14 +374,6 @@
     others = mates([tile] * ny, ("y",))
     mate = mate_of(own, ("core",), 1)
 
-    points = call(
-        functools.partial(vectors_body, planes=planes),
-        shape(peers * planes, CAP * (q // planes // 128 + 1), 128),
-        eig_vectors, nys_owner.reshape(1, count), nys_offset.reshape(1, count),
-    )
-    points, mate = together(points, mate)
-    points = lax.all_to_all(points, OWNERS + PLANES, split_axis=0, concat_axis=0, tiled=True)
-
     def kernel(packs, extra):
         nb = len(packs)
         outs = [shape(nb, 2 * nx * rows, cdev, dtype=BF)] * 2 + [shape(nx, half, wide)] * 2
@@ -405,6 +397,14 @@
 
     khi_a, klo_a, keep_a, send_a, scale, sb = kernel([tile], True)
 
+    points = call(
+        functools.partial(vectors_body, planes=planes),
+        shape(peers * planes, CAP * (q // planes // 128 + 1), 128),
+        eig_vectors, nys_owner.reshape(1, count), nys_offset.reshape(1, count),
+    )
+    points, keep_a = together(points, keep_a)
+    points = lax.all_to_all(points, OWNERS + PLANES, split_axis=0, concat_axis=0, tiled=True)
+
     khi_b, klo_b, keep_b, send_b = kernel(others, False)
 
     (got,) = mates([send_a + send_b] * 2, ("core",))

time: 137 us -> 132 us (0.964)
  waiting for transfers between devices: 54.1 us -> 39.6 us
  starting transfers between devices: 54.4 us -> 62.3 us
    ppermute x29, waiting for transfers between devices: 54.1 us -> 39.6 us  [mate_of(): return lax.ppermute(v, axes, [(i, i ^ o) for i in range(n)])]
    ppermute x29, starting transfers between devices: 41.4 us -> 49.3 us  [mate_of(): return lax.ppermute(v, axes, [(i, i ^ o) for i in range(n)])]
  transfers between devices with their start and end apart: 31 -> 31, of which waited for: 21 -> 22; matrix products, arithmetic and copies ran while one was open for 0% -> 0% of each run, Pallas kernels for 14% -> 16%
where the time goes in v9:
time: 132 us
  starting transfers between devices  62.3 us (47%)
  waiting for transfers between devices  39.6 us (30%)
  Pallas kernels  26.5 us (20%)
  local copies, waits for them, and re-layouts  1.45 us (1%)
    ppermute x29, starting transfers between devices, mate_of(): return lax.ppermute(v, axes, [(i, i ^ o) for i in range(n)])  49.3 us
    ppermute x29, waiting for transfers between devices, mate_of(): return lax.ppermute(v, axes, [(i, i ^ o) for i in range(n)])  39.6 us
    pallas_call x8, Pallas kernels, call(): pl.pallas_call(body, out_shape=outs, in_specs=[smem] * scalars + [VMEM] *...  23.6 us
    all_to_all x1, starting transfers between devices, per_device(): lax.all_to_all(points, OWNERS + PLANES, split_axis=0, concat_axis=0, tile...  8.15 us
    ppermute x1, starting transfers between devices, per_device(): tile = lax.ppermute(pack, ('core', 'zl'), [(0, 0), (2, 1), (1, 2), (3, 3)])  4.94 us
    pallas_call x1, Pallas kernels, per_device(): pl.pallas_call(front_body, out_shape=[shape(rows + half, dim), shape(cdev...  2.96 us
  transfers between devices with their start and end apart: 31, of which 22 were waited for; matrix products, arithmetic and copies ran while one was open for 0% of the time, Pallas kernels for 16%

profile of v9, /device:TPU:1, one launch (start us, length us, event | category | flops | bytes accessed | tf_op | source)
XLA Modules:
  0.0 131.7 jit_solution(13153940993975190398)
XLA Ops:
  0.7 3.0 %shard_map.105 = (f32[96,128]{1,0:T(8,128)}, f32[768,128]{1,0:T(8,128)}) custom-call(s32[1,64]{1,0:T(1,128)} %bitcast.17, f32[1024,128]{1,0:T(8,128)} %pool_f.1, f32[64,1024]{1,0:T(8,128)} %bitcast.14, f32[64,512]{1,0:T(8,128)} %bitcast.15, f32[512,128]{1,0:T(8,128)} %centers.1), custom_call_target="tpu_custom_call" | custom-call | tf_op jit(solution)/shard_map/pallas_call | solution.py:355
  3.6 4.9 %collective-permute-start = (f32[768,128]{1,0:T(8,128)}, f32[768,128]{1,0:T(8,128)S(1)}, u32[]{:S(2)}, u32[]{:S(2)}) collective-permute-start(f32[768,128]{1,0:T(8,128)} %get-tuple-element.29), channel_id=1, source_target_pairs={{0,0},{32,1},{1,32},{33,33},{2,2},{34,3},{3,34},{35,35},{4,4},{36,... | collective-permute-start | bytes 1179656 | tf_op jit(solution)/shard_map/ppermute | solution.py:371
  9.9 2.5 %collective-permute-start.2 = (f32[96,128]{1,0:T(8,128)}, f32[96,128]{1,0:T(8,128)S(1)}, u32[]{:S(2)}, u32[]{:S(2)}) collective-permute-start(f32[96,128]{1,0:T(8,128)} %get-tuple-element.31.refs_0_), channel_id=1, source_target_pairs={{0,16},{8,24},{16,0},{24,8},{1,17},{9,25},{17,1},{25,9},{2,18},{10... | collective-permute-start | bytes 147464 | tf_op jit(solution)/shard_map/ppermute | solution.py:331
  12.5 2.0 %collective-permute-done.2.refs_2_ = f32[96,128]{1,0:T(8,128)S(1)} collective-permute-done((f32[96,128]{1,0:T(8,128)}, f32[96,128]{1,0:T(8,128)S(1)}, u32[]{:S(2)}, u32[]{:S(2)}) %collective-permute-start.2) | collective-permute-done | bytes 49184 | tf_op jit(solution)/shard_map/ppermute | solution.py:331
  14.5 2.1 %collective-permute-done.3.refs_3_ = f32[96,128]{1,0:T(8,128)S(1)} collective-permute-done((f32[96,128]{1,0:T(8,128)}, f32[96,128]{1,0:T(8,128)S(1)}, u32[]{:S(2)}, u32[]{:S(2)}) %collective-permute-start.3) | collective-permute-done | bytes 49184 | tf_op jit(solution)/shard_map/ppermute | solution.py:331
  18.0 2.6 %collective-permute-start.6 = (f32[768,128]{1,0:T(8,128)S(1)}, f32[768,128]{1,0:T(8,128)}, u32[]{:S(2)}, u32[]{:S(2)}) collective-permute-start(f32[768,128]{1,0:T(8,128)S(1)} %collective-permute-done.refs_2_), channel_id=1, source_target_pairs={{0,4},{2,6},{4,0},{6,2},{1,5},{3,7},{5,1},{7,3},{8,12},{10,14},{12... | collective-permute-start | bytes 1179656 | tf_op jit(solution)/shard_map/ppermute | solution.py:331
  22.2 1.9 %shard_map.104 = f32[128,24,128]{2,1,0:T(8,128)} custom-call(f32[128,1024]{1,0:T(8,128)S(1)} %copy-done, s32[1,128]{1,0:T(1,128)S(1)} %bitcast.12, s32[1,128]{1,0:T(1,128)S(1)} %bitcast.13), custom_call_target="tpu_custom_call" | custom-call | tf_op jit(solution)/shard_map/pallas_call | solution.py:311
  24.0 4.1 %shard_map.107 = (bf16[1,512,512]{2,1,0:T(8,128)(2,1)S(1)}, bf16[1,512,512]{2,1,0:T(8,128)(2,1)S(1)}, f32[4,32,128]{2,1,0:T(8,128)S(1)}, f32[4,32,128]{2,1,0:T(8...) custom-call(f32[4,96,128]{2,1,0:T(8,128)S(1)} %shard_map.106.refs_0_.own, ...), custom_call_target="tpu_custom_call" | custom-call | flops 100000000 | bytes 65536 | tf_op jit(solution)/shard_map/pallas_call | solution.py:311
  28.7 8.1 %all-to-all-start = ((f32[128,24,128]{2,1,0:T(8,128)}), f32[128,24,128]{2,1,0:T(8,128)S(1)}, u32[]{:S(2)}, u32[]{:S(2)}) async-start(f32[128,24,128]{2,1,0:T(8,128)} %shard_map.104), calls=%async_computation | async-start | bytes 3145728 | tf_op jit(solution)/shard_map/all_to_all | solution.py:406
  36.9 1.6 %collective-permute-done.6.refs_3_ = f32[768,128]{1,0:T(8,128)} collective-permute-done((f32[768,128]{1,0:T(8,128)S(1)}, f32[768,128]{1,0:T(8,128)}, u32[]{:S(2)}, u32[]{:S(2)}) %collective-permute-start.6) | collective-permute-done | bytes 393248 | tf_op jit(solution)/shard_map/ppermute | solution.py:331
  38.5 2.1 %collective-permute-done.7.refs_4_ = f32[768,128]{1,0:T(8,128)} collective-permute-done((f32[768,128]{1,0:T(8,128)S(1)}, f32[768,128]{1,0:T(8,128)}, u32[]{:S(2)}, u32[]{:S(2)}) %collective-permute-start.7) | collective-permute-done | bytes 393248 | tf_op jit(solution)/shard_map/ppermute | solution.py:331
  40.6 13.5 %shard_map.108 = (bf16[3,512,512]{2,1,0:T(8,128)(2,1)S(1)}, bf16[3,512,512]{2,1,0:T(8,128)(2,1)S(1)}, f32[4,32,128]{2,1,0:T(8,128)S(1)}, f32[4,32,128]{2,1,0:T(8,128)S(1)}) custom-call(f32[4,96,128]{2,1,0:T(8,128)S(1)} %shard_map.106.refs_0_.own, f32[4,96,128]{2,1,0:T(8,128)S(1)} %collective-permute-done.4.refs_1_, ...), custom_call_target="tpu_custom_call" | custom-call | flops 30000001024 | bytes 65536 | tf_op jit(solution)/shard_map/pallas_call | solution.py:311
  54.2 10.9 %collective-permute-start.8 = (f32[4,32,128]{2,1,0:T(8,128)S(1)}, f32[4,32,128]{2,1,0:T(8,128)S(1)}, u32[]{:S(2)}, u32[]{:S(2)}) collective-permute-start(f32[4,32,128]{2,1,0:T(8,128)S(1)} %add.70), channel_id=1, source_target_pairs={{0,32},{32,0},{1,33},{33,1},{2,34},{34,2},{3,35},{35,3},{4,36},{36... | collective-permute-start | bytes 196616 | tf_op jit(solution)/shard_map/ppermute | solution.py:331
  66.2 2.5 %collective-permute-start.9 = (f32[4,32,128]{2,1,0:T(8,128)S(1)}, f32[4,32,128]{2,1,0:T(8,128)S(1)}, u32[]{:S(2)}, u32[]{:S(2)}) collective-permute-start(f32[4,32,128]{2,1,0:T(8,128)S(1)} %add_add_fusion.4), channel_id=1, source_target_pairs={{0,8},{8,0},{16,24},{24,16},{1,9},{9,1},{17,25},{25,17},{2,10},{10... | collective-permute-start | bytes 196616 | tf_op jit(solution)/shard_map/ppermute | solution.py:331
  68.7 2.1 %collective-permute-done.10 = f32[4,32,128]{2,1,0:T(8,128)S(1)} collective-permute-done((f32[4,32,128]{2,1,0:T(8,128)S(1)}, f32[4,32,128]{2,1,0:T(8,128)S(1)}, u32[]{:S(2)}, u32[]{:S(2)}) %collective-permute-start.10) | collective-permute-done | bytes 65568 | tf_op jit(solution)/shard_map/ppermute | solution.py:331
  70.8 1.8 %collective-permute-done.11 = f32[4,32,128]{2,1,0:T(8,128)S(1)} collective-permute-done((f32[4,32,128]{2,1,0:T(8,128)S(1)}, f32[4,32,128]{2,1,0:T(8,128)S(1)}, u32[]{:S(2)}, u32[]{:S(2)}) %collective-permute-start.11) | collective-permute-done | bytes 65568 | tf_op jit(solution)/shard_map/ppermute | solution.py:331
  75.9 3.8 %collective-permute-start.15 = (f32[64,512]{1,0:T(8,128)S(1)}, f32[64,512]{1,0:T(8,128)S(1)}, u32[]{:S(2)}, u32[]{:S(2)}) collective-permute-start(f32[64,512]{1,0:T(8,128)S(1)} %get-tuple-element.52), channel_id=1, source_target_pairs={{0,6},{2,4},{4,2},{6,0},{1,7},{3,5},{5,3},{7,1},{8,14},{10,12},{12... | collective-permute-start | bytes 393224 | tf_op jit(solution)/shard_map/ppermute | solution.py:331
  80.5 1.6 %collective-permute-done.14 = f32[64,512]{1,0:T(8,128)S(1)} collective-permute-done((f32[64,512]{1,0:T(8,128)S(1)}, f32[64,512]{1,0:T(8,128)S(1)}, u32[]{:S(2)}, u32[]{:S(2)}) %collective-permute-start.14) | collective-permute-done | bytes 131104 | tf_op jit(solution)/shard_map/ppermute | solution.py:331
  82.1 3.5 %collective-permute-done.15 = f32[64,512]{1,0:T(8,128)S(1)} collective-permute-done((f32[64,512]{1,0:T(8,128)S(1)}, f32[64,512]{1,0:T(8,128)S(1)}, u32[]{:S(2)}, u32[]{:S(2)}) %collective-permute-start.15) | collective-permute-done | bytes 131104 | tf_op jit(solution)/shard_map/ppermute | solution.py:331
  85.8 4.1 %collective-permute-start.17 = (f32[64,512]{1,0:T(8,128)S(1)}, f32[64,512]{1,0:T(8,128)S(1)}, u32[]{:S(2)}, u32[]{:S(2)}) collective-permute-start(f32[64,512]{1,0:T(8,128)S(1)} %add_multiply_fusion), channel_id=1, source_target_pairs={{0,64},{1,65},{64,0},{65,1},{2,66},{3,67},{66,2},{67,3},{4,68},{5,... | collective-permute-start | bytes 393224 | tf_op jit(solution)/shard_map/ppermute | solution.py:331
  90.4 5.8 %collective-permute-done.17 = f32[64,512]{1,0:T(8,128)S(1)} collective-permute-done((f32[64,512]{1,0:T(8,128)S(1)}, f32[64,512]{1,0:T(8,128)S(1)}, u32[]{:S(2)}, u32[]{:S(2)}) %collective-permute-start.17) | collective-permute-done | bytes 131104 | tf_op jit(solution)/shard_map/ppermute | solution.py:331
  96.1 2.6 %collective-permute-done.18 = f32[64,512]{1,0:T(8,128)S(1)} collective-permute-done((f32[64,512]{1,0:T(8,128)S(1)}, f32[64,512]{1,0:T(8,128)S(1)}, u32[]{:S(2)}, u32[]{:S(2)}) %collective-permute-start.18) | collective-permute-done | bytes 131104 | tf_op jit(solution)/shard_map/ppermute | solution.py:331
  98.8 1.5 %shard_map.111 = f32[64,256]{1,0:T(8,128)S(1)} custom-call(f32[128,24,128]{2,1,0:T(8,128)S(1)} %all-to-all-done.points, f32[64,512]{1,0:T(8,128)S(1)} %add_add_fusion.grads), custom_call_target="tpu_custom_call" | custom-call | tf_op jit(solution)/shard_map/pallas_call | solution.py:311
  102.2 3.5 %collective-permute-start.21 = (f32[64,256]{1,0:T(8,128)S(1)}, f32[64,256]{1,0:T(8,128)S(1)}, u32[]{:S(2)}, u32[]{:S(2)}) collective-permute-start(f32[64,256]{1,0:T(8,128)S(1)} %add.82), channel_id=1, source_target_pairs={{0,4},{2,6},{4,0},{6,2},{1,5},{3,7},{5,1},{7,3},{8,12},{10,14},{12... | collective-permute-start | bytes 196616 | tf_op jit(solution)/shard_map/ppermute | solution.py:331
  106.0 2.6 %collective-permute-done.21 = f32[64,256]{1,0:T(8,128)S(1)} collective-permute-done((f32[64,256]{1,0:T(8,128)S(1)}, f32[64,256]{1,0:T(8,128)S(1)}, u32[]{:S(2)}, u32[]{:S(2)}) %collective-permute-start.21) | collective-permute-done | bytes 65568 | tf_op jit(solution)/shard_map/ppermute | solution.py:331
  108.7 1.5 %collective-permute-done.22 = f32[64,256]{1,0:T(8,128)S(1)} collective-permute-done((f32[64,256]{1,0:T(8,128)S(1)}, f32[64,256]{1,0:T(8,128)S(1)}, u32[]{:S(2)}, u32[]{:S(2)}) %collective-permute-start.22) | collective-permute-done | bytes 65568 | tf_op jit(solution)/shard_map/ppermute | solution.py:331
  112.0 2.1 %collective-permute-start.25 = (f32[64,256]{1,0:T(8,128)S(1)}, f32[64,256]{1,0:T(8,128)S(1)}, u32[]{:S(2)}, u32[]{:S(2)}) collective-permute-start(f32[64,256]{1,0:T(8,128)S(1)} %add_add_fusion.2), channel_id=1, source_target_pairs={{0,24},{8,16},{16,8},{24,0},{1,25},{9,17},{17,9},{25,1},{2,26},{10... | collective-permute-start | bytes 196616 | tf_op jit(solution)/shard_map/ppermute | solution.py:331
  114.1 1.5 %collective-permute-done.24 = f32[64,256]{1,0:T(8,128)S(1)} collective-permute-done((f32[64,256]{1,0:T(8,128)S(1)}, f32[64,256]{1,0:T(8,128)S(1)}, u32[]{:S(2)}, u32[]{:S(2)}) %collective-permute-start.24) | collective-permute-done | bytes 65568 | tf_op jit(solution)/shard_map/ppermute | solution.py:331
  117.7 1.9 %collective-permute-start.27 = (f32[64,512]{1,0:T(8,128)S(1)}, f32[64,512]{1,0:T(8,128)S(1)}, u32[]{:S(2)}, u32[]{:S(2)}) collective-permute-start(f32[64,512]{1,0:T(8,128)S(1)} %shard_map.112), channel_id=1, source_target_pairs={{0,64},{1,65},{64,0},{65,1},{2,66},{3,67},{66,2},{67,3},{4,68},{5,... | collective-permute-start | bytes 393224 | tf_op jit(solution)/shard_map/ppermute | solution.py:331
  119.5 1.9 %collective-permute-start.28 = (f32[64,512]{1,0:T(8,128)S(1)}, f32[64,512]{1,0:T(8,128)S(1)}, u32[]{:S(2)}, u32[]{:S(2)}) collective-permute-start(f32[64,512]{1,0:T(8,128)S(1)} %shard_map.112), channel_id=1, source_target_pairs={{0,65},{1,64},{64,1},{65,0},{2,67},{3,66},{66,3},{67,2},{4,69},{5,... | collective-permute-start | bytes 393224 | tf_op jit(solution)/shard_map/ppermute | solution.py:331
  121.4 1.9 %collective-permute-done.27 = f32[64,512]{1,0:T(8,128)S(1)} collective-permute-done((f32[64,512]{1,0:T(8,128)S(1)}, f32[64,512]{1,0:T(8,128)S(1)}, u32[]{:S(2)}, u32[]{:S(2)}) %collective-permute-start.27) | collective-permute-done | bytes 131104 | tf_op jit(solution)/shard_map/ppermute | solution.py:331
  124.7 5.3 %collective-permute-start.29 = (f32[64,512]{1,0:T(8,128)S(1)}, f32[64,512]{1,0:T(8,128)S(1)}, u32[]{:S(2)}, u32[]{:S(2)}) collective-permute-start(f32[64,512]{1,0:T(8,128)S(1)} %add_subtract_fusion), channel_id=1, source_target_pairs={{0,32},{32,0},{1,33},{33,1},{2,34},{34,2},{3,35},{35,3},{4,36},{36... | collective-permute-start | bytes 393224 | tf_op jit(solution)/shard_map/ppermute | solution.py:331
  (64 shorter events, 20.0 us)
Async XLA Ops:
  3.6 13.0 %collective-permute-start = (f32[768,128]{1,0:T(8,128)}, f32[768,128]{1,0:T(8,128)S(1)}, u32[]{:S(2)}, u32[]{:S(2)}) collective-permute-start(f32[768,128]{1,0:T(8,128)} %get-tuple-element.29), channel_id=1, source_target_pairs={{0,0},{32,1},{1,32},{33,33},{2,2},{34,3},{3,34},{35,35},{4,4},{36,... | collective-permute-start | bytes 1179656 | tf_op jit(solution)/shard_map/ppermute | solution.py:371
  8.6 3.9 %collective-permute-start.1 = (f32[96,128]{1,0:T(8,128)}, f32[96,128]{1,0:T(8,128)S(1)}, u32[]{:S(2)}, u32[]{:S(2)}) collective-permute-start(f32[96,128]{1,0:T(8,128)} %get-tuple-element.31.refs_0_), channel_id=1, source_target_pairs={{0,8},{8,0},{16,24},{24,16},{1,9},{9,1},{17,25},{25,17},{2,10},{10... | collective-permute-start | bytes 147464 | tf_op jit(solution)/shard_map/ppermute | solution.py:331
  9.9 4.7 %collective-permute-start.2 = (f32[96,128]{1,0:T(8,128)}, f32[96,128]{1,0:T(8,128)S(1)}, u32[]{:S(2)}, u32[]{:S(2)}) collective-permute-start(f32[96,128]{1,0:T(8,128)} %get-tuple-element.31.refs_0_), channel_id=1, source_target_pairs={{0,16},{8,24},{16,0},{24,8},{1,17},{9,25},{17,1},{25,9},{2,18},{10... | collective-permute-start | bytes 147464 | tf_op jit(solution)/shard_map/ppermute | solution.py:331
  12.3 4.4 %collective-permute-start.3 = (f32[96,128]{1,0:T(8,128)}, f32[96,128]{1,0:T(8,128)S(1)}, u32[]{:S(2)}, u32[]{:S(2)}) collective-permute-start(f32[96,128]{1,0:T(8,128)} %get-tuple-element.31.refs_0_), channel_id=1, source_target_pairs={{0,24},{8,16},{16,8},{24,0},{1,25},{9,17},{17,9},{25,1},{2,26},{10... | collective-permute-start | bytes 147464 | tf_op jit(solution)/shard_map/ppermute | solution.py:331
  16.7 20.2 %collective-permute-start.5 = (f32[768,128]{1,0:T(8,128)S(1)}, f32[768,128]{1,0:T(8,128)}, u32[]{:S(2)}, u32[]{:S(2)}) collective-permute-start(f32[768,128]{1,0:T(8,128)S(1)} %collective-permute-done.refs_2_), channel_id=1, source_target_pairs={{0,2},{2,0},{4,6},{6,4},{1,3},{3,1},{5,7},{7,5},{8,10},{10,8},{12,... | collective-permute-start | bytes 1179656 | tf_op jit(solution)/shard_map/ppermute | solution.py:331
  18.0 20.6 %collective-permute-start.6 = (f32[768,128]{1,0:T(8,128)S(1)}, f32[768,128]{1,0:T(8,128)}, u32[]{:S(2)}, u32[]{:S(2)}) collective-permute-start(f32[768,128]{1,0:T(8,128)S(1)} %collective-permute-done.refs_2_), channel_id=1, source_target_pairs={{0,4},{2,6},{4,0},{6,2},{1,5},{3,7},{5,1},{7,3},{8,12},{10,14},{12... | collective-permute-start | bytes 1179656 | tf_op jit(solution)/shard_map/ppermute | solution.py:331
  20.6 20.0 %collective-permute-start.7 = (f32[768,128]{1,0:T(8,128)S(1)}, f32[768,128]{1,0:T(8,128)}, u32[]{:S(2)}, u32[]{:S(2)}) collective-permute-start(f32[768,128]{1,0:T(8,128)S(1)} %collective-permute-done.refs_2_), channel_id=1, source_target_pairs={{0,6},{2,4},{4,2},{6,0},{1,7},{3,5},{5,3},{7,1},{8,14},{10,12},{12... | collective-permute-start | bytes 1179656 | tf_op jit(solution)/shard_map/ppermute | solution.py:331
  21.4 2.6 %collective-permute-start.4 = (f32[4,96,128]{2,1,0:T(8,128)S(1)}, f32[4,96,128]{2,1,0:T(8,128)S(1)}, u32[]{:S(2)}, u32[]{:S(2)}) collective-permute-start(f32[4,96,128]{2,1,0:T(8,128)S(1)} %shard_map.106.refs_0_.own), channel_id=1, source_target_pairs={{0,32},{32,0},{1,33},{33,1},{2,34},{34,2},{3,35},{35,3},{4,36},{36... | collective-permute-start | bytes 589832 | tf_op jit(solution)/shard_map/ppermute | solution.py:331
  28.7 57.0 %all-to-all-start = ((f32[128,24,128]{2,1,0:T(8,128)}), f32[128,24,128]{2,1,0:T(8,128)S(1)}, u32[]{:S(2)}, u32[]{:S(2)}) async-start(f32[128,24,128]{2,1,0:T(8,128)} %shard_map.104), calls=%async_computation | async-start | bytes 3145728 | tf_op jit(solution)/shard_map/all_to_all | solution.py:406
  54.2 11.8 %collective-permute-start.8 = (f32[4,32,128]{2,1,0:T(8,128)S(1)}, f32[4,32,128]{2,1,0:T(8,128)S(1)}, u32[]{:S(2)}, u32[]{:S(2)}) collective-permute-start(f32[4,32,128]{2,1,0:T(8,128)S(1)} %add.70), channel_id=1, source_target_pairs={{0,32},{32,0},{1,33},{33,1},{2,34},{34,2},{3,35},{35,3},{4,36},{36... | collective-permute-start | bytes 196616 | tf_op jit(solution)/shard_map/ppermute | solution.py:331
  66.0 4.8 %collective-permute-start.10 = (f32[4,32,128]{2,1,0:T(8,128)S(1)}, f32[4,32,128]{2,1,0:T(8,128)S(1)}, u32[]{:S(2)}, u32[]{:S(2)}) collective-permute-start(f32[4,32,128]{2,1,0:T(8,128)S(1)} %add_add_fusion.4), channel_id=1, source_target_pairs={{0,16},{8,24},{16,0},{24,8},{1,17},{9,25},{17,1},{25,9},{2,18},{10... | collective-permute-start | bytes 196616 | tf_op jit(solution)/shard_map/ppermute | solution.py:331
  66.1 6.5 %collective-permute-start.11 = (f32[4,32,128]{2,1,0:T(8,128)S(1)}, f32[4,32,128]{2,1,0:T(8,128)S(1)}, u32[]{:S(2)}, u32[]{:S(2)}) collective-permute-start(f32[4,32,128]{2,1,0:T(8,128)S(1)} %add_add_fusion.4), channel_id=1, source_target_pairs={{0,24},{8,16},{16,8},{24,0},{1,25},{9,17},{17,9},{25,1},{2,26},{10... | collective-permute-start | bytes 196616 | tf_op jit(solution)/shard_map/ppermute | solution.py:331
  66.2 6.4 %collective-permute-start.9 = (f32[4,32,128]{2,1,0:T(8,128)S(1)}, f32[4,32,128]{2,1,0:T(8,128)S(1)}, u32[]{:S(2)}, u32[]{:S(2)}) collective-permute-start(f32[4,32,128]{2,1,0:T(8,128)S(1)} %add_add_fusion.4), channel_id=1, source_target_pairs={{0,8},{8,0},{16,24},{24,16},{1,9},{9,1},{17,25},{25,17},{2,10},{10... | collective-permute-start | bytes 196616 | tf_op jit(solution)/shard_map/ppermute | solution.py:331
  73.3 1.6 %collective-permute-start.12 = (f32[4,32,128]{2,1,0:T(8,128)S(1)}, f32[4,32,128]{2,1,0:T(8,128)S(1)}, u32[]{:S(2)}, u32[]{:S(2)}) collective-permute-start(f32[4,32,128]{2,1,0:T(8,128)S(1)} %get-tuple-element.44.own), channel_id=1, source_target_pairs={{0,32},{32,0},{1,33},{33,1},{2,34},{34,2},{3,35},{35,3},{4,36},{36... | collective-permute-start | bytes 196616 | tf_op jit(solution)/shard_map/ppermute | solution.py:331
  75.7 4.8 %collective-permute-start.13 = (f32[64,512]{1,0:T(8,128)S(1)}, f32[64,512]{1,0:T(8,128)S(1)}, u32[]{:S(2)}, u32[]{:S(2)}) collective-permute-start(f32[64,512]{1,0:T(8,128)S(1)} %get-tuple-element.50), channel_id=1, source_target_pairs={{0,2},{2,0},{4,6},{6,4},{1,3},{3,1},{5,7},{7,5},{8,10},{10,8},{12,... | collective-permute-start | bytes 393224 | tf_op jit(solution)/shard_map/ppermute | solution.py:331
  75.8 6.3 %collective-permute-start.14 = (f32[64,512]{1,0:T(8,128)S(1)}, f32[64,512]{1,0:T(8,128)S(1)}, u32[]{:S(2)}, u32[]{:S(2)}) collective-permute-start(f32[64,512]{1,0:T(8,128)S(1)} %get-tuple-element.51), channel_id=1, source_target_pairs={{0,4},{2,6},{4,0},{6,2},{1,5},{3,7},{5,1},{7,3},{8,12},{10,14},{12... | collective-permute-start | bytes 393224 | tf_op jit(solution)/shard_map/ppermute | solution.py:331
  75.9 9.7 %collective-permute-start.15 = (f32[64,512]{1,0:T(8,128)S(1)}, f32[64,512]{1,0:T(8,128)S(1)}, u32[]{:S(2)}, u32[]{:S(2)}) collective-permute-start(f32[64,512]{1,0:T(8,128)S(1)} %get-tuple-element.52), channel_id=1, source_target_pairs={{0,6},{2,4},{4,2},{6,0},{1,7},{3,5},{5,3},{7,1},{8,14},{10,12},{12... | collective-permute-start | bytes 393224 | tf_op jit(solution)/shard_map/ppermute | solution.py:331
  85.7 30.7 %copy-start.4 = (f32[1024]{0:T(1024)S(1)}, f32[1024]{0:T(1024)}, u32[]{:S(2)}) copy-start(f32[1024]{0:T(1024)} %param.15) | copy-start | bytes 12292
  85.7 4.7 %collective-permute-start.16 = (f32[64,512]{1,0:T(8,128)S(1)}, f32[64,512]{1,0:T(8,128)S(1)}, u32[]{:S(2)}, u32[]{:S(2)}) collective-permute-start(f32[64,512]{1,0:T(8,128)S(1)} %add_multiply_fusion), channel_id=1, source_target_pairs={{0,1},{1,0},{64,65},{65,64},{2,3},{3,2},{66,67},{67,66},{4,5},{5,4... | collective-permute-start | bytes 393224 | tf_op jit(solution)/shard_map/ppermute | solution.py:331
  85.8 10.3 %collective-permute-start.17 = (f32[64,512]{1,0:T(8,128)S(1)}, f32[64,512]{1,0:T(8,128)S(1)}, u32[]{:S(2)}, u32[]{:S(2)}) collective-permute-start(f32[64,512]{1,0:T(8,128)S(1)} %add_multiply_fusion), channel_id=1, source_target_pairs={{0,64},{1,65},{64,0},{65,1},{2,66},{3,67},{66,2},{67,3},{4,68},{5,... | collective-permute-start | bytes 393224 | tf_op jit(solution)/shard_map/ppermute | solution.py:331
  89.9 8.8 %collective-permute-start.18 = (f32[64,512]{1,0:T(8,128)S(1)}, f32[64,512]{1,0:T(8,128)S(1)}, u32[]{:S(2)}, u32[]{:S(2)}) collective-permute-start(f32[64,512]{1,0:T(8,128)S(1)} %add_multiply_fusion), channel_id=1, source_target_pairs={{0,65},{1,64},{64,1},{65,0},{2,67},{3,66},{66,3},{67,2},{4,69},{5,... | collective-permute-start | bytes 393224 | tf_op jit(solution)/shard_map/ppermute | solution.py:331
  100.2 1.8 %collective-permute-start.19 = (f32[64,256]{1,0:T(8,128)S(1)}, f32[64,256]{1,0:T(8,128)S(1)}, u32[]{:S(2)}, u32[]{:S(2)}) collective-permute-start(f32[64,256]{1,0:T(8,128)S(1)} %shard_map.111), channel_id=1, source_target_pairs={{0,32},{32,0},{1,33},{33,1},{2,34},{34,2},{3,35},{35,3},{4,36},{36... | collective-permute-start | bytes 196616 | tf_op jit(solution)/shard_map/ppermute | solution.py:331
  102.1 3.9 %collective-permute-start.20 = (f32[64,256]{1,0:T(8,128)S(1)}, f32[64,256]{1,0:T(8,128)S(1)}, u32[]{:S(2)}, u32[]{:S(2)}) collective-permute-start(f32[64,256]{1,0:T(8,128)S(1)} %add.82), channel_id=1, source_target_pairs={{0,2},{2,0},{4,6},{6,4},{1,3},{3,1},{5,7},{7,5},{8,10},{10,8},{12,... | collective-permute-start | bytes 196616 | tf_op jit(solution)/shard_map/ppermute | solution.py:331
  102.2 6.5 %collective-permute-start.21 = (f32[64,256]{1,0:T(8,128)S(1)}, f32[64,256]{1,0:T(8,128)S(1)}, u32[]{:S(2)}, u32[]{:S(2)}) collective-permute-start(f32[64,256]{1,0:T(8,128)S(1)} %add.82), channel_id=1, source_target_pairs={{0,4},{2,6},{4,0},{6,2},{1,5},{3,7},{5,1},{7,3},{8,12},{10,14},{12... | collective-permute-start | bytes 196616 | tf_op jit(solution)/shard_map/ppermute | solution.py:331
  105.7 4.5 %collective-permute-start.22 = (f32[64,256]{1,0:T(8,128)S(1)}, f32[64,256]{1,0:T(8,128)S(1)}, u32[]{:S(2)}, u32[]{:S(2)}) collective-permute-start(f32[64,256]{1,0:T(8,128)S(1)} %add.82), channel_id=1, source_target_pairs={{0,6},{2,4},{4,2},{6,0},{1,7},{3,5},{5,3},{7,1},{8,14},{10,12},{12... | collective-permute-start | bytes 196616 | tf_op jit(solution)/shard_map/ppermute | solution.py:331
  110.2 3.9 %collective-permute-start.23 = (f32[64,256]{1,0:T(8,128)S(1)}, f32[64,256]{1,0:T(8,128)S(1)}, u32[]{:S(2)}, u32[]{:S(2)}) collective-permute-start(f32[64,256]{1,0:T(8,128)S(1)} %add_add_fusion.2), channel_id=1, source_target_pairs={{0,8},{8,0},{16,24},{24,16},{1,9},{9,1},{17,25},{25,17},{2,10},{10... | collective-permute-start | bytes 196616 | tf_op jit(solution)/shard_map/ppermute | solution.py:331
  110.9 4.8 %collective-permute-start.24 = (f32[64,256]{1,0:T(8,128)S(1)}, f32[64,256]{1,0:T(8,128)S(1)}, u32[]{:S(2)}, u32[]{:S(2)}) collective-permute-start(f32[64,256]{1,0:T(8,128)S(1)} %add_add_fusion.2), channel_id=1, source_target_pairs={{0,16},{8,24},{16,0},{24,8},{1,17},{9,25},{17,1},{25,9},{2,18},{10... | collective-permute-start | bytes 196616 | tf_op jit(solution)/shard_map/ppermute | solution.py:331
  112.0 4.3 %collective-permute-start.25 = (f32[64,256]{1,0:T(8,128)S(1)}, f32[64,256]{1,0:T(8,128)S(1)}, u32[]{:S(2)}, u32[]{:S(2)}) collective-permute-start(f32[64,256]{1,0:T(8,128)S(1)} %add_add_fusion.2), channel_id=1, source_target_pairs={{0,24},{8,16},{16,8},{24,0},{1,25},{9,17},{17,9},{25,1},{2,26},{10... | collective-permute-start | bytes 196616 | tf_op jit(solution)/shard_map/ppermute | solution.py:331
  117.5 3.9 %collective-permute-start.26 = (f32[64,512]{1,0:T(8,128)S(1)}, f32[64,512]{1,0:T(8,128)S(1)}, u32[]{:S(2)}, u32[]{:S(2)}) collective-permute-start(f32[64,512]{1,0:T(8,128)S(1)} %shard_map.112), channel_id=1, source_target_pairs={{0,1},{1,0},{64,65},{65,64},{2,3},{3,2},{66,67},{67,66},{4,5},{5,4... | collective-permute-start | bytes 393224 | tf_op jit(solution)/shard_map/ppermute | solution.py:331
  117.7 5.6 %collective-permute-start.27 = (f32[64,512]{1,0:T(8,128)S(1)}, f32[64,512]{1,0:T(8,128)S(1)}, u32[]{:S(2)}, u32[]{:S(2)}) collective-permute-start(f32[64,512]{1,0:T(8,128)S(1)} %shard_map.112), channel_id=1, source_target_pairs={{0,64},{1,65},{64,0},{65,1},{2,66},{3,67},{66,2},{67,3},{4,68},{5,... | collective-permute-start | bytes 393224 | tf_op jit(solution)/shard_map/ppermute | solution.py:331
  119.5 5.2 %collective-permute-start.28 = (f32[64,512]{1,0:T(8,128)S(1)}, f32[64,512]{1,0:T(8,128)S(1)}, u32[]{:S(2)}, u32[]{:S(2)}) collective-permute-start(f32[64,512]{1,0:T(8,128)S(1)} %shard_map.112), channel_id=1, source_target_pairs={{0,65},{1,64},{64,1},{65,0},{2,67},{3,66},{66,3},{67,2},{4,69},{5,... | collective-permute-start | bytes 393224 | tf_op jit(solution)/shard_map/ppermute | solution.py:331
  124.7 6.3 %collective-permute-start.29 = (f32[64,512]{1,0:T(8,128)S(1)}, f32[64,512]{1,0:T(8,128)S(1)}, u32[]{:S(2)}, u32[]{:S(2)}) collective-permute-start(f32[64,512]{1,0:T(8,128)S(1)} %add_subtract_fusion), channel_id=1, source_target_pairs={{0,32},{32,0},{1,33},{33,1},{2,34},{34,2},{3,35},{35,3},{4,36},{36... | collective-permute-start | bytes 393224 | tf_op jit(solution)/shard_map/ppermute | solution.py:331
  (6 other events, 95.1 us)

commit v10 on v7

--- a/solution.py
+++ b/solution.py
@@ -394,10 +394,16 @@
             pltpu.VMEM((1, count), jnp.int32),
             pltpu.SemaphoreType.DMA((8,)),
         ],
-        compiler_params=params(60),
+        compiler_params=params(16),
     )(
-        member, batch_index.reshape(1, rows), pool_features, pool_targets.T, weights.T, centers,
-        eig_vectors, nys_owner.reshape(1, count), nys_offset.reshape(1, count),
+        member,
+        *(
+            pltpu.with_memory_space_constraint(v, pltpu.HBM)
+            for v in (
+                batch_index.reshape(1, rows), pool_features, pool_targets.T, weights.T, centers,
+                eig_vectors, nys_owner.reshape(1, count), nys_offset.reshape(1, count),
+            )
+        ),
     )
 
     gathered = mates([drawn] * nx, ("x",))

time: 127 us -> 124 us (0.976)
  local copies, waits for them, and re-layouts: 1.71 us -> 0.01 us
    unnamed x6 -> x2, local copies, waits for them, and re-layouts: 1.71 us -> 0.01 us
where the time goes in v10:
time: 124 us; the launch traced here: 123 us
  starting transfers between devices  56.4 us (45%)
  waiting for transfers between devices  39.4 us (32%)
  Pallas kernels  25.8 us (21%)
    ppermute x32, starting transfers between devices, mate_of(): return lax.ppermute(v, axes, [(i, i ^ o) for i in range(n)])  45.4 us
    ppermute x32, waiting for transfers between devices, mate_of(): return lax.ppermute(v, axes, [(i, i ^ o) for i in range(n)])  39.4 us
    pallas_call x8, Pallas kernels, call(): pl.pallas_call(body, out_shape=outs, in_specs=[smem] * scalars + [VMEM] *...  23.5 us
    all_to_all x1, starting transfers between devices, per_device(): lax.all_to_all(points, OWNERS, split_axis=0, concat_axis=0, tiled=True)  6.04 us
    ppermute x1, starting transfers between devices, per_device(): tile = lax.ppermute(pack, ('core', 'zl'), [(0, 0), (2, 1), (1, 2), (3, 3)])  4.93 us
  transfers between devices with their start and end apart: 34, of which 22 were waited for; matrix products, arithmetic and copies ran while one was open for 0% of the time, Pallas kernels for 17%

profile of v10, /device:TPU:1, one launch (start us, length us, event | category | flops | bytes accessed | tf_op | source)
XLA Modules:
  0.0 123.2 jit_solution(5829757687554364025)
XLA Ops:
  0.6 2.2 %shard_map.104 = (f32[96,128]{1,0:T(8,128)S(1)}, f32[768,128]{1,0:T(8,128)S(1)}, f32[136,256]{1,0:T(8,128)S(1)}, f32[136,256]{1,0:T(8,128)S(1)}, f32[136,256]{1,0:T(8,128)S(1)}, /*index=5*/f32[136,256]{1,0:T(8,128)S(1)}) custom-call(s32[1]{0:T(128)} %bitcast.1.member, s32[1,64]{1,0:T(1,128)} %bitcast.15, f32[1024,128]{1,0:T(8,128)} %refs_1_.1, ...), custom_call_target="tpu_custom_call" | custom-call | tf_op jit(solution)/shard_map/pallas_call | solution.py:381
  2.9 4.9 %collective-permute-start = (f32[768,128]{1,0:T(8,128)S(1)}, f32[768,128]{1,0:T(8,128)S(1)}, u32[]{:S(2)}, u32[]{:S(2)}) collective-permute-start(f32[768,128]{1,0:T(8,128)S(1)} %get-tuple-element.40), channel_id=1, source_target_pairs={{0,0},{32,1},{1,32},{33,33},{2,2},{34,3},{3,34},{35,35},{4,4},{36,... | collective-permute-start | bytes 1179656 | tf_op jit(solution)/shard_map/ppermute | solution.py:410
  7.8 3.4 %collective-permute-start.1 = (f32[136,256]{1,0:T(8,128)S(1)}, f32[136,256]{1,0:T(8,128)S(1)}, u32[]{:S(2)}, u32[]{:S(2)}) collective-permute-start(f32[136,256]{1,0:T(8,128)S(1)} %get-tuple-element.41), channel_id=1, source_target_pairs={{0,64},{1,65},{64,0},{65,1},{2,66},{3,67},{66,2},{67,3},{4,68},{5,... | collective-permute-start | bytes 417800 | tf_op jit(solution)/shard_map/ppermute | solution.py:357
  12.4 2.5 %collective-permute-start.3 = (f32[96,128]{1,0:T(8,128)S(1)}, f32[96,128]{1,0:T(8,128)S(1)}, u32[]{:S(2)}, u32[]{:S(2)}) collective-permute-start(f32[96,128]{1,0:T(8,128)S(1)} %get-tuple-element.43.refs_0_), channel_id=1, source_target_pairs={{0,16},{8,24},{16,0},{24,8},{1,17},{9,25},{17,1},{25,9},{2,18},{10... | collective-permute-start | bytes 147464 | tf_op jit(solution)/shard_map/ppermute | solution.py:357
  15.1 1.8 %collective-permute-done.3.refs_2_ = f32[96,128]{1,0:T(8,128)S(1)} collective-permute-done((f32[96,128]{1,0:T(8,128)S(1)}, f32[96,128]{1,0:T(8,128)S(1)}, u32[]{:S(2)}, u32[]{:S(2)}) %collective-permute-start.3) | collective-permute-done | bytes 49184 | tf_op jit(solution)/shard_map/ppermute | solution.py:357
  16.9 2.1 %collective-permute-done.4.refs_3_ = f32[96,128]{1,0:T(8,128)S(1)} collective-permute-done((f32[96,128]{1,0:T(8,128)S(1)}, f32[96,128]{1,0:T(8,128)S(1)}, u32[]{:S(2)}, u32[]{:S(2)}) %collective-permute-start.4) | collective-permute-done | bytes 49184 | tf_op jit(solution)/shard_map/ppermute | solution.py:357
  19.0 2.7 %collective-permute-start.10 = (f32[768,128]{1,0:T(8,128)S(1)}, f32[768,128]{1,0:T(8,128)}, u32[]{:S(2)}, u32[]{:S(2)}) collective-permute-start(f32[768,128]{1,0:T(8,128)S(1)} %collective-permute-done.refs_2_), channel_id=1, source_target_pairs={{0,6},{2,4},{4,2},{6,0},{1,7},{3,5},{5,3},{7,1},{8,14},{10,12},{12... | collective-permute-start | bytes 1179656 | tf_op jit(solution)/shard_map/ppermute | solution.py:357
  24.6 1.8 %collective-permute-start.6 = (f32[136,256]{1,0:T(8,128)S(1)}, f32[136,256]{1,0:T(8,128)S(1)}, u32[]{:S(2)}, u32[]{:S(2)}) collective-permute-start(f32[136,256]{1,0:T(8,128)S(1)} %get-tuple-element.54), channel_id=1, source_target_pairs={{0,1},{1,0},{64,65},{65,64},{2,3},{3,2},{66,67},{67,66},{4,5},{5,4... | collective-permute-start | bytes 417800 | tf_op jit(solution)/shard_map/ppermute | solution.py:357
  26.4 4.1 %shard_map.106 = (bf16[1,512,512]{2,1,0:T(8,128)(2,1)S(1)}, bf16[1,512,512]{2,1,0:T(8,128)(2,1)S(1)}, f32[4,32,128]{2,1,0:T(8,128)S(1)}, f32[4,32,128]{2,1,0:T(8...) custom-call(f32[4,96,128]{2,1,0:T(8,128)S(1)} %shard_map.105.refs_0_.own, ...), custom_call_target="tpu_custom_call" | custom-call | flops 100000000 | bytes 65536 | tf_op jit(solution)/shard_map/pallas_call | solution.py:337
  30.5 1.7 %collective-permute-done.7.refs_3_ = f32[136,256]{1,0:T(8,128)S(1)} collective-permute-done((f32[136,256]{1,0:T(8,128)S(1)}, f32[136,256]{1,0:T(8,128)S(1)}, u32[]{:S(2)}, u32[]{:S(2)}) %collective-permute-start.7) | collective-permute-done | bytes 139296 | tf_op jit(solution)/shard_map/ppermute | solution.py:357
  32.2 1.7 %shard_map.109 = f32[32,72,128]{2,1,0:T(8,128)} custom-call(f32[136,256]{1,0:T(8,128)S(1)} %get-tuple-element.62.refs_0_, f32[136,256]{1,0:T(8,128)S(1)} %collective-permute-done.1.refs_1_, f32[136,256]{1,0:T(8,128)S(1)} %collective-permute-done.6.refs_2_, f32[136,256]{1,0:T(8,128)S(1)} %collective-permute-done.7.refs_3_), custom_call_target="tpu_custom_call" | custom-call | tf_op jit(solution)/shard_map/pallas_call | solution.py:337
  33.9 6.0 %all-to-all-start = ((f32[32,72,128]{2,1,0:T(8,128)}), f32[32,72,128]{2,1,0:T(8,128)S(1)}, u32[]{:S(2)}, u32[]{:S(2)}) async-start(f32[32,72,128]{2,1,0:T(8,128)} %shard_map.109), calls=%async_computation | async-start | bytes 2359296 | tf_op jit(solution)/shard_map/all_to_all | solution.py:448
  41.1 13.5 %shard_map.107 = (bf16[3,512,512]{2,1,0:T(8,128)(2,1)S(1)}, bf16[3,512,512]{2,1,0:T(8,128)(2,1)S(1)}, f32[4,32,128]{2,1,0:T(8,128)S(1)}, f32[4,32,128]{2,1,0:T(8,128)S(1)}) custom-call(f32[4,96,128]{2,1,0:T(8,128)S(1)} %shard_map.105.refs_0_.own, f32[4,96,128]{2,1,0:T(8,128)S(1)} %collective-permute-done.5.refs_1_, ...), custom_call_target="tpu_custom_call" | custom-call | flops 30000001024 | bytes 65536 | tf_op jit(solution)/shard_map/pallas_call | solution.py:337
  56.4 2.4 %collective-permute-start.13 = (f32[4,32,128]{2,1,0:T(8,128)S(1)}, f32[4,32,128]{2,1,0:T(8,128)S(1)}, u32[]{:S(2)}, u32[]{:S(2)}) collective-permute-start(f32[4,32,128]{2,1,0:T(8,128)S(1)} %add_add_fusion.4), channel_id=1, source_target_pairs={{0,16},{8,24},{16,0},{24,8},{1,17},{9,25},{17,1},{25,9},{2,18},{10... | collective-permute-start | bytes 196616 | tf_op jit(solution)/shard_map/ppermute | solution.py:357
  60.1 1.7 %collective-permute-done.13 = f32[4,32,128]{2,1,0:T(8,128)S(1)} collective-permute-done((f32[4,32,128]{2,1,0:T(8,128)S(1)}, f32[4,32,128]{2,1,0:T(8,128)S(1)}, u32[]{:S(2)}, u32[]{:S(2)}) %collective-permute-start.13) | collective-permute-done | bytes 65568 | tf_op jit(solution)/shard_map/ppermute | solution.py:357
  61.8 1.5 %collective-permute-done.14 = f32[4,32,128]{2,1,0:T(8,128)S(1)} collective-permute-done((f32[4,32,128]{2,1,0:T(8,128)S(1)}, f32[4,32,128]{2,1,0:T(8,128)S(1)}, u32[]{:S(2)}, u32[]{:S(2)}) %collective-permute-start.14) | collective-permute-done | bytes 65568 | tf_op jit(solution)/shard_map/ppermute | solution.py:357
  64.0 1.9 %collective-permute-start.15 = (f32[4,32,128]{2,1,0:T(8,128)S(1)}, f32[4,32,128]{2,1,0:T(8,128)S(1)}, u32[]{:S(2)}, u32[]{:S(2)}) collective-permute-start(f32[4,32,128]{2,1,0:T(8,128)S(1)} %get-tuple-element.66.own), channel_id=1, source_target_pairs={{0,32},{32,0},{1,33},{33,1},{2,34},{34,2},{3,35},{35,3},{4,36},{36... | collective-permute-start | bytes 196616 | tf_op jit(solution)/shard_map/ppermute | solution.py:357
  68.9 2.4 %collective-permute-start.17 = (f32[64,512]{1,0:T(8,128)S(1)}, f32[64,512]{1,0:T(8,128)S(1)}, u32[]{:S(2)}, u32[]{:S(2)}) collective-permute-start(f32[64,512]{1,0:T(8,128)S(1)} %get-tuple-element.73), channel_id=1, source_target_pairs={{0,4},{2,6},{4,0},{6,2},{1,5},{3,7},{5,1},{7,3},{8,12},{10,14},{12... | collective-permute-start | bytes 393224 | tf_op jit(solution)/shard_map/ppermute | solution.py:357
  72.5 5.0 %collective-permute-done.17 = f32[64,512]{1,0:T(8,128)S(1)} collective-permute-done((f32[64,512]{1,0:T(8,128)S(1)}, f32[64,512]{1,0:T(8,128)S(1)}, u32[]{:S(2)}, u32[]{:S(2)}) %collective-permute-start.17) | collective-permute-done | bytes 131104 | tf_op jit(solution)/shard_map/ppermute | solution.py:357
  77.5 2.5 %collective-permute-done.18 = f32[64,512]{1,0:T(8,128)S(1)} collective-permute-done((f32[64,512]{1,0:T(8,128)S(1)}, f32[64,512]{1,0:T(8,128)S(1)}, u32[]{:S(2)}, u32[]{:S(2)}) %collective-permute-start.18) | collective-permute-done | bytes 131104 | tf_op jit(solution)/shard_map/ppermute | solution.py:357
  80.1 2.4 %collective-permute-start.20 = (f32[64,512]{1,0:T(8,128)S(1)}, f32[64,512]{1,0:T(8,128)S(1)}, u32[]{:S(2)}, u32[]{:S(2)}) collective-permute-start(f32[64,512]{1,0:T(8,128)S(1)} %add_multiply_fusion), channel_id=1, source_target_pairs={{0,64},{1,65},{64,0},{65,1},{2,66},{3,67},{66,2},{67,3},{4,68},{5,... | collective-permute-start | bytes 393224 | tf_op jit(solution)/shard_map/ppermute | solution.py:357
  82.5 1.5 %collective-permute-start.21 = (f32[64,512]{1,0:T(8,128)S(1)}, f32[64,512]{1,0:T(8,128)S(1)}, u32[]{:S(2)}, u32[]{:S(2)}) collective-permute-start(f32[64,512]{1,0:T(8,128)S(1)} %add_multiply_fusion), channel_id=1, source_target_pairs={{0,65},{1,64},{64,1},{65,0},{2,67},{3,66},{66,3},{67,2},{4,69},{5,... | collective-permute-start | bytes 393224 | tf_op jit(solution)/shard_map/ppermute | solution.py:357
  84.0 3.5 %collective-permute-done.20 = f32[64,512]{1,0:T(8,128)S(1)} collective-permute-done((f32[64,512]{1,0:T(8,128)S(1)}, f32[64,512]{1,0:T(8,128)S(1)}, u32[]{:S(2)}, u32[]{:S(2)}) %collective-permute-start.20) | collective-permute-done | bytes 131104 | tf_op jit(solution)/shard_map/ppermute | solution.py:357
  87.5 2.8 %collective-permute-done.21 = f32[64,512]{1,0:T(8,128)S(1)} collective-permute-done((f32[64,512]{1,0:T(8,128)S(1)}, f32[64,512]{1,0:T(8,128)S(1)}, u32[]{:S(2)}, u32[]{:S(2)}) %collective-permute-start.21) | collective-permute-done | bytes 131104 | tf_op jit(solution)/shard_map/ppermute | solution.py:357
  90.4 1.6 %shard_map.111 = f32[64,256]{1,0:T(8,128)S(1)} custom-call(f32[32,72,128]{2,1,0:T(8,128)S(1)} %all-to-all-done.points, f32[64,512]{1,0:T(8,128)S(1)} %add_add_fusion.grads), custom_call_target="tpu_custom_call" | custom-call | tf_op jit(solution)/shard_map/pallas_call | solution.py:337
  94.4 1.6 %collective-permute-start.24 = (f32[64,256]{1,0:T(8,128)S(1)}, f32[64,256]{1,0:T(8,128)S(1)}, u32[]{:S(2)}, u32[]{:S(2)}) collective-permute-start(f32[64,256]{1,0:T(8,128)S(1)} %add.82), channel_id=1, source_target_pairs={{0,4},{2,6},{4,0},{6,2},{1,5},{3,7},{5,1},{7,3},{8,12},{10,14},{12... | collective-permute-start | bytes 196616 | tf_op jit(solution)/shard_map/ppermute | solution.py:357
  96.0 2.3 %collective-permute-start.25 = (f32[64,256]{1,0:T(8,128)S(1)}, f32[64,256]{1,0:T(8,128)S(1)}, u32[]{:S(2)}, u32[]{:S(2)}) collective-permute-start(f32[64,256]{1,0:T(8,128)S(1)} %add.82), channel_id=1, source_target_pairs={{0,6},{2,4},{4,2},{6,0},{1,7},{3,5},{5,3},{7,1},{8,14},{10,12},{12... | collective-permute-start | bytes 196616 | tf_op jit(solution)/shard_map/ppermute | solution.py:357
  100.7 1.8 %collective-permute-start.27 = (f32[64,256]{1,0:T(8,128)S(1)}, f32[64,256]{1,0:T(8,128)S(1)}, u32[]{:S(2)}, u32[]{:S(2)}) collective-permute-start(f32[64,256]{1,0:T(8,128)S(1)} %add_add_fusion.2), channel_id=1, source_target_pairs={{0,16},{8,24},{16,0},{24,8},{1,17},{9,25},{17,1},{25,9},{2,18},{10... | collective-permute-start | bytes 196616 | tf_op jit(solution)/shard_map/ppermute | solution.py:357
  102.5 2.1 %collective-permute-start.28 = (f32[64,256]{1,0:T(8,128)S(1)}, f32[64,256]{1,0:T(8,128)S(1)}, u32[]{:S(2)}, u32[]{:S(2)}) collective-permute-start(f32[64,256]{1,0:T(8,128)S(1)} %add_add_fusion.2), channel_id=1, source_target_pairs={{0,24},{8,16},{16,8},{24,0},{1,25},{9,17},{17,9},{25,1},{2,26},{10... | collective-permute-start | bytes 196616 | tf_op jit(solution)/shard_map/ppermute | solution.py:357
  108.3 3.9 %collective-permute-start.30 = (f32[64,512]{1,0:T(8,128)S(1)}, f32[64,512]{1,0:T(8,128)S(1)}, u32[]{:S(2)}, u32[]{:S(2)}) collective-permute-start(f32[64,512]{1,0:T(8,128)S(1)} %shard_map.112), channel_id=1, source_target_pairs={{0,64},{1,65},{64,0},{65,1},{2,66},{3,67},{66,2},{67,3},{4,68},{5,... | collective-permute-start | bytes 393224 | tf_op jit(solution)/shard_map/ppermute | solution.py:357
  112.3 3.8 %collective-permute-done.30 = f32[64,512]{1,0:T(8,128)S(1)} collective-permute-done((f32[64,512]{1,0:T(8,128)S(1)}, f32[64,512]{1,0:T(8,128)S(1)}, u32[]{:S(2)}, u32[]{:S(2)}) %collective-permute-start.30) | collective-permute-done | bytes 131104 | tf_op jit(solution)/shard_map/ppermute | solution.py:357
  117.5 4.1 %collective-permute-start.32 = (f32[64,512]{1,0:T(8,128)S(1)}, f32[64,512]{1,0:T(8,128)S(1)}, u32[]{:S(2)}, u32[]{:S(2)}) collective-permute-start(f32[64,512]{1,0:T(8,128)S(1)} %add_subtract_fusion), channel_id=1, source_target_pairs={{0,32},{32,0},{1,33},{33,1},{2,34},{34,2},{3,35},{35,3},{4,36},{36... | collective-permute-start | bytes 393224 | tf_op jit(solution)/shard_map/ppermute | solution.py:357
  (58 shorter events, 25.1 us)
Async XLA Ops:
  2.9 16.1 %collective-permute-start = (f32[768,128]{1,0:T(8,128)S(1)}, f32[768,128]{1,0:T(8,128)S(1)}, u32[]{:S(2)}, u32[]{:S(2)}) collective-permute-start(f32[768,128]{1,0:T(8,128)S(1)} %get-tuple-element.40), channel_id=1, source_target_pairs={{0,0},{32,1},{1,32},{33,33},{2,2},{34,3},{3,34},{35,35},{4,4},{36,... | collective-permute-start | bytes 1179656 | tf_op jit(solution)/shard_map/ppermute | solution.py:410
  7.8 11.2 %collective-permute-start.1 = (f32[136,256]{1,0:T(8,128)S(1)}, f32[136,256]{1,0:T(8,128)S(1)}, u32[]{:S(2)}, u32[]{:S(2)}) collective-permute-start(f32[136,256]{1,0:T(8,128)S(1)} %get-tuple-element.41), channel_id=1, source_target_pairs={{0,64},{1,65},{64,0},{65,1},{2,66},{3,67},{66,2},{67,3},{4,68},{5,... | collective-permute-start | bytes 417800 | tf_op jit(solution)/shard_map/ppermute | solution.py:357
  11.2 3.9 %collective-permute-start.2 = (f32[96,128]{1,0:T(8,128)S(1)}, f32[96,128]{1,0:T(8,128)S(1)}, u32[]{:S(2)}, u32[]{:S(2)}) collective-permute-start(f32[96,128]{1,0:T(8,128)S(1)} %get-tuple-element.43.refs_0_), channel_id=1, source_target_pairs={{0,8},{8,0},{16,24},{24,16},{1,9},{9,1},{17,25},{25,17},{2,10},{10... | collective-permute-start | bytes 147464 | tf_op jit(solution)/shard_map/ppermute | solution.py:357
  12.4 4.5 %collective-permute-start.3 = (f32[96,128]{1,0:T(8,128)S(1)}, f32[96,128]{1,0:T(8,128)S(1)}, u32[]{:S(2)}, u32[]{:S(2)}) collective-permute-start(f32[96,128]{1,0:T(8,128)S(1)} %get-tuple-element.43.refs_0_), channel_id=1, source_target_pairs={{0,16},{8,24},{16,0},{24,8},{1,17},{9,25},{17,1},{25,9},{2,18},{10... | collective-permute-start | bytes 147464 | tf_op jit(solution)/shard_map/ppermute | solution.py:357
  14.9 4.2 %collective-permute-start.4 = (f32[96,128]{1,0:T(8,128)S(1)}, f32[96,128]{1,0:T(8,128)S(1)}, u32[]{:S(2)}, u32[]{:S(2)}) collective-permute-start(f32[96,128]{1,0:T(8,128)S(1)} %get-tuple-element.43.refs_0_), channel_id=1, source_target_pairs={{0,24},{8,16},{16,8},{24,0},{1,25},{9,17},{17,9},{25,1},{2,26},{10... | collective-permute-start | bytes 147464 | tf_op jit(solution)/shard_map/ppermute | solution.py:357
  19.0 21.0 %collective-permute-start.10 = (f32[768,128]{1,0:T(8,128)S(1)}, f32[768,128]{1,0:T(8,128)}, u32[]{:S(2)}, u32[]{:S(2)}) collective-permute-start(f32[768,128]{1,0:T(8,128)S(1)} %collective-permute-done.refs_2_), channel_id=1, source_target_pairs={{0,6},{2,4},{4,2},{6,0},{1,7},{3,5},{5,3},{7,1},{8,14},{10,12},{12... | collective-permute-start | bytes 1179656 | tf_op jit(solution)/shard_map/ppermute | solution.py:357
  21.8 18.2 %collective-permute-start.8 = (f32[768,128]{1,0:T(8,128)S(1)}, f32[768,128]{1,0:T(8,128)}, u32[]{:S(2)}, u32[]{:S(2)}) collective-permute-start(f32[768,128]{1,0:T(8,128)S(1)} %collective-permute-done.refs_2_), channel_id=1, source_target_pairs={{0,2},{2,0},{4,6},{6,4},{1,3},{3,1},{5,7},{7,5},{8,10},{10,8},{12,... | collective-permute-start | bytes 1179656 | tf_op jit(solution)/shard_map/ppermute | solution.py:357
  21.8 19.3 %collective-permute-start.9 = (f32[768,128]{1,0:T(8,128)S(1)}, f32[768,128]{1,0:T(8,128)}, u32[]{:S(2)}, u32[]{:S(2)}) collective-permute-start(f32[768,128]{1,0:T(8,128)S(1)} %collective-permute-done.refs_2_), channel_id=1, source_target_pairs={{0,4},{2,6},{4,0},{6,2},{1,5},{3,7},{5,1},{7,3},{8,12},{10,14},{12... | collective-permute-start | bytes 1179656 | tf_op jit(solution)/shard_map/ppermute | solution.py:357
  24.6 5.9 %collective-permute-start.6 = (f32[136,256]{1,0:T(8,128)S(1)}, f32[136,256]{1,0:T(8,128)S(1)}, u32[]{:S(2)}, u32[]{:S(2)}) collective-permute-start(f32[136,256]{1,0:T(8,128)S(1)} %get-tuple-element.54), channel_id=1, source_target_pairs={{0,1},{1,0},{64,65},{65,64},{2,3},{3,2},{66,67},{67,66},{4,5},{5,4... | collective-permute-start | bytes 417800 | tf_op jit(solution)/shard_map/ppermute | solution.py:357
  26.4 5.8 %collective-permute-start.7 = (f32[136,256]{1,0:T(8,128)S(1)}, f32[136,256]{1,0:T(8,128)S(1)}, u32[]{:S(2)}, u32[]{:S(2)}) collective-permute-start(f32[136,256]{1,0:T(8,128)S(1)} %get-tuple-element.55), channel_id=1, source_target_pairs={{0,65},{1,64},{64,1},{65,0},{2,67},{3,66},{66,3},{67,2},{4,69},{5,... | collective-permute-start | bytes 417800 | tf_op jit(solution)/shard_map/ppermute | solution.py:357
  33.9 46.1 %all-to-all-start = ((f32[32,72,128]{2,1,0:T(8,128)}), f32[32,72,128]{2,1,0:T(8,128)S(1)}, u32[]{:S(2)}, u32[]{:S(2)}) async-start(f32[32,72,128]{2,1,0:T(8,128)} %shard_map.109), calls=%async_computation | async-start | bytes 2359296 | tf_op jit(solution)/shard_map/all_to_all | solution.py:448
  56.2 3.9 %collective-permute-start.12 = (f32[4,32,128]{2,1,0:T(8,128)S(1)}, f32[4,32,128]{2,1,0:T(8,128)S(1)}, u32[]{:S(2)}, u32[]{:S(2)}) collective-permute-start(f32[4,32,128]{2,1,0:T(8,128)S(1)} %add_add_fusion.4), channel_id=1, source_target_pairs={{0,8},{8,0},{16,24},{24,16},{1,9},{9,1},{17,25},{25,17},{2,10},{10... | collective-permute-start | bytes 196616 | tf_op jit(solution)/shard_map/ppermute | solution.py:357
  56.4 5.4 %collective-permute-start.13 = (f32[4,32,128]{2,1,0:T(8,128)S(1)}, f32[4,32,128]{2,1,0:T(8,128)S(1)}, u32[]{:S(2)}, u32[]{:S(2)}) collective-permute-start(f32[4,32,128]{2,1,0:T(8,128)S(1)} %add_add_fusion.4), channel_id=1, source_target_pairs={{0,16},{8,24},{16,0},{24,8},{1,17},{9,25},{17,1},{25,9},{2,18},{10... | collective-permute-start | bytes 196616 | tf_op jit(solution)/shard_map/ppermute | solution.py:357
  58.8 4.5 %collective-permute-start.14 = (f32[4,32,128]{2,1,0:T(8,128)S(1)}, f32[4,32,128]{2,1,0:T(8,128)S(1)}, u32[]{:S(2)}, u32[]{:S(2)}) collective-permute-start(f32[4,32,128]{2,1,0:T(8,128)S(1)} %add_add_fusion.4), channel_id=1, source_target_pairs={{0,24},{8,16},{16,8},{24,0},{1,25},{9,17},{17,9},{25,1},{2,26},{10... | collective-permute-start | bytes 196616 | tf_op jit(solution)/shard_map/ppermute | solution.py:357
  64.0 2.8 %collective-permute-start.15 = (f32[4,32,128]{2,1,0:T(8,128)S(1)}, f32[4,32,128]{2,1,0:T(8,128)S(1)}, u32[]{:S(2)}, u32[]{:S(2)}) collective-permute-start(f32[4,32,128]{2,1,0:T(8,128)S(1)} %get-tuple-element.66.own), channel_id=1, source_target_pairs={{0,32},{32,0},{1,33},{33,1},{2,34},{34,2},{3,35},{35,3},{4,36},{36... | collective-permute-start | bytes 196616 | tf_op jit(solution)/shard_map/ppermute | solution.py:357
  67.7 4.8 %collective-permute-start.16 = (f32[64,512]{1,0:T(8,128)S(1)}, f32[64,512]{1,0:T(8,128)S(1)}, u32[]{:S(2)}, u32[]{:S(2)}) collective-permute-start(f32[64,512]{1,0:T(8,128)S(1)} %get-tuple-element.72), channel_id=1, source_target_pairs={{0,2},{2,0},{4,6},{6,4},{1,3},{3,1},{5,7},{7,5},{8,10},{10,8},{12,... | collective-permute-start | bytes 393224 | tf_op jit(solution)/shard_map/ppermute | solution.py:357
  68.9 8.5 %collective-permute-start.17 = (f32[64,512]{1,0:T(8,128)S(1)}, f32[64,512]{1,0:T(8,128)S(1)}, u32[]{:S(2)}, u32[]{:S(2)}) collective-permute-start(f32[64,512]{1,0:T(8,128)S(1)} %get-tuple-element.73), channel_id=1, source_target_pairs={{0,4},{2,6},{4,0},{6,2},{1,5},{3,7},{5,1},{7,3},{8,12},{10,14},{12... | collective-permute-start | bytes 393224 | tf_op jit(solution)/shard_map/ppermute | solution.py:357
  71.4 8.6 %collective-permute-start.18 = (f32[64,512]{1,0:T(8,128)S(1)}, f32[64,512]{1,0:T(8,128)S(1)}, u32[]{:S(2)}, u32[]{:S(2)}) collective-permute-start(f32[64,512]{1,0:T(8,128)S(1)} %get-tuple-element.74), channel_id=1, source_target_pairs={{0,6},{2,4},{4,2},{6,0},{1,7},{3,5},{5,3},{7,1},{8,14},{10,12},{12... | collective-permute-start | bytes 393224 | tf_op jit(solution)/shard_map/ppermute | solution.py:357
  80.0 3.9 %collective-permute-start.19 = (f32[64,512]{1,0:T(8,128)S(1)}, f32[64,512]{1,0:T(8,128)S(1)}, u32[]{:S(2)}, u32[]{:S(2)}) collective-permute-start(f32[64,512]{1,0:T(8,128)S(1)} %add_multiply_fusion), channel_id=1, source_target_pairs={{0,1},{1,0},{64,65},{65,64},{2,3},{3,2},{66,67},{67,66},{4,5},{5,4... | collective-permute-start | bytes 393224 | tf_op jit(solution)/shard_map/ppermute | solution.py:357
  80.1 7.4 %collective-permute-start.20 = (f32[64,512]{1,0:T(8,128)S(1)}, f32[64,512]{1,0:T(8,128)S(1)}, u32[]{:S(2)}, u32[]{:S(2)}) collective-permute-start(f32[64,512]{1,0:T(8,128)S(1)} %add_multiply_fusion), channel_id=1, source_target_pairs={{0,64},{1,65},{64,0},{65,1},{2,66},{3,67},{66,2},{67,3},{4,68},{5,... | collective-permute-start | bytes 393224 | tf_op jit(solution)/shard_map/ppermute | solution.py:357
  82.5 7.8 %collective-permute-start.21 = (f32[64,512]{1,0:T(8,128)S(1)}, f32[64,512]{1,0:T(8,128)S(1)}, u32[]{:S(2)}, u32[]{:S(2)}) collective-permute-start(f32[64,512]{1,0:T(8,128)S(1)} %add_multiply_fusion), channel_id=1, source_target_pairs={{0,65},{1,64},{64,1},{65,0},{2,67},{3,66},{66,3},{67,2},{4,69},{5,... | collective-permute-start | bytes 393224 | tf_op jit(solution)/shard_map/ppermute | solution.py:357
  91.9 2.4 %collective-permute-start.22 = (f32[64,256]{1,0:T(8,128)S(1)}, f32[64,256]{1,0:T(8,128)S(1)}, u32[]{:S(2)}, u32[]{:S(2)}) collective-permute-start(f32[64,256]{1,0:T(8,128)S(1)} %shard_map.111), channel_id=1, source_target_pairs={{0,32},{32,0},{1,33},{33,1},{2,34},{34,2},{3,35},{35,3},{4,36},{36... | collective-permute-start | bytes 196616 | tf_op jit(solution)/shard_map/ppermute | solution.py:357
  94.3 3.9 %collective-permute-start.23 = (f32[64,256]{1,0:T(8,128)S(1)}, f32[64,256]{1,0:T(8,128)S(1)}, u32[]{:S(2)}, u32[]{:S(2)}) collective-permute-start(f32[64,256]{1,0:T(8,128)S(1)} %add.82), channel_id=1, source_target_pairs={{0,2},{2,0},{4,6},{6,4},{1,3},{3,1},{5,7},{7,5},{8,10},{10,8},{12,... | collective-permute-start | bytes 196616 | tf_op jit(solution)/shard_map/ppermute | solution.py:357
  94.4 4.7 %collective-permute-start.24 = (f32[64,256]{1,0:T(8,128)S(1)}, f32[64,256]{1,0:T(8,128)S(1)}, u32[]{:S(2)}, u32[]{:S(2)}) collective-permute-start(f32[64,256]{1,0:T(8,128)S(1)} %add.82), channel_id=1, source_target_pairs={{0,4},{2,6},{4,0},{6,2},{1,5},{3,7},{5,1},{7,3},{8,12},{10,14},{12... | collective-permute-start | bytes 196616 | tf_op jit(solution)/shard_map/ppermute | solution.py:357
  96.0 4.6 %collective-permute-start.25 = (f32[64,256]{1,0:T(8,128)S(1)}, f32[64,256]{1,0:T(8,128)S(1)}, u32[]{:S(2)}, u32[]{:S(2)}) collective-permute-start(f32[64,256]{1,0:T(8,128)S(1)} %add.82), channel_id=1, source_target_pairs={{0,6},{2,4},{4,2},{6,0},{1,7},{3,5},{5,3},{7,1},{8,14},{10,12},{12... | collective-permute-start | bytes 196616 | tf_op jit(solution)/shard_map/ppermute | solution.py:357
  100.6 3.9 %collective-permute-start.26 = (f32[64,256]{1,0:T(8,128)S(1)}, f32[64,256]{1,0:T(8,128)S(1)}, u32[]{:S(2)}, u32[]{:S(2)}) collective-permute-start(f32[64,256]{1,0:T(8,128)S(1)} %add_add_fusion.2), channel_id=1, source_target_pairs={{0,8},{8,0},{16,24},{24,16},{1,9},{9,1},{17,25},{25,17},{2,10},{10... | collective-permute-start | bytes 196616 | tf_op jit(solution)/shard_map/ppermute | solution.py:357
  100.7 4.7 %collective-permute-start.27 = (f32[64,256]{1,0:T(8,128)S(1)}, f32[64,256]{1,0:T(8,128)S(1)}, u32[]{:S(2)}, u32[]{:S(2)}) collective-permute-start(f32[64,256]{1,0:T(8,128)S(1)} %add_add_fusion.2), channel_id=1, source_target_pairs={{0,16},{8,24},{16,0},{24,8},{1,17},{9,25},{17,1},{25,9},{2,18},{10... | collective-permute-start | bytes 196616 | tf_op jit(solution)/shard_map/ppermute | solution.py:357
  102.5 4.3 %collective-permute-start.28 = (f32[64,256]{1,0:T(8,128)S(1)}, f32[64,256]{1,0:T(8,128)S(1)}, u32[]{:S(2)}, u32[]{:S(2)}) collective-permute-start(f32[64,256]{1,0:T(8,128)S(1)} %add_add_fusion.2), channel_id=1, source_target_pairs={{0,24},{8,16},{16,8},{24,0},{1,25},{9,17},{17,9},{25,1},{2,26},{10... | collective-permute-start | bytes 196616 | tf_op jit(solution)/shard_map/ppermute | solution.py:357
  108.0 4.3 %collective-permute-start.29 = (f32[64,512]{1,0:T(8,128)S(1)}, f32[64,512]{1,0:T(8,128)S(1)}, u32[]{:S(2)}, u32[]{:S(2)}) collective-permute-start(f32[64,512]{1,0:T(8,128)S(1)} %shard_map.112), channel_id=1, source_target_pairs={{0,1},{1,0},{64,65},{65,64},{2,3},{3,2},{66,67},{67,66},{4,5},{5,4... | collective-permute-start | bytes 393224 | tf_op jit(solution)/shard_map/ppermute | solution.py:357
  108.3 7.7 %collective-permute-start.30 = (f32[64,512]{1,0:T(8,128)S(1)}, f32[64,512]{1,0:T(8,128)S(1)}, u32[]{:S(2)}, u32[]{:S(2)}) collective-permute-start(f32[64,512]{1,0:T(8,128)S(1)} %shard_map.112), channel_id=1, source_target_pairs={{0,64},{1,65},{64,0},{65,1},{2,66},{3,67},{66,2},{67,3},{4,68},{5,... | collective-permute-start | bytes 393224 | tf_op jit(solution)/shard_map/ppermute | solution.py:357
  112.2 5.2 %collective-permute-start.31 = (f32[64,512]{1,0:T(8,128)S(1)}, f32[64,512]{1,0:T(8,128)S(1)}, u32[]{:S(2)}, u32[]{:S(2)}) collective-permute-start(f32[64,512]{1,0:T(8,128)S(1)} %shard_map.112), channel_id=1, source_target_pairs={{0,65},{1,64},{64,1},{65,0},{2,67},{3,66},{66,3},{67,2},{4,69},{5,... | collective-permute-start | bytes 393224 | tf_op jit(solution)/shard_map/ppermute | solution.py:357
  117.5 5.1 %collective-permute-start.32 = (f32[64,512]{1,0:T(8,128)S(1)}, f32[64,512]{1,0:T(8,128)S(1)}, u32[]{:S(2)}, u32[]{:S(2)}) collective-permute-start(f32[64,512]{1,0:T(8,128)S(1)} %add_subtract_fusion), channel_id=1, source_target_pairs={{0,32},{32,0},{1,33},{33,1},{2,34},{34,2},{3,35},{35,3},{4,36},{36... | collective-permute-start | bytes 393224 | tf_op jit(solution)/shard_map/ppermute | solution.py:357
  (3 other events, 29.9 us)

commit v11 on v10

--- a/solution.py
+++ b/solution.py
@@ -20,13 +20,12 @@
 VMEM = pl.BlockSpec(memory_space=pltpu.VMEM)
 
 ACOS_FULL = (
-    0.4999999701976776, -0.31830424070358276, 0.24984024465084076, -0.210431307554245,
-    0.17730562388896942, -0.13514360785484314, 0.0806083083152771, -0.031184406951069832,
-    0.005619336850941181,
+    0.49999988079071045, -0.3182917535305023, 0.24954961240291595, -0.20787927508354187,
+    0.1663874238729477, -0.10994759202003479, 0.04858129099011421, -0.01009112037718296,
 )
 ACOS_HIGH = (
-    0.4999392330646515, -0.3173876106739044, 0.24387668073177338, -0.18864932656288147,
-    0.12859871983528137, -0.06701970100402832, 0.02248113788664341, -0.003529248759150505,
+    0.4998512864112854, -0.3162611424922943, 0.2378545105457306, -0.17122769355773926,
+    0.09912680834533784, -0.03783833235502243, 0.006804656237363815,
 )
 
 NN = (((1,), (0,)), ((), ()))
@@ -345,11 +344,16 @@
 
 
 def exchange(v, axes):
-    return functools.reduce(jnp.add, [v] + mates([v] * math.prod(SIZES[a] for a in axes), axes))
+    return add_up([v] * math.prod(SIZES[a] for a in axes), axes)
 
 
 def mates(parts, axes):
     return [mate_of(parts[o], axes, o) for o in range(1, len(parts))]
+
+
+def add_up(parts, axes):
+    order = sorted(range(1, len(parts)), key=lambda o: o != 2)
+    return functools.reduce(jnp.add, [mate_of(parts[o], axes, o) for o in order], parts[0])
 
 
 def mate_of(v, axes, o):
@@ -462,7 +466,7 @@
     parts = call(
         grads_body, [shape(out, cdev)] * 4, ready, ready_mate, khi_a, klo_a, khi_b, klo_b
     )
-    grads = functools.reduce(jnp.add, mates(parts, ("y",)), parts[0]) * sb[0:1]
+    grads = add_up(parts, ("y",)) * sb[0:1]
     points, grads = together(points, grads)
     grads = exchange(grads, PLANES)
     coeff = call(

time: 124 us -> 118 us (0.952)
  waiting for transfers between devices: 39.4 us -> 36.2 us
  starting transfers between devices: 56.4 us -> 55.1 us
    ppermute x32, waiting for transfers between devices: 39.4 us -> 36.2 us  [mate_of(): return lax.ppermute(v, axes, [(i, i ^ o) for i in range(n)])]
    ppermute x32, starting transfers between devices: 45.4 us -> 44.1 us  [mate_of(): return lax.ppermute(v, axes, [(i, i ^ o) for i in range(n)])]
  transfers between devices with their start and end apart: 34 -> 34, of which waited for: 22 -> 25; matrix products, arithmetic and copies ran while one was open for 0% -> 0% of each run, Pallas kernels for 17% -> 17%
where the time goes in v11:
time: 118 us
  starting transfers between devices  55.1 us (47%)
  waiting for transfers between devices  36.2 us (31%)
  Pallas kernels  24.9 us (21%)
    ppermute x32, starting transfers between devices, mate_of(): return lax.ppermute(v, axes, [(i, i ^ o) for i in range(n)])  44.1 us
    ppermute x32, waiting for transfers between devices, mate_of(): return lax.ppermute(v, axes, [(i, i ^ o) for i in range(n)])  36.2 us
    pallas_call x8, Pallas kernels, call(): pl.pallas_call(body, out_shape=outs, in_specs=[smem] * scalars + [VMEM] *...  22.6 us
    all_to_all x1, starting transfers between devices, per_device(): lax.all_to_all(points, OWNERS, split_axis=0, concat_axis=0, tiled=True)  6.04 us
    ppermute x1, starting transfers between devices, per_device(): tile = lax.ppermute(pack, ('core', 'zl'), [(0, 0), (2, 1), (1, 2), (3, 3)])  4.93 us
  transfers between devices with their start and end apart: 34, of which 25 were waited for; matrix products, arithmetic and copies ran while one was open for 0% of the time, Pallas kernels for 17%

profile of v11, /device:TPU:1, one launch (start us, length us, event | category | flops | bytes accessed | tf_op | source)
XLA Modules:
  0.0 117.8 jit_solution(6773600040406218751)
XLA Ops:
  0.6 2.2 %shard_map.104 = (f32[96,128]{1,0:T(8,128)S(1)}, f32[768,128]{1,0:T(8,128)S(1)}, f32[136,256]{1,0:T(8,128)S(1)}, f32[136,256]{1,0:T(8,128)S(1)}, f32[136,256]{1,0:T(8,128)S(1)}, /*index=5*/f32[136,256]{1,0:T(8,128)S(1)}) custom-call(s32[1]{0:T(128)} %bitcast.1.member, s32[1,64]{1,0:T(1,128)} %bitcast.15, f32[1024,128]{1,0:T(8,128)} %refs_1_.1, ...), custom_call_target="tpu_custom_call" | custom-call | tf_op jit(solution)/shard_map/pallas_call | solution.py:385
  2.9 4.9 %collective-permute-start = (f32[768,128]{1,0:T(8,128)S(1)}, f32[768,128]{1,0:T(8,128)S(1)}, u32[]{:S(2)}, u32[]{:S(2)}) collective-permute-start(f32[768,128]{1,0:T(8,128)S(1)} %get-tuple-element.40), channel_id=1, source_target_pairs={{0,0},{32,1},{1,32},{33,33},{2,2},{34,3},{3,34},{35,35},{4,4},{36,... | collective-permute-start | bytes 1179656 | tf_op jit(solution)/shard_map/ppermute | solution.py:414
  7.8 3.4 %collective-permute-start.1 = (f32[136,256]{1,0:T(8,128)S(1)}, f32[136,256]{1,0:T(8,128)S(1)}, u32[]{:S(2)}, u32[]{:S(2)}) collective-permute-start(f32[136,256]{1,0:T(8,128)S(1)} %get-tuple-element.41), channel_id=1, source_target_pairs={{0,64},{1,65},{64,0},{65,1},{2,66},{3,67},{66,2},{67,3},{4,68},{5,... | collective-permute-start | bytes 417800 | tf_op jit(solution)/shard_map/ppermute | solution.py:361
  12.4 2.5 %collective-permute-start.3 = (f32[96,128]{1,0:T(8,128)S(1)}, f32[96,128]{1,0:T(8,128)S(1)}, u32[]{:S(2)}, u32[]{:S(2)}) collective-permute-start(f32[96,128]{1,0:T(8,128)S(1)} %get-tuple-element.43.refs_0_), channel_id=1, source_target_pairs={{0,16},{8,24},{16,0},{24,8},{1,17},{9,25},{17,1},{25,9},{2,18},{10... | collective-permute-start | bytes 147464 | tf_op jit(solution)/shard_map/ppermute | solution.py:361
  15.1 1.8 %collective-permute-done.3.refs_2_ = f32[96,128]{1,0:T(8,128)S(1)} collective-permute-done((f32[96,128]{1,0:T(8,128)S(1)}, f32[96,128]{1,0:T(8,128)S(1)}, u32[]{:S(2)}, u32[]{:S(2)}) %collective-permute-start.3) | collective-permute-done | bytes 49184 | tf_op jit(solution)/shard_map/ppermute | solution.py:361
  16.9 2.1 %collective-permute-done.4.refs_3_ = f32[96,128]{1,0:T(8,128)S(1)} collective-permute-done((f32[96,128]{1,0:T(8,128)S(1)}, f32[96,128]{1,0:T(8,128)S(1)}, u32[]{:S(2)}, u32[]{:S(2)}) %collective-permute-start.4) | collective-permute-done | bytes 49184 | tf_op jit(solution)/shard_map/ppermute | solution.py:361
  19.0 2.7 %collective-permute-start.10 = (f32[768,128]{1,0:T(8,128)S(1)}, f32[768,128]{1,0:T(8,128)}, u32[]{:S(2)}, u32[]{:S(2)}) collective-permute-start(f32[768,128]{1,0:T(8,128)S(1)} %collective-permute-done.refs_2_), channel_id=1, source_target_pairs={{0,6},{2,4},{4,2},{6,0},{1,7},{3,5},{5,3},{7,1},{8,14},{10,12},{12... | collective-permute-start | bytes 1179656 | tf_op jit(solution)/shard_map/ppermute | solution.py:361
  24.6 1.8 %collective-permute-start.6 = (f32[136,256]{1,0:T(8,128)S(1)}, f32[136,256]{1,0:T(8,128)S(1)}, u32[]{:S(2)}, u32[]{:S(2)}) collective-permute-start(f32[136,256]{1,0:T(8,128)S(1)} %get-tuple-element.54), channel_id=1, source_target_pairs={{0,1},{1,0},{64,65},{65,64},{2,3},{3,2},{66,67},{67,66},{4,5},{5,4... | collective-permute-start | bytes 417800 | tf_op jit(solution)/shard_map/ppermute | solution.py:361
  26.4 3.9 %shard_map.106 = (bf16[1,512,512]{2,1,0:T(8,128)(2,1)S(1)}, bf16[1,512,512]{2,1,0:T(8,128)(2,1)S(1)}, f32[4,32,128]{2,1,0:T(8,128)S(1)}, f32[4,32,128]{2,1,0:T(8...) custom-call(f32[4,96,128]{2,1,0:T(8,128)S(1)} %shard_map.105.refs_0_.own, ...), custom_call_target="tpu_custom_call" | custom-call | flops 100000000 | bytes 65536 | tf_op jit(solution)/shard_map/pallas_call | solution.py:336
  30.3 1.9 %collective-permute-done.7.refs_3_ = f32[136,256]{1,0:T(8,128)S(1)} collective-permute-done((f32[136,256]{1,0:T(8,128)S(1)}, f32[136,256]{1,0:T(8,128)S(1)}, u32[]{:S(2)}, u32[]{:S(2)}) %collective-permute-start.7) | collective-permute-done | bytes 139296 | tf_op jit(solution)/shard_map/ppermute | solution.py:361
  32.2 1.7 %shard_map.109 = f32[32,72,128]{2,1,0:T(8,128)} custom-call(f32[136,256]{1,0:T(8,128)S(1)} %get-tuple-element.62.refs_0_, f32[136,256]{1,0:T(8,128)S(1)} %collective-permute-done.1.refs_1_, f32[136,256]{1,0:T(8,128)S(1)} %collective-permute-done.6.refs_2_, f32[136,256]{1,0:T(8,128)S(1)} %collective-permute-done.7.refs_3_), custom_call_target="tpu_custom_call" | custom-call | tf_op jit(solution)/shard_map/pallas_call | solution.py:336
  33.9 6.0 %all-to-all-start = ((f32[32,72,128]{2,1,0:T(8,128)}), f32[32,72,128]{2,1,0:T(8,128)S(1)}, u32[]{:S(2)}, u32[]{:S(2)}) async-start(f32[32,72,128]{2,1,0:T(8,128)} %shard_map.109), calls=%async_computation | async-start | bytes 2359296 | tf_op jit(solution)/shard_map/all_to_all | solution.py:452
  41.1 12.8 %shard_map.107 = (bf16[3,512,512]{2,1,0:T(8,128)(2,1)S(1)}, bf16[3,512,512]{2,1,0:T(8,128)(2,1)S(1)}, f32[4,32,128]{2,1,0:T(8,128)S(1)}, f32[4,32,128]{2,1,0:T(8,128)S(1)}) custom-call(f32[4,96,128]{2,1,0:T(8,128)S(1)} %shard_map.105.refs_0_.own, f32[4,96,128]{2,1,0:T(8,128)S(1)} %collective-permute-done.5.refs_1_, ...), custom_call_target="tpu_custom_call" | custom-call | flops 30000001024 | bytes 65536 | tf_op jit(solution)/shard_map/pallas_call | solution.py:336
  55.5 1.7 %collective-permute-start.12 = (f32[4,32,128]{2,1,0:T(8,128)S(1)}, f32[4,32,128]{2,1,0:T(8,128)S(1)}, u32[]{:S(2)}, u32[]{:S(2)}) collective-permute-start(f32[4,32,128]{2,1,0:T(8,128)S(1)} %add_add_fusion.4), channel_id=1, source_target_pairs={{0,16},{8,24},{16,0},{24,8},{1,17},{9,25},{17,1},{25,9},{2,18},{10... | collective-permute-start | bytes 196616 | tf_op jit(solution)/shard_map/ppermute | solution.py:361
  58.8 1.4 %collective-permute-done.12 = f32[4,32,128]{2,1,0:T(8,128)S(1)} collective-permute-done((f32[4,32,128]{2,1,0:T(8,128)S(1)}, f32[4,32,128]{2,1,0:T(8,128)S(1)}, u32[]{:S(2)}, u32[]{:S(2)}) %collective-permute-start.12) | collective-permute-done | bytes 65568 | tf_op jit(solution)/shard_map/ppermute | solution.py:361
  62.8 1.8 %collective-permute-start.15 = (f32[4,32,128]{2,1,0:T(8,128)S(1)}, f32[4,32,128]{2,1,0:T(8,128)S(1)}, u32[]{:S(2)}, u32[]{:S(2)}) collective-permute-start(f32[4,32,128]{2,1,0:T(8,128)S(1)} %get-tuple-element.66.own), channel_id=1, source_target_pairs={{0,32},{32,0},{1,33},{33,1},{2,34},{34,2},{3,35},{35,3},{4,36},{36... | collective-permute-start | bytes 196616 | tf_op jit(solution)/shard_map/ppermute | solution.py:361
  66.4 2.8 %collective-permute-start.16 = (f32[64,512]{1,0:T(8,128)S(1)}, f32[64,512]{1,0:T(8,128)S(1)}, u32[]{:S(2)}, u32[]{:S(2)}) collective-permute-start(f32[64,512]{1,0:T(8,128)S(1)} %get-tuple-element.72), channel_id=1, source_target_pairs={{0,4},{2,6},{4,0},{6,2},{1,5},{3,7},{5,1},{7,3},{8,12},{10,14},{12... | collective-permute-start | bytes 393224 | tf_op jit(solution)/shard_map/ppermute | solution.py:361
  70.0 2.6 %collective-permute-done.16 = f32[64,512]{1,0:T(8,128)S(1)} collective-permute-done((f32[64,512]{1,0:T(8,128)S(1)}, f32[64,512]{1,0:T(8,128)S(1)}, u32[]{:S(2)}, u32[]{:S(2)}) %collective-permute-start.16) | collective-permute-done | bytes 131104 | tf_op jit(solution)/shard_map/ppermute | solution.py:361
  72.7 2.8 %collective-permute-done.17 = f32[64,512]{1,0:T(8,128)S(1)} collective-permute-done((f32[64,512]{1,0:T(8,128)S(1)}, f32[64,512]{1,0:T(8,128)S(1)}, u32[]{:S(2)}, u32[]{:S(2)}) %collective-permute-start.17) | collective-permute-done | bytes 131104 | tf_op jit(solution)/shard_map/ppermute | solution.py:361
  77.5 1.5 %collective-permute-start.21 = (f32[64,512]{1,0:T(8,128)S(1)}, f32[64,512]{1,0:T(8,128)S(1)}, u32[]{:S(2)}, u32[]{:S(2)}) collective-permute-start(f32[64,512]{1,0:T(8,128)S(1)} %add_multiply_fusion), channel_id=1, source_target_pairs={{0,65},{1,64},{64,1},{65,0},{2,67},{3,66},{66,3},{67,2},{4,69},{5,... | collective-permute-start | bytes 393224 | tf_op jit(solution)/shard_map/ppermute | solution.py:361
  79.0 2.1 %collective-permute-done.19 = f32[64,512]{1,0:T(8,128)S(1)} collective-permute-done((f32[64,512]{1,0:T(8,128)S(1)}, f32[64,512]{1,0:T(8,128)S(1)}, u32[]{:S(2)}, u32[]{:S(2)}) %collective-permute-start.19) | collective-permute-done | bytes 131104 | tf_op jit(solution)/shard_map/ppermute | solution.py:361
  81.1 1.4 %collective-permute-done.20 = f32[64,512]{1,0:T(8,128)S(1)} collective-permute-done((f32[64,512]{1,0:T(8,128)S(1)}, f32[64,512]{1,0:T(8,128)S(1)}, u32[]{:S(2)}, u32[]{:S(2)}) %collective-permute-start.20) | collective-permute-done | bytes 131104 | tf_op jit(solution)/shard_map/ppermute | solution.py:361
  83.8 1.6 %shard_map.111 = f32[64,256]{1,0:T(8,128)S(1)} custom-call(f32[32,72,128]{2,1,0:T(8,128)S(1)} %all-to-all-done.points, f32[64,512]{1,0:T(8,128)S(1)} %add_add_fusion.grads), custom_call_target="tpu_custom_call" | custom-call | tf_op jit(solution)/shard_map/pallas_call | solution.py:336
  85.4 2.4 %collective-permute-start.22 = (f32[64,256]{1,0:T(8,128)S(1)}, f32[64,256]{1,0:T(8,128)S(1)}, u32[]{:S(2)}, u32[]{:S(2)}) collective-permute-start(f32[64,256]{1,0:T(8,128)S(1)} %shard_map.111), channel_id=1, source_target_pairs={{0,32},{32,0},{1,33},{33,1},{2,34},{34,2},{3,35},{35,3},{4,36},{36... | collective-permute-start | bytes 196616 | tf_op jit(solution)/shard_map/ppermute | solution.py:361
  88.7 3.3 %collective-permute-start.23 = (f32[64,256]{1,0:T(8,128)S(1)}, f32[64,256]{1,0:T(8,128)S(1)}, u32[]{:S(2)}, u32[]{:S(2)}) collective-permute-start(f32[64,256]{1,0:T(8,128)S(1)} %add.82), channel_id=1, source_target_pairs={{0,4},{2,6},{4,0},{6,2},{1,5},{3,7},{5,1},{7,3},{8,12},{10,14},{12... | collective-permute-start | bytes 196616 | tf_op jit(solution)/shard_map/ppermute | solution.py:361
  92.5 1.6 %collective-permute-done.23 = f32[64,256]{1,0:T(8,128)S(1)} collective-permute-done((f32[64,256]{1,0:T(8,128)S(1)}, f32[64,256]{1,0:T(8,128)S(1)}, u32[]{:S(2)}, u32[]{:S(2)}) %collective-permute-start.23) | collective-permute-done | bytes 65568 | tf_op jit(solution)/shard_map/ppermute | solution.py:361
  99.9 1.4 %collective-permute-done.26 = f32[64,256]{1,0:T(8,128)S(1)} collective-permute-done((f32[64,256]{1,0:T(8,128)S(1)}, f32[64,256]{1,0:T(8,128)S(1)}, u32[]{:S(2)}, u32[]{:S(2)}) %collective-permute-start.26) | collective-permute-done | bytes 65568 | tf_op jit(solution)/shard_map/ppermute | solution.py:361
  101.3 1.7 %collective-permute-done.28 = f32[64,256]{1,0:T(8,128)S(1)} collective-permute-done((f32[64,256]{1,0:T(8,128)S(1)}, f32[64,256]{1,0:T(8,128)S(1)}, u32[]{:S(2)}, u32[]{:S(2)}) %collective-permute-start.28) | collective-permute-done | bytes 65568 | tf_op jit(solution)/shard_map/ppermute | solution.py:361
  105.5 2.0 %collective-permute-start.31 = (f32[64,512]{1,0:T(8,128)S(1)}, f32[64,512]{1,0:T(8,128)S(1)}, u32[]{:S(2)}, u32[]{:S(2)}) collective-permute-start(f32[64,512]{1,0:T(8,128)S(1)} %shard_map.112), channel_id=1, source_target_pairs={{0,65},{1,64},{64,1},{65,0},{2,67},{3,66},{66,3},{67,2},{4,69},{5,... | collective-permute-start | bytes 393224 | tf_op jit(solution)/shard_map/ppermute | solution.py:361
  107.5 2.1 %collective-permute-done.29 = f32[64,512]{1,0:T(8,128)S(1)} collective-permute-done((f32[64,512]{1,0:T(8,128)S(1)}, f32[64,512]{1,0:T(8,128)S(1)}, u32[]{:S(2)}, u32[]{:S(2)}) %collective-permute-start.29) | collective-permute-done | bytes 131104 | tf_op jit(solution)/shard_map/ppermute | solution.py:361
  109.6 1.4 %collective-permute-done.31 = f32[64,512]{1,0:T(8,128)S(1)} collective-permute-done((f32[64,512]{1,0:T(8,128)S(1)}, f32[64,512]{1,0:T(8,128)S(1)}, u32[]{:S(2)}, u32[]{:S(2)}) %collective-permute-start.31) | collective-permute-done | bytes 131104 | tf_op jit(solution)/shard_map/ppermute | solution.py:361
  111.0 5.1 %collective-permute-start.32 = (f32[64,512]{1,0:T(8,128)S(1)}, f32[64,512]{1,0:T(8,128)S(1)}, u32[]{:S(2)}, u32[]{:S(2)}) collective-permute-start(f32[64,512]{1,0:T(8,128)S(1)} %add_subtract_fusion), channel_id=1, source_target_pairs={{0,32},{32,0},{1,33},{33,1},{2,34},{34,2},{3,35},{35,3},{4,36},{36... | collective-permute-start | bytes 393224 | tf_op jit(solution)/shard_map/ppermute | solution.py:361
  (58 shorter events, 28.5 us)
Async XLA Ops:
  2.9 16.1 %collective-permute-start = (f32[768,128]{1,0:T(8,128)S(1)}, f32[768,128]{1,0:T(8,128)S(1)}, u32[]{:S(2)}, u32[]{:S(2)}) collective-permute-start(f32[768,128]{1,0:T(8,128)S(1)} %get-tuple-element.40), channel_id=1, source_target_pairs={{0,0},{32,1},{1,32},{33,33},{2,2},{34,3},{3,34},{35,35},{4,4},{36,... | collective-permute-start | bytes 1179656 | tf_op jit(solution)/shard_map/ppermute | solution.py:414
  7.8 11.2 %collective-permute-start.1 = (f32[136,256]{1,0:T(8,128)S(1)}, f32[136,256]{1,0:T(8,128)S(1)}, u32[]{:S(2)}, u32[]{:S(2)}) collective-permute-start(f32[136,256]{1,0:T(8,128)S(1)} %get-tuple-element.41), channel_id=1, source_target_pairs={{0,64},{1,65},{64,0},{65,1},{2,66},{3,67},{66,2},{67,3},{4,68},{5,... | collective-permute-start | bytes 417800 | tf_op jit(solution)/shard_map/ppermute | solution.py:361
  11.2 3.9 %collective-permute-start.2 = (f32[96,128]{1,0:T(8,128)S(1)}, f32[96,128]{1,0:T(8,128)S(1)}, u32[]{:S(2)}, u32[]{:S(2)}) collective-permute-start(f32[96,128]{1,0:T(8,128)S(1)} %get-tuple-element.43.refs_0_), channel_id=1, source_target_pairs={{0,8},{8,0},{16,24},{24,16},{1,9},{9,1},{17,25},{25,17},{2,10},{10... | collective-permute-start | bytes 147464 | tf_op jit(solution)/shard_map/ppermute | solution.py:361
  12.4 4.5 %collective-permute-start.3 = (f32[96,128]{1,0:T(8,128)S(1)}, f32[96,128]{1,0:T(8,128)S(1)}, u32[]{:S(2)}, u32[]{:S(2)}) collective-permute-start(f32[96,128]{1,0:T(8,128)S(1)} %get-tuple-element.43.refs_0_), channel_id=1, source_target_pairs={{0,16},{8,24},{16,0},{24,8},{1,17},{9,25},{17,1},{25,9},{2,18},{10... | collective-permute-start | bytes 147464 | tf_op jit(solution)/shard_map/ppermute | solution.py:361
  14.9 4.2 %collective-permute-start.4 = (f32[96,128]{1,0:T(8,128)S(1)}, f32[96,128]{1,0:T(8,128)S(1)}, u32[]{:S(2)}, u32[]{:S(2)}) collective-permute-start(f32[96,128]{1,0:T(8,128)S(1)} %get-tuple-element.43.refs_0_), channel_id=1, source_target_pairs={{0,24},{8,16},{16,8},{24,0},{1,25},{9,17},{17,9},{25,1},{2,26},{10... | collective-permute-start | bytes 147464 | tf_op jit(solution)/shard_map/ppermute | solution.py:361
  19.0 21.0 %collective-permute-start.10 = (f32[768,128]{1,0:T(8,128)S(1)}, f32[768,128]{1,0:T(8,128)}, u32[]{:S(2)}, u32[]{:S(2)}) collective-permute-start(f32[768,128]{1,0:T(8,128)S(1)} %collective-permute-done.refs_2_), channel_id=1, source_target_pairs={{0,6},{2,4},{4,2},{6,0},{1,7},{3,5},{5,3},{7,1},{8,14},{10,12},{12... | collective-permute-start | bytes 1179656 | tf_op jit(solution)/shard_map/ppermute | solution.py:361
  21.8 18.2 %collective-permute-start.8 = (f32[768,128]{1,0:T(8,128)S(1)}, f32[768,128]{1,0:T(8,128)}, u32[]{:S(2)}, u32[]{:S(2)}) collective-permute-start(f32[768,128]{1,0:T(8,128)S(1)} %collective-permute-done.refs_2_), channel_id=1, source_target_pairs={{0,2},{2,0},{4,6},{6,4},{1,3},{3,1},{5,7},{7,5},{8,10},{10,8},{12,... | collective-permute-start | bytes 1179656 | tf_op jit(solution)/shard_map/ppermute | solution.py:361
  21.8 19.3 %collective-permute-start.9 = (f32[768,128]{1,0:T(8,128)S(1)}, f32[768,128]{1,0:T(8,128)}, u32[]{:S(2)}, u32[]{:S(2)}) collective-permute-start(f32[768,128]{1,0:T(8,128)S(1)} %collective-permute-done.refs_2_), channel_id=1, source_target_pairs={{0,4},{2,6},{4,0},{6,2},{1,5},{3,7},{5,1},{7,3},{8,12},{10,14},{12... | collective-permute-start | bytes 1179656 | tf_op jit(solution)/shard_map/ppermute | solution.py:361
  24.6 5.7 %collective-permute-start.6 = (f32[136,256]{1,0:T(8,128)S(1)}, f32[136,256]{1,0:T(8,128)S(1)}, u32[]{:S(2)}, u32[]{:S(2)}) collective-permute-start(f32[136,256]{1,0:T(8,128)S(1)} %get-tuple-element.54), channel_id=1, source_target_pairs={{0,1},{1,0},{64,65},{65,64},{2,3},{3,2},{66,67},{67,66},{4,5},{5,4... | collective-permute-start | bytes 417800 | tf_op jit(solution)/shard_map/ppermute | solution.py:361
  26.4 5.8 %collective-permute-start.7 = (f32[136,256]{1,0:T(8,128)S(1)}, f32[136,256]{1,0:T(8,128)S(1)}, u32[]{:S(2)}, u32[]{:S(2)}) collective-permute-start(f32[136,256]{1,0:T(8,128)S(1)} %get-tuple-element.55), channel_id=1, source_target_pairs={{0,65},{1,64},{64,1},{65,0},{2,67},{3,66},{66,3},{67,2},{4,69},{5,... | collective-permute-start | bytes 417800 | tf_op jit(solution)/shard_map/ppermute | solution.py:361
  33.9 41.8 %all-to-all-start = ((f32[32,72,128]{2,1,0:T(8,128)}), f32[32,72,128]{2,1,0:T(8,128)S(1)}, u32[]{:S(2)}, u32[]{:S(2)}) async-start(f32[32,72,128]{2,1,0:T(8,128)} %shard_map.109), calls=%async_computation | async-start | bytes 2359296 | tf_op jit(solution)/shard_map/all_to_all | solution.py:452
  55.5 4.7 %collective-permute-start.12 = (f32[4,32,128]{2,1,0:T(8,128)S(1)}, f32[4,32,128]{2,1,0:T(8,128)S(1)}, u32[]{:S(2)}, u32[]{:S(2)}) collective-permute-start(f32[4,32,128]{2,1,0:T(8,128)S(1)} %add_add_fusion.4), channel_id=1, source_target_pairs={{0,16},{8,24},{16,0},{24,8},{1,17},{9,25},{17,1},{25,9},{2,18},{10... | collective-permute-start | bytes 196616 | tf_op jit(solution)/shard_map/ppermute | solution.py:361
  57.2 3.8 %collective-permute-start.13 = (f32[4,32,128]{2,1,0:T(8,128)S(1)}, f32[4,32,128]{2,1,0:T(8,128)S(1)}, u32[]{:S(2)}, u32[]{:S(2)}) collective-permute-start(f32[4,32,128]{2,1,0:T(8,128)S(1)} %add_add_fusion.4), channel_id=1, source_target_pairs={{0,8},{8,0},{16,24},{24,16},{1,9},{9,1},{17,25},{25,17},{2,10},{10... | collective-permute-start | bytes 196616 | tf_op jit(solution)/shard_map/ppermute | solution.py:361
  57.5 4.6 %collective-permute-start.14 = (f32[4,32,128]{2,1,0:T(8,128)S(1)}, f32[4,32,128]{2,1,0:T(8,128)S(1)}, u32[]{:S(2)}, u32[]{:S(2)}) collective-permute-start(f32[4,32,128]{2,1,0:T(8,128)S(1)} %add_add_fusion.4), channel_id=1, source_target_pairs={{0,24},{8,16},{16,8},{24,0},{1,25},{9,17},{17,9},{25,1},{2,26},{10... | collective-permute-start | bytes 196616 | tf_op jit(solution)/shard_map/ppermute | solution.py:361
  62.8 2.7 %collective-permute-start.15 = (f32[4,32,128]{2,1,0:T(8,128)S(1)}, f32[4,32,128]{2,1,0:T(8,128)S(1)}, u32[]{:S(2)}, u32[]{:S(2)}) collective-permute-start(f32[4,32,128]{2,1,0:T(8,128)S(1)} %get-tuple-element.66.own), channel_id=1, source_target_pairs={{0,32},{32,0},{1,33},{33,1},{2,34},{34,2},{3,35},{35,3},{4,36},{36... | collective-permute-start | bytes 196616 | tf_op jit(solution)/shard_map/ppermute | solution.py:361
  66.4 6.3 %collective-permute-start.16 = (f32[64,512]{1,0:T(8,128)S(1)}, f32[64,512]{1,0:T(8,128)S(1)}, u32[]{:S(2)}, u32[]{:S(2)}) collective-permute-start(f32[64,512]{1,0:T(8,128)S(1)} %get-tuple-element.72), channel_id=1, source_target_pairs={{0,4},{2,6},{4,0},{6,2},{1,5},{3,7},{5,1},{7,3},{8,12},{10,14},{12... | collective-permute-start | bytes 393224 | tf_op jit(solution)/shard_map/ppermute | solution.py:361
  69.2 6.4 %collective-permute-start.17 = (f32[64,512]{1,0:T(8,128)S(1)}, f32[64,512]{1,0:T(8,128)S(1)}, u32[]{:S(2)}, u32[]{:S(2)}) collective-permute-start(f32[64,512]{1,0:T(8,128)S(1)} %get-tuple-element.73), channel_id=1, source_target_pairs={{0,2},{2,0},{4,6},{6,4},{1,3},{3,1},{5,7},{7,5},{8,10},{10,8},{12,... | collective-permute-start | bytes 393224 | tf_op jit(solution)/shard_map/ppermute | solution.py:361
  69.4 6.2 %collective-permute-start.18 = (f32[64,512]{1,0:T(8,128)S(1)}, f32[64,512]{1,0:T(8,128)S(1)}, u32[]{:S(2)}, u32[]{:S(2)}) collective-permute-start(f32[64,512]{1,0:T(8,128)S(1)} %get-tuple-element.74), channel_id=1, source_target_pairs={{0,6},{2,4},{4,2},{6,0},{1,7},{3,5},{5,3},{7,1},{8,14},{10,12},{12... | collective-permute-start | bytes 393224 | tf_op jit(solution)/shard_map/ppermute | solution.py:361
  75.7 5.4 %collective-permute-start.19 = (f32[64,512]{1,0:T(8,128)S(1)}, f32[64,512]{1,0:T(8,128)S(1)}, u32[]{:S(2)}, u32[]{:S(2)}) collective-permute-start(f32[64,512]{1,0:T(8,128)S(1)} %add_multiply_fusion), channel_id=1, source_target_pairs={{0,64},{1,65},{64,0},{65,1},{2,66},{3,67},{66,2},{67,3},{4,68},{5,... | collective-permute-start | bytes 393224 | tf_op jit(solution)/shard_map/ppermute | solution.py:361
  76.9 5.5 %collective-permute-start.20 = (f32[64,512]{1,0:T(8,128)S(1)}, f32[64,512]{1,0:T(8,128)S(1)}, u32[]{:S(2)}, u32[]{:S(2)}) collective-permute-start(f32[64,512]{1,0:T(8,128)S(1)} %add_multiply_fusion), channel_id=1, source_target_pairs={{0,1},{1,0},{64,65},{65,64},{2,3},{3,2},{66,67},{67,66},{4,5},{5,4... | collective-permute-start | bytes 393224 | tf_op jit(solution)/shard_map/ppermute | solution.py:361
  77.5 6.2 %collective-permute-start.21 = (f32[64,512]{1,0:T(8,128)S(1)}, f32[64,512]{1,0:T(8,128)S(1)}, u32[]{:S(2)}, u32[]{:S(2)}) collective-permute-start(f32[64,512]{1,0:T(8,128)S(1)} %add_multiply_fusion), channel_id=1, source_target_pairs={{0,65},{1,64},{64,1},{65,0},{2,67},{3,66},{66,3},{67,2},{4,69},{5,... | collective-permute-start | bytes 393224 | tf_op jit(solution)/shard_map/ppermute | solution.py:361
  85.4 3.3 %collective-permute-start.22 = (f32[64,256]{1,0:T(8,128)S(1)}, f32[64,256]{1,0:T(8,128)S(1)}, u32[]{:S(2)}, u32[]{:S(2)}) collective-permute-start(f32[64,256]{1,0:T(8,128)S(1)} %shard_map.111), channel_id=1, source_target_pairs={{0,32},{32,0},{1,33},{33,1},{2,34},{34,2},{3,35},{35,3},{4,36},{36... | collective-permute-start | bytes 196616 | tf_op jit(solution)/shard_map/ppermute | solution.py:361
  88.7 5.4 %collective-permute-start.23 = (f32[64,256]{1,0:T(8,128)S(1)}, f32[64,256]{1,0:T(8,128)S(1)}, u32[]{:S(2)}, u32[]{:S(2)}) collective-permute-start(f32[64,256]{1,0:T(8,128)S(1)} %add.82), channel_id=1, source_target_pairs={{0,4},{2,6},{4,0},{6,2},{1,5},{3,7},{5,1},{7,3},{8,12},{10,14},{12... | collective-permute-start | bytes 196616 | tf_op jit(solution)/shard_map/ppermute | solution.py:361
  91.9 3.5 %collective-permute-start.24 = (f32[64,256]{1,0:T(8,128)S(1)}, f32[64,256]{1,0:T(8,128)S(1)}, u32[]{:S(2)}, u32[]{:S(2)}) collective-permute-start(f32[64,256]{1,0:T(8,128)S(1)} %add.82), channel_id=1, source_target_pairs={{0,2},{2,0},{4,6},{6,4},{1,3},{3,1},{5,7},{7,5},{8,10},{10,8},{12,... | collective-permute-start | bytes 196616 | tf_op jit(solution)/shard_map/ppermute | solution.py:361
  92.2 4.3 %collective-permute-start.25 = (f32[64,256]{1,0:T(8,128)S(1)}, f32[64,256]{1,0:T(8,128)S(1)}, u32[]{:S(2)}, u32[]{:S(2)}) collective-permute-start(f32[64,256]{1,0:T(8,128)S(1)} %add.82), channel_id=1, source_target_pairs={{0,6},{2,4},{4,2},{6,0},{1,7},{3,5},{5,3},{7,1},{8,14},{10,12},{12... | collective-permute-start | bytes 196616 | tf_op jit(solution)/shard_map/ppermute | solution.py:361
  96.6 4.7 %collective-permute-start.26 = (f32[64,256]{1,0:T(8,128)S(1)}, f32[64,256]{1,0:T(8,128)S(1)}, u32[]{:S(2)}, u32[]{:S(2)}) collective-permute-start(f32[64,256]{1,0:T(8,128)S(1)} %add_add_fusion.2), channel_id=1, source_target_pairs={{0,16},{8,24},{16,0},{24,8},{1,17},{9,25},{17,1},{25,9},{2,18},{10... | collective-permute-start | bytes 196616 | tf_op jit(solution)/shard_map/ppermute | solution.py:361
  97.4 3.9 %collective-permute-start.27 = (f32[64,256]{1,0:T(8,128)S(1)}, f32[64,256]{1,0:T(8,128)S(1)}, u32[]{:S(2)}, u32[]{:S(2)}) collective-permute-start(f32[64,256]{1,0:T(8,128)S(1)} %add_add_fusion.2), channel_id=1, source_target_pairs={{0,8},{8,0},{16,24},{24,16},{1,9},{9,1},{17,25},{25,17},{2,10},{10... | collective-permute-start | bytes 196616 | tf_op jit(solution)/shard_map/ppermute | solution.py:361
  98.7 4.3 %collective-permute-start.28 = (f32[64,256]{1,0:T(8,128)S(1)}, f32[64,256]{1,0:T(8,128)S(1)}, u32[]{:S(2)}, u32[]{:S(2)}) collective-permute-start(f32[64,256]{1,0:T(8,128)S(1)} %add_add_fusion.2), channel_id=1, source_target_pairs={{0,24},{8,16},{16,8},{24,0},{1,25},{9,17},{17,9},{25,1},{2,26},{10... | collective-permute-start | bytes 196616 | tf_op jit(solution)/shard_map/ppermute | solution.py:361
  104.2 5.4 %collective-permute-start.29 = (f32[64,512]{1,0:T(8,128)S(1)}, f32[64,512]{1,0:T(8,128)S(1)}, u32[]{:S(2)}, u32[]{:S(2)}) collective-permute-start(f32[64,512]{1,0:T(8,128)S(1)} %shard_map.112), channel_id=1, source_target_pairs={{0,64},{1,65},{64,0},{65,1},{2,66},{3,67},{66,2},{67,3},{4,68},{5,... | collective-permute-start | bytes 393224 | tf_op jit(solution)/shard_map/ppermute | solution.py:361
  104.5 5.1 %collective-permute-start.30 = (f32[64,512]{1,0:T(8,128)S(1)}, f32[64,512]{1,0:T(8,128)S(1)}, u32[]{:S(2)}, u32[]{:S(2)}) collective-permute-start(f32[64,512]{1,0:T(8,128)S(1)} %shard_map.112), channel_id=1, source_target_pairs={{0,1},{1,0},{64,65},{65,64},{2,3},{3,2},{66,67},{67,66},{4,5},{5,4... | collective-permute-start | bytes 393224 | tf_op jit(solution)/shard_map/ppermute | solution.py:361
  105.5 5.5 %collective-permute-start.31 = (f32[64,512]{1,0:T(8,128)S(1)}, f32[64,512]{1,0:T(8,128)S(1)}, u32[]{:S(2)}, u32[]{:S(2)}) collective-permute-start(f32[64,512]{1,0:T(8,128)S(1)} %shard_map.112), channel_id=1, source_target_pairs={{0,65},{1,64},{64,1},{65,0},{2,67},{3,66},{66,3},{67,2},{4,69},{5,... | collective-permute-start | bytes 393224 | tf_op jit(solution)/shard_map/ppermute | solution.py:361
  111.0 6.1 %collective-permute-start.32 = (f32[64,512]{1,0:T(8,128)S(1)}, f32[64,512]{1,0:T(8,128)S(1)}, u32[]{:S(2)}, u32[]{:S(2)}) collective-permute-start(f32[64,512]{1,0:T(8,128)S(1)} %add_subtract_fusion), channel_id=1, source_target_pairs={{0,32},{32,0},{1,33},{33,1},{2,34},{34,2},{3,35},{35,3},{4,36},{36... | collective-permute-start | bytes 393224 | tf_op jit(solution)/shard_map/ppermute | solution.py:361
  (3 other events, 30.4 us)

commit v12 on v11

--- a/solution.py
+++ b/solution.py
@@ -16,6 +16,7 @@
 ALL = ("zh", "core", "x", "y", "zl")
 CENTERS = ("x", "y", "zl")
 PLANES = ("zh", "zl")
+TILES = (0, 1, 3, 2)
 OWNERS = ("x", "y", "core")
 VMEM = pl.BlockSpec(memory_space=pltpu.VMEM)
 
@@ -142,9 +143,9 @@
         out[count:, :] = row
 
 
-def order_body(x, *refs):
+def order_body(x, *refs, offsets):
     parts, out = refs[:-1], refs[-1]
-    for o, part in enumerate(parts):
+    for o, part in zip(offsets, parts):
         out[x[0] ^ o] = part[...]
 
 
@@ -410,12 +411,17 @@
         ),
     )
 
-    gathered = mates([drawn] * nx, ("x",))
+    hops = (2, 1, 3)
+    gathered = [mate_of(drawn, ("x",), o) for o in hops]
     tile = lax.ppermute(pack, ("core", "zl"), [(0, 0), (2, 1), (1, 2), (3, 3)])
     first = mate_of(parted[2], PLANES, 2)
     tile, first, drawn, *gathered = together(tile, first, drawn, *gathered)
-    own = call(order_body, shape(nx, rows + half, dim), x, drawn, *gathered, scalars=1)
-    others = mates([tile] * ny, ("y",))
+    own = call(
+        functools.partial(order_body, offsets=(0,) + hops),
+        shape(nx, rows + half, dim), x, drawn, *gathered,
+        scalars=1,
+    )
+    others = [mate_of(tile, ("y",), o) for o in TILES[1:]]
     mate = mate_of(own, ("core",), 1)
     mate, second, third = together(mate, parted[1], parted[3])
     parted = [parted[0], first, mate_of(second, PLANES, 1), mate_of(third, PLANES, 3)]
@@ -466,6 +472,7 @@
     parts = call(
         grads_body, [shape(out, cdev)] * 4, ready, ready_mate, khi_a, klo_a, khi_b, klo_b
     )
+    parts = [parts[TILES.index(o)] for o in range(ny)]
     grads = add_up(parts, ("y",)) * sb[0:1]
     points, grads = together(points, grads)
     grads = exchange(grads, PLANES)

time: 118 us -> 117 us (level)
  waiting for transfers between devices: 36.2 us -> 35 us
    ppermute x32, waiting for transfers between devices: 36.2 us -> 35 us  [mate_of(): return lax.ppermute(v, axes, [(i, i ^ o) for i in range(n)])]
  transfers between devices with their start and end apart: 34 -> 34, of which waited for: 25 -> 27; matrix products, arithmetic and copies ran while one was open for 0% -> 0% of each run, Pallas kernels for 17% -> 17%
where the time goes in v12:
time: 117 us
  starting transfers between devices  55.4 us (47%)
  waiting for transfers between devices  35 us (30%)
  Pallas kernels  24.9 us (21%)
    ppermute x32, starting transfers between devices, mate_of(): return lax.ppermute(v, axes, [(i, i ^ o) for i in range(n)])  43.9 us
    ppermute x32, waiting for transfers between devices, mate_of(): return lax.ppermute(v, axes, [(i, i ^ o) for i in range(n)])  35 us
    pallas_call x8, Pallas kernels, call(): pl.pallas_call(body, out_shape=outs, in_specs=[smem] * scalars + [VMEM] *...  22.6 us
    all_to_all x1, starting transfers between devices, per_device(): lax.all_to_all(points, OWNERS, split_axis=0, concat_axis=0, tiled=True)  6.56 us
    ppermute x1, starting transfers between devices, per_device(): tile = lax.ppermute(pack, ('core', 'zl'), [(0, 0), (2, 1), (1, 2), (3, 3)])  4.93 us
  transfers between devices with their start and end apart: 34, of which 27 were waited for; matrix products, arithmetic and copies ran while one was open for 0% of the time, Pallas kernels for 17%

profile of v12, /device:TPU:1, one launch (start us, length us, event | category | flops | bytes accessed | tf_op | source)
XLA Modules:
  0.0 117.0 jit_solution(1395143262824310938)
XLA Ops:
  0.6 2.2 %shard_map.104 = (f32[96,128]{1,0:T(8,128)S(1)}, f32[768,128]{1,0:T(8,128)S(1)}, f32[136,256]{1,0:T(8,128)S(1)}, f32[136,256]{1,0:T(8,128)S(1)}, f32[136,256]{1,0:T(8,128)S(1)}, /*index=5*/f32[136,256]{1,0:T(8,128)S(1)}) custom-call(s32[1]{0:T(128)} %bitcast.1.member, s32[1,64]{1,0:T(1,128)} %bitcast.15, f32[1024,128]{1,0:T(8,128)} %refs_1_.1, ...), custom_call_target="tpu_custom_call" | custom-call | tf_op jit(solution)/shard_map/pallas_call | solution.py:386
  2.9 4.9 %collective-permute-start = (f32[768,128]{1,0:T(8,128)S(1)}, f32[768,128]{1,0:T(8,128)S(1)}, u32[]{:S(2)}, u32[]{:S(2)}) collective-permute-start(f32[768,128]{1,0:T(8,128)S(1)} %get-tuple-element.40), channel_id=1, source_target_pairs={{0,0},{32,1},{1,32},{33,33},{2,2},{34,3},{3,34},{35,35},{4,4},{36,... | collective-permute-start | bytes 1179656 | tf_op jit(solution)/shard_map/ppermute | solution.py:416
  7.8 3.4 %collective-permute-start.1 = (f32[136,256]{1,0:T(8,128)S(1)}, f32[136,256]{1,0:T(8,128)S(1)}, u32[]{:S(2)}, u32[]{:S(2)}) collective-permute-start(f32[136,256]{1,0:T(8,128)S(1)} %get-tuple-element.41), channel_id=1, source_target_pairs={{0,64},{1,65},{64,0},{65,1},{2,66},{3,67},{66,2},{67,3},{4,68},{5,... | collective-permute-start | bytes 417800 | tf_op jit(solution)/shard_map/ppermute | solution.py:362
  11.2 2.7 %collective-permute-start.2 = (f32[96,128]{1,0:T(8,128)S(1)}, f32[96,128]{1,0:T(8,128)S(1)}, u32[]{:S(2)}, u32[]{:S(2)}) collective-permute-start(f32[96,128]{1,0:T(8,128)S(1)} %get-tuple-element.43.refs_0_), channel_id=1, source_target_pairs={{0,16},{8,24},{16,0},{24,8},{1,17},{9,25},{17,1},{25,9},{2,18},{10... | collective-permute-start | bytes 147464 | tf_op jit(solution)/shard_map/ppermute | solution.py:362
  15.9 1.3 %collective-permute-done.3.refs_2_ = f32[96,128]{1,0:T(8,128)S(1)} collective-permute-done((f32[96,128]{1,0:T(8,128)S(1)}, f32[96,128]{1,0:T(8,128)S(1)}, u32[]{:S(2)}, u32[]{:S(2)}) %collective-permute-start.3) | collective-permute-done | bytes 49184 | tf_op jit(solution)/shard_map/ppermute | solution.py:362
  18.4 2.9 %collective-permute-start.10 = (f32[768,128]{1,0:T(8,128)S(1)}, f32[768,128]{1,0:T(8,128)}, u32[]{:S(2)}, u32[]{:S(2)}) collective-permute-start(f32[768,128]{1,0:T(8,128)S(1)} %collective-permute-done.refs_2_), channel_id=1, source_target_pairs={{0,4},{2,6},{4,0},{6,2},{1,5},{3,7},{5,1},{7,3},{8,12},{10,14},{12... | collective-permute-start | bytes 1179656 | tf_op jit(solution)/shard_map/ppermute | solution.py:362
  22.3 1.3 %collective-permute-done.5.refs_1_ = f32[4,96,128]{2,1,0:T(8,128)S(1)} collective-permute-done((f32[4,96,128]{2,1,0:T(8,128)S(1)}, f32[4,96,128]{2,1,0:T(8,128)S(1)}, u32[]{:S(2)}, u32[]{:S(2)}) %collective-permute-start.5) | collective-permute-done | bytes 196640 | tf_op jit(solution)/shard_map/ppermute | solution.py:362
  23.6 1.7 %collective-permute-start.6 = (f32[136,256]{1,0:T(8,128)S(1)}, f32[136,256]{1,0:T(8,128)S(1)}, u32[]{:S(2)}, u32[]{:S(2)}) collective-permute-start(f32[136,256]{1,0:T(8,128)S(1)} %get-tuple-element.54), channel_id=1, source_target_pairs={{0,1},{1,0},{64,65},{65,64},{2,3},{3,2},{66,67},{67,66},{4,5},{5,4... | collective-permute-start | bytes 417800 | tf_op jit(solution)/shard_map/ppermute | solution.py:362
  25.3 3.9 %shard_map.106 = (bf16[1,512,512]{2,1,0:T(8,128)(2,1)S(1)}, bf16[1,512,512]{2,1,0:T(8,128)(2,1)S(1)}, f32[4,32,128]{2,1,0:T(8,128)S(1)}, f32[4,32,128]{2,1,0:T(8...) custom-call(f32[4,96,128]{2,1,0:T(8,128)S(1)} %shard_map.105.refs_0_.own, ...), custom_call_target="tpu_custom_call" | custom-call | flops 100000000 | bytes 65536 | tf_op jit(solution)/shard_map/pallas_call | solution.py:337
  29.2 2.0 %collective-permute-done.7.refs_3_ = f32[136,256]{1,0:T(8,128)S(1)} collective-permute-done((f32[136,256]{1,0:T(8,128)S(1)}, f32[136,256]{1,0:T(8,128)S(1)}, u32[]{:S(2)}, u32[]{:S(2)}) %collective-permute-start.7) | collective-permute-done | bytes 139296 | tf_op jit(solution)/shard_map/ppermute | solution.py:362
  31.2 1.7 %shard_map.109 = f32[32,72,128]{2,1,0:T(8,128)} custom-call(f32[136,256]{1,0:T(8,128)S(1)} %get-tuple-element.62.refs_0_, f32[136,256]{1,0:T(8,128)S(1)} %collective-permute-done.1.refs_1_, f32[136,256]{1,0:T(8,128)S(1)} %collective-permute-done.6.refs_2_, f32[136,256]{1,0:T(8,128)S(1)} %collective-permute-done.7.refs_3_), custom_call_target="tpu_custom_call" | custom-call | tf_op jit(solution)/shard_map/pallas_call | solution.py:337
  33.0 6.6 %all-to-all-start = ((f32[32,72,128]{2,1,0:T(8,128)}), f32[32,72,128]{2,1,0:T(8,128)S(1)}, u32[]{:S(2)}, u32[]{:S(2)}) async-start(f32[32,72,128]{2,1,0:T(8,128)} %shard_map.109), calls=%async_computation | async-start | bytes 2359296 | tf_op jit(solution)/shard_map/all_to_all | solution.py:458
  40.0 12.8 %shard_map.107 = (bf16[3,512,512]{2,1,0:T(8,128)(2,1)S(1)}, bf16[3,512,512]{2,1,0:T(8,128)(2,1)S(1)}, f32[4,32,128]{2,1,0:T(8,128)S(1)}, f32[4,32,128]{2,1,0:T(8,128)S(1)}) custom-call(f32[4,96,128]{2,1,0:T(8,128)S(1)} %shard_map.105.refs_0_.own, f32[4,96,128]{2,1,0:T(8,128)S(1)} %collective-permute-done.5.refs_1_, ...), custom_call_target="tpu_custom_call" | custom-call | flops 30000001024 | bytes 65536 | tf_op jit(solution)/shard_map/pallas_call | solution.py:337
  54.2 2.6 %collective-permute-start.12 = (f32[4,32,128]{2,1,0:T(8,128)S(1)}, f32[4,32,128]{2,1,0:T(8,128)S(1)}, u32[]{:S(2)}, u32[]{:S(2)}) collective-permute-start(f32[4,32,128]{2,1,0:T(8,128)S(1)} %add_add_fusion.4), channel_id=1, source_target_pairs={{0,16},{8,24},{16,0},{24,8},{1,17},{9,25},{17,1},{25,9},{2,18},{10... | collective-permute-start | bytes 196616 | tf_op jit(solution)/shard_map/ppermute | solution.py:362
  58.9 1.3 %collective-permute-done.13 = f32[4,32,128]{2,1,0:T(8,128)S(1)} collective-permute-done((f32[4,32,128]{2,1,0:T(8,128)S(1)}, f32[4,32,128]{2,1,0:T(8,128)S(1)}, u32[]{:S(2)}, u32[]{:S(2)}) %collective-permute-start.13) | collective-permute-done | bytes 65568 | tf_op jit(solution)/shard_map/ppermute | solution.py:362
  62.1 2.1 %collective-permute-start.15 = (f32[4,32,128]{2,1,0:T(8,128)S(1)}, f32[4,32,128]{2,1,0:T(8,128)S(1)}, u32[]{:S(2)}, u32[]{:S(2)}) collective-permute-start(f32[4,32,128]{2,1,0:T(8,128)S(1)} %get-tuple-element.66.own), channel_id=1, source_target_pairs={{0,32},{32,0},{1,33},{33,1},{2,34},{34,2},{3,35},{35,3},{4,36},{36... | collective-permute-start | bytes 196616 | tf_op jit(solution)/shard_map/ppermute | solution.py:362
  65.9 2.8 %collective-permute-start.16 = (f32[64,512]{1,0:T(8,128)S(1)}, f32[64,512]{1,0:T(8,128)S(1)}, u32[]{:S(2)}, u32[]{:S(2)}) collective-permute-start(f32[64,512]{1,0:T(8,128)S(1)} %get-tuple-element.72), channel_id=1, source_target_pairs={{0,4},{2,6},{4,0},{6,2},{1,5},{3,7},{5,1},{7,3},{8,12},{10,14},{12... | collective-permute-start | bytes 393224 | tf_op jit(solution)/shard_map/ppermute | solution.py:362
  69.6 2.6 %collective-permute-done.16 = f32[64,512]{1,0:T(8,128)S(1)} collective-permute-done((f32[64,512]{1,0:T(8,128)S(1)}, f32[64,512]{1,0:T(8,128)S(1)}, u32[]{:S(2)}, u32[]{:S(2)}) %collective-permute-start.16) | collective-permute-done | bytes 131104 | tf_op jit(solution)/shard_map/ppermute | solution.py:362
  72.2 2.8 %collective-permute-done.17 = f32[64,512]{1,0:T(8,128)S(1)} collective-permute-done((f32[64,512]{1,0:T(8,128)S(1)}, f32[64,512]{1,0:T(8,128)S(1)}, u32[]{:S(2)}, u32[]{:S(2)}) %collective-permute-start.17) | collective-permute-done | bytes 131104 | tf_op jit(solution)/shard_map/ppermute | solution.py:362
  77.1 1.5 %collective-permute-start.21 = (f32[64,512]{1,0:T(8,128)S(1)}, f32[64,512]{1,0:T(8,128)S(1)}, u32[]{:S(2)}, u32[]{:S(2)}) collective-permute-start(f32[64,512]{1,0:T(8,128)S(1)} %add_multiply_fusion), channel_id=1, source_target_pairs={{0,65},{1,64},{64,1},{65,0},{2,67},{3,66},{66,3},{67,2},{4,69},{5,... | collective-permute-start | bytes 393224 | tf_op jit(solution)/shard_map/ppermute | solution.py:362
  78.6 2.1 %collective-permute-done.19 = f32[64,512]{1,0:T(8,128)S(1)} collective-permute-done((f32[64,512]{1,0:T(8,128)S(1)}, f32[64,512]{1,0:T(8,128)S(1)}, u32[]{:S(2)}, u32[]{:S(2)}) %collective-permute-start.19) | collective-permute-done | bytes 131104 | tf_op jit(solution)/shard_map/ppermute | solution.py:362
  80.7 1.4 %collective-permute-done.20 = f32[64,512]{1,0:T(8,128)S(1)} collective-permute-done((f32[64,512]{1,0:T(8,128)S(1)}, f32[64,512]{1,0:T(8,128)S(1)}, u32[]{:S(2)}, u32[]{:S(2)}) %collective-permute-start.20) | collective-permute-done | bytes 131104 | tf_op jit(solution)/shard_map/ppermute | solution.py:362
  83.4 1.6 %shard_map.111 = f32[64,256]{1,0:T(8,128)S(1)} custom-call(f32[32,72,128]{2,1,0:T(8,128)S(1)} %all-to-all-done.points, f32[64,512]{1,0:T(8,128)S(1)} %add_add_fusion.grads), custom_call_target="tpu_custom_call" | custom-call | tf_op jit(solution)/shard_map/pallas_call | solution.py:337
  85.0 2.4 %collective-permute-start.22 = (f32[64,256]{1,0:T(8,128)S(1)}, f32[64,256]{1,0:T(8,128)S(1)}, u32[]{:S(2)}, u32[]{:S(2)}) collective-permute-start(f32[64,256]{1,0:T(8,128)S(1)} %shard_map.111), channel_id=1, source_target_pairs={{0,32},{32,0},{1,33},{33,1},{2,34},{34,2},{3,35},{35,3},{4,36},{36... | collective-permute-start | bytes 196616 | tf_op jit(solution)/shard_map/ppermute | solution.py:362
  88.3 3.3 %collective-permute-start.23 = (f32[64,256]{1,0:T(8,128)S(1)}, f32[64,256]{1,0:T(8,128)S(1)}, u32[]{:S(2)}, u32[]{:S(2)}) collective-permute-start(f32[64,256]{1,0:T(8,128)S(1)} %add.82), channel_id=1, source_target_pairs={{0,4},{2,6},{4,0},{6,2},{1,5},{3,7},{5,1},{7,3},{8,12},{10,14},{12... | collective-permute-start | bytes 196616 | tf_op jit(solution)/shard_map/ppermute | solution.py:362
  92.1 1.6 %collective-permute-done.23 = f32[64,256]{1,0:T(8,128)S(1)} collective-permute-done((f32[64,256]{1,0:T(8,128)S(1)}, f32[64,256]{1,0:T(8,128)S(1)}, u32[]{:S(2)}, u32[]{:S(2)}) %collective-permute-start.23) | collective-permute-done | bytes 65568 | tf_op jit(solution)/shard_map/ppermute | solution.py:362
  93.6 1.3 %collective-permute-done.24 = f32[64,256]{1,0:T(8,128)S(1)} collective-permute-done((f32[64,256]{1,0:T(8,128)S(1)}, f32[64,256]{1,0:T(8,128)S(1)}, u32[]{:S(2)}, u32[]{:S(2)}) %collective-permute-start.24) | collective-permute-done | bytes 65568 | tf_op jit(solution)/shard_map/ppermute | solution.py:362
  97.4 2.1 %collective-permute-start.28 = (f32[64,256]{1,0:T(8,128)S(1)}, f32[64,256]{1,0:T(8,128)S(1)}, u32[]{:S(2)}, u32[]{:S(2)}) collective-permute-start(f32[64,256]{1,0:T(8,128)S(1)} %add_add_fusion.2), channel_id=1, source_target_pairs={{0,24},{8,16},{16,8},{24,0},{1,25},{9,17},{17,9},{25,1},{2,26},{10... | collective-permute-start | bytes 196616 | tf_op jit(solution)/shard_map/ppermute | solution.py:362
  99.5 1.4 %collective-permute-done.26 = f32[64,256]{1,0:T(8,128)S(1)} collective-permute-done((f32[64,256]{1,0:T(8,128)S(1)}, f32[64,256]{1,0:T(8,128)S(1)}, u32[]{:S(2)}, u32[]{:S(2)}) %collective-permute-start.26) | collective-permute-done | bytes 65568 | tf_op jit(solution)/shard_map/ppermute | solution.py:362
  104.7 1.5 %collective-permute-start.31 = (f32[64,512]{1,0:T(8,128)S(1)}, f32[64,512]{1,0:T(8,128)S(1)}, u32[]{:S(2)}, u32[]{:S(2)}) collective-permute-start(f32[64,512]{1,0:T(8,128)S(1)} %shard_map.112), channel_id=1, source_target_pairs={{0,65},{1,64},{64,1},{65,0},{2,67},{3,66},{66,3},{67,2},{4,69},{5,... | collective-permute-start | bytes 393224 | tf_op jit(solution)/shard_map/ppermute | solution.py:362
  106.2 2.1 %collective-permute-done.29 = f32[64,512]{1,0:T(8,128)S(1)} collective-permute-done((f32[64,512]{1,0:T(8,128)S(1)}, f32[64,512]{1,0:T(8,128)S(1)}, u32[]{:S(2)}, u32[]{:S(2)}) %collective-permute-start.29) | collective-permute-done | bytes 131104 | tf_op jit(solution)/shard_map/ppermute | solution.py:362
  109.8 5.6 %collective-permute-start.32 = (f32[64,512]{1,0:T(8,128)S(1)}, f32[64,512]{1,0:T(8,128)S(1)}, u32[]{:S(2)}, u32[]{:S(2)}) collective-permute-start(f32[64,512]{1,0:T(8,128)S(1)} %add_subtract_fusion), channel_id=1, source_target_pairs={{0,32},{32,0},{1,33},{33,1},{2,34},{34,2},{3,35},{35,3},{4,36},{36... | collective-permute-start | bytes 393224 | tf_op jit(solution)/shard_map/ppermute | solution.py:362
  (58 shorter events, 26.7 us)
Async XLA Ops:
  2.9 15.5 %collective-permute-start = (f32[768,128]{1,0:T(8,128)S(1)}, f32[768,128]{1,0:T(8,128)S(1)}, u32[]{:S(2)}, u32[]{:S(2)}) collective-permute-start(f32[768,128]{1,0:T(8,128)S(1)} %get-tuple-element.40), channel_id=1, source_target_pairs={{0,0},{32,1},{1,32},{33,33},{2,2},{34,3},{3,34},{35,35},{4,4},{36,... | collective-permute-start | bytes 1179656 | tf_op jit(solution)/shard_map/ppermute | solution.py:416
  7.8 10.6 %collective-permute-start.1 = (f32[136,256]{1,0:T(8,128)S(1)}, f32[136,256]{1,0:T(8,128)S(1)}, u32[]{:S(2)}, u32[]{:S(2)}) collective-permute-start(f32[136,256]{1,0:T(8,128)S(1)} %get-tuple-element.41), channel_id=1, source_target_pairs={{0,64},{1,65},{64,0},{65,1},{2,66},{3,67},{66,2},{67,3},{4,68},{5,... | collective-permute-start | bytes 417800 | tf_op jit(solution)/shard_map/ppermute | solution.py:362
  11.2 4.7 %collective-permute-start.2 = (f32[96,128]{1,0:T(8,128)S(1)}, f32[96,128]{1,0:T(8,128)S(1)}, u32[]{:S(2)}, u32[]{:S(2)}) collective-permute-start(f32[96,128]{1,0:T(8,128)S(1)} %get-tuple-element.43.refs_0_), channel_id=1, source_target_pairs={{0,16},{8,24},{16,0},{24,8},{1,17},{9,25},{17,1},{25,9},{2,18},{10... | collective-permute-start | bytes 147464 | tf_op jit(solution)/shard_map/ppermute | solution.py:362
  13.9 3.2 %collective-permute-start.3 = (f32[96,128]{1,0:T(8,128)S(1)}, f32[96,128]{1,0:T(8,128)S(1)}, u32[]{:S(2)}, u32[]{:S(2)}) collective-permute-start(f32[96,128]{1,0:T(8,128)S(1)} %get-tuple-element.43.refs_0_), channel_id=1, source_target_pairs={{0,8},{8,0},{16,24},{24,16},{1,9},{9,1},{17,25},{25,17},{2,10},{10... | collective-permute-start | bytes 147464 | tf_op jit(solution)/shard_map/ppermute | solution.py:362
  14.2 4.2 %collective-permute-start.4 = (f32[96,128]{1,0:T(8,128)S(1)}, f32[96,128]{1,0:T(8,128)S(1)}, u32[]{:S(2)}, u32[]{:S(2)}) collective-permute-start(f32[96,128]{1,0:T(8,128)S(1)} %get-tuple-element.43.refs_0_), channel_id=1, source_target_pairs={{0,24},{8,16},{16,8},{24,0},{1,25},{9,17},{17,9},{25,1},{2,26},{10... | collective-permute-start | bytes 147464 | tf_op jit(solution)/shard_map/ppermute | solution.py:362
  18.4 21.1 %collective-permute-start.10 = (f32[768,128]{1,0:T(8,128)S(1)}, f32[768,128]{1,0:T(8,128)}, u32[]{:S(2)}, u32[]{:S(2)}) collective-permute-start(f32[768,128]{1,0:T(8,128)S(1)} %collective-permute-done.refs_2_), channel_id=1, source_target_pairs={{0,4},{2,6},{4,0},{6,2},{1,5},{3,7},{5,1},{7,3},{8,12},{10,14},{12... | collective-permute-start | bytes 1179656 | tf_op jit(solution)/shard_map/ppermute | solution.py:362
  21.3 18.6 %collective-permute-start.8 = (f32[768,128]{1,0:T(8,128)S(1)}, f32[768,128]{1,0:T(8,128)}, u32[]{:S(2)}, u32[]{:S(2)}) collective-permute-start(f32[768,128]{1,0:T(8,128)S(1)} %collective-permute-done.refs_2_), channel_id=1, source_target_pairs={{0,2},{2,0},{4,6},{6,4},{1,3},{3,1},{5,7},{7,5},{8,10},{10,8},{12,... | collective-permute-start | bytes 1179656 | tf_op jit(solution)/shard_map/ppermute | solution.py:362
  21.7 18.2 %collective-permute-start.9 = (f32[768,128]{1,0:T(8,128)S(1)}, f32[768,128]{1,0:T(8,128)}, u32[]{:S(2)}, u32[]{:S(2)}) collective-permute-start(f32[768,128]{1,0:T(8,128)S(1)} %collective-permute-done.refs_2_), channel_id=1, source_target_pairs={{0,6},{2,4},{4,2},{6,0},{1,7},{3,5},{5,3},{7,1},{8,14},{10,12},{12... | collective-permute-start | bytes 1179656 | tf_op jit(solution)/shard_map/ppermute | solution.py:362
  23.6 5.6 %collective-permute-start.6 = (f32[136,256]{1,0:T(8,128)S(1)}, f32[136,256]{1,0:T(8,128)S(1)}, u32[]{:S(2)}, u32[]{:S(2)}) collective-permute-start(f32[136,256]{1,0:T(8,128)S(1)} %get-tuple-element.54), channel_id=1, source_target_pairs={{0,1},{1,0},{64,65},{65,64},{2,3},{3,2},{66,67},{67,66},{4,5},{5,4... | collective-permute-start | bytes 417800 | tf_op jit(solution)/shard_map/ppermute | solution.py:362
  25.3 5.9 %collective-permute-start.7 = (f32[136,256]{1,0:T(8,128)S(1)}, f32[136,256]{1,0:T(8,128)S(1)}, u32[]{:S(2)}, u32[]{:S(2)}) collective-permute-start(f32[136,256]{1,0:T(8,128)S(1)} %get-tuple-element.55), channel_id=1, source_target_pairs={{0,65},{1,64},{64,1},{65,0},{2,67},{3,66},{66,3},{67,2},{4,69},{5,... | collective-permute-start | bytes 417800 | tf_op jit(solution)/shard_map/ppermute | solution.py:362
  33.0 42.3 %all-to-all-start = ((f32[32,72,128]{2,1,0:T(8,128)}), f32[32,72,128]{2,1,0:T(8,128)S(1)}, u32[]{:S(2)}, u32[]{:S(2)}) async-start(f32[32,72,128]{2,1,0:T(8,128)} %shard_map.109), calls=%async_computation | async-start | bytes 2359296 | tf_op jit(solution)/shard_map/all_to_all | solution.py:458
  54.2 4.7 %collective-permute-start.12 = (f32[4,32,128]{2,1,0:T(8,128)S(1)}, f32[4,32,128]{2,1,0:T(8,128)S(1)}, u32[]{:S(2)}, u32[]{:S(2)}) collective-permute-start(f32[4,32,128]{2,1,0:T(8,128)S(1)} %add_add_fusion.4), channel_id=1, source_target_pairs={{0,16},{8,24},{16,0},{24,8},{1,17},{9,25},{17,1},{25,9},{2,18},{10... | collective-permute-start | bytes 196616 | tf_op jit(solution)/shard_map/ppermute | solution.py:362
  56.8 3.5 %collective-permute-start.13 = (f32[4,32,128]{2,1,0:T(8,128)S(1)}, f32[4,32,128]{2,1,0:T(8,128)S(1)}, u32[]{:S(2)}, u32[]{:S(2)}) collective-permute-start(f32[4,32,128]{2,1,0:T(8,128)S(1)} %add_add_fusion.4), channel_id=1, source_target_pairs={{0,8},{8,0},{16,24},{24,16},{1,9},{9,1},{17,25},{25,17},{2,10},{10... | collective-permute-start | bytes 196616 | tf_op jit(solution)/shard_map/ppermute | solution.py:362
  57.1 4.3 %collective-permute-start.14 = (f32[4,32,128]{2,1,0:T(8,128)S(1)}, f32[4,32,128]{2,1,0:T(8,128)S(1)}, u32[]{:S(2)}, u32[]{:S(2)}) collective-permute-start(f32[4,32,128]{2,1,0:T(8,128)S(1)} %add_add_fusion.4), channel_id=1, source_target_pairs={{0,24},{8,16},{16,8},{24,0},{1,25},{9,17},{17,9},{25,1},{2,26},{10... | collective-permute-start | bytes 196616 | tf_op jit(solution)/shard_map/ppermute | solution.py:362
  62.1 3.0 %collective-permute-start.15 = (f32[4,32,128]{2,1,0:T(8,128)S(1)}, f32[4,32,128]{2,1,0:T(8,128)S(1)}, u32[]{:S(2)}, u32[]{:S(2)}) collective-permute-start(f32[4,32,128]{2,1,0:T(8,128)S(1)} %get-tuple-element.66.own), channel_id=1, source_target_pairs={{0,32},{32,0},{1,33},{33,1},{2,34},{34,2},{3,35},{35,3},{4,36},{36... | collective-permute-start | bytes 196616 | tf_op jit(solution)/shard_map/ppermute | solution.py:362
  65.9 6.3 %collective-permute-start.16 = (f32[64,512]{1,0:T(8,128)S(1)}, f32[64,512]{1,0:T(8,128)S(1)}, u32[]{:S(2)}, u32[]{:S(2)}) collective-permute-start(f32[64,512]{1,0:T(8,128)S(1)} %get-tuple-element.72), channel_id=1, source_target_pairs={{0,4},{2,6},{4,0},{6,2},{1,5},{3,7},{5,1},{7,3},{8,12},{10,14},{12... | collective-permute-start | bytes 393224 | tf_op jit(solution)/shard_map/ppermute | solution.py:362
  68.7 6.4 %collective-permute-start.17 = (f32[64,512]{1,0:T(8,128)S(1)}, f32[64,512]{1,0:T(8,128)S(1)}, u32[]{:S(2)}, u32[]{:S(2)}) collective-permute-start(f32[64,512]{1,0:T(8,128)S(1)} %get-tuple-element.73), channel_id=1, source_target_pairs={{0,2},{2,0},{4,6},{6,4},{1,3},{3,1},{5,7},{7,5},{8,10},{10,8},{12,... | collective-permute-start | bytes 393224 | tf_op jit(solution)/shard_map/ppermute | solution.py:362
  69.0 6.2 %collective-permute-start.18 = (f32[64,512]{1,0:T(8,128)S(1)}, f32[64,512]{1,0:T(8,128)S(1)}, u32[]{:S(2)}, u32[]{:S(2)}) collective-permute-start(f32[64,512]{1,0:T(8,128)S(1)} %get-tuple-element.74), channel_id=1, source_target_pairs={{0,6},{2,4},{4,2},{6,0},{1,7},{3,5},{5,3},{7,1},{8,14},{10,12},{12... | collective-permute-start | bytes 393224 | tf_op jit(solution)/shard_map/ppermute | solution.py:362
  75.3 5.4 %collective-permute-start.19 = (f32[64,512]{1,0:T(8,128)S(1)}, f32[64,512]{1,0:T(8,128)S(1)}, u32[]{:S(2)}, u32[]{:S(2)}) collective-permute-start(f32[64,512]{1,0:T(8,128)S(1)} %add_multiply_fusion), channel_id=1, source_target_pairs={{0,64},{1,65},{64,0},{65,1},{2,66},{3,67},{66,2},{67,3},{4,68},{5,... | collective-permute-start | bytes 393224 | tf_op jit(solution)/shard_map/ppermute | solution.py:362
  76.5 5.6 %collective-permute-start.20 = (f32[64,512]{1,0:T(8,128)S(1)}, f32[64,512]{1,0:T(8,128)S(1)}, u32[]{:S(2)}, u32[]{:S(2)}) collective-permute-start(f32[64,512]{1,0:T(8,128)S(1)} %add_multiply_fusion), channel_id=1, source_target_pairs={{0,1},{1,0},{64,65},{65,64},{2,3},{3,2},{66,67},{67,66},{4,5},{5,4... | collective-permute-start | bytes 393224 | tf_op jit(solution)/shard_map/ppermute | solution.py:362
  77.1 6.2 %collective-permute-start.21 = (f32[64,512]{1,0:T(8,128)S(1)}, f32[64,512]{1,0:T(8,128)S(1)}, u32[]{:S(2)}, u32[]{:S(2)}) collective-permute-start(f32[64,512]{1,0:T(8,128)S(1)} %add_multiply_fusion), channel_id=1, source_target_pairs={{0,65},{1,64},{64,1},{65,0},{2,67},{3,66},{66,3},{67,2},{4,69},{5,... | collective-permute-start | bytes 393224 | tf_op jit(solution)/shard_map/ppermute | solution.py:362
  85.0 3.3 %collective-permute-start.22 = (f32[64,256]{1,0:T(8,128)S(1)}, f32[64,256]{1,0:T(8,128)S(1)}, u32[]{:S(2)}, u32[]{:S(2)}) collective-permute-start(f32[64,256]{1,0:T(8,128)S(1)} %shard_map.111), channel_id=1, source_target_pairs={{0,32},{32,0},{1,33},{33,1},{2,34},{34,2},{3,35},{35,3},{4,36},{36... | collective-permute-start | bytes 196616 | tf_op jit(solution)/shard_map/ppermute | solution.py:362
  88.3 5.4 %collective-permute-start.23 = (f32[64,256]{1,0:T(8,128)S(1)}, f32[64,256]{1,0:T(8,128)S(1)}, u32[]{:S(2)}, u32[]{:S(2)}) collective-permute-start(f32[64,256]{1,0:T(8,128)S(1)} %add.82), channel_id=1, source_target_pairs={{0,4},{2,6},{4,0},{6,2},{1,5},{3,7},{5,1},{7,3},{8,12},{10,14},{12... | collective-permute-start | bytes 196616 | tf_op jit(solution)/shard_map/ppermute | solution.py:362
  91.5 3.5 %collective-permute-start.24 = (f32[64,256]{1,0:T(8,128)S(1)}, f32[64,256]{1,0:T(8,128)S(1)}, u32[]{:S(2)}, u32[]{:S(2)}) collective-permute-start(f32[64,256]{1,0:T(8,128)S(1)} %add.82), channel_id=1, source_target_pairs={{0,2},{2,0},{4,6},{6,4},{1,3},{3,1},{5,7},{7,5},{8,10},{10,8},{12,... | collective-permute-start | bytes 196616 | tf_op jit(solution)/shard_map/ppermute | solution.py:362
  91.8 4.3 %collective-permute-start.25 = (f32[64,256]{1,0:T(8,128)S(1)}, f32[64,256]{1,0:T(8,128)S(1)}, u32[]{:S(2)}, u32[]{:S(2)}) collective-permute-start(f32[64,256]{1,0:T(8,128)S(1)} %add.82), channel_id=1, source_target_pairs={{0,6},{2,4},{4,2},{6,0},{1,7},{3,5},{5,3},{7,1},{8,14},{10,12},{12... | collective-permute-start | bytes 196616 | tf_op jit(solution)/shard_map/ppermute | solution.py:362
  96.2 4.7 %collective-permute-start.26 = (f32[64,256]{1,0:T(8,128)S(1)}, f32[64,256]{1,0:T(8,128)S(1)}, u32[]{:S(2)}, u32[]{:S(2)}) collective-permute-start(f32[64,256]{1,0:T(8,128)S(1)} %add_add_fusion.2), channel_id=1, source_target_pairs={{0,16},{8,24},{16,0},{24,8},{1,17},{9,25},{17,1},{25,9},{2,18},{10... | collective-permute-start | bytes 196616 | tf_op jit(solution)/shard_map/ppermute | solution.py:362
  96.9 3.9 %collective-permute-start.27 = (f32[64,256]{1,0:T(8,128)S(1)}, f32[64,256]{1,0:T(8,128)S(1)}, u32[]{:S(2)}, u32[]{:S(2)}) collective-permute-start(f32[64,256]{1,0:T(8,128)S(1)} %add_add_fusion.2), channel_id=1, source_target_pairs={{0,8},{8,0},{16,24},{24,16},{1,9},{9,1},{17,25},{25,17},{2,10},{10... | collective-permute-start | bytes 196616 | tf_op jit(solution)/shard_map/ppermute | solution.py:362
  97.4 4.3 %collective-permute-start.28 = (f32[64,256]{1,0:T(8,128)S(1)}, f32[64,256]{1,0:T(8,128)S(1)}, u32[]{:S(2)}, u32[]{:S(2)}) collective-permute-start(f32[64,256]{1,0:T(8,128)S(1)} %add_add_fusion.2), channel_id=1, source_target_pairs={{0,24},{8,16},{16,8},{24,0},{1,25},{9,17},{17,9},{25,1},{2,26},{10... | collective-permute-start | bytes 196616 | tf_op jit(solution)/shard_map/ppermute | solution.py:362
  102.8 5.4 %collective-permute-start.29 = (f32[64,512]{1,0:T(8,128)S(1)}, f32[64,512]{1,0:T(8,128)S(1)}, u32[]{:S(2)}, u32[]{:S(2)}) collective-permute-start(f32[64,512]{1,0:T(8,128)S(1)} %shard_map.112), channel_id=1, source_target_pairs={{0,64},{1,65},{64,0},{65,1},{2,66},{3,67},{66,2},{67,3},{4,68},{5,... | collective-permute-start | bytes 393224 | tf_op jit(solution)/shard_map/ppermute | solution.py:362
  104.1 4.4 %collective-permute-start.30 = (f32[64,512]{1,0:T(8,128)S(1)}, f32[64,512]{1,0:T(8,128)S(1)}, u32[]{:S(2)}, u32[]{:S(2)}) collective-permute-start(f32[64,512]{1,0:T(8,128)S(1)} %shard_map.112), channel_id=1, source_target_pairs={{0,1},{1,0},{64,65},{65,64},{2,3},{3,2},{66,67},{67,66},{4,5},{5,4... | collective-permute-start | bytes 393224 | tf_op jit(solution)/shard_map/ppermute | solution.py:362
  104.7 5.0 %collective-permute-start.31 = (f32[64,512]{1,0:T(8,128)S(1)}, f32[64,512]{1,0:T(8,128)S(1)}, u32[]{:S(2)}, u32[]{:S(2)}) collective-permute-start(f32[64,512]{1,0:T(8,128)S(1)} %shard_map.112), channel_id=1, source_target_pairs={{0,65},{1,64},{64,1},{65,0},{2,67},{3,66},{66,3},{67,2},{4,69},{5,... | collective-permute-start | bytes 393224 | tf_op jit(solution)/shard_map/ppermute | solution.py:362
  109.8 6.5 %collective-permute-start.32 = (f32[64,512]{1,0:T(8,128)S(1)}, f32[64,512]{1,0:T(8,128)S(1)}, u32[]{:S(2)}, u32[]{:S(2)}) collective-permute-start(f32[64,512]{1,0:T(8,128)S(1)} %add_subtract_fusion), channel_id=1, source_target_pairs={{0,32},{32,0},{1,33},{33,1},{2,34},{34,2},{3,35},{35,3},{4,36},{36... | collective-permute-start | bytes 393224 | tf_op jit(solution)/shard_map/ppermute | solution.py:362
  (3 other events, 29.4 us)

commit v13 on v12

--- a/solution.py
+++ b/solution.py
@@ -280,7 +280,9 @@
     return points[:, group * j : group * (j + 1), :].reshape(peers * group, 128)
 
 
-def points_hot(points, blocks, tables, width):
+def gather_body(points, summed, *, tables):
+    cdev, part = summed.shape[0], summed.shape[1] // 2
+    blocks = part // 128
     peers, lanes = points.shape[0], 128 // tables
     offs = points[:, CAP * tables * blocks :, :]
     offs = jnp.concatenate(
@@ -289,38 +291,32 @@
             for t in range(tables)
         ],
         axis=1,
-    ).reshape(peers * CAP * tables, 128)
-    lane = lax.broadcasted_iota(jnp.int32, offs.shape, 1).astype(F32)
-    return jnp.concatenate(
-        [(offs == lane + float(128 * k)).astype(BF) for k in range(width // 128)], axis=1
-    )
-
-
-def coeff_body(points, grads, coeff, *, tables):
+    ).reshape(peers * CAP * tables, 128).T
+    center = lax.broadcasted_iota(jnp.int32, offs.shape, 0).astype(F32)
+    hot = jnp.concatenate(
+        [(offs == center + float(128 * k)).astype(BF) for k in range(cdev // 128)], axis=0
+    )
+    for j in range(blocks):
+        hi, lo = split2(pick(hot, block_of(points, j, tables), NN))
+        summed[:, 128 * j : 128 * (j + 1)] = hi
+        summed[:, part + 128 * j : part + 128 * (j + 1)] = lo
+
+
+def coeff_body(summed, grads, coeff):
     out, part = coeff.shape
-    blocks = part // 128
-    hot = points_hot(points, blocks, tables, grads.shape[1])
-    g1, g2 = split2(pick(hot, grads[...], NT, flip=True))
-    gg = jnp.concatenate([g1, g2], axis=0)
-    for j in range(blocks):
-        e1, e2 = split2(block_of(points, j, tables))
-        both = mm(gg, e1, NN) + mm(gg, e2, NN)
-        coeff[:, 128 * j : 128 * (j + 1)] = both[:out] + both[out:]
-
-
-def corr_body(member, points, coeff, eig_scale, corr, *, tables):
+    g1, g2 = split2(grads[...])
+    both = mm(jnp.concatenate([g1, g2], axis=0), summed[...], NN)
+    both = both[:out] + both[out:]
+    coeff[...] = both[:, :part] + both[:, part:]
+
+
+def corr_body(member, summed, coeff, eig_scale, corr):
     out, part = coeff.shape
-    blocks = part // 128
-    hot = points_hot(points, blocks, tables, corr.shape[1])
-    total = jnp.zeros((2 * out, hot.shape[0]), F32)
-    for j in range(blocks):
-        at = slice(128 * j, 128 * (j + 1))
-        e1, e2 = split2(block_of(points, j, tables))
-        scale = eig_scale[:, pl.ds(pl.multiple_of(member[0] * part + 128 * j, 128), 128)]
-        c1, c2 = split2(coeff[:, at] * scale)
-        cc = jnp.concatenate([c1, c2], axis=0)
-        total = total + mm(cc, e1, NT) + mm(cc, e2, NT)
-    corr[...] = pick(hot, total[:out] + total[out:], NN, flip=True)
+    scale = eig_scale[:, pl.ds(pl.multiple_of(member[0] * part, part), part)]
+    c1, c2 = split2(coeff[...] * scale)
+    cc = jnp.concatenate([c1, c2], axis=0)
+    both = mm(cc, summed[:, :part], NT) + mm(cc, summed[:, part:], NT)
+    corr[...] = both[:out] + both[out:]
 
 
 def shape(*dims, dtype=F32):
@@ -475,16 +471,19 @@
     parts = [parts[TILES.index(o)] for o in range(ny)]
     grads = add_up(parts, ("y",)) * sb[0:1]
     points, grads = together(points, grads)
+    summed = call(
+        functools.partial(gather_body, tables=tables),
+        shape(cdev, 2 * q // tables, dtype=BF), points,
+        cost_estimate=pl.CostEstimate(
+            flops=800_000_000, bytes_accessed=1 << 21, transcendentals=0
+        ),
+    )
     grads = exchange(grads, PLANES)
-    coeff = call(
-        functools.partial(coeff_body, tables=tables), shape(out, q // tables), points, grads
-    )
+    coeff = call(coeff_body, shape(out, q // tables), summed, grads)
     for axis in OWNERS[::-1]:
         coeff = exchange(coeff, (axis,))
     corr = call(
-        functools.partial(corr_body, tables=tables),
-        shape(out, cdev), member, points, coeff, eig_scale[None, :],
-        scalars=1,
+        corr_body, shape(out, cdev), member, summed, coeff, eig_scale[None, :], scalars=1
     )
     update = exchange(corr, PLANES) - grads
     (swapped,) = mates([update] * 2, ("core",))

time: 117 us -> 115 us (0.983)
  waiting for transfers between devices: 35 us -> 33 us
    ppermute x32, waiting for transfers between devices: 35 us -> 33 us  [mate_of(): return lax.ppermute(v, axes, [(i, i ^ o) for i in range(n)])]
    pallas_call x8 -> x9, Pallas kernels: 22.6 us -> 22.5 us  [call(): pl.pallas_call(body, out_shape=outs, in_specs=[smem] * scalars + [VMEM] *...]
  transfers between devices with their start and end apart: 34 -> 34, of which waited for: 27 -> 27; matrix products, arithmetic and copies ran while one was open for 0% -> 0% of each run, Pallas kernels for 17% -> 19%
where the time goes in v13:
time: 115 us
  starting transfers between devices  55.4 us (48%)
  waiting for transfers between devices  33 us (29%)
  Pallas kernels  24.7 us (21%)
    ppermute x32, starting transfers between devices, mate_of(): return lax.ppermute(v, axes, [(i, i ^ o) for i in range(n)])  43.9 us
    ppermute x32, waiting for transfers between devices, mate_of(): return lax.ppermute(v, axes, [(i, i ^ o) for i in range(n)])  33 us
    pallas_call x9, Pallas kernels, call(): pl.pallas_call(body, out_shape=outs, in_specs=[smem] * scalars + [VMEM] *...  22.5 us
    all_to_all x1, starting transfers between devices, per_device(): lax.all_to_all(points, OWNERS, split_axis=0, concat_axis=0, tiled=True)  6.56 us
    ppermute x1, starting transfers between devices, per_device(): tile = lax.ppermute(pack, ('core', 'zl'), [(0, 0), (2, 1), (1, 2), (3, 3)])  4.93 us
  transfers between devices with their start and end apart: 34, of which 27 were waited for; matrix products, arithmetic and copies ran while one was open for 0% of the time, Pallas kernels for 19%

profile of v13, /device:TPU:1, one launch (start us, length us, event | category | flops | bytes accessed | tf_op | source)
XLA Modules:
  0.0 114.9 jit_solution(15341669816822465843)
XLA Ops:
  0.6 2.2 %shard_map.104 = (f32[96,128]{1,0:T(8,128)S(1)}, f32[768,128]{1,0:T(8,128)S(1)}, f32[136,256]{1,0:T(8,128)S(1)}, f32[136,256]{1,0:T(8,128)S(1)}, f32[136,256]{1,0:T(8,128)S(1)}, /*index=5*/f32[136,256]{1,0:T(8,128)S(1)}) custom-call(s32[1]{0:T(128)} %bitcast.1.member, s32[1,64]{1,0:T(1,128)} %bitcast.15, f32[1024,128]{1,0:T(8,128)} %refs_1_.1, ...), custom_call_target="tpu_custom_call" | custom-call | tf_op jit(solution)/shard_map/pallas_call | solution.py:382
  2.9 4.9 %collective-permute-start = (f32[768,128]{1,0:T(8,128)S(1)}, f32[768,128]{1,0:T(8,128)S(1)}, u32[]{:S(2)}, u32[]{:S(2)}) collective-permute-start(f32[768,128]{1,0:T(8,128)S(1)} %get-tuple-element.40), channel_id=1, source_target_pairs={{0,0},{32,1},{1,32},{33,33},{2,2},{34,3},{3,34},{35,35},{4,4},{36,... | collective-permute-start | bytes 1179656 | tf_op jit(solution)/shard_map/ppermute | solution.py:412
  7.8 3.4 %collective-permute-start.1 = (f32[136,256]{1,0:T(8,128)S(1)}, f32[136,256]{1,0:T(8,128)S(1)}, u32[]{:S(2)}, u32[]{:S(2)}) collective-permute-start(f32[136,256]{1,0:T(8,128)S(1)} %get-tuple-element.41), channel_id=1, source_target_pairs={{0,64},{1,65},{64,0},{65,1},{2,66},{3,67},{66,2},{67,3},{4,68},{5,... | collective-permute-start | bytes 417800 | tf_op jit(solution)/shard_map/ppermute | solution.py:358
  11.2 2.7 %collective-permute-start.2 = (f32[96,128]{1,0:T(8,128)S(1)}, f32[96,128]{1,0:T(8,128)S(1)}, u32[]{:S(2)}, u32[]{:S(2)}) collective-permute-start(f32[96,128]{1,0:T(8,128)S(1)} %get-tuple-element.43.refs_0_), channel_id=1, source_target_pairs={{0,16},{8,24},{16,0},{24,8},{1,17},{9,25},{17,1},{25,9},{2,18},{10... | collective-permute-start | bytes 147464 | tf_op jit(solution)/shard_map/ppermute | solution.py:358
  15.9 1.3 %collective-permute-done.3.refs_2_ = f32[96,128]{1,0:T(8,128)S(1)} collective-permute-done((f32[96,128]{1,0:T(8,128)S(1)}, f32[96,128]{1,0:T(8,128)S(1)}, u32[]{:S(2)}, u32[]{:S(2)}) %collective-permute-start.3) | collective-permute-done | bytes 49184 | tf_op jit(solution)/shard_map/ppermute | solution.py:358
  18.4 2.9 %collective-permute-start.10 = (f32[768,128]{1,0:T(8,128)S(1)}, f32[768,128]{1,0:T(8,128)}, u32[]{:S(2)}, u32[]{:S(2)}) collective-permute-start(f32[768,128]{1,0:T(8,128)S(1)} %collective-permute-done.refs_2_), channel_id=1, source_target_pairs={{0,4},{2,6},{4,0},{6,2},{1,5},{3,7},{5,1},{7,3},{8,12},{10,14},{12... | collective-permute-start | bytes 1179656 | tf_op jit(solution)/shard_map/ppermute | solution.py:358
  22.3 1.3 %collective-permute-done.5.refs_1_ = f32[4,96,128]{2,1,0:T(8,128)S(1)} collective-permute-done((f32[4,96,128]{2,1,0:T(8,128)S(1)}, f32[4,96,128]{2,1,0:T(8,128)S(1)}, u32[]{:S(2)}, u32[]{:S(2)}) %collective-permute-start.5) | collective-permute-done | bytes 196640 | tf_op jit(solution)/shard_map/ppermute | solution.py:358
  23.6 1.7 %collective-permute-start.6 = (f32[136,256]{1,0:T(8,128)S(1)}, f32[136,256]{1,0:T(8,128)S(1)}, u32[]{:S(2)}, u32[]{:S(2)}) collective-permute-start(f32[136,256]{1,0:T(8,128)S(1)} %get-tuple-element.54), channel_id=1, source_target_pairs={{0,1},{1,0},{64,65},{65,64},{2,3},{3,2},{66,67},{67,66},{4,5},{5,4... | collective-permute-start | bytes 417800 | tf_op jit(solution)/shard_map/ppermute | solution.py:358
  25.3 3.9 %shard_map.106 = (bf16[1,512,512]{2,1,0:T(8,128)(2,1)S(1)}, bf16[1,512,512]{2,1,0:T(8,128)(2,1)S(1)}, f32[4,32,128]{2,1,0:T(8,128)S(1)}, f32[4,32,128]{2,1,0:T(8...) custom-call(f32[4,96,128]{2,1,0:T(8,128)S(1)} %shard_map.105.refs_0_.own, ...), custom_call_target="tpu_custom_call" | custom-call | flops 100000000 | bytes 65536 | tf_op jit(solution)/shard_map/pallas_call | solution.py:333
  29.2 2.0 %collective-permute-done.7.refs_3_ = f32[136,256]{1,0:T(8,128)S(1)} collective-permute-done((f32[136,256]{1,0:T(8,128)S(1)}, f32[136,256]{1,0:T(8,128)S(1)}, u32[]{:S(2)}, u32[]{:S(2)}) %collective-permute-start.7) | collective-permute-done | bytes 139296 | tf_op jit(solution)/shard_map/ppermute | solution.py:358
  31.2 1.7 %shard_map.109 = f32[32,72,128]{2,1,0:T(8,128)} custom-call(f32[136,256]{1,0:T(8,128)S(1)} %get-tuple-element.62.refs_0_, f32[136,256]{1,0:T(8,128)S(1)} %collective-permute-done.1.refs_1_, f32[136,256]{1,0:T(8,128)S(1)} %collective-permute-done.6.refs_2_, f32[136,256]{1,0:T(8,128)S(1)} %collective-permute-done.7.refs_3_), custom_call_target="tpu_custom_call" | custom-call | tf_op jit(solution)/shard_map/pallas_call | solution.py:333
  33.0 6.6 %all-to-all-start = ((f32[32,72,128]{2,1,0:T(8,128)}), f32[32,72,128]{2,1,0:T(8,128)S(1)}, u32[]{:S(2)}, u32[]{:S(2)}) async-start(f32[32,72,128]{2,1,0:T(8,128)} %shard_map.109), calls=%async_computation | async-start | bytes 2359296 | tf_op jit(solution)/shard_map/all_to_all | solution.py:454
  40.0 12.8 %shard_map.107 = (bf16[3,512,512]{2,1,0:T(8,128)(2,1)S(1)}, bf16[3,512,512]{2,1,0:T(8,128)(2,1)S(1)}, f32[4,32,128]{2,1,0:T(8,128)S(1)}, f32[4,32,128]{2,1,0:T(8,128)S(1)}) custom-call(f32[4,96,128]{2,1,0:T(8,128)S(1)} %shard_map.105.refs_0_.own, f32[4,96,128]{2,1,0:T(8,128)S(1)} %collective-permute-done.5.refs_1_, ...), custom_call_target="tpu_custom_call" | custom-call | flops 30000001024 | bytes 65536 | tf_op jit(solution)/shard_map/pallas_call | solution.py:333
  54.2 2.6 %collective-permute-start.12 = (f32[4,32,128]{2,1,0:T(8,128)S(1)}, f32[4,32,128]{2,1,0:T(8,128)S(1)}, u32[]{:S(2)}, u32[]{:S(2)}) collective-permute-start(f32[4,32,128]{2,1,0:T(8,128)S(1)} %add_add_fusion.4), channel_id=1, source_target_pairs={{0,16},{8,24},{16,0},{24,8},{1,17},{9,25},{17,1},{25,9},{2,18},{10... | collective-permute-start | bytes 196616 | tf_op jit(solution)/shard_map/ppermute | solution.py:358
  58.9 1.3 %collective-permute-done.13 = f32[4,32,128]{2,1,0:T(8,128)S(1)} collective-permute-done((f32[4,32,128]{2,1,0:T(8,128)S(1)}, f32[4,32,128]{2,1,0:T(8,128)S(1)}, u32[]{:S(2)}, u32[]{:S(2)}) %collective-permute-start.13) | collective-permute-done | bytes 65568 | tf_op jit(solution)/shard_map/ppermute | solution.py:358
  62.1 2.1 %collective-permute-start.15 = (f32[4,32,128]{2,1,0:T(8,128)S(1)}, f32[4,32,128]{2,1,0:T(8,128)S(1)}, u32[]{:S(2)}, u32[]{:S(2)}) collective-permute-start(f32[4,32,128]{2,1,0:T(8,128)S(1)} %get-tuple-element.66.own), channel_id=1, source_target_pairs={{0,32},{32,0},{1,33},{33,1},{2,34},{34,2},{3,35},{35,3},{4,36},{36... | collective-permute-start | bytes 196616 | tf_op jit(solution)/shard_map/ppermute | solution.py:358
  65.9 2.8 %collective-permute-start.16 = (f32[64,512]{1,0:T(8,128)S(1)}, f32[64,512]{1,0:T(8,128)S(1)}, u32[]{:S(2)}, u32[]{:S(2)}) collective-permute-start(f32[64,512]{1,0:T(8,128)S(1)} %get-tuple-element.72), channel_id=1, source_target_pairs={{0,4},{2,6},{4,0},{6,2},{1,5},{3,7},{5,1},{7,3},{8,12},{10,14},{12... | collective-permute-start | bytes 393224 | tf_op jit(solution)/shard_map/ppermute | solution.py:358
  69.6 2.6 %collective-permute-done.16 = f32[64,512]{1,0:T(8,128)S(1)} collective-permute-done((f32[64,512]{1,0:T(8,128)S(1)}, f32[64,512]{1,0:T(8,128)S(1)}, u32[]{:S(2)}, u32[]{:S(2)}) %collective-permute-start.16) | collective-permute-done | bytes 131104 | tf_op jit(solution)/shard_map/ppermute | solution.py:358
  72.2 2.8 %collective-permute-done.17 = f32[64,512]{1,0:T(8,128)S(1)} collective-permute-done((f32[64,512]{1,0:T(8,128)S(1)}, f32[64,512]{1,0:T(8,128)S(1)}, u32[]{:S(2)}, u32[]{:S(2)}) %collective-permute-start.17) | collective-permute-done | bytes 131104 | tf_op jit(solution)/shard_map/ppermute | solution.py:358
  77.1 1.5 %collective-permute-start.21 = (f32[64,512]{1,0:T(8,128)S(1)}, f32[64,512]{1,0:T(8,128)S(1)}, u32[]{:S(2)}, u32[]{:S(2)}) collective-permute-start(f32[64,512]{1,0:T(8,128)S(1)} %add_multiply_fusion), channel_id=1, source_target_pairs={{0,65},{1,64},{64,1},{65,0},{2,67},{3,66},{66,3},{67,2},{4,69},{5,... | collective-permute-start | bytes 393224 | tf_op jit(solution)/shard_map/ppermute | solution.py:358
  78.6 2.0 %shard_map.111.summed = bf16[512,512]{1,0:T(8,128)(2,1)S(1)} custom-call(f32[32,72,128]{2,1,0:T(8,128)S(1)} %all-to-all-done.points), custom_call_target="tpu_custom_call" | custom-call | flops 800000000 | bytes 2097152 | tf_op jit(solution)/shard_map/pallas_call | solution.py:333
  80.7 1.4 %collective-permute-done.20 = f32[64,512]{1,0:T(8,128)S(1)} collective-permute-done((f32[64,512]{1,0:T(8,128)S(1)}, f32[64,512]{1,0:T(8,128)S(1)}, u32[]{:S(2)}, u32[]{:S(2)}) %collective-permute-start.20) | collective-permute-done | bytes 131104 | tf_op jit(solution)/shard_map/ppermute | solution.py:358
  82.1 1.3 %collective-permute-done.21 = f32[64,512]{1,0:T(8,128)S(1)} collective-permute-done((f32[64,512]{1,0:T(8,128)S(1)}, f32[64,512]{1,0:T(8,128)S(1)}, u32[]{:S(2)}, u32[]{:S(2)}) %collective-permute-start.21) | collective-permute-done | bytes 131104 | tf_op jit(solution)/shard_map/ppermute | solution.py:358
  83.6 2.4 %collective-permute-start.22 = (f32[64,256]{1,0:T(8,128)S(1)}, f32[64,256]{1,0:T(8,128)S(1)}, u32[]{:S(2)}, u32[]{:S(2)}) collective-permute-start(f32[64,256]{1,0:T(8,128)S(1)} %shard_map.112), channel_id=1, source_target_pairs={{0,32},{32,0},{1,33},{33,1},{2,34},{34,2},{3,35},{35,3},{4,36},{36... | collective-permute-start | bytes 196616 | tf_op jit(solution)/shard_map/ppermute | solution.py:358
  86.9 3.3 %collective-permute-start.23 = (f32[64,256]{1,0:T(8,128)S(1)}, f32[64,256]{1,0:T(8,128)S(1)}, u32[]{:S(2)}, u32[]{:S(2)}) collective-permute-start(f32[64,256]{1,0:T(8,128)S(1)} %add.82), channel_id=1, source_target_pairs={{0,4},{2,6},{4,0},{6,2},{1,5},{3,7},{5,1},{7,3},{8,12},{10,14},{12... | collective-permute-start | bytes 196616 | tf_op jit(solution)/shard_map/ppermute | solution.py:358
  90.7 1.6 %collective-permute-done.23 = f32[64,256]{1,0:T(8,128)S(1)} collective-permute-done((f32[64,256]{1,0:T(8,128)S(1)}, f32[64,256]{1,0:T(8,128)S(1)}, u32[]{:S(2)}, u32[]{:S(2)}) %collective-permute-start.23) | collective-permute-done | bytes 65568 | tf_op jit(solution)/shard_map/ppermute | solution.py:358
  92.3 1.3 %collective-permute-done.24 = f32[64,256]{1,0:T(8,128)S(1)} collective-permute-done((f32[64,256]{1,0:T(8,128)S(1)}, f32[64,256]{1,0:T(8,128)S(1)}, u32[]{:S(2)}, u32[]{:S(2)}) %collective-permute-start.24) | collective-permute-done | bytes 65568 | tf_op jit(solution)/shard_map/ppermute | solution.py:358
  96.0 2.1 %collective-permute-start.28 = (f32[64,256]{1,0:T(8,128)S(1)}, f32[64,256]{1,0:T(8,128)S(1)}, u32[]{:S(2)}, u32[]{:S(2)}) collective-permute-start(f32[64,256]{1,0:T(8,128)S(1)} %add_add_fusion.2), channel_id=1, source_target_pairs={{0,24},{8,16},{16,8},{24,0},{1,25},{9,17},{17,9},{25,1},{2,26},{10... | collective-permute-start | bytes 196616 | tf_op jit(solution)/shard_map/ppermute | solution.py:358
  98.2 1.4 %collective-permute-done.26 = f32[64,256]{1,0:T(8,128)S(1)} collective-permute-done((f32[64,256]{1,0:T(8,128)S(1)}, f32[64,256]{1,0:T(8,128)S(1)}, u32[]{:S(2)}, u32[]{:S(2)}) %collective-permute-start.26) | collective-permute-done | bytes 65568 | tf_op jit(solution)/shard_map/ppermute | solution.py:358
  102.5 1.5 %collective-permute-start.31 = (f32[64,512]{1,0:T(8,128)S(1)}, f32[64,512]{1,0:T(8,128)S(1)}, u32[]{:S(2)}, u32[]{:S(2)}) collective-permute-start(f32[64,512]{1,0:T(8,128)S(1)} %shard_map.113), channel_id=1, source_target_pairs={{0,65},{1,64},{64,1},{65,0},{2,67},{3,66},{66,3},{67,2},{4,69},{5,... | collective-permute-start | bytes 393224 | tf_op jit(solution)/shard_map/ppermute | solution.py:358
  104.0 2.1 %collective-permute-done.29 = f32[64,512]{1,0:T(8,128)S(1)} collective-permute-done((f32[64,512]{1,0:T(8,128)S(1)}, f32[64,512]{1,0:T(8,128)S(1)}, u32[]{:S(2)}, u32[]{:S(2)}) %collective-permute-start.29) | collective-permute-done | bytes 131104 | tf_op jit(solution)/shard_map/ppermute | solution.py:358
  107.6 5.6 %collective-permute-start.32 = (f32[64,512]{1,0:T(8,128)S(1)}, f32[64,512]{1,0:T(8,128)S(1)}, u32[]{:S(2)}, u32[]{:S(2)}) collective-permute-start(f32[64,512]{1,0:T(8,128)S(1)} %add_subtract_fusion), channel_id=1, source_target_pairs={{0,32},{32,0},{1,33},{33,1},{2,34},{34,2},{3,35},{35,3},{4,36},{36... | collective-permute-start | bytes 393224 | tf_op jit(solution)/shard_map/ppermute | solution.py:358
  (59 shorter events, 25.0 us)
Async XLA Ops:
  2.9 15.5 %collective-permute-start = (f32[768,128]{1,0:T(8,128)S(1)}, f32[768,128]{1,0:T(8,128)S(1)}, u32[]{:S(2)}, u32[]{:S(2)}) collective-permute-start(f32[768,128]{1,0:T(8,128)S(1)} %get-tuple-element.40), channel_id=1, source_target_pairs={{0,0},{32,1},{1,32},{33,33},{2,2},{34,3},{3,34},{35,35},{4,4},{36,... | collective-permute-start | bytes 1179656 | tf_op jit(solution)/shard_map/ppermute | solution.py:412
  7.8 10.6 %collective-permute-start.1 = (f32[136,256]{1,0:T(8,128)S(1)}, f32[136,256]{1,0:T(8,128)S(1)}, u32[]{:S(2)}, u32[]{:S(2)}) collective-permute-start(f32[136,256]{1,0:T(8,128)S(1)} %get-tuple-element.41), channel_id=1, source_target_pairs={{0,64},{1,65},{64,0},{65,1},{2,66},{3,67},{66,2},{67,3},{4,68},{5,... | collective-permute-start | bytes 417800 | tf_op jit(solution)/shard_map/ppermute | solution.py:358
  11.2 4.7 %collective-permute-start.2 = (f32[96,128]{1,0:T(8,128)S(1)}, f32[96,128]{1,0:T(8,128)S(1)}, u32[]{:S(2)}, u32[]{:S(2)}) collective-permute-start(f32[96,128]{1,0:T(8,128)S(1)} %get-tuple-element.43.refs_0_), channel_id=1, source_target_pairs={{0,16},{8,24},{16,0},{24,8},{1,17},{9,25},{17,1},{25,9},{2,18},{10... | collective-permute-start | bytes 147464 | tf_op jit(solution)/shard_map/ppermute | solution.py:358
  13.9 3.2 %collective-permute-start.3 = (f32[96,128]{1,0:T(8,128)S(1)}, f32[96,128]{1,0:T(8,128)S(1)}, u32[]{:S(2)}, u32[]{:S(2)}) collective-permute-start(f32[96,128]{1,0:T(8,128)S(1)} %get-tuple-element.43.refs_0_), channel_id=1, source_target_pairs={{0,8},{8,0},{16,24},{24,16},{1,9},{9,1},{17,25},{25,17},{2,10},{10... | collective-permute-start | bytes 147464 | tf_op jit(solution)/shard_map/ppermute | solution.py:358
  14.2 4.2 %collective-permute-start.4 = (f32[96,128]{1,0:T(8,128)S(1)}, f32[96,128]{1,0:T(8,128)S(1)}, u32[]{:S(2)}, u32[]{:S(2)}) collective-permute-start(f32[96,128]{1,0:T(8,128)S(1)} %get-tuple-element.43.refs_0_), channel_id=1, source_target_pairs={{0,24},{8,16},{16,8},{24,0},{1,25},{9,17},{17,9},{25,1},{2,26},{10... | collective-permute-start | bytes 147464 | tf_op jit(solution)/shard_map/ppermute | solution.py:358
  18.4 21.1 %collective-permute-start.10 = (f32[768,128]{1,0:T(8,128)S(1)}, f32[768,128]{1,0:T(8,128)}, u32[]{:S(2)}, u32[]{:S(2)}) collective-permute-start(f32[768,128]{1,0:T(8,128)S(1)} %collective-permute-done.refs_2_), channel_id=1, source_target_pairs={{0,4},{2,6},{4,0},{6,2},{1,5},{3,7},{5,1},{7,3},{8,12},{10,14},{12... | collective-permute-start | bytes 1179656 | tf_op jit(solution)/shard_map/ppermute | solution.py:358
  21.3 18.6 %collective-permute-start.8 = (f32[768,128]{1,0:T(8,128)S(1)}, f32[768,128]{1,0:T(8,128)}, u32[]{:S(2)}, u32[]{:S(2)}) collective-permute-start(f32[768,128]{1,0:T(8,128)S(1)} %collective-permute-done.refs_2_), channel_id=1, source_target_pairs={{0,2},{2,0},{4,6},{6,4},{1,3},{3,1},{5,7},{7,5},{8,10},{10,8},{12,... | collective-permute-start | bytes 1179656 | tf_op jit(solution)/shard_map/ppermute | solution.py:358
  21.7 18.2 %collective-permute-start.9 = (f32[768,128]{1,0:T(8,128)S(1)}, f32[768,128]{1,0:T(8,128)}, u32[]{:S(2)}, u32[]{:S(2)}) collective-permute-start(f32[768,128]{1,0:T(8,128)S(1)} %collective-permute-done.refs_2_), channel_id=1, source_target_pairs={{0,6},{2,4},{4,2},{6,0},{1,7},{3,5},{5,3},{7,1},{8,14},{10,12},{12... | collective-permute-start | bytes 1179656 | tf_op jit(solution)/shard_map/ppermute | solution.py:358
  23.6 5.6 %collective-permute-start.6 = (f32[136,256]{1,0:T(8,128)S(1)}, f32[136,256]{1,0:T(8,128)S(1)}, u32[]{:S(2)}, u32[]{:S(2)}) collective-permute-start(f32[136,256]{1,0:T(8,128)S(1)} %get-tuple-element.54), channel_id=1, source_target_pairs={{0,1},{1,0},{64,65},{65,64},{2,3},{3,2},{66,67},{67,66},{4,5},{5,4... | collective-permute-start | bytes 417800 | tf_op jit(solution)/shard_map/ppermute | solution.py:358
  25.3 5.9 %collective-permute-start.7 = (f32[136,256]{1,0:T(8,128)S(1)}, f32[136,256]{1,0:T(8,128)S(1)}, u32[]{:S(2)}, u32[]{:S(2)}) collective-permute-start(f32[136,256]{1,0:T(8,128)S(1)} %get-tuple-element.55), channel_id=1, source_target_pairs={{0,65},{1,64},{64,1},{65,0},{2,67},{3,66},{66,3},{67,2},{4,69},{5,... | collective-permute-start | bytes 417800 | tf_op jit(solution)/shard_map/ppermute | solution.py:358
  33.0 42.3 %all-to-all-start = ((f32[32,72,128]{2,1,0:T(8,128)}), f32[32,72,128]{2,1,0:T(8,128)S(1)}, u32[]{:S(2)}, u32[]{:S(2)}) async-start(f32[32,72,128]{2,1,0:T(8,128)} %shard_map.109), calls=%async_computation | async-start | bytes 2359296 | tf_op jit(solution)/shard_map/all_to_all | solution.py:454
  54.2 4.7 %collective-permute-start.12 = (f32[4,32,128]{2,1,0:T(8,128)S(1)}, f32[4,32,128]{2,1,0:T(8,128)S(1)}, u32[]{:S(2)}, u32[]{:S(2)}) collective-permute-start(f32[4,32,128]{2,1,0:T(8,128)S(1)} %add_add_fusion.4), channel_id=1, source_target_pairs={{0,16},{8,24},{16,0},{24,8},{1,17},{9,25},{17,1},{25,9},{2,18},{10... | collective-permute-start | bytes 196616 | tf_op jit(solution)/shard_map/ppermute | solution.py:358
  56.8 3.5 %collective-permute-start.13 = (f32[4,32,128]{2,1,0:T(8,128)S(1)}, f32[4,32,128]{2,1,0:T(8,128)S(1)}, u32[]{:S(2)}, u32[]{:S(2)}) collective-permute-start(f32[4,32,128]{2,1,0:T(8,128)S(1)} %add_add_fusion.4), channel_id=1, source_target_pairs={{0,8},{8,0},{16,24},{24,16},{1,9},{9,1},{17,25},{25,17},{2,10},{10... | collective-permute-start | bytes 196616 | tf_op jit(solution)/shard_map/ppermute | solution.py:358
  57.1 4.3 %collective-permute-start.14 = (f32[4,32,128]{2,1,0:T(8,128)S(1)}, f32[4,32,128]{2,1,0:T(8,128)S(1)}, u32[]{:S(2)}, u32[]{:S(2)}) collective-permute-start(f32[4,32,128]{2,1,0:T(8,128)S(1)} %add_add_fusion.4), channel_id=1, source_target_pairs={{0,24},{8,16},{16,8},{24,0},{1,25},{9,17},{17,9},{25,1},{2,26},{10... | collective-permute-start | bytes 196616 | tf_op jit(solution)/shard_map/ppermute | solution.py:358
  62.1 3.0 %collective-permute-start.15 = (f32[4,32,128]{2,1,0:T(8,128)S(1)}, f32[4,32,128]{2,1,0:T(8,128)S(1)}, u32[]{:S(2)}, u32[]{:S(2)}) collective-permute-start(f32[4,32,128]{2,1,0:T(8,128)S(1)} %get-tuple-element.66.own), channel_id=1, source_target_pairs={{0,32},{32,0},{1,33},{33,1},{2,34},{34,2},{3,35},{35,3},{4,36},{36... | collective-permute-start | bytes 196616 | tf_op jit(solution)/shard_map/ppermute | solution.py:358
  65.9 6.3 %collective-permute-start.16 = (f32[64,512]{1,0:T(8,128)S(1)}, f32[64,512]{1,0:T(8,128)S(1)}, u32[]{:S(2)}, u32[]{:S(2)}) collective-permute-start(f32[64,512]{1,0:T(8,128)S(1)} %get-tuple-element.72), channel_id=1, source_target_pairs={{0,4},{2,6},{4,0},{6,2},{1,5},{3,7},{5,1},{7,3},{8,12},{10,14},{12... | collective-permute-start | bytes 393224 | tf_op jit(solution)/shard_map/ppermute | solution.py:358
  68.7 6.4 %collective-permute-start.17 = (f32[64,512]{1,0:T(8,128)S(1)}, f32[64,512]{1,0:T(8,128)S(1)}, u32[]{:S(2)}, u32[]{:S(2)}) collective-permute-start(f32[64,512]{1,0:T(8,128)S(1)} %get-tuple-element.73), channel_id=1, source_target_pairs={{0,2},{2,0},{4,6},{6,4},{1,3},{3,1},{5,7},{7,5},{8,10},{10,8},{12,... | collective-permute-start | bytes 393224 | tf_op jit(solution)/shard_map/ppermute | solution.py:358
  69.0 6.2 %collective-permute-start.18 = (f32[64,512]{1,0:T(8,128)S(1)}, f32[64,512]{1,0:T(8,128)S(1)}, u32[]{:S(2)}, u32[]{:S(2)}) collective-permute-start(f32[64,512]{1,0:T(8,128)S(1)} %get-tuple-element.74), channel_id=1, source_target_pairs={{0,6},{2,4},{4,2},{6,0},{1,7},{3,5},{5,3},{7,1},{8,14},{10,12},{12... | collective-permute-start | bytes 393224 | tf_op jit(solution)/shard_map/ppermute | solution.py:358
  75.3 5.4 %collective-permute-start.19 = (f32[64,512]{1,0:T(8,128)S(1)}, f32[64,512]{1,0:T(8,128)S(1)}, u32[]{:S(2)}, u32[]{:S(2)}) collective-permute-start(f32[64,512]{1,0:T(8,128)S(1)} %add_multiply_fusion), channel_id=1, source_target_pairs={{0,64},{1,65},{64,0},{65,1},{2,66},{3,67},{66,2},{67,3},{4,68},{5,... | collective-permute-start | bytes 393224 | tf_op jit(solution)/shard_map/ppermute | solution.py:358
  76.5 5.6 %collective-permute-start.20 = (f32[64,512]{1,0:T(8,128)S(1)}, f32[64,512]{1,0:T(8,128)S(1)}, u32[]{:S(2)}, u32[]{:S(2)}) collective-permute-start(f32[64,512]{1,0:T(8,128)S(1)} %add_multiply_fusion), channel_id=1, source_target_pairs={{0,1},{1,0},{64,65},{65,64},{2,3},{3,2},{66,67},{67,66},{4,5},{5,4... | collective-permute-start | bytes 393224 | tf_op jit(solution)/shard_map/ppermute | solution.py:358
  77.1 6.2 %collective-permute-start.21 = (f32[64,512]{1,0:T(8,128)S(1)}, f32[64,512]{1,0:T(8,128)S(1)}, u32[]{:S(2)}, u32[]{:S(2)}) collective-permute-start(f32[64,512]{1,0:T(8,128)S(1)} %add_multiply_fusion), channel_id=1, source_target_pairs={{0,65},{1,64},{64,1},{65,0},{2,67},{3,66},{66,3},{67,2},{4,69},{5,... | collective-permute-start | bytes 393224 | tf_op jit(solution)/shard_map/ppermute | solution.py:358
  83.6 3.3 %collective-permute-start.22 = (f32[64,256]{1,0:T(8,128)S(1)}, f32[64,256]{1,0:T(8,128)S(1)}, u32[]{:S(2)}, u32[]{:S(2)}) collective-permute-start(f32[64,256]{1,0:T(8,128)S(1)} %shard_map.112), channel_id=1, source_target_pairs={{0,32},{32,0},{1,33},{33,1},{2,34},{34,2},{3,35},{35,3},{4,36},{36... | collective-permute-start | bytes 196616 | tf_op jit(solution)/shard_map/ppermute | solution.py:358
  86.9 5.4 %collective-permute-start.23 = (f32[64,256]{1,0:T(8,128)S(1)}, f32[64,256]{1,0:T(8,128)S(1)}, u32[]{:S(2)}, u32[]{:S(2)}) collective-permute-start(f32[64,256]{1,0:T(8,128)S(1)} %add.82), channel_id=1, source_target_pairs={{0,4},{2,6},{4,0},{6,2},{1,5},{3,7},{5,1},{7,3},{8,12},{10,14},{12... | collective-permute-start | bytes 196616 | tf_op jit(solution)/shard_map/ppermute | solution.py:358
  90.2 3.5 %collective-permute-start.24 = (f32[64,256]{1,0:T(8,128)S(1)}, f32[64,256]{1,0:T(8,128)S(1)}, u32[]{:S(2)}, u32[]{:S(2)}) collective-permute-start(f32[64,256]{1,0:T(8,128)S(1)} %add.82), channel_id=1, source_target_pairs={{0,2},{2,0},{4,6},{6,4},{1,3},{3,1},{5,7},{7,5},{8,10},{10,8},{12,... | collective-permute-start | bytes 196616 | tf_op jit(solution)/shard_map/ppermute | solution.py:358
  90.5 4.3 %collective-permute-start.25 = (f32[64,256]{1,0:T(8,128)S(1)}, f32[64,256]{1,0:T(8,128)S(1)}, u32[]{:S(2)}, u32[]{:S(2)}) collective-permute-start(f32[64,256]{1,0:T(8,128)S(1)} %add.82), channel_id=1, source_target_pairs={{0,6},{2,4},{4,2},{6,0},{1,7},{3,5},{5,3},{7,1},{8,14},{10,12},{12... | collective-permute-start | bytes 196616 | tf_op jit(solution)/shard_map/ppermute | solution.py:358
  94.8 4.7 %collective-permute-start.26 = (f32[64,256]{1,0:T(8,128)S(1)}, f32[64,256]{1,0:T(8,128)S(1)}, u32[]{:S(2)}, u32[]{:S(2)}) collective-permute-start(f32[64,256]{1,0:T(8,128)S(1)} %add_add_fusion.2), channel_id=1, source_target_pairs={{0,16},{8,24},{16,0},{24,8},{1,17},{9,25},{17,1},{25,9},{2,18},{10... | collective-permute-start | bytes 196616 | tf_op jit(solution)/shard_map/ppermute | solution.py:358
  95.6 3.9 %collective-permute-start.27 = (f32[64,256]{1,0:T(8,128)S(1)}, f32[64,256]{1,0:T(8,128)S(1)}, u32[]{:S(2)}, u32[]{:S(2)}) collective-permute-start(f32[64,256]{1,0:T(8,128)S(1)} %add_add_fusion.2), channel_id=1, source_target_pairs={{0,8},{8,0},{16,24},{24,16},{1,9},{9,1},{17,25},{25,17},{2,10},{10... | collective-permute-start | bytes 196616 | tf_op jit(solution)/shard_map/ppermute | solution.py:358
  96.0 4.3 %collective-permute-start.28 = (f32[64,256]{1,0:T(8,128)S(1)}, f32[64,256]{1,0:T(8,128)S(1)}, u32[]{:S(2)}, u32[]{:S(2)}) collective-permute-start(f32[64,256]{1,0:T(8,128)S(1)} %add_add_fusion.2), channel_id=1, source_target_pairs={{0,24},{8,16},{16,8},{24,0},{1,25},{9,17},{17,9},{25,1},{2,26},{10... | collective-permute-start | bytes 196616 | tf_op jit(solution)/shard_map/ppermute | solution.py:358
  100.7 5.4 %collective-permute-start.29 = (f32[64,512]{1,0:T(8,128)S(1)}, f32[64,512]{1,0:T(8,128)S(1)}, u32[]{:S(2)}, u32[]{:S(2)}) collective-permute-start(f32[64,512]{1,0:T(8,128)S(1)} %shard_map.113), channel_id=1, source_target_pairs={{0,64},{1,65},{64,0},{65,1},{2,66},{3,67},{66,2},{67,3},{4,68},{5,... | collective-permute-start | bytes 393224 | tf_op jit(solution)/shard_map/ppermute | solution.py:358
  101.9 4.4 %collective-permute-start.30 = (f32[64,512]{1,0:T(8,128)S(1)}, f32[64,512]{1,0:T(8,128)S(1)}, u32[]{:S(2)}, u32[]{:S(2)}) collective-permute-start(f32[64,512]{1,0:T(8,128)S(1)} %shard_map.113), channel_id=1, source_target_pairs={{0,1},{1,0},{64,65},{65,64},{2,3},{3,2},{66,67},{67,66},{4,5},{5,4... | collective-permute-start | bytes 393224 | tf_op jit(solution)/shard_map/ppermute | solution.py:358
  102.5 5.0 %collective-permute-start.31 = (f32[64,512]{1,0:T(8,128)S(1)}, f32[64,512]{1,0:T(8,128)S(1)}, u32[]{:S(2)}, u32[]{:S(2)}) collective-permute-start(f32[64,512]{1,0:T(8,128)S(1)} %shard_map.113), channel_id=1, source_target_pairs={{0,65},{1,64},{64,1},{65,0},{2,67},{3,66},{66,3},{67,2},{4,69},{5,... | collective-permute-start | bytes 393224 | tf_op jit(solution)/shard_map/ppermute | solution.py:358
  107.6 6.5 %collective-permute-start.32 = (f32[64,512]{1,0:T(8,128)S(1)}, f32[64,512]{1,0:T(8,128)S(1)}, u32[]{:S(2)}, u32[]{:S(2)}) collective-permute-start(f32[64,512]{1,0:T(8,128)S(1)} %add_subtract_fusion), channel_id=1, source_target_pairs={{0,32},{32,0},{1,33},{33,1},{2,34},{34,2},{3,35},{35,3},{4,36},{36... | collective-permute-start | bytes 393224 | tf_op jit(solution)/shard_map/ppermute | solution.py:358
  (3 other events, 22.7 us)

commit v14 on v13

--- a/solution.py
+++ b/solution.py
@@ -310,13 +310,13 @@
     coeff[...] = both[:, :part] + both[:, part:]
 
 
-def corr_body(member, summed, coeff, eig_scale, corr):
+def corr_body(member, summed, coeff, eig_scale, grads, corr):
     out, part = coeff.shape
     scale = eig_scale[:, pl.ds(pl.multiple_of(member[0] * part, part), part)]
     c1, c2 = split2(coeff[...] * scale)
     cc = jnp.concatenate([c1, c2], axis=0)
     both = mm(cc, summed[:, :part], NT) + mm(cc, summed[:, part:], NT)
-    corr[...] = both[:out] + both[out:]
+    corr[...] = both[:out] + both[out:] - grads[...] * 0.25
 
 
 def shape(*dims, dtype=F32):
@@ -375,7 +375,6 @@
     norm = 1.0 / math.sqrt(rows * math.prod(SIZES[a] for a in ALL))
     x = lax.axis_index("x").astype(jnp.int32)[None]
     member = lax.axis_index(PLANES).astype(jnp.int32)[None]
-    straight = lax.axis_index("core") == lax.axis_index("zl")
     wide = 2 * out
 
     hbm = pl.BlockSpec(memory_space=pltpu.HBM)
@@ -483,11 +482,16 @@
     for axis in OWNERS[::-1]:
         coeff = exchange(coeff, (axis,))
     corr = call(
-        corr_body, shape(out, cdev), member, summed, coeff, eig_scale[None, :], scalars=1
-    )
-    update = exchange(corr, PLANES) - grads
-    (swapped,) = mates([update] * 2, ("core",))
-    return resid, jnp.where(straight, update, swapped).T
+        corr_body, shape(out, cdev), member, summed, coeff, eig_scale[None, :], grads, scalars=1
+    )
+    received = []
+    for r in (2, 3, 1, 0):
+        perm = [
+            ((z // 2) * 4 + k * 2 + z % 2, ((z ^ r) // 2) * 4 + ((z ^ r) % 2) * 2 + k)
+            for k in range(2) for z in range(4)
+        ]
+        received.append(lax.ppermute(corr, ("zh", "core", "zl"), perm))
+    return resid, functools.reduce(jnp.add, received).T
 
 
 def solution(mesh):

time: 115 us -> 114 us (level)
  waiting for transfers between devices: 33 us -> 31.7 us
    ppermute x0 -> x4, starting transfers between devices: none -> 9.1 us  [per_device(): received.append(lax.ppermute(corr, ('zh', 'core', 'zl'), perm))]
    ppermute x32 -> x28, starting transfers between devices: 43.9 us -> 35 us  [mate_of(): return lax.ppermute(v, axes, [(i, i ^ o) for i in range(n)])]
    ppermute x32 -> x28, waiting for transfers between devices: 33 us -> 28.5 us  [mate_of(): return lax.ppermute(v, axes, [(i, i ^ o) for i in range(n)])]
    ppermute x0 -> x4, waiting for transfers between devices: none -> 3.21 us  [per_device(): received.append(lax.ppermute(corr, ('zh', 'core', 'zl'), perm))]
  transfers between devices with their start and end apart: 34 -> 34, of which waited for: 27 -> 24; matrix products, arithmetic and copies ran while one was open for 0% -> 0% of each run, Pallas kernels for 19% -> 19%
where the time goes in v14:
time: 114 us
  starting transfers between devices  55.6 us (49%)
  waiting for transfers between devices  31.7 us (28%)
  Pallas kernels  24.7 us (22%)
    ppermute x28, starting transfers between devices, mate_of(): return lax.ppermute(v, axes, [(i, i ^ o) for i in range(n)])  35 us
    ppermute x28, waiting for transfers between devices, mate_of(): return lax.ppermute(v, axes, [(i, i ^ o) for i in range(n)])  28.5 us
    pallas_call x9, Pallas kernels, call(): pl.pallas_call(body, out_shape=outs, in_specs=[smem] * scalars + [VMEM] *...  22.5 us
    ppermute x4, starting transfers between devices, per_device(): received.append(lax.ppermute(corr, ('zh', 'core', 'zl'), perm))  9.1 us
    all_to_all x1, starting transfers between devices, per_device(): lax.all_to_all(points, OWNERS, split_axis=0, concat_axis=0, tiled=True)  6.56 us
    ppermute x1, starting transfers between devices, per_device(): tile = lax.ppermute(pack, ('core', 'zl'), [(0, 0), (2, 1), (1, 2), (3, 3)])  4.93 us
    ppermute x4, waiting for transfers between devices, per_device(): received.append(lax.ppermute(corr, ('zh', 'core', 'zl'), perm))  3.21 us
  transfers between devices with their start and end apart: 34, of which 24 were waited for; matrix products, arithmetic and copies ran while one was open for 0% of the time, Pallas kernels for 19%

profile of v14, /device:TPU:1, one launch (start us, length us, event | category | flops | bytes accessed | tf_op | source)
XLA Modules:
  0.0 113.7 jit_solution(12265122082615637909)
XLA Ops:
  0.6 2.2 %shard_map.104 = (f32[96,128]{1,0:T(8,128)S(1)}, f32[768,128]{1,0:T(8,128)S(1)}, f32[136,256]{1,0:T(8,128)S(1)}, f32[136,256]{1,0:T(8,128)S(1)}, f32[136,256]{1,0:T(8,128)S(1)}, /*index=5*/f32[136,256]{1,0:T(8,128)S(1)}) custom-call(s32[1]{0:T(128)} %bitcast.1.member, s32[1,64]{1,0:T(1,128)} %bitcast.15, f32[1024,128]{1,0:T(8,128)} %refs_1_.1, ...), custom_call_target="tpu_custom_call" | custom-call | tf_op jit(solution)/shard_map/pallas_call | solution.py:381
  2.9 4.9 %collective-permute-start = (f32[768,128]{1,0:T(8,128)S(1)}, f32[768,128]{1,0:T(8,128)S(1)}, u32[]{:S(2)}, u32[]{:S(2)}) collective-permute-start(f32[768,128]{1,0:T(8,128)S(1)} %get-tuple-element.40), channel_id=1, source_target_pairs={{0,0},{32,1},{1,32},{33,33},{2,2},{34,3},{3,34},{35,35},{4,4},{36,... | collective-permute-start | bytes 1179656 | tf_op jit(solution)/shard_map/ppermute | solution.py:411
  7.8 3.4 %collective-permute-start.1 = (f32[136,256]{1,0:T(8,128)S(1)}, f32[136,256]{1,0:T(8,128)S(1)}, u32[]{:S(2)}, u32[]{:S(2)}) collective-permute-start(f32[136,256]{1,0:T(8,128)S(1)} %get-tuple-element.41), channel_id=1, source_target_pairs={{0,64},{1,65},{64,0},{65,1},{2,66},{3,67},{66,2},{67,3},{4,68},{5,... | collective-permute-start | bytes 417800 | tf_op jit(solution)/shard_map/ppermute | solution.py:358
  11.2 2.7 %collective-permute-start.2 = (f32[96,128]{1,0:T(8,128)S(1)}, f32[96,128]{1,0:T(8,128)S(1)}, u32[]{:S(2)}, u32[]{:S(2)}) collective-permute-start(f32[96,128]{1,0:T(8,128)S(1)} %get-tuple-element.43.refs_0_), channel_id=1, source_target_pairs={{0,16},{8,24},{16,0},{24,8},{1,17},{9,25},{17,1},{25,9},{2,18},{10... | collective-permute-start | bytes 147464 | tf_op jit(solution)/shard_map/ppermute | solution.py:358
  15.9 1.3 %collective-permute-done.3.refs_2_ = f32[96,128]{1,0:T(8,128)S(1)} collective-permute-done((f32[96,128]{1,0:T(8,128)S(1)}, f32[96,128]{1,0:T(8,128)S(1)}, u32[]{:S(2)}, u32[]{:S(2)}) %collective-permute-start.3) | collective-permute-done | bytes 49184 | tf_op jit(solution)/shard_map/ppermute | solution.py:358
  18.4 2.9 %collective-permute-start.10 = (f32[768,128]{1,0:T(8,128)S(1)}, f32[768,128]{1,0:T(8,128)}, u32[]{:S(2)}, u32[]{:S(2)}) collective-permute-start(f32[768,128]{1,0:T(8,128)S(1)} %collective-permute-done.refs_2_), channel_id=1, source_target_pairs={{0,4},{2,6},{4,0},{6,2},{1,5},{3,7},{5,1},{7,3},{8,12},{10,14},{12... | collective-permute-start | bytes 1179656 | tf_op jit(solution)/shard_map/ppermute | solution.py:358
  22.3 1.3 %collective-permute-done.5.refs_1_ = f32[4,96,128]{2,1,0:T(8,128)S(1)} collective-permute-done((f32[4,96,128]{2,1,0:T(8,128)S(1)}, f32[4,96,128]{2,1,0:T(8,128)S(1)}, u32[]{:S(2)}, u32[]{:S(2)}) %collective-permute-start.5) | collective-permute-done | bytes 196640 | tf_op jit(solution)/shard_map/ppermute | solution.py:358
  23.6 1.7 %collective-permute-start.6 = (f32[136,256]{1,0:T(8,128)S(1)}, f32[136,256]{1,0:T(8,128)S(1)}, u32[]{:S(2)}, u32[]{:S(2)}) collective-permute-start(f32[136,256]{1,0:T(8,128)S(1)} %get-tuple-element.54), channel_id=1, source_target_pairs={{0,1},{1,0},{64,65},{65,64},{2,3},{3,2},{66,67},{67,66},{4,5},{5,4... | collective-permute-start | bytes 417800 | tf_op jit(solution)/shard_map/ppermute | solution.py:358
  25.3 3.9 %shard_map.106 = (bf16[1,512,512]{2,1,0:T(8,128)(2,1)S(1)}, bf16[1,512,512]{2,1,0:T(8,128)(2,1)S(1)}, f32[4,32,128]{2,1,0:T(8,128)S(1)}, f32[4,32,128]{2,1,0:T(8...) custom-call(f32[4,96,128]{2,1,0:T(8,128)S(1)} %shard_map.105.refs_0_.own, ...), custom_call_target="tpu_custom_call" | custom-call | flops 100000000 | bytes 65536 | tf_op jit(solution)/shard_map/pallas_call | solution.py:333
  29.2 2.0 %collective-permute-done.7.refs_3_ = f32[136,256]{1,0:T(8,128)S(1)} collective-permute-done((f32[136,256]{1,0:T(8,128)S(1)}, f32[136,256]{1,0:T(8,128)S(1)}, u32[]{:S(2)}, u32[]{:S(2)}) %collective-permute-start.7) | collective-permute-done | bytes 139296 | tf_op jit(solution)/shard_map/ppermute | solution.py:358
  31.2 1.7 %shard_map.109 = f32[32,72,128]{2,1,0:T(8,128)} custom-call(f32[136,256]{1,0:T(8,128)S(1)} %get-tuple-element.62.refs_0_, f32[136,256]{1,0:T(8,128)S(1)} %collective-permute-done.1.refs_1_, f32[136,256]{1,0:T(8,128)S(1)} %collective-permute-done.6.refs_2_, f32[136,256]{1,0:T(8,128)S(1)} %collective-permute-done.7.refs_3_), custom_call_target="tpu_custom_call" | custom-call | tf_op jit(solution)/shard_map/pallas_call | solution.py:333
  33.0 6.6 %all-to-all-start = ((f32[32,72,128]{2,1,0:T(8,128)}), f32[32,72,128]{2,1,0:T(8,128)S(1)}, u32[]{:S(2)}, u32[]{:S(2)}) async-start(f32[32,72,128]{2,1,0:T(8,128)} %shard_map.109), calls=%async_computation | async-start | bytes 2359296 | tf_op jit(solution)/shard_map/all_to_all | solution.py:453
  40.0 12.8 %shard_map.107 = (bf16[3,512,512]{2,1,0:T(8,128)(2,1)S(1)}, bf16[3,512,512]{2,1,0:T(8,128)(2,1)S(1)}, f32[4,32,128]{2,1,0:T(8,128)S(1)}, f32[4,32,128]{2,1,0:T(8,128)S(1)}) custom-call(f32[4,96,128]{2,1,0:T(8,128)S(1)} %shard_map.105.refs_0_.own, f32[4,96,128]{2,1,0:T(8,128)S(1)} %collective-permute-done.5.refs_1_, ...), custom_call_target="tpu_custom_call" | custom-call | flops 30000001024 | bytes 65536 | tf_op jit(solution)/shard_map/pallas_call | solution.py:333
  54.2 2.6 %collective-permute-start.12 = (f32[4,32,128]{2,1,0:T(8,128)S(1)}, f32[4,32,128]{2,1,0:T(8,128)S(1)}, u32[]{:S(2)}, u32[]{:S(2)}) collective-permute-start(f32[4,32,128]{2,1,0:T(8,128)S(1)} %add_add_fusion.4), channel_id=1, source_target_pairs={{0,16},{8,24},{16,0},{24,8},{1,17},{9,25},{17,1},{25,9},{2,18},{10... | collective-permute-start | bytes 196616 | tf_op jit(solution)/shard_map/ppermute | solution.py:358
  58.9 1.3 %collective-permute-done.13 = f32[4,32,128]{2,1,0:T(8,128)S(1)} collective-permute-done((f32[4,32,128]{2,1,0:T(8,128)S(1)}, f32[4,32,128]{2,1,0:T(8,128)S(1)}, u32[]{:S(2)}, u32[]{:S(2)}) %collective-permute-start.13) | collective-permute-done | bytes 65568 | tf_op jit(solution)/shard_map/ppermute | solution.py:358
  62.1 2.1 %collective-permute-start.15 = (f32[4,32,128]{2,1,0:T(8,128)S(1)}, f32[4,32,128]{2,1,0:T(8,128)S(1)}, u32[]{:S(2)}, u32[]{:S(2)}) collective-permute-start(f32[4,32,128]{2,1,0:T(8,128)S(1)} %get-tuple-element.66.own), channel_id=1, source_target_pairs={{0,32},{32,0},{1,33},{33,1},{2,34},{34,2},{3,35},{35,3},{4,36},{36... | collective-permute-start | bytes 196616 | tf_op jit(solution)/shard_map/ppermute | solution.py:358
  65.9 2.8 %collective-permute-start.16 = (f32[64,512]{1,0:T(8,128)S(1)}, f32[64,512]{1,0:T(8,128)S(1)}, u32[]{:S(2)}, u32[]{:S(2)}) collective-permute-start(f32[64,512]{1,0:T(8,128)S(1)} %get-tuple-element.72), channel_id=1, source_target_pairs={{0,4},{2,6},{4,0},{6,2},{1,5},{3,7},{5,1},{7,3},{8,12},{10,14},{12... | collective-permute-start | bytes 393224 | tf_op jit(solution)/shard_map/ppermute | solution.py:358
  69.6 2.6 %collective-permute-done.16 = f32[64,512]{1,0:T(8,128)S(1)} collective-permute-done((f32[64,512]{1,0:T(8,128)S(1)}, f32[64,512]{1,0:T(8,128)S(1)}, u32[]{:S(2)}, u32[]{:S(2)}) %collective-permute-start.16) | collective-permute-done | bytes 131104 | tf_op jit(solution)/shard_map/ppermute | solution.py:358
  72.2 2.9 %collective-permute-done.17 = f32[64,512]{1,0:T(8,128)S(1)} collective-permute-done((f32[64,512]{1,0:T(8,128)S(1)}, f32[64,512]{1,0:T(8,128)S(1)}, u32[]{:S(2)}, u32[]{:S(2)}) %collective-permute-start.17) | collective-permute-done | bytes 131104 | tf_op jit(solution)/shard_map/ppermute | solution.py:358
  77.1 1.5 %collective-permute-start.21 = (f32[64,512]{1,0:T(8,128)S(1)}, f32[64,512]{1,0:T(8,128)S(1)}, u32[]{:S(2)}, u32[]{:S(2)}) collective-permute-start(f32[64,512]{1,0:T(8,128)S(1)} %add_multiply_fusion), channel_id=1, source_target_pairs={{0,65},{1,64},{64,1},{65,0},{2,67},{3,66},{66,3},{67,2},{4,69},{5,... | collective-permute-start | bytes 393224 | tf_op jit(solution)/shard_map/ppermute | solution.py:358
  78.6 2.0 %shard_map.111.summed = bf16[512,512]{1,0:T(8,128)(2,1)S(1)} custom-call(f32[32,72,128]{2,1,0:T(8,128)S(1)} %all-to-all-done.points), custom_call_target="tpu_custom_call" | custom-call | flops 800000000 | bytes 2097152 | tf_op jit(solution)/shard_map/pallas_call | solution.py:333
  80.7 1.4 %collective-permute-done.20 = f32[64,512]{1,0:T(8,128)S(1)} collective-permute-done((f32[64,512]{1,0:T(8,128)S(1)}, f32[64,512]{1,0:T(8,128)S(1)}, u32[]{:S(2)}, u32[]{:S(2)}) %collective-permute-start.20) | collective-permute-done | bytes 131104 | tf_op jit(solution)/shard_map/ppermute | solution.py:358
  82.1 1.3 %collective-permute-done.21 = f32[64,512]{1,0:T(8,128)S(1)} collective-permute-done((f32[64,512]{1,0:T(8,128)S(1)}, f32[64,512]{1,0:T(8,128)S(1)}, u32[]{:S(2)}, u32[]{:S(2)}) %collective-permute-start.21) | collective-permute-done | bytes 131104 | tf_op jit(solution)/shard_map/ppermute | solution.py:358
  83.6 2.4 %collective-permute-start.22 = (f32[64,256]{1,0:T(8,128)S(1)}, f32[64,256]{1,0:T(8,128)S(1)}, u32[]{:S(2)}, u32[]{:S(2)}) collective-permute-start(f32[64,256]{1,0:T(8,128)S(1)} %shard_map.112), channel_id=1, source_target_pairs={{0,32},{32,0},{1,33},{33,1},{2,34},{34,2},{3,35},{35,3},{4,36},{36... | collective-permute-start | bytes 196616 | tf_op jit(solution)/shard_map/ppermute | solution.py:358
  86.9 3.3 %collective-permute-start.23 = (f32[64,256]{1,0:T(8,128)S(1)}, f32[64,256]{1,0:T(8,128)S(1)}, u32[]{:S(2)}, u32[]{:S(2)}) collective-permute-start(f32[64,256]{1,0:T(8,128)S(1)} %add.82), channel_id=1, source_target_pairs={{0,4},{2,6},{4,0},{6,2},{1,5},{3,7},{5,1},{7,3},{8,12},{10,14},{12... | collective-permute-start | bytes 196616 | tf_op jit(solution)/shard_map/ppermute | solution.py:358
  90.7 1.6 %collective-permute-done.23 = f32[64,256]{1,0:T(8,128)S(1)} collective-permute-done((f32[64,256]{1,0:T(8,128)S(1)}, f32[64,256]{1,0:T(8,128)S(1)}, u32[]{:S(2)}, u32[]{:S(2)}) %collective-permute-start.23) | collective-permute-done | bytes 65568 | tf_op jit(solution)/shard_map/ppermute | solution.py:358
  92.3 1.3 %collective-permute-done.24 = f32[64,256]{1,0:T(8,128)S(1)} collective-permute-done((f32[64,256]{1,0:T(8,128)S(1)}, f32[64,256]{1,0:T(8,128)S(1)}, u32[]{:S(2)}, u32[]{:S(2)}) %collective-permute-start.24) | collective-permute-done | bytes 65568 | tf_op jit(solution)/shard_map/ppermute | solution.py:358
  96.0 2.1 %collective-permute-start.28 = (f32[64,256]{1,0:T(8,128)S(1)}, f32[64,256]{1,0:T(8,128)S(1)}, u32[]{:S(2)}, u32[]{:S(2)}) collective-permute-start(f32[64,256]{1,0:T(8,128)S(1)} %add_add_fusion.2), channel_id=1, source_target_pairs={{0,24},{8,16},{16,8},{24,0},{1,25},{9,17},{17,9},{25,1},{2,26},{10... | collective-permute-start | bytes 196616 | tf_op jit(solution)/shard_map/ppermute | solution.py:358
  98.1 1.4 %collective-permute-done.26 = f32[64,256]{1,0:T(8,128)S(1)} collective-permute-done((f32[64,256]{1,0:T(8,128)S(1)}, f32[64,256]{1,0:T(8,128)S(1)}, u32[]{:S(2)}, u32[]{:S(2)}) %collective-permute-start.26) | collective-permute-done | bytes 65568 | tf_op jit(solution)/shard_map/ppermute | solution.py:358
  100.7 4.9 %collective-permute-start.29 = (f32[64,512]{1,0:T(8,128)S(1)}, f32[64,512]{1,0:T(8,128)S(1)}, u32[]{:S(2)}, u32[]{:S(2)}) collective-permute-start(f32[64,512]{1,0:T(8,128)S(1)} %shard_map.113), channel_id=1, source_target_pairs={{0,64},{1,96},{64,0},{65,32},{32,65},{33,97},{96,1},{97,33},{2,66}... | collective-permute-start | bytes 393224 | tf_op jit(solution)/shard_map/ppermute | solution.py:493
  106.3 3.5 %collective-permute-start.32 = (f32[64,512]{1,0:T(8,128)S(1)}, f32[64,512]{1,0:T(8,128)S(1)}, u32[]{:S(2)}, u32[]{:S(2)}) collective-permute-start(f32[64,512]{1,0:T(8,128)S(1)} %shard_map.113), channel_id=1, source_target_pairs={{0,0},{1,32},{64,64},{65,96},{32,1},{33,33},{96,65},{97,97},{2,2},... | collective-permute-start | bytes 393224 | tf_op jit(solution)/shard_map/ppermute | solution.py:493
  109.8 3.2 %collective-permute-done.30 = f32[64,512]{1,0:T(8,128)S(1)} collective-permute-done((f32[64,512]{1,0:T(8,128)S(1)}, f32[64,512]{1,0:T(8,128)S(1)}, u32[]{:S(2)}, u32[]{:S(2)}) %collective-permute-start.30) | collective-permute-done | bytes 131104 | tf_op jit(solution)/shard_map/ppermute | solution.py:493
  (58 shorter events, 21.3 us)
Async XLA Ops:
  2.9 15.5 %collective-permute-start = (f32[768,128]{1,0:T(8,128)S(1)}, f32[768,128]{1,0:T(8,128)S(1)}, u32[]{:S(2)}, u32[]{:S(2)}) collective-permute-start(f32[768,128]{1,0:T(8,128)S(1)} %get-tuple-element.40), channel_id=1, source_target_pairs={{0,0},{32,1},{1,32},{33,33},{2,2},{34,3},{3,34},{35,35},{4,4},{36,... | collective-permute-start | bytes 1179656 | tf_op jit(solution)/shard_map/ppermute | solution.py:411
  7.8 10.6 %collective-permute-start.1 = (f32[136,256]{1,0:T(8,128)S(1)}, f32[136,256]{1,0:T(8,128)S(1)}, u32[]{:S(2)}, u32[]{:S(2)}) collective-permute-start(f32[136,256]{1,0:T(8,128)S(1)} %get-tuple-element.41), channel_id=1, source_target_pairs={{0,64},{1,65},{64,0},{65,1},{2,66},{3,67},{66,2},{67,3},{4,68},{5,... | collective-permute-start | bytes 417800 | tf_op jit(solution)/shard_map/ppermute | solution.py:358
  11.2 4.7 %collective-permute-start.2 = (f32[96,128]{1,0:T(8,128)S(1)}, f32[96,128]{1,0:T(8,128)S(1)}, u32[]{:S(2)}, u32[]{:S(2)}) collective-permute-start(f32[96,128]{1,0:T(8,128)S(1)} %get-tuple-element.43.refs_0_), channel_id=1, source_target_pairs={{0,16},{8,24},{16,0},{24,8},{1,17},{9,25},{17,1},{25,9},{2,18},{10... | collective-permute-start | bytes 147464 | tf_op jit(solution)/shard_map/ppermute | solution.py:358
  13.9 3.2 %collective-permute-start.3 = (f32[96,128]{1,0:T(8,128)S(1)}, f32[96,128]{1,0:T(8,128)S(1)}, u32[]{:S(2)}, u32[]{:S(2)}) collective-permute-start(f32[96,128]{1,0:T(8,128)S(1)} %get-tuple-element.43.refs_0_), channel_id=1, source_target_pairs={{0,8},{8,0},{16,24},{24,16},{1,9},{9,1},{17,25},{25,17},{2,10},{10... | collective-permute-start | bytes 147464 | tf_op jit(solution)/shard_map/ppermute | solution.py:358
  14.2 4.2 %collective-permute-start.4 = (f32[96,128]{1,0:T(8,128)S(1)}, f32[96,128]{1,0:T(8,128)S(1)}, u32[]{:S(2)}, u32[]{:S(2)}) collective-permute-start(f32[96,128]{1,0:T(8,128)S(1)} %get-tuple-element.43.refs_0_), channel_id=1, source_target_pairs={{0,24},{8,16},{16,8},{24,0},{1,25},{9,17},{17,9},{25,1},{2,26},{10... | collective-permute-start | bytes 147464 | tf_op jit(solution)/shard_map/ppermute | solution.py:358
  18.4 21.1 %collective-permute-start.10 = (f32[768,128]{1,0:T(8,128)S(1)}, f32[768,128]{1,0:T(8,128)}, u32[]{:S(2)}, u32[]{:S(2)}) collective-permute-start(f32[768,128]{1,0:T(8,128)S(1)} %collective-permute-done.refs_2_), channel_id=1, source_target_pairs={{0,4},{2,6},{4,0},{6,2},{1,5},{3,7},{5,1},{7,3},{8,12},{10,14},{12... | collective-permute-start | bytes 1179656 | tf_op jit(solution)/shard_map/ppermute | solution.py:358
  21.3 18.6 %collective-permute-start.8 = (f32[768,128]{1,0:T(8,128)S(1)}, f32[768,128]{1,0:T(8,128)}, u32[]{:S(2)}, u32[]{:S(2)}) collective-permute-start(f32[768,128]{1,0:T(8,128)S(1)} %collective-permute-done.refs_2_), channel_id=1, source_target_pairs={{0,2},{2,0},{4,6},{6,4},{1,3},{3,1},{5,7},{7,5},{8,10},{10,8},{12,... | collective-permute-start | bytes 1179656 | tf_op jit(solution)/shard_map/ppermute | solution.py:358
  21.7 18.2 %collective-permute-start.9 = (f32[768,128]{1,0:T(8,128)S(1)}, f32[768,128]{1,0:T(8,128)}, u32[]{:S(2)}, u32[]{:S(2)}) collective-permute-start(f32[768,128]{1,0:T(8,128)S(1)} %collective-permute-done.refs_2_), channel_id=1, source_target_pairs={{0,6},{2,4},{4,2},{6,0},{1,7},{3,5},{5,3},{7,1},{8,14},{10,12},{12... | collective-permute-start | bytes 1179656 | tf_op jit(solution)/shard_map/ppermute | solution.py:358
  23.6 5.6 %collective-permute-start.6 = (f32[136,256]{1,0:T(8,128)S(1)}, f32[136,256]{1,0:T(8,128)S(1)}, u32[]{:S(2)}, u32[]{:S(2)}) collective-permute-start(f32[136,256]{1,0:T(8,128)S(1)} %get-tuple-element.54), channel_id=1, source_target_pairs={{0,1},{1,0},{64,65},{65,64},{2,3},{3,2},{66,67},{67,66},{4,5},{5,4... | collective-permute-start | bytes 417800 | tf_op jit(solution)/shard_map/ppermute | solution.py:358
  25.3 5.9 %collective-permute-start.7 = (f32[136,256]{1,0:T(8,128)S(1)}, f32[136,256]{1,0:T(8,128)S(1)}, u32[]{:S(2)}, u32[]{:S(2)}) collective-permute-start(f32[136,256]{1,0:T(8,128)S(1)} %get-tuple-element.55), channel_id=1, source_target_pairs={{0,65},{1,64},{64,1},{65,0},{2,67},{3,66},{66,3},{67,2},{4,69},{5,... | collective-permute-start | bytes 417800 | tf_op jit(solution)/shard_map/ppermute | solution.py:358
  33.0 42.3 %all-to-all-start = ((f32[32,72,128]{2,1,0:T(8,128)}), f32[32,72,128]{2,1,0:T(8,128)S(1)}, u32[]{:S(2)}, u32[]{:S(2)}) async-start(f32[32,72,128]{2,1,0:T(8,128)} %shard_map.109), calls=%async_computation | async-start | bytes 2359296 | tf_op jit(solution)/shard_map/all_to_all | solution.py:453
  54.2 4.7 %collective-permute-start.12 = (f32[4,32,128]{2,1,0:T(8,128)S(1)}, f32[4,32,128]{2,1,0:T(8,128)S(1)}, u32[]{:S(2)}, u32[]{:S(2)}) collective-permute-start(f32[4,32,128]{2,1,0:T(8,128)S(1)} %add_add_fusion.4), channel_id=1, source_target_pairs={{0,16},{8,24},{16,0},{24,8},{1,17},{9,25},{17,1},{25,9},{2,18},{10... | collective-permute-start | bytes 196616 | tf_op jit(solution)/shard_map/ppermute | solution.py:358
  56.8 3.5 %collective-permute-start.13 = (f32[4,32,128]{2,1,0:T(8,128)S(1)}, f32[4,32,128]{2,1,0:T(8,128)S(1)}, u32[]{:S(2)}, u32[]{:S(2)}) collective-permute-start(f32[4,32,128]{2,1,0:T(8,128)S(1)} %add_add_fusion.4), channel_id=1, source_target_pairs={{0,8},{8,0},{16,24},{24,16},{1,9},{9,1},{17,25},{25,17},{2,10},{10... | collective-permute-start | bytes 196616 | tf_op jit(solution)/shard_map/ppermute | solution.py:358
  57.1 4.3 %collective-permute-start.14 = (f32[4,32,128]{2,1,0:T(8,128)S(1)}, f32[4,32,128]{2,1,0:T(8,128)S(1)}, u32[]{:S(2)}, u32[]{:S(2)}) collective-permute-start(f32[4,32,128]{2,1,0:T(8,128)S(1)} %add_add_fusion.4), channel_id=1, source_target_pairs={{0,24},{8,16},{16,8},{24,0},{1,25},{9,17},{17,9},{25,1},{2,26},{10... | collective-permute-start | bytes 196616 | tf_op jit(solution)/shard_map/ppermute | solution.py:358
  62.1 3.0 %collective-permute-start.15 = (f32[4,32,128]{2,1,0:T(8,128)S(1)}, f32[4,32,128]{2,1,0:T(8,128)S(1)}, u32[]{:S(2)}, u32[]{:S(2)}) collective-permute-start(f32[4,32,128]{2,1,0:T(8,128)S(1)} %get-tuple-element.66.own), channel_id=1, source_target_pairs={{0,32},{32,0},{1,33},{33,1},{2,34},{34,2},{3,35},{35,3},{4,36},{36... | collective-permute-start | bytes 196616 | tf_op jit(solution)/shard_map/ppermute | solution.py:358
  65.9 6.3 %collective-permute-start.16 = (f32[64,512]{1,0:T(8,128)S(1)}, f32[64,512]{1,0:T(8,128)S(1)}, u32[]{:S(2)}, u32[]{:S(2)}) collective-permute-start(f32[64,512]{1,0:T(8,128)S(1)} %get-tuple-element.72), channel_id=1, source_target_pairs={{0,4},{2,6},{4,0},{6,2},{1,5},{3,7},{5,1},{7,3},{8,12},{10,14},{12... | collective-permute-start | bytes 393224 | tf_op jit(solution)/shard_map/ppermute | solution.py:358
  68.7 6.4 %collective-permute-start.17 = (f32[64,512]{1,0:T(8,128)S(1)}, f32[64,512]{1,0:T(8,128)S(1)}, u32[]{:S(2)}, u32[]{:S(2)}) collective-permute-start(f32[64,512]{1,0:T(8,128)S(1)} %get-tuple-element.73), channel_id=1, source_target_pairs={{0,2},{2,0},{4,6},{6,4},{1,3},{3,1},{5,7},{7,5},{8,10},{10,8},{12,... | collective-permute-start | bytes 393224 | tf_op jit(solution)/shard_map/ppermute | solution.py:358
  69.0 6.2 %collective-permute-start.18 = (f32[64,512]{1,0:T(8,128)S(1)}, f32[64,512]{1,0:T(8,128)S(1)}, u32[]{:S(2)}, u32[]{:S(2)}) collective-permute-start(f32[64,512]{1,0:T(8,128)S(1)} %get-tuple-element.74), channel_id=1, source_target_pairs={{0,6},{2,4},{4,2},{6,0},{1,7},{3,5},{5,3},{7,1},{8,14},{10,12},{12... | collective-permute-start | bytes 393224 | tf_op jit(solution)/shard_map/ppermute | solution.py:358
  75.3 5.4 %collective-permute-start.19 = (f32[64,512]{1,0:T(8,128)S(1)}, f32[64,512]{1,0:T(8,128)S(1)}, u32[]{:S(2)}, u32[]{:S(2)}) collective-permute-start(f32[64,512]{1,0:T(8,128)S(1)} %add_multiply_fusion), channel_id=1, source_target_pairs={{0,64},{1,65},{64,0},{65,1},{2,66},{3,67},{66,2},{67,3},{4,68},{5,... | collective-permute-start | bytes 393224 | tf_op jit(solution)/shard_map/ppermute | solution.py:358
  76.5 5.6 %collective-permute-start.20 = (f32[64,512]{1,0:T(8,128)S(1)}, f32[64,512]{1,0:T(8,128)S(1)}, u32[]{:S(2)}, u32[]{:S(2)}) collective-permute-start(f32[64,512]{1,0:T(8,128)S(1)} %add_multiply_fusion), channel_id=1, source_target_pairs={{0,1},{1,0},{64,65},{65,64},{2,3},{3,2},{66,67},{67,66},{4,5},{5,4... | collective-permute-start | bytes 393224 | tf_op jit(solution)/shard_map/ppermute | solution.py:358
  77.1 6.2 %collective-permute-start.21 = (f32[64,512]{1,0:T(8,128)S(1)}, f32[64,512]{1,0:T(8,128)S(1)}, u32[]{:S(2)}, u32[]{:S(2)}) collective-permute-start(f32[64,512]{1,0:T(8,128)S(1)} %add_multiply_fusion), channel_id=1, source_target_pairs={{0,65},{1,64},{64,1},{65,0},{2,67},{3,66},{66,3},{67,2},{4,69},{5,... | collective-permute-start | bytes 393224 | tf_op jit(solution)/shard_map/ppermute | solution.py:358
  83.6 3.3 %collective-permute-start.22 = (f32[64,256]{1,0:T(8,128)S(1)}, f32[64,256]{1,0:T(8,128)S(1)}, u32[]{:S(2)}, u32[]{:S(2)}) collective-permute-start(f32[64,256]{1,0:T(8,128)S(1)} %shard_map.112), channel_id=1, source_target_pairs={{0,32},{32,0},{1,33},{33,1},{2,34},{34,2},{3,35},{35,3},{4,36},{36... | collective-permute-start | bytes 196616 | tf_op jit(solution)/shard_map/ppermute | solution.py:358
  86.9 5.4 %collective-permute-start.23 = (f32[64,256]{1,0:T(8,128)S(1)}, f32[64,256]{1,0:T(8,128)S(1)}, u32[]{:S(2)}, u32[]{:S(2)}) collective-permute-start(f32[64,256]{1,0:T(8,128)S(1)} %add.82), channel_id=1, source_target_pairs={{0,4},{2,6},{4,0},{6,2},{1,5},{3,7},{5,1},{7,3},{8,12},{10,14},{12... | collective-permute-start | bytes 196616 | tf_op jit(solution)/shard_map/ppermute | solution.py:358
  90.2 3.5 %collective-permute-start.24 = (f32[64,256]{1,0:T(8,128)S(1)}, f32[64,256]{1,0:T(8,128)S(1)}, u32[]{:S(2)}, u32[]{:S(2)}) collective-permute-start(f32[64,256]{1,0:T(8,128)S(1)} %add.82), channel_id=1, source_target_pairs={{0,2},{2,0},{4,6},{6,4},{1,3},{3,1},{5,7},{7,5},{8,10},{10,8},{12,... | collective-permute-start | bytes 196616 | tf_op jit(solution)/shard_map/ppermute | solution.py:358
  90.5 4.3 %collective-permute-start.25 = (f32[64,256]{1,0:T(8,128)S(1)}, f32[64,256]{1,0:T(8,128)S(1)}, u32[]{:S(2)}, u32[]{:S(2)}) collective-permute-start(f32[64,256]{1,0:T(8,128)S(1)} %add.82), channel_id=1, source_target_pairs={{0,6},{2,4},{4,2},{6,0},{1,7},{3,5},{5,3},{7,1},{8,14},{10,12},{12... | collective-permute-start | bytes 196616 | tf_op jit(solution)/shard_map/ppermute | solution.py:358
  94.8 4.7 %collective-permute-start.26 = (f32[64,256]{1,0:T(8,128)S(1)}, f32[64,256]{1,0:T(8,128)S(1)}, u32[]{:S(2)}, u32[]{:S(2)}) collective-permute-start(f32[64,256]{1,0:T(8,128)S(1)} %add_add_fusion.2), channel_id=1, source_target_pairs={{0,16},{8,24},{16,0},{24,8},{1,17},{9,25},{17,1},{25,9},{2,18},{10... | collective-permute-start | bytes 196616 | tf_op jit(solution)/shard_map/ppermute | solution.py:358
  95.6 3.9 %collective-permute-start.27 = (f32[64,256]{1,0:T(8,128)S(1)}, f32[64,256]{1,0:T(8,128)S(1)}, u32[]{:S(2)}, u32[]{:S(2)}) collective-permute-start(f32[64,256]{1,0:T(8,128)S(1)} %add_add_fusion.2), channel_id=1, source_target_pairs={{0,8},{8,0},{16,24},{24,16},{1,9},{9,1},{17,25},{25,17},{2,10},{10... | collective-permute-start | bytes 196616 | tf_op jit(solution)/shard_map/ppermute | solution.py:358
  96.0 4.3 %collective-permute-start.28 = (f32[64,256]{1,0:T(8,128)S(1)}, f32[64,256]{1,0:T(8,128)S(1)}, u32[]{:S(2)}, u32[]{:S(2)}) collective-permute-start(f32[64,256]{1,0:T(8,128)S(1)} %add_add_fusion.2), channel_id=1, source_target_pairs={{0,24},{8,16},{16,8},{24,0},{1,25},{9,17},{17,9},{25,1},{2,26},{10... | collective-permute-start | bytes 196616 | tf_op jit(solution)/shard_map/ppermute | solution.py:358
  100.7 9.1 %collective-permute-start.29 = (f32[64,512]{1,0:T(8,128)S(1)}, f32[64,512]{1,0:T(8,128)S(1)}, u32[]{:S(2)}, u32[]{:S(2)}) collective-permute-start(f32[64,512]{1,0:T(8,128)S(1)} %shard_map.113), channel_id=1, source_target_pairs={{0,64},{1,96},{64,0},{65,32},{32,65},{33,97},{96,1},{97,33},{2,66}... | collective-permute-start | bytes 393224 | tf_op jit(solution)/shard_map/ppermute | solution.py:493
  105.6 7.4 %collective-permute-start.30 = (f32[64,512]{1,0:T(8,128)S(1)}, f32[64,512]{1,0:T(8,128)S(1)}, u32[]{:S(2)}, u32[]{:S(2)}) collective-permute-start(f32[64,512]{1,0:T(8,128)S(1)} %shard_map.113), channel_id=1, source_target_pairs={{0,96},{1,64},{64,32},{65,0},{32,97},{33,65},{96,33},{97,1},{2,98}... | collective-permute-start | bytes 393224 | tf_op jit(solution)/shard_map/ppermute | solution.py:493
  105.6 7.4 %collective-permute-start.31 = (f32[64,512]{1,0:T(8,128)S(1)}, f32[64,512]{1,0:T(8,128)S(1)}, u32[]{:S(2)}, u32[]{:S(2)}) collective-permute-start(f32[64,512]{1,0:T(8,128)S(1)} %shard_map.113), channel_id=1, source_target_pairs={{0,32},{1,0},{64,96},{65,64},{32,33},{33,1},{96,97},{97,65},{2,34}... | collective-permute-start | bytes 393224 | tf_op jit(solution)/shard_map/ppermute | solution.py:493
  106.3 6.7 %collective-permute-start.32 = (f32[64,512]{1,0:T(8,128)S(1)}, f32[64,512]{1,0:T(8,128)S(1)}, u32[]{:S(2)}, u32[]{:S(2)}) collective-permute-start(f32[64,512]{1,0:T(8,128)S(1)} %shard_map.113), channel_id=1, source_target_pairs={{0,0},{1,32},{64,64},{65,96},{32,1},{33,33},{96,65},{97,97},{2,2},... | collective-permute-start | bytes 393224 | tf_op jit(solution)/shard_map/ppermute | solution.py:493
  (3 other events, 22.7 us)

commit v15 on v14

--- a/solution.py
+++ b/solution.py
@@ -409,7 +409,7 @@
     hops = (2, 1, 3)
     gathered = [mate_of(drawn, ("x",), o) for o in hops]
     tile = lax.ppermute(pack, ("core", "zl"), [(0, 0), (2, 1), (1, 2), (3, 3)])
-    first = mate_of(parted[2], PLANES, 2)
+    first = mate_of(parted[3], PLANES, 3)
     tile, first, drawn, *gathered = together(tile, first, drawn, *gathered)
     own = call(
         functools.partial(order_body, offsets=(0,) + hops),
@@ -418,8 +418,8 @@
     )
     others = [mate_of(tile, ("y",), o) for o in TILES[1:]]
     mate = mate_of(own, ("core",), 1)
-    mate, second, third = together(mate, parted[1], parted[3])
-    parted = [parted[0], first, mate_of(second, PLANES, 1), mate_of(third, PLANES, 3)]
+    mate, second, third = together(mate, parted[2], parted[1])
+    parted = [parted[0], first, mate_of(second, PLANES, 2), mate_of(third, PLANES, 1)]
 
     def kernel(packs, extra):
         nb = len(packs)

time: 114 us -> 115 us (level)
  no operation moved by 1% of the time
where the time goes in v15:
time: 115 us
  starting transfers between devices  56.1 us (49%)
  waiting for transfers between devices  32.4 us (28%)
  Pallas kernels  24.7 us (21%)
    ppermute x28, starting transfers between devices, mate_of(): return lax.ppermute(v, axes, [(i, i ^ o) for i in range(n)])  34.8 us
    ppermute x28, waiting for transfers between devices, mate_of(): return lax.ppermute(v, axes, [(i, i ^ o) for i in range(n)])  29.6 us
    pallas_call x9, Pallas kernels, call(): pl.pallas_call(body, out_shape=outs, in_specs=[smem] * scalars + [VMEM] *...  22.5 us
    ppermute x4, starting transfers between devices, per_device(): received.append(lax.ppermute(corr, ('zh', 'core', 'zl'), perm))  10.1 us
    all_to_all x1, starting transfers between devices, per_device(): lax.all_to_all(points, OWNERS, split_axis=0, concat_axis=0, tiled=True)  6.2 us
    ppermute x1, starting transfers between devices, per_device(): tile = lax.ppermute(pack, ('core', 'zl'), [(0, 0), (2, 1), (1, 2), (3, 3)])  4.94 us
    ppermute x4, waiting for transfers between devices, per_device(): received.append(lax.ppermute(corr, ('zh', 'core', 'zl'), perm))  2.83 us
  transfers between devices with their start and end apart: 34, of which 24 were waited for; matrix products, arithmetic and copies ran while one was open for 0% of the time, Pallas kernels for 19%

profile of v15, /device:TPU:1, one launch (start us, length us, event | category | flops | bytes accessed | tf_op | source)
XLA Modules:
  0.0 114.9 jit_solution(7435687149587297753)
XLA Ops:
  0.6 2.2 %shard_map.104 = (f32[96,128]{1,0:T(8,128)S(1)}, f32[768,128]{1,0:T(8,128)S(1)}, f32[136,256]{1,0:T(8,128)S(1)}, f32[136,256]{1,0:T(8,128)S(1)}, f32[136,256]{1,0:T(8,128)S(1)}, /*index=5*/f32[136,256]{1,0:T(8,128)S(1)}) custom-call(s32[1]{0:T(128)} %bitcast.1.member, s32[1,64]{1,0:T(1,128)} %bitcast.15, f32[1024,128]{1,0:T(8,128)} %refs_1_.1, ...), custom_call_target="tpu_custom_call" | custom-call | tf_op jit(solution)/shard_map/pallas_call | solution.py:381
  2.9 4.9 %collective-permute-start = (f32[768,128]{1,0:T(8,128)S(1)}, f32[768,128]{1,0:T(8,128)S(1)}, u32[]{:S(2)}, u32[]{:S(2)}) collective-permute-start(f32[768,128]{1,0:T(8,128)S(1)} %get-tuple-element.40), channel_id=1, source_target_pairs={{0,0},{32,1},{1,32},{33,33},{2,2},{34,3},{3,34},{35,35},{4,4},{36,... | collective-permute-start | bytes 1179656 | tf_op jit(solution)/shard_map/ppermute | solution.py:411
  8.2 2.7 %collective-permute-start.2 = (f32[96,128]{1,0:T(8,128)S(1)}, f32[96,128]{1,0:T(8,128)S(1)}, u32[]{:S(2)}, u32[]{:S(2)}) collective-permute-start(f32[96,128]{1,0:T(8,128)S(1)} %get-tuple-element.43.refs_0_), channel_id=1, source_target_pairs={{0,16},{8,24},{16,0},{24,8},{1,17},{9,25},{17,1},{25,9},{2,18},{10... | collective-permute-start | bytes 147464 | tf_op jit(solution)/shard_map/ppermute | solution.py:358
  12.7 1.5 %collective-permute-done.3.refs_2_ = f32[96,128]{1,0:T(8,128)S(1)} collective-permute-done((f32[96,128]{1,0:T(8,128)S(1)}, f32[96,128]{1,0:T(8,128)S(1)}, u32[]{:S(2)}, u32[]{:S(2)}) %collective-permute-start.3) | collective-permute-done | bytes 49184 | tf_op jit(solution)/shard_map/ppermute | solution.py:358
  14.2 1.6 %collective-permute-done.4.refs_3_ = f32[96,128]{1,0:T(8,128)S(1)} collective-permute-done((f32[96,128]{1,0:T(8,128)S(1)}, f32[96,128]{1,0:T(8,128)S(1)}, u32[]{:S(2)}, u32[]{:S(2)}) %collective-permute-start.4) | collective-permute-done | bytes 49184 | tf_op jit(solution)/shard_map/ppermute | solution.py:358
  15.9 2.9 %collective-permute-start.10 = (f32[768,128]{1,0:T(8,128)S(1)}, f32[768,128]{1,0:T(8,128)}, u32[]{:S(2)}, u32[]{:S(2)}) collective-permute-start(f32[768,128]{1,0:T(8,128)S(1)} %collective-permute-done.refs_2_), channel_id=1, source_target_pairs={{0,4},{2,6},{4,0},{6,2},{1,5},{3,7},{5,1},{7,3},{8,12},{10,14},{12... | collective-permute-start | bytes 1179656 | tf_op jit(solution)/shard_map/ppermute | solution.py:358
  19.6 4.1 %collective-permute-start.5 = (f32[4,96,128]{2,1,0:T(8,128)S(1)}, f32[4,96,128]{2,1,0:T(8,128)S(1)}, u32[]{:S(2)}, u32[]{:S(2)}) collective-permute-start(f32[4,96,128]{2,1,0:T(8,128)S(1)} %shard_map.105.refs_0_.own), channel_id=1, source_target_pairs={{0,32},{32,0},{1,33},{33,1},{2,34},{34,2},{3,35},{35,3},{4,36},{36... | collective-permute-start | bytes 589832 | tf_op jit(solution)/shard_map/ppermute | solution.py:358
  25.2 3.9 %shard_map.106 = (bf16[1,512,512]{2,1,0:T(8,128)(2,1)S(1)}, bf16[1,512,512]{2,1,0:T(8,128)(2,1)S(1)}, f32[4,32,128]{2,1,0:T(8,128)S(1)}, f32[4,32,128]{2,1,0:T(8...) custom-call(f32[4,96,128]{2,1,0:T(8,128)S(1)} %shard_map.105.refs_0_.own, ...), custom_call_target="tpu_custom_call" | custom-call | flops 100000000 | bytes 65536 | tf_op jit(solution)/shard_map/pallas_call | solution.py:333
  29.0 2.2 %collective-permute-done.6.refs_2_ = f32[136,256]{1,0:T(8,128)S(1)} collective-permute-done((f32[136,256]{1,0:T(8,128)S(1)}, f32[136,256]{1,0:T(8,128)S(1)}, u32[]{:S(2)}, u32[]{:S(2)}) %collective-permute-start.6) | collective-permute-done | bytes 139296 | tf_op jit(solution)/shard_map/ppermute | solution.py:358
  31.7 1.7 %shard_map.109 = f32[32,72,128]{2,1,0:T(8,128)} custom-call(f32[136,256]{1,0:T(8,128)S(1)} %get-tuple-element.62.refs_0_, f32[136,256]{1,0:T(8,128)S(1)} %collective-permute-done.1.refs_1_, f32[136,256]{1,0:T(8,128)S(1)} %collective-permute-done.6.refs_2_, f32[136,256]{1,0:T(8,128)S(1)} %collective-permute-done.7.refs_3_), custom_call_target="tpu_custom_call" | custom-call | tf_op jit(solution)/shard_map/pallas_call | solution.py:333
  33.4 6.2 %all-to-all-start = ((f32[32,72,128]{2,1,0:T(8,128)}), f32[32,72,128]{2,1,0:T(8,128)S(1)}, u32[]{:S(2)}, u32[]{:S(2)}) async-start(f32[32,72,128]{2,1,0:T(8,128)} %shard_map.109), calls=%async_computation | async-start | bytes 2359296 | tf_op jit(solution)/shard_map/all_to_all | solution.py:453
  39.6 12.8 %shard_map.107 = (bf16[3,512,512]{2,1,0:T(8,128)(2,1)S(1)}, bf16[3,512,512]{2,1,0:T(8,128)(2,1)S(1)}, f32[4,32,128]{2,1,0:T(8,128)S(1)}, f32[4,32,128]{2,1,0:T(8,128)S(1)}) custom-call(f32[4,96,128]{2,1,0:T(8,128)S(1)} %shard_map.105.refs_0_.own, f32[4,96,128]{2,1,0:T(8,128)S(1)} %collective-permute-done.5.refs_1_, ...), custom_call_target="tpu_custom_call" | custom-call | flops 30000001024 | bytes 65536 | tf_op jit(solution)/shard_map/pallas_call | solution.py:333
  53.9 2.9 %collective-permute-start.12 = (f32[4,32,128]{2,1,0:T(8,128)S(1)}, f32[4,32,128]{2,1,0:T(8,128)S(1)}, u32[]{:S(2)}, u32[]{:S(2)}) collective-permute-start(f32[4,32,128]{2,1,0:T(8,128)S(1)} %add_add_fusion.4), channel_id=1, source_target_pairs={{0,16},{8,24},{16,0},{24,8},{1,17},{9,25},{17,1},{25,9},{2,18},{10... | collective-permute-start | bytes 196616 | tf_op jit(solution)/shard_map/ppermute | solution.py:358
  58.6 1.7 %collective-permute-done.13 = f32[4,32,128]{2,1,0:T(8,128)S(1)} collective-permute-done((f32[4,32,128]{2,1,0:T(8,128)S(1)}, f32[4,32,128]{2,1,0:T(8,128)S(1)}, u32[]{:S(2)}, u32[]{:S(2)}) %collective-permute-start.13) | collective-permute-done | bytes 65568 | tf_op jit(solution)/shard_map/ppermute | solution.py:358
  62.2 2.1 %collective-permute-start.15 = (f32[4,32,128]{2,1,0:T(8,128)S(1)}, f32[4,32,128]{2,1,0:T(8,128)S(1)}, u32[]{:S(2)}, u32[]{:S(2)}) collective-permute-start(f32[4,32,128]{2,1,0:T(8,128)S(1)} %get-tuple-element.66.own), channel_id=1, source_target_pairs={{0,32},{32,0},{1,33},{33,1},{2,34},{34,2},{3,35},{35,3},{4,36},{36... | collective-permute-start | bytes 196616 | tf_op jit(solution)/shard_map/ppermute | solution.py:358
  66.0 2.8 %collective-permute-start.16 = (f32[64,512]{1,0:T(8,128)S(1)}, f32[64,512]{1,0:T(8,128)S(1)}, u32[]{:S(2)}, u32[]{:S(2)}) collective-permute-start(f32[64,512]{1,0:T(8,128)S(1)} %get-tuple-element.72), channel_id=1, source_target_pairs={{0,4},{2,6},{4,0},{6,2},{1,5},{3,7},{5,1},{7,3},{8,12},{10,14},{12... | collective-permute-start | bytes 393224 | tf_op jit(solution)/shard_map/ppermute | solution.py:358
  69.7 2.6 %collective-permute-done.16 = f32[64,512]{1,0:T(8,128)S(1)} collective-permute-done((f32[64,512]{1,0:T(8,128)S(1)}, f32[64,512]{1,0:T(8,128)S(1)}, u32[]{:S(2)}, u32[]{:S(2)}) %collective-permute-start.16) | collective-permute-done | bytes 131104 | tf_op jit(solution)/shard_map/ppermute | solution.py:358
  72.3 2.9 %collective-permute-done.17 = f32[64,512]{1,0:T(8,128)S(1)} collective-permute-done((f32[64,512]{1,0:T(8,128)S(1)}, f32[64,512]{1,0:T(8,128)S(1)}, u32[]{:S(2)}, u32[]{:S(2)}) %collective-permute-start.17) | collective-permute-done | bytes 131104 | tf_op jit(solution)/shard_map/ppermute | solution.py:358
  75.3 1.5 %collective-permute-start.19 = (f32[64,512]{1,0:T(8,128)S(1)}, f32[64,512]{1,0:T(8,128)S(1)}, u32[]{:S(2)}, u32[]{:S(2)}) collective-permute-start(f32[64,512]{1,0:T(8,128)S(1)} %add_multiply_fusion), channel_id=1, source_target_pairs={{0,64},{1,65},{64,0},{65,1},{2,66},{3,67},{66,2},{67,3},{4,68},{5,... | collective-permute-start | bytes 393224 | tf_op jit(solution)/shard_map/ppermute | solution.py:358
  76.9 1.6 %collective-permute-start.20 = (f32[64,512]{1,0:T(8,128)S(1)}, f32[64,512]{1,0:T(8,128)S(1)}, u32[]{:S(2)}, u32[]{:S(2)}) collective-permute-start(f32[64,512]{1,0:T(8,128)S(1)} %add_multiply_fusion), channel_id=1, source_target_pairs={{0,1},{1,0},{64,65},{65,64},{2,3},{3,2},{66,67},{67,66},{4,5},{5,4... | collective-permute-start | bytes 393224 | tf_op jit(solution)/shard_map/ppermute | solution.py:358
  78.9 2.0 %shard_map.111.summed = bf16[512,512]{1,0:T(8,128)(2,1)S(1)} custom-call(f32[32,72,128]{2,1,0:T(8,128)S(1)} %all-to-all-done.points), custom_call_target="tpu_custom_call" | custom-call | flops 800000000 | bytes 2097152 | tf_op jit(solution)/shard_map/pallas_call | solution.py:333
  80.9 2.5 %collective-permute-done.20 = f32[64,512]{1,0:T(8,128)S(1)} collective-permute-done((f32[64,512]{1,0:T(8,128)S(1)}, f32[64,512]{1,0:T(8,128)S(1)}, u32[]{:S(2)}, u32[]{:S(2)}) %collective-permute-start.20) | collective-permute-done | bytes 131104 | tf_op jit(solution)/shard_map/ppermute | solution.py:358
  84.7 2.2 %collective-permute-start.22 = (f32[64,256]{1,0:T(8,128)S(1)}, f32[64,256]{1,0:T(8,128)S(1)}, u32[]{:S(2)}, u32[]{:S(2)}) collective-permute-start(f32[64,256]{1,0:T(8,128)S(1)} %shard_map.112), channel_id=1, source_target_pairs={{0,32},{32,0},{1,33},{33,1},{2,34},{34,2},{3,35},{35,3},{4,36},{36... | collective-permute-start | bytes 196616 | tf_op jit(solution)/shard_map/ppermute | solution.py:358
  87.8 2.8 %collective-permute-start.23 = (f32[64,256]{1,0:T(8,128)S(1)}, f32[64,256]{1,0:T(8,128)S(1)}, u32[]{:S(2)}, u32[]{:S(2)}) collective-permute-start(f32[64,256]{1,0:T(8,128)S(1)} %add.82), channel_id=1, source_target_pairs={{0,4},{2,6},{4,0},{6,2},{1,5},{3,7},{5,1},{7,3},{8,12},{10,14},{12... | collective-permute-start | bytes 196616 | tf_op jit(solution)/shard_map/ppermute | solution.py:358
  91.3 1.3 %collective-permute-done.23 = f32[64,256]{1,0:T(8,128)S(1)} collective-permute-done((f32[64,256]{1,0:T(8,128)S(1)}, f32[64,256]{1,0:T(8,128)S(1)}, u32[]{:S(2)}, u32[]{:S(2)}) %collective-permute-start.23) | collective-permute-done | bytes 65568 | tf_op jit(solution)/shard_map/ppermute | solution.py:358
  92.5 1.6 %collective-permute-done.24 = f32[64,256]{1,0:T(8,128)S(1)} collective-permute-done((f32[64,256]{1,0:T(8,128)S(1)}, f32[64,256]{1,0:T(8,128)S(1)}, u32[]{:S(2)}, u32[]{:S(2)}) %collective-permute-start.24) | collective-permute-done | bytes 65568 | tf_op jit(solution)/shard_map/ppermute | solution.py:358
  94.1 1.2 %collective-permute-done.25 = f32[64,256]{1,0:T(8,128)S(1)} collective-permute-done((f32[64,256]{1,0:T(8,128)S(1)}, f32[64,256]{1,0:T(8,128)S(1)}, u32[]{:S(2)}, u32[]{:S(2)}) %collective-permute-start.25) | collective-permute-done | bytes 65568 | tf_op jit(solution)/shard_map/ppermute | solution.py:358
  96.5 2.1 %collective-permute-start.28 = (f32[64,256]{1,0:T(8,128)S(1)}, f32[64,256]{1,0:T(8,128)S(1)}, u32[]{:S(2)}, u32[]{:S(2)}) collective-permute-start(f32[64,256]{1,0:T(8,128)S(1)} %add_add_fusion.2), channel_id=1, source_target_pairs={{0,24},{8,16},{16,8},{24,0},{1,25},{9,17},{17,9},{25,1},{2,26},{10... | collective-permute-start | bytes 196616 | tf_op jit(solution)/shard_map/ppermute | solution.py:358
  98.7 1.4 %collective-permute-done.26 = f32[64,256]{1,0:T(8,128)S(1)} collective-permute-done((f32[64,256]{1,0:T(8,128)S(1)}, f32[64,256]{1,0:T(8,128)S(1)}, u32[]{:S(2)}, u32[]{:S(2)}) %collective-permute-start.26) | collective-permute-done | bytes 65568 | tf_op jit(solution)/shard_map/ppermute | solution.py:358
  101.2 5.8 %collective-permute-start.29 = (f32[64,512]{1,0:T(8,128)S(1)}, f32[64,512]{1,0:T(8,128)S(1)}, u32[]{:S(2)}, u32[]{:S(2)}) collective-permute-start(f32[64,512]{1,0:T(8,128)S(1)} %shard_map.113), channel_id=1, source_target_pairs={{0,64},{1,96},{64,0},{65,32},{32,65},{33,97},{96,1},{97,33},{2,66}... | collective-permute-start | bytes 393224 | tf_op jit(solution)/shard_map/ppermute | solution.py:493
  107.7 3.7 %collective-permute-start.32 = (f32[64,512]{1,0:T(8,128)S(1)}, f32[64,512]{1,0:T(8,128)S(1)}, u32[]{:S(2)}, u32[]{:S(2)}) collective-permute-start(f32[64,512]{1,0:T(8,128)S(1)} %shard_map.113), channel_id=1, source_target_pairs={{0,0},{1,32},{64,64},{65,96},{32,1},{33,33},{96,65},{97,97},{2,2},... | collective-permute-start | bytes 393224 | tf_op jit(solution)/shard_map/ppermute | solution.py:493
  111.4 2.3 %collective-permute-done.30 = f32[64,512]{1,0:T(8,128)S(1)} collective-permute-done((f32[64,512]{1,0:T(8,128)S(1)}, f32[64,512]{1,0:T(8,128)S(1)}, u32[]{:S(2)}, u32[]{:S(2)}) %collective-permute-start.30) | collective-permute-done | bytes 131104 | tf_op jit(solution)/shard_map/ppermute | solution.py:493
  (58 shorter events, 20.1 us)
Async XLA Ops:
  2.9 13.0 %collective-permute-start = (f32[768,128]{1,0:T(8,128)S(1)}, f32[768,128]{1,0:T(8,128)S(1)}, u32[]{:S(2)}, u32[]{:S(2)}) collective-permute-start(f32[768,128]{1,0:T(8,128)S(1)} %get-tuple-element.40), channel_id=1, source_target_pairs={{0,0},{32,1},{1,32},{33,33},{2,2},{34,3},{3,34},{35,35},{4,4},{36,... | collective-permute-start | bytes 1179656 | tf_op jit(solution)/shard_map/ppermute | solution.py:411
  7.8 8.0 %collective-permute-start.1 = (f32[136,256]{1,0:T(8,128)S(1)}, f32[136,256]{1,0:T(8,128)S(1)}, u32[]{:S(2)}, u32[]{:S(2)}) collective-permute-start(f32[136,256]{1,0:T(8,128)S(1)} %get-tuple-element.41), channel_id=1, source_target_pairs={{0,65},{1,64},{64,1},{65,0},{2,67},{3,66},{66,3},{67,2},{4,69},{5,... | collective-permute-start | bytes 417800 | tf_op jit(solution)/shard_map/ppermute | solution.py:358
  8.2 4.4 %collective-permute-start.2 = (f32[96,128]{1,0:T(8,128)S(1)}, f32[96,128]{1,0:T(8,128)S(1)}, u32[]{:S(2)}, u32[]{:S(2)}) collective-permute-start(f32[96,128]{1,0:T(8,128)S(1)} %get-tuple-element.43.refs_0_), channel_id=1, source_target_pairs={{0,16},{8,24},{16,0},{24,8},{1,17},{9,25},{17,1},{25,9},{2,18},{10... | collective-permute-start | bytes 147464 | tf_op jit(solution)/shard_map/ppermute | solution.py:358
  11.0 3.2 %collective-permute-start.3 = (f32[96,128]{1,0:T(8,128)S(1)}, f32[96,128]{1,0:T(8,128)S(1)}, u32[]{:S(2)}, u32[]{:S(2)}) collective-permute-start(f32[96,128]{1,0:T(8,128)S(1)} %get-tuple-element.43.refs_0_), channel_id=1, source_target_pairs={{0,8},{8,0},{16,24},{24,16},{1,9},{9,1},{17,25},{25,17},{2,10},{10... | collective-permute-start | bytes 147464 | tf_op jit(solution)/shard_map/ppermute | solution.py:358
  11.3 4.6 %collective-permute-start.4 = (f32[96,128]{1,0:T(8,128)S(1)}, f32[96,128]{1,0:T(8,128)S(1)}, u32[]{:S(2)}, u32[]{:S(2)}) collective-permute-start(f32[96,128]{1,0:T(8,128)S(1)} %get-tuple-element.43.refs_0_), channel_id=1, source_target_pairs={{0,24},{8,16},{16,8},{24,0},{1,25},{9,17},{17,9},{25,1},{2,26},{10... | collective-permute-start | bytes 147464 | tf_op jit(solution)/shard_map/ppermute | solution.py:358
  15.9 23.8 %collective-permute-start.10 = (f32[768,128]{1,0:T(8,128)S(1)}, f32[768,128]{1,0:T(8,128)}, u32[]{:S(2)}, u32[]{:S(2)}) collective-permute-start(f32[768,128]{1,0:T(8,128)S(1)} %collective-permute-done.refs_2_), channel_id=1, source_target_pairs={{0,4},{2,6},{4,0},{6,2},{1,5},{3,7},{5,1},{7,3},{8,12},{10,14},{12... | collective-permute-start | bytes 1179656 | tf_op jit(solution)/shard_map/ppermute | solution.py:358
  18.8 20.9 %collective-permute-start.8 = (f32[768,128]{1,0:T(8,128)S(1)}, f32[768,128]{1,0:T(8,128)}, u32[]{:S(2)}, u32[]{:S(2)}) collective-permute-start(f32[768,128]{1,0:T(8,128)S(1)} %collective-permute-done.refs_2_), channel_id=1, source_target_pairs={{0,2},{2,0},{4,6},{6,4},{1,3},{3,1},{5,7},{7,5},{8,10},{10,8},{12,... | collective-permute-start | bytes 1179656 | tf_op jit(solution)/shard_map/ppermute | solution.py:358
  19.2 20.5 %collective-permute-start.9 = (f32[768,128]{1,0:T(8,128)S(1)}, f32[768,128]{1,0:T(8,128)}, u32[]{:S(2)}, u32[]{:S(2)}) collective-permute-start(f32[768,128]{1,0:T(8,128)S(1)} %collective-permute-done.refs_2_), channel_id=1, source_target_pairs={{0,6},{2,4},{4,2},{6,0},{1,7},{3,5},{5,3},{7,1},{8,14},{10,12},{12... | collective-permute-start | bytes 1179656 | tf_op jit(solution)/shard_map/ppermute | solution.py:358
  19.6 5.2 %collective-permute-start.5 = (f32[4,96,128]{2,1,0:T(8,128)S(1)}, f32[4,96,128]{2,1,0:T(8,128)S(1)}, u32[]{:S(2)}, u32[]{:S(2)}) collective-permute-start(f32[4,96,128]{2,1,0:T(8,128)S(1)} %shard_map.105.refs_0_.own), channel_id=1, source_target_pairs={{0,32},{32,0},{1,33},{33,1},{2,34},{34,2},{3,35},{35,3},{4,36},{36... | collective-permute-start | bytes 589832 | tf_op jit(solution)/shard_map/ppermute | solution.py:358
  24.8 6.5 %collective-permute-start.6 = (f32[136,256]{1,0:T(8,128)S(1)}, f32[136,256]{1,0:T(8,128)S(1)}, u32[]{:S(2)}, u32[]{:S(2)}) collective-permute-start(f32[136,256]{1,0:T(8,128)S(1)} %get-tuple-element.54), channel_id=1, source_target_pairs={{0,64},{1,65},{64,0},{65,1},{2,66},{3,67},{66,2},{67,3},{4,68},{5,... | collective-permute-start | bytes 417800 | tf_op jit(solution)/shard_map/ppermute | solution.py:358
  24.8 6.9 %collective-permute-start.7 = (f32[136,256]{1,0:T(8,128)S(1)}, f32[136,256]{1,0:T(8,128)S(1)}, u32[]{:S(2)}, u32[]{:S(2)}) collective-permute-start(f32[136,256]{1,0:T(8,128)S(1)} %get-tuple-element.55), channel_id=1, source_target_pairs={{0,1},{1,0},{64,65},{65,64},{2,3},{3,2},{66,67},{67,66},{4,5},{5,4... | collective-permute-start | bytes 417800 | tf_op jit(solution)/shard_map/ppermute | solution.py:358
  33.4 41.9 %all-to-all-start = ((f32[32,72,128]{2,1,0:T(8,128)}), f32[32,72,128]{2,1,0:T(8,128)S(1)}, u32[]{:S(2)}, u32[]{:S(2)}) async-start(f32[32,72,128]{2,1,0:T(8,128)} %shard_map.109), calls=%async_computation | async-start | bytes 2359296 | tf_op jit(solution)/shard_map/all_to_all | solution.py:453
  53.9 4.7 %collective-permute-start.12 = (f32[4,32,128]{2,1,0:T(8,128)S(1)}, f32[4,32,128]{2,1,0:T(8,128)S(1)}, u32[]{:S(2)}, u32[]{:S(2)}) collective-permute-start(f32[4,32,128]{2,1,0:T(8,128)S(1)} %add_add_fusion.4), channel_id=1, source_target_pairs={{0,16},{8,24},{16,0},{24,8},{1,17},{9,25},{17,1},{25,9},{2,18},{10... | collective-permute-start | bytes 196616 | tf_op jit(solution)/shard_map/ppermute | solution.py:358
  56.8 3.5 %collective-permute-start.13 = (f32[4,32,128]{2,1,0:T(8,128)S(1)}, f32[4,32,128]{2,1,0:T(8,128)S(1)}, u32[]{:S(2)}, u32[]{:S(2)}) collective-permute-start(f32[4,32,128]{2,1,0:T(8,128)S(1)} %add_add_fusion.4), channel_id=1, source_target_pairs={{0,8},{8,0},{16,24},{24,16},{1,9},{9,1},{17,25},{25,17},{2,10},{10... | collective-permute-start | bytes 196616 | tf_op jit(solution)/shard_map/ppermute | solution.py:358
  57.2 4.3 %collective-permute-start.14 = (f32[4,32,128]{2,1,0:T(8,128)S(1)}, f32[4,32,128]{2,1,0:T(8,128)S(1)}, u32[]{:S(2)}, u32[]{:S(2)}) collective-permute-start(f32[4,32,128]{2,1,0:T(8,128)S(1)} %add_add_fusion.4), channel_id=1, source_target_pairs={{0,24},{8,16},{16,8},{24,0},{1,25},{9,17},{17,9},{25,1},{2,26},{10... | collective-permute-start | bytes 196616 | tf_op jit(solution)/shard_map/ppermute | solution.py:358
  66.0 6.3 %collective-permute-start.16 = (f32[64,512]{1,0:T(8,128)S(1)}, f32[64,512]{1,0:T(8,128)S(1)}, u32[]{:S(2)}, u32[]{:S(2)}) collective-permute-start(f32[64,512]{1,0:T(8,128)S(1)} %get-tuple-element.72), channel_id=1, source_target_pairs={{0,4},{2,6},{4,0},{6,2},{1,5},{3,7},{5,1},{7,3},{8,12},{10,14},{12... | collective-permute-start | bytes 393224 | tf_op jit(solution)/shard_map/ppermute | solution.py:358
  68.8 6.4 %collective-permute-start.17 = (f32[64,512]{1,0:T(8,128)S(1)}, f32[64,512]{1,0:T(8,128)S(1)}, u32[]{:S(2)}, u32[]{:S(2)}) collective-permute-start(f32[64,512]{1,0:T(8,128)S(1)} %get-tuple-element.73), channel_id=1, source_target_pairs={{0,2},{2,0},{4,6},{6,4},{1,3},{3,1},{5,7},{7,5},{8,10},{10,8},{12,... | collective-permute-start | bytes 393224 | tf_op jit(solution)/shard_map/ppermute | solution.py:358
  69.1 6.2 %collective-permute-start.18 = (f32[64,512]{1,0:T(8,128)S(1)}, f32[64,512]{1,0:T(8,128)S(1)}, u32[]{:S(2)}, u32[]{:S(2)}) collective-permute-start(f32[64,512]{1,0:T(8,128)S(1)} %get-tuple-element.74), channel_id=1, source_target_pairs={{0,6},{2,4},{4,2},{6,0},{1,7},{3,5},{5,3},{7,1},{8,14},{10,12},{12... | collective-permute-start | bytes 393224 | tf_op jit(solution)/shard_map/ppermute | solution.py:358
  75.3 5.6 %collective-permute-start.19 = (f32[64,512]{1,0:T(8,128)S(1)}, f32[64,512]{1,0:T(8,128)S(1)}, u32[]{:S(2)}, u32[]{:S(2)}) collective-permute-start(f32[64,512]{1,0:T(8,128)S(1)} %add_multiply_fusion), channel_id=1, source_target_pairs={{0,64},{1,65},{64,0},{65,1},{2,66},{3,67},{66,2},{67,3},{4,68},{5,... | collective-permute-start | bytes 393224 | tf_op jit(solution)/shard_map/ppermute | solution.py:358
  76.9 6.5 %collective-permute-start.20 = (f32[64,512]{1,0:T(8,128)S(1)}, f32[64,512]{1,0:T(8,128)S(1)}, u32[]{:S(2)}, u32[]{:S(2)}) collective-permute-start(f32[64,512]{1,0:T(8,128)S(1)} %add_multiply_fusion), channel_id=1, source_target_pairs={{0,1},{1,0},{64,65},{65,64},{2,3},{3,2},{66,67},{67,66},{4,5},{5,4... | collective-permute-start | bytes 393224 | tf_op jit(solution)/shard_map/ppermute | solution.py:358
  78.5 6.0 %collective-permute-start.21 = (f32[64,512]{1,0:T(8,128)S(1)}, f32[64,512]{1,0:T(8,128)S(1)}, u32[]{:S(2)}, u32[]{:S(2)}) collective-permute-start(f32[64,512]{1,0:T(8,128)S(1)} %add_multiply_fusion), channel_id=1, source_target_pairs={{0,65},{1,64},{64,1},{65,0},{2,67},{3,66},{66,3},{67,2},{4,69},{5,... | collective-permute-start | bytes 393224 | tf_op jit(solution)/shard_map/ppermute | solution.py:358
  84.7 3.1 %collective-permute-start.22 = (f32[64,256]{1,0:T(8,128)S(1)}, f32[64,256]{1,0:T(8,128)S(1)}, u32[]{:S(2)}, u32[]{:S(2)}) collective-permute-start(f32[64,256]{1,0:T(8,128)S(1)} %shard_map.112), channel_id=1, source_target_pairs={{0,32},{32,0},{1,33},{33,1},{2,34},{34,2},{3,35},{35,3},{4,36},{36... | collective-permute-start | bytes 196616 | tf_op jit(solution)/shard_map/ppermute | solution.py:358
  87.8 4.7 %collective-permute-start.23 = (f32[64,256]{1,0:T(8,128)S(1)}, f32[64,256]{1,0:T(8,128)S(1)}, u32[]{:S(2)}, u32[]{:S(2)}) collective-permute-start(f32[64,256]{1,0:T(8,128)S(1)} %add.82), channel_id=1, source_target_pairs={{0,4},{2,6},{4,0},{6,2},{1,5},{3,7},{5,1},{7,3},{8,12},{10,14},{12... | collective-permute-start | bytes 196616 | tf_op jit(solution)/shard_map/ppermute | solution.py:358
  90.7 3.5 %collective-permute-start.24 = (f32[64,256]{1,0:T(8,128)S(1)}, f32[64,256]{1,0:T(8,128)S(1)}, u32[]{:S(2)}, u32[]{:S(2)}) collective-permute-start(f32[64,256]{1,0:T(8,128)S(1)} %add.82), channel_id=1, source_target_pairs={{0,2},{2,0},{4,6},{6,4},{1,3},{3,1},{5,7},{7,5},{8,10},{10,8},{12,... | collective-permute-start | bytes 196616 | tf_op jit(solution)/shard_map/ppermute | solution.py:358
  91.0 4.3 %collective-permute-start.25 = (f32[64,256]{1,0:T(8,128)S(1)}, f32[64,256]{1,0:T(8,128)S(1)}, u32[]{:S(2)}, u32[]{:S(2)}) collective-permute-start(f32[64,256]{1,0:T(8,128)S(1)} %add.82), channel_id=1, source_target_pairs={{0,6},{2,4},{4,2},{6,0},{1,7},{3,5},{5,3},{7,1},{8,14},{10,12},{12... | collective-permute-start | bytes 196616 | tf_op jit(solution)/shard_map/ppermute | solution.py:358
  95.3 4.7 %collective-permute-start.26 = (f32[64,256]{1,0:T(8,128)S(1)}, f32[64,256]{1,0:T(8,128)S(1)}, u32[]{:S(2)}, u32[]{:S(2)}) collective-permute-start(f32[64,256]{1,0:T(8,128)S(1)} %add_add_fusion.2), channel_id=1, source_target_pairs={{0,16},{8,24},{16,0},{24,8},{1,17},{9,25},{17,1},{25,9},{2,18},{10... | collective-permute-start | bytes 196616 | tf_op jit(solution)/shard_map/ppermute | solution.py:358
  96.1 3.9 %collective-permute-start.27 = (f32[64,256]{1,0:T(8,128)S(1)}, f32[64,256]{1,0:T(8,128)S(1)}, u32[]{:S(2)}, u32[]{:S(2)}) collective-permute-start(f32[64,256]{1,0:T(8,128)S(1)} %add_add_fusion.2), channel_id=1, source_target_pairs={{0,8},{8,0},{16,24},{24,16},{1,9},{9,1},{17,25},{25,17},{2,10},{10... | collective-permute-start | bytes 196616 | tf_op jit(solution)/shard_map/ppermute | solution.py:358
  96.5 4.3 %collective-permute-start.28 = (f32[64,256]{1,0:T(8,128)S(1)}, f32[64,256]{1,0:T(8,128)S(1)}, u32[]{:S(2)}, u32[]{:S(2)}) collective-permute-start(f32[64,256]{1,0:T(8,128)S(1)} %add_add_fusion.2), channel_id=1, source_target_pairs={{0,24},{8,16},{16,8},{24,0},{1,25},{9,17},{17,9},{25,1},{2,26},{10... | collective-permute-start | bytes 196616 | tf_op jit(solution)/shard_map/ppermute | solution.py:358
  101.2 10.1 %collective-permute-start.29 = (f32[64,512]{1,0:T(8,128)S(1)}, f32[64,512]{1,0:T(8,128)S(1)}, u32[]{:S(2)}, u32[]{:S(2)}) collective-permute-start(f32[64,512]{1,0:T(8,128)S(1)} %shard_map.113), channel_id=1, source_target_pairs={{0,64},{1,96},{64,0},{65,32},{32,65},{33,97},{96,1},{97,33},{2,66}... | collective-permute-start | bytes 393224 | tf_op jit(solution)/shard_map/ppermute | solution.py:493
  107.0 6.7 %collective-permute-start.30 = (f32[64,512]{1,0:T(8,128)S(1)}, f32[64,512]{1,0:T(8,128)S(1)}, u32[]{:S(2)}, u32[]{:S(2)}) collective-permute-start(f32[64,512]{1,0:T(8,128)S(1)} %shard_map.113), channel_id=1, source_target_pairs={{0,96},{1,64},{64,32},{65,0},{32,97},{33,65},{96,33},{97,1},{2,98}... | collective-permute-start | bytes 393224 | tf_op jit(solution)/shard_map/ppermute | solution.py:493
  107.0 6.7 %collective-permute-start.31 = (f32[64,512]{1,0:T(8,128)S(1)}, f32[64,512]{1,0:T(8,128)S(1)}, u32[]{:S(2)}, u32[]{:S(2)}) collective-permute-start(f32[64,512]{1,0:T(8,128)S(1)} %shard_map.113), channel_id=1, source_target_pairs={{0,32},{1,0},{64,96},{65,64},{32,33},{33,1},{96,97},{97,65},{2,34}... | collective-permute-start | bytes 393224 | tf_op jit(solution)/shard_map/ppermute | solution.py:493
  107.7 6.5 %collective-permute-start.32 = (f32[64,512]{1,0:T(8,128)S(1)}, f32[64,512]{1,0:T(8,128)S(1)}, u32[]{:S(2)}, u32[]{:S(2)}) collective-permute-start(f32[64,512]{1,0:T(8,128)S(1)} %shard_map.113), channel_id=1, source_target_pairs={{0,0},{1,32},{64,64},{65,96},{32,1},{33,33},{96,65},{97,97},{2,2},... | collective-permute-start | bytes 393224 | tf_op jit(solution)/shard_map/ppermute | solution.py:493
  (3 other events, 24.4 us)

commit v16 on v14

--- a/solution.py
+++ b/solution.py
@@ -418,7 +418,8 @@
     )
     others = [mate_of(tile, ("y",), o) for o in TILES[1:]]
     mate = mate_of(own, ("core",), 1)
-    mate, second, third = together(mate, parted[1], parted[3])
+    own, second = together(own, parted[1])
+    mate, third = together(mate, parted[3])
     parted = [parted[0], first, mate_of(second, PLANES, 1), mate_of(third, PLANES, 3)]
 
     def kernel(packs, extra):

time: 114 us -> 114 us (level)
  no operation moved by 1% of the time
where the time goes in v16:
time: 114 us
  starting transfers between devices  55.1 us (48%)
  waiting for transfers between devices  32.1 us (28%)
  Pallas kernels  24.7 us (22%)
    ppermute x28, starting transfers between devices, mate_of(): return lax.ppermute(v, axes, [(i, i ^ o) for i in range(n)])  34.8 us
    ppermute x28, waiting for transfers between devices, mate_of(): return lax.ppermute(v, axes, [(i, i ^ o) for i in range(n)])  28.7 us
    pallas_call x9, Pallas kernels, call(): pl.pallas_call(body, out_shape=outs, in_specs=[smem] * scalars + [VMEM] *...  22.5 us
    ppermute x4, starting transfers between devices, per_device(): received.append(lax.ppermute(corr, ('zh', 'core', 'zl'), perm))  8.85 us
    all_to_all x1, starting transfers between devices, per_device(): lax.all_to_all(points, OWNERS, split_axis=0, concat_axis=0, tiled=True)  6.43 us
    ppermute x1, starting transfers between devices, per_device(): tile = lax.ppermute(pack, ('core', 'zl'), [(0, 0), (2, 1), (1, 2), (3, 3)])  4.93 us
    ppermute x4, waiting for transfers between devices, per_device(): received.append(lax.ppermute(corr, ('zh', 'core', 'zl'), perm))  3.49 us
  transfers between devices with their start and end apart: 34, of which 24 were waited for; matrix products, arithmetic and copies ran while one was open for 0% of the time, Pallas kernels for 19%

profile of v16, /device:TPU:1, one launch (start us, length us, event | category | flops | bytes accessed | tf_op | source)
XLA Modules:
  0.0 113.6 jit_solution(10003181992881597156)
XLA Ops:
  0.6 2.2 %shard_map.104 = (f32[96,128]{1,0:T(8,128)S(1)}, f32[768,128]{1,0:T(8,128)S(1)}, f32[136,256]{1,0:T(8,128)S(1)}, f32[136,256]{1,0:T(8,128)S(1)}, f32[136,256]{1,0:T(8,128)S(1)}, /*index=5*/f32[136,256]{1,0:T(8,128)S(1)}) custom-call(s32[1]{0:T(128)} %bitcast.1.member, s32[1,64]{1,0:T(1,128)} %bitcast.15, f32[1024,128]{1,0:T(8,128)} %refs_1_.1, ...), custom_call_target="tpu_custom_call" | custom-call | tf_op jit(solution)/shard_map/pallas_call | solution.py:381
  2.9 4.9 %collective-permute-start = (f32[768,128]{1,0:T(8,128)S(1)}, f32[768,128]{1,0:T(8,128)S(1)}, u32[]{:S(2)}, u32[]{:S(2)}) collective-permute-start(f32[768,128]{1,0:T(8,128)S(1)} %get-tuple-element.41), channel_id=1, source_target_pairs={{0,0},{32,1},{1,32},{33,33},{2,2},{34,3},{3,34},{35,35},{4,4},{36,... | collective-permute-start | bytes 1179656 | tf_op jit(solution)/shard_map/ppermute | solution.py:411
  7.8 3.4 %collective-permute-start.1 = (f32[136,256]{1,0:T(8,128)S(1)}, f32[136,256]{1,0:T(8,128)S(1)}, u32[]{:S(2)}, u32[]{:S(2)}) collective-permute-start(f32[136,256]{1,0:T(8,128)S(1)} %get-tuple-element.42), channel_id=1, source_target_pairs={{0,64},{1,65},{64,0},{65,1},{2,66},{3,67},{66,2},{67,3},{4,68},{5,... | collective-permute-start | bytes 417800 | tf_op jit(solution)/shard_map/ppermute | solution.py:358
  11.2 2.7 %collective-permute-start.2 = (f32[96,128]{1,0:T(8,128)S(1)}, f32[96,128]{1,0:T(8,128)S(1)}, u32[]{:S(2)}, u32[]{:S(2)}) collective-permute-start(f32[96,128]{1,0:T(8,128)S(1)} %get-tuple-element.44.refs_0_), channel_id=1, source_target_pairs={{0,16},{8,24},{16,0},{24,8},{1,17},{9,25},{17,1},{25,9},{2,18},{10... | collective-permute-start | bytes 147464 | tf_op jit(solution)/shard_map/ppermute | solution.py:358
  15.9 1.3 %collective-permute-done.3.refs_2_ = f32[96,128]{1,0:T(8,128)S(1)} collective-permute-done((f32[96,128]{1,0:T(8,128)S(1)}, f32[96,128]{1,0:T(8,128)S(1)}, u32[]{:S(2)}, u32[]{:S(2)}) %collective-permute-start.3) | collective-permute-done | bytes 49184 | tf_op jit(solution)/shard_map/ppermute | solution.py:358
  18.4 2.9 %collective-permute-start.10 = (f32[768,128]{1,0:T(8,128)S(1)}, f32[768,128]{1,0:T(8,128)}, u32[]{:S(2)}, u32[]{:S(2)}) collective-permute-start(f32[768,128]{1,0:T(8,128)S(1)} %collective-permute-done.refs_2_), channel_id=1, source_target_pairs={{0,4},{2,6},{4,0},{6,2},{1,5},{3,7},{5,1},{7,3},{8,12},{10,14},{12... | collective-permute-start | bytes 1179656 | tf_op jit(solution)/shard_map/ppermute | solution.py:358
  22.3 2.0 %collective-permute-start.6 = (f32[136,256]{1,0:T(8,128)S(1)}, f32[136,256]{1,0:T(8,128)S(1)}, u32[]{:S(2)}, u32[]{:S(2)}) collective-permute-start(f32[136,256]{1,0:T(8,128)S(1)} %get-tuple-element.56), channel_id=1, source_target_pairs={{0,1},{1,0},{64,65},{65,64},{2,3},{3,2},{66,67},{67,66},{4,5},{5,4... | collective-permute-start | bytes 417800 | tf_op jit(solution)/shard_map/ppermute | solution.py:358
  25.0 3.9 %shard_map.106 = (bf16[1,512,512]{2,1,0:T(8,128)(2,1)S(1)}, bf16[1,512,512]{2,1,0:T(8,128)(2,1)S(1)}, f32[4,32,128]{2,1,0:T(8,128)S(1)}, f32[4,32,128]{2,1,0:T(8...) custom-call(f32[4,96,128]{2,1,0:T(8,128)S(1)} %shard_map.105.refs_0_.own, ...), custom_call_target="tpu_custom_call" | custom-call | flops 100000000 | bytes 65536 | tf_op jit(solution)/shard_map/pallas_call | solution.py:333
  28.9 1.6 %collective-permute-done.7.refs_3_ = f32[136,256]{1,0:T(8,128)S(1)} collective-permute-done((f32[136,256]{1,0:T(8,128)S(1)}, f32[136,256]{1,0:T(8,128)S(1)}, u32[]{:S(2)}, u32[]{:S(2)}) %collective-permute-start.7) | collective-permute-done | bytes 139296 | tf_op jit(solution)/shard_map/ppermute | solution.py:358
  30.5 1.7 %shard_map.109 = f32[32,72,128]{2,1,0:T(8,128)} custom-call(f32[136,256]{1,0:T(8,128)S(1)} %get-tuple-element.64.refs_0_, f32[136,256]{1,0:T(8,128)S(1)} %collective-permute-done.1.refs_1_, f32[136,256]{1,0:T(8,128)S(1)} %collective-permute-done.6.refs_2_, f32[136,256]{1,0:T(8,128)S(1)} %collective-permute-done.7.refs_3_), custom_call_target="tpu_custom_call" | custom-call | tf_op jit(solution)/shard_map/pallas_call | solution.py:333
  32.2 6.4 %all-to-all-start = ((f32[32,72,128]{2,1,0:T(8,128)}), f32[32,72,128]{2,1,0:T(8,128)S(1)}, u32[]{:S(2)}, u32[]{:S(2)}) async-start(f32[32,72,128]{2,1,0:T(8,128)} %shard_map.109), calls=%async_computation | async-start | bytes 2359296 | tf_op jit(solution)/shard_map/all_to_all | solution.py:454
  40.0 12.8 %shard_map.107 = (bf16[3,512,512]{2,1,0:T(8,128)(2,1)S(1)}, bf16[3,512,512]{2,1,0:T(8,128)(2,1)S(1)}, f32[4,32,128]{2,1,0:T(8,128)S(1)}, f32[4,32,128]{2,1,0:T(8,128)S(1)}) custom-call(f32[4,96,128]{2,1,0:T(8,128)S(1)} %shard_map.105.refs_0_.own, f32[4,96,128]{2,1,0:T(8,128)S(1)} %collective-permute-done.5.refs_1_, ...), custom_call_target="tpu_custom_call" | custom-call | flops 30000001024 | bytes 65536 | tf_op jit(solution)/shard_map/pallas_call | solution.py:333
  54.2 1.7 %collective-permute-start.12 = (f32[4,32,128]{2,1,0:T(8,128)S(1)}, f32[4,32,128]{2,1,0:T(8,128)S(1)}, u32[]{:S(2)}, u32[]{:S(2)}) collective-permute-start(f32[4,32,128]{2,1,0:T(8,128)S(1)} %add_add_fusion.4), channel_id=1, source_target_pairs={{0,16},{8,24},{16,0},{24,8},{1,17},{9,25},{17,1},{25,9},{2,18},{10... | collective-permute-start | bytes 196616 | tf_op jit(solution)/shard_map/ppermute | solution.py:358
  56.2 1.3 %collective-permute-start.14 = (f32[4,32,128]{2,1,0:T(8,128)S(1)}, f32[4,32,128]{2,1,0:T(8,128)S(1)}, u32[]{:S(2)}, u32[]{:S(2)}) collective-permute-start(f32[4,32,128]{2,1,0:T(8,128)S(1)} %add_add_fusion.4), channel_id=1, source_target_pairs={{0,24},{8,16},{16,8},{24,0},{1,25},{9,17},{17,9},{25,1},{2,26},{10... | collective-permute-start | bytes 196616 | tf_op jit(solution)/shard_map/ppermute | solution.py:358
  57.5 1.4 %collective-permute-done.12 = f32[4,32,128]{2,1,0:T(8,128)S(1)} collective-permute-done((f32[4,32,128]{2,1,0:T(8,128)S(1)}, f32[4,32,128]{2,1,0:T(8,128)S(1)}, u32[]{:S(2)}, u32[]{:S(2)}) %collective-permute-start.12) | collective-permute-done | bytes 65568 | tf_op jit(solution)/shard_map/ppermute | solution.py:358
  61.6 1.8 %collective-permute-start.15 = (f32[4,32,128]{2,1,0:T(8,128)S(1)}, f32[4,32,128]{2,1,0:T(8,128)S(1)}, u32[]{:S(2)}, u32[]{:S(2)}) collective-permute-start(f32[4,32,128]{2,1,0:T(8,128)S(1)} %get-tuple-element.68.own), channel_id=1, source_target_pairs={{0,32},{32,0},{1,33},{33,1},{2,34},{34,2},{3,35},{35,3},{4,36},{36... | collective-permute-start | bytes 196616 | tf_op jit(solution)/shard_map/ppermute | solution.py:358
  65.1 2.8 %collective-permute-start.16 = (f32[64,512]{1,0:T(8,128)S(1)}, f32[64,512]{1,0:T(8,128)S(1)}, u32[]{:S(2)}, u32[]{:S(2)}) collective-permute-start(f32[64,512]{1,0:T(8,128)S(1)} %get-tuple-element.74), channel_id=1, source_target_pairs={{0,4},{2,6},{4,0},{6,2},{1,5},{3,7},{5,1},{7,3},{8,12},{10,14},{12... | collective-permute-start | bytes 393224 | tf_op jit(solution)/shard_map/ppermute | solution.py:358
  68.7 2.6 %collective-permute-done.16 = f32[64,512]{1,0:T(8,128)S(1)} collective-permute-done((f32[64,512]{1,0:T(8,128)S(1)}, f32[64,512]{1,0:T(8,128)S(1)}, u32[]{:S(2)}, u32[]{:S(2)}) %collective-permute-start.16) | collective-permute-done | bytes 131104 | tf_op jit(solution)/shard_map/ppermute | solution.py:358
  71.4 2.8 %collective-permute-done.17 = f32[64,512]{1,0:T(8,128)S(1)} collective-permute-done((f32[64,512]{1,0:T(8,128)S(1)}, f32[64,512]{1,0:T(8,128)S(1)}, u32[]{:S(2)}, u32[]{:S(2)}) %collective-permute-start.17) | collective-permute-done | bytes 131104 | tf_op jit(solution)/shard_map/ppermute | solution.py:358
  75.4 1.7 %collective-permute-start.20 = (f32[64,512]{1,0:T(8,128)S(1)}, f32[64,512]{1,0:T(8,128)S(1)}, u32[]{:S(2)}, u32[]{:S(2)}) collective-permute-start(f32[64,512]{1,0:T(8,128)S(1)} %add_multiply_fusion), channel_id=1, source_target_pairs={{0,1},{1,0},{64,65},{65,64},{2,3},{3,2},{66,67},{67,66},{4,5},{5,4... | collective-permute-start | bytes 393224 | tf_op jit(solution)/shard_map/ppermute | solution.py:358
  77.7 2.0 %shard_map.111.summed = bf16[512,512]{1,0:T(8,128)(2,1)S(1)} custom-call(f32[32,72,128]{2,1,0:T(8,128)S(1)} %all-to-all-done.points), custom_call_target="tpu_custom_call" | custom-call | flops 800000000 | bytes 2097152 | tf_op jit(solution)/shard_map/pallas_call | solution.py:333
  79.8 2.3 %collective-permute-done.20 = f32[64,512]{1,0:T(8,128)S(1)} collective-permute-done((f32[64,512]{1,0:T(8,128)S(1)}, f32[64,512]{1,0:T(8,128)S(1)}, u32[]{:S(2)}, u32[]{:S(2)}) %collective-permute-start.20) | collective-permute-done | bytes 131104 | tf_op jit(solution)/shard_map/ppermute | solution.py:358
  82.0 1.7 %collective-permute-done.21 = f32[64,512]{1,0:T(8,128)S(1)} collective-permute-done((f32[64,512]{1,0:T(8,128)S(1)}, f32[64,512]{1,0:T(8,128)S(1)}, u32[]{:S(2)}, u32[]{:S(2)}) %collective-permute-start.21) | collective-permute-done | bytes 131104 | tf_op jit(solution)/shard_map/ppermute | solution.py:358
  84.0 1.7 %collective-permute-start.22 = (f32[64,256]{1,0:T(8,128)S(1)}, f32[64,256]{1,0:T(8,128)S(1)}, u32[]{:S(2)}, u32[]{:S(2)}) collective-permute-start(f32[64,256]{1,0:T(8,128)S(1)} %shard_map.112), channel_id=1, source_target_pairs={{0,32},{32,0},{1,33},{33,1},{2,34},{34,2},{3,35},{35,3},{4,36},{36... | collective-permute-start | bytes 196616 | tf_op jit(solution)/shard_map/ppermute | solution.py:358
  86.7 2.9 %collective-permute-start.23 = (f32[64,256]{1,0:T(8,128)S(1)}, f32[64,256]{1,0:T(8,128)S(1)}, u32[]{:S(2)}, u32[]{:S(2)}) collective-permute-start(f32[64,256]{1,0:T(8,128)S(1)} %add.82), channel_id=1, source_target_pairs={{0,4},{2,6},{4,0},{6,2},{1,5},{3,7},{5,1},{7,3},{8,12},{10,14},{12... | collective-permute-start | bytes 196616 | tf_op jit(solution)/shard_map/ppermute | solution.py:358
  91.4 1.6 %collective-permute-done.24 = f32[64,256]{1,0:T(8,128)S(1)} collective-permute-done((f32[64,256]{1,0:T(8,128)S(1)}, f32[64,256]{1,0:T(8,128)S(1)}, u32[]{:S(2)}, u32[]{:S(2)}) %collective-permute-start.24) | collective-permute-done | bytes 65568 | tf_op jit(solution)/shard_map/ppermute | solution.py:358
  95.8 1.7 %collective-permute-start.28 = (f32[64,256]{1,0:T(8,128)S(1)}, f32[64,256]{1,0:T(8,128)S(1)}, u32[]{:S(2)}, u32[]{:S(2)}) collective-permute-start(f32[64,256]{1,0:T(8,128)S(1)} %add_add_fusion.2), channel_id=1, source_target_pairs={{0,24},{8,16},{16,8},{24,0},{1,25},{9,17},{17,9},{25,1},{2,26},{10... | collective-permute-start | bytes 196616 | tf_op jit(solution)/shard_map/ppermute | solution.py:358
  97.5 1.4 %collective-permute-done.26 = f32[64,256]{1,0:T(8,128)S(1)} collective-permute-done((f32[64,256]{1,0:T(8,128)S(1)}, f32[64,256]{1,0:T(8,128)S(1)}, u32[]{:S(2)}, u32[]{:S(2)}) %collective-permute-start.26) | collective-permute-done | bytes 65568 | tf_op jit(solution)/shard_map/ppermute | solution.py:358
  98.9 1.3 %collective-permute-done.28 = f32[64,256]{1,0:T(8,128)S(1)} collective-permute-done((f32[64,256]{1,0:T(8,128)S(1)}, f32[64,256]{1,0:T(8,128)S(1)}, u32[]{:S(2)}, u32[]{:S(2)}) %collective-permute-start.28) | collective-permute-done | bytes 65568 | tf_op jit(solution)/shard_map/ppermute | solution.py:358
  100.5 5.1 %collective-permute-start.29 = (f32[64,512]{1,0:T(8,128)S(1)}, f32[64,512]{1,0:T(8,128)S(1)}, u32[]{:S(2)}, u32[]{:S(2)}) collective-permute-start(f32[64,512]{1,0:T(8,128)S(1)} %shard_map.113), channel_id=1, source_target_pairs={{0,64},{1,96},{64,0},{65,32},{32,65},{33,97},{96,1},{97,33},{2,66}... | collective-permute-start | bytes 393224 | tf_op jit(solution)/shard_map/ppermute | solution.py:494
  106.3 3.1 %collective-permute-start.32 = (f32[64,512]{1,0:T(8,128)S(1)}, f32[64,512]{1,0:T(8,128)S(1)}, u32[]{:S(2)}, u32[]{:S(2)}) collective-permute-start(f32[64,512]{1,0:T(8,128)S(1)} %shard_map.113), channel_id=1, source_target_pairs={{0,0},{1,32},{64,64},{65,96},{32,1},{33,33},{96,65},{97,97},{2,2},... | collective-permute-start | bytes 393224 | tf_op jit(solution)/shard_map/ppermute | solution.py:494
  109.4 2.8 %collective-permute-done.30 = f32[64,512]{1,0:T(8,128)S(1)} collective-permute-done((f32[64,512]{1,0:T(8,128)S(1)}, f32[64,512]{1,0:T(8,128)S(1)}, u32[]{:S(2)}, u32[]{:S(2)}) %collective-permute-start.30) | collective-permute-done | bytes 131104 | tf_op jit(solution)/shard_map/ppermute | solution.py:494
  (58 shorter events, 23.3 us)
Async XLA Ops:
  2.9 15.5 %collective-permute-start = (f32[768,128]{1,0:T(8,128)S(1)}, f32[768,128]{1,0:T(8,128)S(1)}, u32[]{:S(2)}, u32[]{:S(2)}) collective-permute-start(f32[768,128]{1,0:T(8,128)S(1)} %get-tuple-element.41), channel_id=1, source_target_pairs={{0,0},{32,1},{1,32},{33,33},{2,2},{34,3},{3,34},{35,35},{4,4},{36,... | collective-permute-start | bytes 1179656 | tf_op jit(solution)/shard_map/ppermute | solution.py:411
  7.8 10.6 %collective-permute-start.1 = (f32[136,256]{1,0:T(8,128)S(1)}, f32[136,256]{1,0:T(8,128)S(1)}, u32[]{:S(2)}, u32[]{:S(2)}) collective-permute-start(f32[136,256]{1,0:T(8,128)S(1)} %get-tuple-element.42), channel_id=1, source_target_pairs={{0,64},{1,65},{64,0},{65,1},{2,66},{3,67},{66,2},{67,3},{4,68},{5,... | collective-permute-start | bytes 417800 | tf_op jit(solution)/shard_map/ppermute | solution.py:358
  11.2 4.7 %collective-permute-start.2 = (f32[96,128]{1,0:T(8,128)S(1)}, f32[96,128]{1,0:T(8,128)S(1)}, u32[]{:S(2)}, u32[]{:S(2)}) collective-permute-start(f32[96,128]{1,0:T(8,128)S(1)} %get-tuple-element.44.refs_0_), channel_id=1, source_target_pairs={{0,16},{8,24},{16,0},{24,8},{1,17},{9,25},{17,1},{25,9},{2,18},{10... | collective-permute-start | bytes 147464 | tf_op jit(solution)/shard_map/ppermute | solution.py:358
  13.9 3.2 %collective-permute-start.3 = (f32[96,128]{1,0:T(8,128)S(1)}, f32[96,128]{1,0:T(8,128)S(1)}, u32[]{:S(2)}, u32[]{:S(2)}) collective-permute-start(f32[96,128]{1,0:T(8,128)S(1)} %get-tuple-element.44.refs_0_), channel_id=1, source_target_pairs={{0,8},{8,0},{16,24},{24,16},{1,9},{9,1},{17,25},{25,17},{2,10},{10... | collective-permute-start | bytes 147464 | tf_op jit(solution)/shard_map/ppermute | solution.py:358
  14.2 4.2 %collective-permute-start.4 = (f32[96,128]{1,0:T(8,128)S(1)}, f32[96,128]{1,0:T(8,128)S(1)}, u32[]{:S(2)}, u32[]{:S(2)}) collective-permute-start(f32[96,128]{1,0:T(8,128)S(1)} %get-tuple-element.44.refs_0_), channel_id=1, source_target_pairs={{0,24},{8,16},{16,8},{24,0},{1,25},{9,17},{17,9},{25,1},{2,26},{10... | collective-permute-start | bytes 147464 | tf_op jit(solution)/shard_map/ppermute | solution.py:358
  18.4 20.3 %collective-permute-start.10 = (f32[768,128]{1,0:T(8,128)S(1)}, f32[768,128]{1,0:T(8,128)}, u32[]{:S(2)}, u32[]{:S(2)}) collective-permute-start(f32[768,128]{1,0:T(8,128)S(1)} %collective-permute-done.refs_2_), channel_id=1, source_target_pairs={{0,4},{2,6},{4,0},{6,2},{1,5},{3,7},{5,1},{7,3},{8,12},{10,14},{12... | collective-permute-start | bytes 1179656 | tf_op jit(solution)/shard_map/ppermute | solution.py:358
  21.3 18.6 %collective-permute-start.8 = (f32[768,128]{1,0:T(8,128)S(1)}, f32[768,128]{1,0:T(8,128)}, u32[]{:S(2)}, u32[]{:S(2)}) collective-permute-start(f32[768,128]{1,0:T(8,128)S(1)} %collective-permute-done.refs_2_), channel_id=1, source_target_pairs={{0,2},{2,0},{4,6},{6,4},{1,3},{3,1},{5,7},{7,5},{8,10},{10,8},{12,... | collective-permute-start | bytes 1179656 | tf_op jit(solution)/shard_map/ppermute | solution.py:358
  21.7 18.2 %collective-permute-start.9 = (f32[768,128]{1,0:T(8,128)S(1)}, f32[768,128]{1,0:T(8,128)}, u32[]{:S(2)}, u32[]{:S(2)}) collective-permute-start(f32[768,128]{1,0:T(8,128)S(1)} %collective-permute-done.refs_2_), channel_id=1, source_target_pairs={{0,6},{2,4},{4,2},{6,0},{1,7},{3,5},{5,3},{7,1},{8,14},{10,12},{12... | collective-permute-start | bytes 1179656 | tf_op jit(solution)/shard_map/ppermute | solution.py:358
  22.3 6.6 %collective-permute-start.6 = (f32[136,256]{1,0:T(8,128)S(1)}, f32[136,256]{1,0:T(8,128)S(1)}, u32[]{:S(2)}, u32[]{:S(2)}) collective-permute-start(f32[136,256]{1,0:T(8,128)S(1)} %get-tuple-element.56), channel_id=1, source_target_pairs={{0,1},{1,0},{64,65},{65,64},{2,3},{3,2},{66,67},{67,66},{4,5},{5,4... | collective-permute-start | bytes 417800 | tf_op jit(solution)/shard_map/ppermute | solution.py:358
  24.3 6.2 %collective-permute-start.7 = (f32[136,256]{1,0:T(8,128)S(1)}, f32[136,256]{1,0:T(8,128)S(1)}, u32[]{:S(2)}, u32[]{:S(2)}) collective-permute-start(f32[136,256]{1,0:T(8,128)S(1)} %get-tuple-element.57), channel_id=1, source_target_pairs={{0,65},{1,64},{64,1},{65,0},{2,67},{3,66},{66,3},{67,2},{4,69},{5,... | collective-permute-start | bytes 417800 | tf_op jit(solution)/shard_map/ppermute | solution.py:358
  32.2 42.1 %all-to-all-start = ((f32[32,72,128]{2,1,0:T(8,128)}), f32[32,72,128]{2,1,0:T(8,128)S(1)}, u32[]{:S(2)}, u32[]{:S(2)}) async-start(f32[32,72,128]{2,1,0:T(8,128)} %shard_map.109), calls=%async_computation | async-start | bytes 2359296 | tf_op jit(solution)/shard_map/all_to_all | solution.py:454
  54.2 4.7 %collective-permute-start.12 = (f32[4,32,128]{2,1,0:T(8,128)S(1)}, f32[4,32,128]{2,1,0:T(8,128)S(1)}, u32[]{:S(2)}, u32[]{:S(2)}) collective-permute-start(f32[4,32,128]{2,1,0:T(8,128)S(1)} %add_add_fusion.4), channel_id=1, source_target_pairs={{0,16},{8,24},{16,0},{24,8},{1,17},{9,25},{17,1},{25,9},{2,18},{10... | collective-permute-start | bytes 196616 | tf_op jit(solution)/shard_map/ppermute | solution.py:358
  55.9 3.8 %collective-permute-start.13 = (f32[4,32,128]{2,1,0:T(8,128)S(1)}, f32[4,32,128]{2,1,0:T(8,128)S(1)}, u32[]{:S(2)}, u32[]{:S(2)}) collective-permute-start(f32[4,32,128]{2,1,0:T(8,128)S(1)} %add_add_fusion.4), channel_id=1, source_target_pairs={{0,8},{8,0},{16,24},{24,16},{1,9},{9,1},{17,25},{25,17},{2,10},{10... | collective-permute-start | bytes 196616 | tf_op jit(solution)/shard_map/ppermute | solution.py:358
  56.2 4.6 %collective-permute-start.14 = (f32[4,32,128]{2,1,0:T(8,128)S(1)}, f32[4,32,128]{2,1,0:T(8,128)S(1)}, u32[]{:S(2)}, u32[]{:S(2)}) collective-permute-start(f32[4,32,128]{2,1,0:T(8,128)S(1)} %add_add_fusion.4), channel_id=1, source_target_pairs={{0,24},{8,16},{16,8},{24,0},{1,25},{9,17},{17,9},{25,1},{2,26},{10... | collective-permute-start | bytes 196616 | tf_op jit(solution)/shard_map/ppermute | solution.py:358
  61.6 2.7 %collective-permute-start.15 = (f32[4,32,128]{2,1,0:T(8,128)S(1)}, f32[4,32,128]{2,1,0:T(8,128)S(1)}, u32[]{:S(2)}, u32[]{:S(2)}) collective-permute-start(f32[4,32,128]{2,1,0:T(8,128)S(1)} %get-tuple-element.68.own), channel_id=1, source_target_pairs={{0,32},{32,0},{1,33},{33,1},{2,34},{34,2},{3,35},{35,3},{4,36},{36... | collective-permute-start | bytes 196616 | tf_op jit(solution)/shard_map/ppermute | solution.py:358
  65.1 6.3 %collective-permute-start.16 = (f32[64,512]{1,0:T(8,128)S(1)}, f32[64,512]{1,0:T(8,128)S(1)}, u32[]{:S(2)}, u32[]{:S(2)}) collective-permute-start(f32[64,512]{1,0:T(8,128)S(1)} %get-tuple-element.74), channel_id=1, source_target_pairs={{0,4},{2,6},{4,0},{6,2},{1,5},{3,7},{5,1},{7,3},{8,12},{10,14},{12... | collective-permute-start | bytes 393224 | tf_op jit(solution)/shard_map/ppermute | solution.py:358
  67.9 6.4 %collective-permute-start.17 = (f32[64,512]{1,0:T(8,128)S(1)}, f32[64,512]{1,0:T(8,128)S(1)}, u32[]{:S(2)}, u32[]{:S(2)}) collective-permute-start(f32[64,512]{1,0:T(8,128)S(1)} %get-tuple-element.75), channel_id=1, source_target_pairs={{0,2},{2,0},{4,6},{6,4},{1,3},{3,1},{5,7},{7,5},{8,10},{10,8},{12,... | collective-permute-start | bytes 393224 | tf_op jit(solution)/shard_map/ppermute | solution.py:358
  68.2 6.2 %collective-permute-start.18 = (f32[64,512]{1,0:T(8,128)S(1)}, f32[64,512]{1,0:T(8,128)S(1)}, u32[]{:S(2)}, u32[]{:S(2)}) collective-permute-start(f32[64,512]{1,0:T(8,128)S(1)} %get-tuple-element.76), channel_id=1, source_target_pairs={{0,6},{2,4},{4,2},{6,0},{1,7},{3,5},{5,3},{7,1},{8,14},{10,12},{12... | collective-permute-start | bytes 393224 | tf_op jit(solution)/shard_map/ppermute | solution.py:358
  74.4 5.4 %collective-permute-start.19 = (f32[64,512]{1,0:T(8,128)S(1)}, f32[64,512]{1,0:T(8,128)S(1)}, u32[]{:S(2)}, u32[]{:S(2)}) collective-permute-start(f32[64,512]{1,0:T(8,128)S(1)} %add_multiply_fusion), channel_id=1, source_target_pairs={{0,64},{1,65},{64,0},{65,1},{2,66},{3,67},{66,2},{67,3},{4,68},{5,... | collective-permute-start | bytes 393224 | tf_op jit(solution)/shard_map/ppermute | solution.py:358
  75.4 6.6 %collective-permute-start.20 = (f32[64,512]{1,0:T(8,128)S(1)}, f32[64,512]{1,0:T(8,128)S(1)}, u32[]{:S(2)}, u32[]{:S(2)}) collective-permute-start(f32[64,512]{1,0:T(8,128)S(1)} %add_multiply_fusion), channel_id=1, source_target_pairs={{0,1},{1,0},{64,65},{65,64},{2,3},{3,2},{66,67},{67,66},{4,5},{5,4... | collective-permute-start | bytes 393224 | tf_op jit(solution)/shard_map/ppermute | solution.py:358
  77.1 6.6 %collective-permute-start.21 = (f32[64,512]{1,0:T(8,128)S(1)}, f32[64,512]{1,0:T(8,128)S(1)}, u32[]{:S(2)}, u32[]{:S(2)}) collective-permute-start(f32[64,512]{1,0:T(8,128)S(1)} %add_multiply_fusion), channel_id=1, source_target_pairs={{0,65},{1,64},{64,1},{65,0},{2,67},{3,66},{66,3},{67,2},{4,69},{5,... | collective-permute-start | bytes 393224 | tf_op jit(solution)/shard_map/ppermute | solution.py:358
  84.0 2.7 %collective-permute-start.22 = (f32[64,256]{1,0:T(8,128)S(1)}, f32[64,256]{1,0:T(8,128)S(1)}, u32[]{:S(2)}, u32[]{:S(2)}) collective-permute-start(f32[64,256]{1,0:T(8,128)S(1)} %shard_map.112), channel_id=1, source_target_pairs={{0,32},{32,0},{1,33},{33,1},{2,34},{34,2},{3,35},{35,3},{4,36},{36... | collective-permute-start | bytes 196616 | tf_op jit(solution)/shard_map/ppermute | solution.py:358
  86.7 4.7 %collective-permute-start.23 = (f32[64,256]{1,0:T(8,128)S(1)}, f32[64,256]{1,0:T(8,128)S(1)}, u32[]{:S(2)}, u32[]{:S(2)}) collective-permute-start(f32[64,256]{1,0:T(8,128)S(1)} %add.82), channel_id=1, source_target_pairs={{0,4},{2,6},{4,0},{6,2},{1,5},{3,7},{5,1},{7,3},{8,12},{10,14},{12... | collective-permute-start | bytes 196616 | tf_op jit(solution)/shard_map/ppermute | solution.py:358
  89.5 3.5 %collective-permute-start.24 = (f32[64,256]{1,0:T(8,128)S(1)}, f32[64,256]{1,0:T(8,128)S(1)}, u32[]{:S(2)}, u32[]{:S(2)}) collective-permute-start(f32[64,256]{1,0:T(8,128)S(1)} %add.82), channel_id=1, source_target_pairs={{0,2},{2,0},{4,6},{6,4},{1,3},{3,1},{5,7},{7,5},{8,10},{10,8},{12,... | collective-permute-start | bytes 196616 | tf_op jit(solution)/shard_map/ppermute | solution.py:358
  89.8 4.3 %collective-permute-start.25 = (f32[64,256]{1,0:T(8,128)S(1)}, f32[64,256]{1,0:T(8,128)S(1)}, u32[]{:S(2)}, u32[]{:S(2)}) collective-permute-start(f32[64,256]{1,0:T(8,128)S(1)} %add.82), channel_id=1, source_target_pairs={{0,6},{2,4},{4,2},{6,0},{1,7},{3,5},{5,3},{7,1},{8,14},{10,12},{12... | collective-permute-start | bytes 196616 | tf_op jit(solution)/shard_map/ppermute | solution.py:358
  94.2 4.7 %collective-permute-start.26 = (f32[64,256]{1,0:T(8,128)S(1)}, f32[64,256]{1,0:T(8,128)S(1)}, u32[]{:S(2)}, u32[]{:S(2)}) collective-permute-start(f32[64,256]{1,0:T(8,128)S(1)} %add_add_fusion.2), channel_id=1, source_target_pairs={{0,16},{8,24},{16,0},{24,8},{1,17},{9,25},{17,1},{25,9},{2,18},{10... | collective-permute-start | bytes 196616 | tf_op jit(solution)/shard_map/ppermute | solution.py:358
  94.9 3.9 %collective-permute-start.27 = (f32[64,256]{1,0:T(8,128)S(1)}, f32[64,256]{1,0:T(8,128)S(1)}, u32[]{:S(2)}, u32[]{:S(2)}) collective-permute-start(f32[64,256]{1,0:T(8,128)S(1)} %add_add_fusion.2), channel_id=1, source_target_pairs={{0,8},{8,0},{16,24},{24,16},{1,9},{9,1},{17,25},{25,17},{2,10},{10... | collective-permute-start | bytes 196616 | tf_op jit(solution)/shard_map/ppermute | solution.py:358
  95.8 4.3 %collective-permute-start.28 = (f32[64,256]{1,0:T(8,128)S(1)}, f32[64,256]{1,0:T(8,128)S(1)}, u32[]{:S(2)}, u32[]{:S(2)}) collective-permute-start(f32[64,256]{1,0:T(8,128)S(1)} %add_add_fusion.2), channel_id=1, source_target_pairs={{0,24},{8,16},{16,8},{24,0},{1,25},{9,17},{17,9},{25,1},{2,26},{10... | collective-permute-start | bytes 196616 | tf_op jit(solution)/shard_map/ppermute | solution.py:358
  100.5 8.9 %collective-permute-start.29 = (f32[64,512]{1,0:T(8,128)S(1)}, f32[64,512]{1,0:T(8,128)S(1)}, u32[]{:S(2)}, u32[]{:S(2)}) collective-permute-start(f32[64,512]{1,0:T(8,128)S(1)} %shard_map.113), channel_id=1, source_target_pairs={{0,64},{1,96},{64,0},{65,32},{32,65},{33,97},{96,1},{97,33},{2,66}... | collective-permute-start | bytes 393224 | tf_op jit(solution)/shard_map/ppermute | solution.py:494
  105.6 6.6 %collective-permute-start.30 = (f32[64,512]{1,0:T(8,128)S(1)}, f32[64,512]{1,0:T(8,128)S(1)}, u32[]{:S(2)}, u32[]{:S(2)}) collective-permute-start(f32[64,512]{1,0:T(8,128)S(1)} %shard_map.113), channel_id=1, source_target_pairs={{0,96},{1,64},{64,32},{65,0},{32,97},{33,65},{96,33},{97,1},{2,98}... | collective-permute-start | bytes 393224 | tf_op jit(solution)/shard_map/ppermute | solution.py:494
  105.6 6.6 %collective-permute-start.31 = (f32[64,512]{1,0:T(8,128)S(1)}, f32[64,512]{1,0:T(8,128)S(1)}, u32[]{:S(2)}, u32[]{:S(2)}) collective-permute-start(f32[64,512]{1,0:T(8,128)S(1)} %shard_map.113), channel_id=1, source_target_pairs={{0,32},{1,0},{64,96},{65,64},{32,33},{33,1},{96,97},{97,65},{2,34}... | collective-permute-start | bytes 393224 | tf_op jit(solution)/shard_map/ppermute | solution.py:494
  106.3 6.6 %collective-permute-start.32 = (f32[64,512]{1,0:T(8,128)S(1)}, f32[64,512]{1,0:T(8,128)S(1)}, u32[]{:S(2)}, u32[]{:S(2)}) collective-permute-start(f32[64,512]{1,0:T(8,128)S(1)} %shard_map.113), channel_id=1, source_target_pairs={{0,0},{1,32},{64,64},{65,96},{32,1},{33,33},{96,65},{97,97},{2,2},... | collective-permute-start | bytes 393224 | tf_op jit(solution)/shard_map/ppermute | solution.py:494
  (3 other events, 24.0 us)

commit v17 on v16

--- a/solution.py
+++ b/solution.py
@@ -428,7 +428,7 @@
         if extra:
             outs = outs + [shape(nx, half, wide), shape(8, cdev)]
         return call(
-            functools.partial(kernel_body, nb=nb, rows=rows, sub=32, extra=extra),
+            functools.partial(kernel_body, nb=nb, rows=rows, sub=16, extra=extra),
             outs, own, mate, *packs,
             scratch_shapes=[
                 pltpu.VMEM((2, nx * rows, 6 * dim), BF),

time: 114 us -> 114 us (level)
  no operation moved by 1% of the time
where the time goes in v17:
time: 114 us
  starting transfers between devices  55.1 us (48%)
  waiting for transfers between devices  32.1 us (28%)
  Pallas kernels  24.7 us (22%)
    ppermute x28, starting transfers between devices, mate_of(): return lax.ppermute(v, axes, [(i, i ^ o) for i in range(n)])  34.8 us
    ppermute x28, waiting for transfers between devices, mate_of(): return lax.ppermute(v, axes, [(i, i ^ o) for i in range(n)])  28.7 us
    pallas_call x9, Pallas kernels, call(): pl.pallas_call(body, out_shape=outs, in_specs=[smem] * scalars + [VMEM] *...  22.5 us
    ppermute x4, starting transfers between devices, per_device(): received.append(lax.ppermute(corr, ('zh', 'core', 'zl'), perm))  8.85 us
    all_to_all x1, starting transfers between devices, per_device(): lax.all_to_all(points, OWNERS, split_axis=0, concat_axis=0, tiled=True)  6.43 us
    ppermute x1, starting transfers between devices, per_device(): tile = lax.ppermute(pack, ('core', 'zl'), [(0, 0), (2, 1), (1, 2), (3, 3)])  4.93 us
    ppermute x4, waiting for transfers between devices, per_device(): received.append(lax.ppermute(corr, ('zh', 'core', 'zl'), perm))  3.49 us
  transfers between devices with their start and end apart: 34, of which 24 were waited for; matrix products, arithmetic and copies ran while one was open for 0% of the time, Pallas kernels for 19%

profile of v17, /device:TPU:1, one launch (start us, length us, event | category | flops | bytes accessed | tf_op | source)
XLA Modules:
  0.0 113.6 jit_solution(10003181992881597156)
XLA Ops:
  0.6 2.2 %shard_map.104 = (f32[96,128]{1,0:T(8,128)S(1)}, f32[768,128]{1,0:T(8,128)S(1)}, f32[136,256]{1,0:T(8,128)S(1)}, f32[136,256]{1,0:T(8,128)S(1)}, f32[136,256]{1,0:T(8,128)S(1)}, /*index=5*/f32[136,256]{1,0:T(8,128)S(1)}) custom-call(s32[1]{0:T(128)} %bitcast.1.member, s32[1,64]{1,0:T(1,128)} %bitcast.15, f32[1024,128]{1,0:T(8,128)} %refs_1_.1, ...), custom_call_target="tpu_custom_call" | custom-call | tf_op jit(solution)/shard_map/pallas_call | solution.py:381
  2.9 4.9 %collective-permute-start = (f32[768,128]{1,0:T(8,128)S(1)}, f32[768,128]{1,0:T(8,128)S(1)}, u32[]{:S(2)}, u32[]{:S(2)}) collective-permute-start(f32[768,128]{1,0:T(8,128)S(1)} %get-tuple-element.41), channel_id=1, source_target_pairs={{0,0},{32,1},{1,32},{33,33},{2,2},{34,3},{3,34},{35,35},{4,4},{36,... | collective-permute-start | bytes 1179656 | tf_op jit(solution)/shard_map/ppermute | solution.py:411
  7.8 3.4 %collective-permute-start.1 = (f32[136,256]{1,0:T(8,128)S(1)}, f32[136,256]{1,0:T(8,128)S(1)}, u32[]{:S(2)}, u32[]{:S(2)}) collective-permute-start(f32[136,256]{1,0:T(8,128)S(1)} %get-tuple-element.42), channel_id=1, source_target_pairs={{0,64},{1,65},{64,0},{65,1},{2,66},{3,67},{66,2},{67,3},{4,68},{5,... | collective-permute-start | bytes 417800 | tf_op jit(solution)/shard_map/ppermute | solution.py:358
  11.2 2.7 %collective-permute-start.2 = (f32[96,128]{1,0:T(8,128)S(1)}, f32[96,128]{1,0:T(8,128)S(1)}, u32[]{:S(2)}, u32[]{:S(2)}) collective-permute-start(f32[96,128]{1,0:T(8,128)S(1)} %get-tuple-element.44.refs_0_), channel_id=1, source_target_pairs={{0,16},{8,24},{16,0},{24,8},{1,17},{9,25},{17,1},{25,9},{2,18},{10... | collective-permute-start | bytes 147464 | tf_op jit(solution)/shard_map/ppermute | solution.py:358
  15.9 1.3 %collective-permute-done.3.refs_2_ = f32[96,128]{1,0:T(8,128)S(1)} collective-permute-done((f32[96,128]{1,0:T(8,128)S(1)}, f32[96,128]{1,0:T(8,128)S(1)}, u32[]{:S(2)}, u32[]{:S(2)}) %collective-permute-start.3) | collective-permute-done | bytes 49184 | tf_op jit(solution)/shard_map/ppermute | solution.py:358
  18.4 2.9 %collective-permute-start.10 = (f32[768,128]{1,0:T(8,128)S(1)}, f32[768,128]{1,0:T(8,128)}, u32[]{:S(2)}, u32[]{:S(2)}) collective-permute-start(f32[768,128]{1,0:T(8,128)S(1)} %collective-permute-done.refs_2_), channel_id=1, source_target_pairs={{0,4},{2,6},{4,0},{6,2},{1,5},{3,7},{5,1},{7,3},{8,12},{10,14},{12... | collective-permute-start | bytes 1179656 | tf_op jit(solution)/shard_map/ppermute | solution.py:358
  22.3 2.0 %collective-permute-start.6 = (f32[136,256]{1,0:T(8,128)S(1)}, f32[136,256]{1,0:T(8,128)S(1)}, u32[]{:S(2)}, u32[]{:S(2)}) collective-permute-start(f32[136,256]{1,0:T(8,128)S(1)} %get-tuple-element.56), channel_id=1, source_target_pairs={{0,1},{1,0},{64,65},{65,64},{2,3},{3,2},{66,67},{67,66},{4,5},{5,4... | collective-permute-start | bytes 417800 | tf_op jit(solution)/shard_map/ppermute | solution.py:358
  25.0 3.9 %shard_map.106 = (bf16[1,512,512]{2,1,0:T(8,128)(2,1)S(1)}, bf16[1,512,512]{2,1,0:T(8,128)(2,1)S(1)}, f32[4,32,128]{2,1,0:T(8,128)S(1)}, f32[4,32,128]{2,1,0:T(8...) custom-call(f32[4,96,128]{2,1,0:T(8,128)S(1)} %shard_map.105.refs_0_.own, ...), custom_call_target="tpu_custom_call" | custom-call | flops 100000000 | bytes 65536 | tf_op jit(solution)/shard_map/pallas_call | solution.py:333
  28.9 1.6 %collective-permute-done.7.refs_3_ = f32[136,256]{1,0:T(8,128)S(1)} collective-permute-done((f32[136,256]{1,0:T(8,128)S(1)}, f32[136,256]{1,0:T(8,128)S(1)}, u32[]{:S(2)}, u32[]{:S(2)}) %collective-permute-start.7) | collective-permute-done | bytes 139296 | tf_op jit(solution)/shard_map/ppermute | solution.py:358
  30.5 1.7 %shard_map.109 = f32[32,72,128]{2,1,0:T(8,128)} custom-call(f32[136,256]{1,0:T(8,128)S(1)} %get-tuple-element.64.refs_0_, f32[136,256]{1,0:T(8,128)S(1)} %collective-permute-done.1.refs_1_, f32[136,256]{1,0:T(8,128)S(1)} %collective-permute-done.6.refs_2_, f32[136,256]{1,0:T(8,128)S(1)} %collective-permute-done.7.refs_3_), custom_call_target="tpu_custom_call" | custom-call | tf_op jit(solution)/shard_map/pallas_call | solution.py:333
  32.2 6.4 %all-to-all-start = ((f32[32,72,128]{2,1,0:T(8,128)}), f32[32,72,128]{2,1,0:T(8,128)S(1)}, u32[]{:S(2)}, u32[]{:S(2)}) async-start(f32[32,72,128]{2,1,0:T(8,128)} %shard_map.109), calls=%async_computation | async-start | bytes 2359296 | tf_op jit(solution)/shard_map/all_to_all | solution.py:454
  40.0 12.8 %shard_map.107 = (bf16[3,512,512]{2,1,0:T(8,128)(2,1)S(1)}, bf16[3,512,512]{2,1,0:T(8,128)(2,1)S(1)}, f32[4,32,128]{2,1,0:T(8,128)S(1)}, f32[4,32,128]{2,1,0:T(8,128)S(1)}) custom-call(f32[4,96,128]{2,1,0:T(8,128)S(1)} %shard_map.105.refs_0_.own, f32[4,96,128]{2,1,0:T(8,128)S(1)} %collective-permute-done.5.refs_1_, ...), custom_call_target="tpu_custom_call" | custom-call | flops 30000001024 | bytes 65536 | tf_op jit(solution)/shard_map/pallas_call | solution.py:333
  54.2 1.7 %collective-permute-start.12 = (f32[4,32,128]{2,1,0:T(8,128)S(1)}, f32[4,32,128]{2,1,0:T(8,128)S(1)}, u32[]{:S(2)}, u32[]{:S(2)}) collective-permute-start(f32[4,32,128]{2,1,0:T(8,128)S(1)} %add_add_fusion.4), channel_id=1, source_target_pairs={{0,16},{8,24},{16,0},{24,8},{1,17},{9,25},{17,1},{25,9},{2,18},{10... | collective-permute-start | bytes 196616 | tf_op jit(solution)/shard_map/ppermute | solution.py:358
  56.2 1.3 %collective-permute-start.14 = (f32[4,32,128]{2,1,0:T(8,128)S(1)}, f32[4,32,128]{2,1,0:T(8,128)S(1)}, u32[]{:S(2)}, u32[]{:S(2)}) collective-permute-start(f32[4,32,128]{2,1,0:T(8,128)S(1)} %add_add_fusion.4), channel_id=1, source_target_pairs={{0,24},{8,16},{16,8},{24,0},{1,25},{9,17},{17,9},{25,1},{2,26},{10... | collective-permute-start | bytes 196616 | tf_op jit(solution)/shard_map/ppermute | solution.py:358
  57.5 1.4 %collective-permute-done.12 = f32[4,32,128]{2,1,0:T(8,128)S(1)} collective-permute-done((f32[4,32,128]{2,1,0:T(8,128)S(1)}, f32[4,32,128]{2,1,0:T(8,128)S(1)}, u32[]{:S(2)}, u32[]{:S(2)}) %collective-permute-start.12) | collective-permute-done | bytes 65568 | tf_op jit(solution)/shard_map/ppermute | solution.py:358
  61.6 1.8 %collective-permute-start.15 = (f32[4,32,128]{2,1,0:T(8,128)S(1)}, f32[4,32,128]{2,1,0:T(8,128)S(1)}, u32[]{:S(2)}, u32[]{:S(2)}) collective-permute-start(f32[4,32,128]{2,1,0:T(8,128)S(1)} %get-tuple-element.68.own), channel_id=1, source_target_pairs={{0,32},{32,0},{1,33},{33,1},{2,34},{34,2},{3,35},{35,3},{4,36},{36... | collective-permute-start | bytes 196616 | tf_op jit(solution)/shard_map/ppermute | solution.py:358
  65.1 2.8 %collective-permute-start.16 = (f32[64,512]{1,0:T(8,128)S(1)}, f32[64,512]{1,0:T(8,128)S(1)}, u32[]{:S(2)}, u32[]{:S(2)}) collective-permute-start(f32[64,512]{1,0:T(8,128)S(1)} %get-tuple-element.74), channel_id=1, source_target_pairs={{0,4},{2,6},{4,0},{6,2},{1,5},{3,7},{5,1},{7,3},{8,12},{10,14},{12... | collective-permute-start | bytes 393224 | tf_op jit(solution)/shard_map/ppermute | solution.py:358
  68.7 2.6 %collective-permute-done.16 = f32[64,512]{1,0:T(8,128)S(1)} collective-permute-done((f32[64,512]{1,0:T(8,128)S(1)}, f32[64,512]{1,0:T(8,128)S(1)}, u32[]{:S(2)}, u32[]{:S(2)}) %collective-permute-start.16) | collective-permute-done | bytes 131104 | tf_op jit(solution)/shard_map/ppermute | solution.py:358
  71.4 2.8 %collective-permute-done.17 = f32[64,512]{1,0:T(8,128)S(1)} collective-permute-done((f32[64,512]{1,0:T(8,128)S(1)}, f32[64,512]{1,0:T(8,128)S(1)}, u32[]{:S(2)}, u32[]{:S(2)}) %collective-permute-start.17) | collective-permute-done | bytes 131104 | tf_op jit(solution)/shard_map/ppermute | solution.py:358
  75.4 1.7 %collective-permute-start.20 = (f32[64,512]{1,0:T(8,128)S(1)}, f32[64,512]{1,0:T(8,128)S(1)}, u32[]{:S(2)}, u32[]{:S(2)}) collective-permute-start(f32[64,512]{1,0:T(8,128)S(1)} %add_multiply_fusion), channel_id=1, source_target_pairs={{0,1},{1,0},{64,65},{65,64},{2,3},{3,2},{66,67},{67,66},{4,5},{5,4... | collective-permute-start | bytes 393224 | tf_op jit(solution)/shard_map/ppermute | solution.py:358
  77.7 2.0 %shard_map.111.summed = bf16[512,512]{1,0:T(8,128)(2,1)S(1)} custom-call(f32[32,72,128]{2,1,0:T(8,128)S(1)} %all-to-all-done.points), custom_call_target="tpu_custom_call" | custom-call | flops 800000000 | bytes 2097152 | tf_op jit(solution)/shard_map/pallas_call | solution.py:333
  79.8 2.3 %collective-permute-done.20 = f32[64,512]{1,0:T(8,128)S(1)} collective-permute-done((f32[64,512]{1,0:T(8,128)S(1)}, f32[64,512]{1,0:T(8,128)S(1)}, u32[]{:S(2)}, u32[]{:S(2)}) %collective-permute-start.20) | collective-permute-done | bytes 131104 | tf_op jit(solution)/shard_map/ppermute | solution.py:358
  82.0 1.7 %collective-permute-done.21 = f32[64,512]{1,0:T(8,128)S(1)} collective-permute-done((f32[64,512]{1,0:T(8,128)S(1)}, f32[64,512]{1,0:T(8,128)S(1)}, u32[]{:S(2)}, u32[]{:S(2)}) %collective-permute-start.21) | collective-permute-done | bytes 131104 | tf_op jit(solution)/shard_map/ppermute | solution.py:358
  84.0 1.7 %collective-permute-start.22 = (f32[64,256]{1,0:T(8,128)S(1)}, f32[64,256]{1,0:T(8,128)S(1)}, u32[]{:S(2)}, u32[]{:S(2)}) collective-permute-start(f32[64,256]{1,0:T(8,128)S(1)} %shard_map.112), channel_id=1, source_target_pairs={{0,32},{32,0},{1,33},{33,1},{2,34},{34,2},{3,35},{35,3},{4,36},{36... | collective-permute-start | bytes 196616 | tf_op jit(solution)/shard_map/ppermute | solution.py:358
  86.7 2.9 %collective-permute-start.23 = (f32[64,256]{1,0:T(8,128)S(1)}, f32[64,256]{1,0:T(8,128)S(1)}, u32[]{:S(2)}, u32[]{:S(2)}) collective-permute-start(f32[64,256]{1,0:T(8,128)S(1)} %add.82), channel_id=1, source_target_pairs={{0,4},{2,6},{4,0},{6,2},{1,5},{3,7},{5,1},{7,3},{8,12},{10,14},{12... | collective-permute-start | bytes 196616 | tf_op jit(solution)/shard_map/ppermute | solution.py:358
  91.4 1.6 %collective-permute-done.24 = f32[64,256]{1,0:T(8,128)S(1)} collective-permute-done((f32[64,256]{1,0:T(8,128)S(1)}, f32[64,256]{1,0:T(8,128)S(1)}, u32[]{:S(2)}, u32[]{:S(2)}) %collective-permute-start.24) | collective-permute-done | bytes 65568 | tf_op jit(solution)/shard_map/ppermute | solution.py:358
  95.8 1.7 %collective-permute-start.28 = (f32[64,256]{1,0:T(8,128)S(1)}, f32[64,256]{1,0:T(8,128)S(1)}, u32[]{:S(2)}, u32[]{:S(2)}) collective-permute-start(f32[64,256]{1,0:T(8,128)S(1)} %add_add_fusion.2), channel_id=1, source_target_pairs={{0,24},{8,16},{16,8},{24,0},{1,25},{9,17},{17,9},{25,1},{2,26},{10... | collective-permute-start | bytes 196616 | tf_op jit(solution)/shard_map/ppermute | solution.py:358
  97.5 1.4 %collective-permute-done.26 = f32[64,256]{1,0:T(8,128)S(1)} collective-permute-done((f32[64,256]{1,0:T(8,128)S(1)}, f32[64,256]{1,0:T(8,128)S(1)}, u32[]{:S(2)}, u32[]{:S(2)}) %collective-permute-start.26) | collective-permute-done | bytes 65568 | tf_op jit(solution)/shard_map/ppermute | solution.py:358
  98.9 1.3 %collective-permute-done.28 = f32[64,256]{1,0:T(8,128)S(1)} collective-permute-done((f32[64,256]{1,0:T(8,128)S(1)}, f32[64,256]{1,0:T(8,128)S(1)}, u32[]{:S(2)}, u32[]{:S(2)}) %collective-permute-start.28) | collective-permute-done | bytes 65568 | tf_op jit(solution)/shard_map/ppermute | solution.py:358
  100.5 5.1 %collective-permute-start.29 = (f32[64,512]{1,0:T(8,128)S(1)}, f32[64,512]{1,0:T(8,128)S(1)}, u32[]{:S(2)}, u32[]{:S(2)}) collective-permute-start(f32[64,512]{1,0:T(8,128)S(1)} %shard_map.113), channel_id=1, source_target_pairs={{0,64},{1,96},{64,0},{65,32},{32,65},{33,97},{96,1},{97,33},{2,66}... | collective-permute-start | bytes 393224 | tf_op jit(solution)/shard_map/ppermute | solution.py:494
  106.3 3.1 %collective-permute-start.32 = (f32[64,512]{1,0:T(8,128)S(1)}, f32[64,512]{1,0:T(8,128)S(1)}, u32[]{:S(2)}, u32[]{:S(2)}) collective-permute-start(f32[64,512]{1,0:T(8,128)S(1)} %shard_map.113), channel_id=1, source_target_pairs={{0,0},{1,32},{64,64},{65,96},{32,1},{33,33},{96,65},{97,97},{2,2},... | collective-permute-start | bytes 393224 | tf_op jit(solution)/shard_map/ppermute | solution.py:494
  109.4 2.8 %collective-permute-done.30 = f32[64,512]{1,0:T(8,128)S(1)} collective-permute-done((f32[64,512]{1,0:T(8,128)S(1)}, f32[64,512]{1,0:T(8,128)S(1)}, u32[]{:S(2)}, u32[]{:S(2)}) %collective-permute-start.30) | collective-permute-done | bytes 131104 | tf_op jit(solution)/shard_map/ppermute | solution.py:494
  (58 shorter events, 23.3 us)
Async XLA Ops:
  2.9 15.5 %collective-permute-start = (f32[768,128]{1,0:T(8,128)S(1)}, f32[768,128]{1,0:T(8,128)S(1)}, u32[]{:S(2)}, u32[]{:S(2)}) collective-permute-start(f32[768,128]{1,0:T(8,128)S(1)} %get-tuple-element.41), channel_id=1, source_target_pairs={{0,0},{32,1},{1,32},{33,33},{2,2},{34,3},{3,34},{35,35},{4,4},{36,... | collective-permute-start | bytes 1179656 | tf_op jit(solution)/shard_map/ppermute | solution.py:411
  7.8 10.6 %collective-permute-start.1 = (f32[136,256]{1,0:T(8,128)S(1)}, f32[136,256]{1,0:T(8,128)S(1)}, u32[]{:S(2)}, u32[]{:S(2)}) collective-permute-start(f32[136,256]{1,0:T(8,128)S(1)} %get-tuple-element.42), channel_id=1, source_target_pairs={{0,64},{1,65},{64,0},{65,1},{2,66},{3,67},{66,2},{67,3},{4,68},{5,... | collective-permute-start | bytes 417800 | tf_op jit(solution)/shard_map/ppermute | solution.py:358
  11.2 4.7 %collective-permute-start.2 = (f32[96,128]{1,0:T(8,128)S(1)}, f32[96,128]{1,0:T(8,128)S(1)}, u32[]{:S(2)}, u32[]{:S(2)}) collective-permute-start(f32[96,128]{1,0:T(8,128)S(1)} %get-tuple-element.44.refs_0_), channel_id=1, source_target_pairs={{0,16},{8,24},{16,0},{24,8},{1,17},{9,25},{17,1},{25,9},{2,18},{10... | collective-permute-start | bytes 147464 | tf_op jit(solution)/shard_map/ppermute | solution.py:358
  13.9 3.2 %collective-permute-start.3 = (f32[96,128]{1,0:T(8,128)S(1)}, f32[96,128]{1,0:T(8,128)S(1)}, u32[]{:S(2)}, u32[]{:S(2)}) collective-permute-start(f32[96,128]{1,0:T(8,128)S(1)} %get-tuple-element.44.refs_0_), channel_id=1, source_target_pairs={{0,8},{8,0},{16,24},{24,16},{1,9},{9,1},{17,25},{25,17},{2,10},{10... | collective-permute-start | bytes 147464 | tf_op jit(solution)/shard_map/ppermute | solution.py:358
  14.2 4.2 %collective-permute-start.4 = (f32[96,128]{1,0:T(8,128)S(1)}, f32[96,128]{1,0:T(8,128)S(1)}, u32[]{:S(2)}, u32[]{:S(2)}) collective-permute-start(f32[96,128]{1,0:T(8,128)S(1)} %get-tuple-element.44.refs_0_), channel_id=1, source_target_pairs={{0,24},{8,16},{16,8},{24,0},{1,25},{9,17},{17,9},{25,1},{2,26},{10... | collective-permute-start | bytes 147464 | tf_op jit(solution)/shard_map/ppermute | solution.py:358
  18.4 20.3 %collective-permute-start.10 = (f32[768,128]{1,0:T(8,128)S(1)}, f32[768,128]{1,0:T(8,128)}, u32[]{:S(2)}, u32[]{:S(2)}) collective-permute-start(f32[768,128]{1,0:T(8,128)S(1)} %collective-permute-done.refs_2_), channel_id=1, source_target_pairs={{0,4},{2,6},{4,0},{6,2},{1,5},{3,7},{5,1},{7,3},{8,12},{10,14},{12... | collective-permute-start | bytes 1179656 | tf_op jit(solution)/shard_map/ppermute | solution.py:358
  21.3 18.6 %collective-permute-start.8 = (f32[768,128]{1,0:T(8,128)S(1)}, f32[768,128]{1,0:T(8,128)}, u32[]{:S(2)}, u32[]{:S(2)}) collective-permute-start(f32[768,128]{1,0:T(8,128)S(1)} %collective-permute-done.refs_2_), channel_id=1, source_target_pairs={{0,2},{2,0},{4,6},{6,4},{1,3},{3,1},{5,7},{7,5},{8,10},{10,8},{12,... | collective-permute-start | bytes 1179656 | tf_op jit(solution)/shard_map/ppermute | solution.py:358
  21.7 18.2 %collective-permute-start.9 = (f32[768,128]{1,0:T(8,128)S(1)}, f32[768,128]{1,0:T(8,128)}, u32[]{:S(2)}, u32[]{:S(2)}) collective-permute-start(f32[768,128]{1,0:T(8,128)S(1)} %collective-permute-done.refs_2_), channel_id=1, source_target_pairs={{0,6},{2,4},{4,2},{6,0},{1,7},{3,5},{5,3},{7,1},{8,14},{10,12},{12... | collective-permute-start | bytes 1179656 | tf_op jit(solution)/shard_map/ppermute | solution.py:358
  22.3 6.6 %collective-permute-start.6 = (f32[136,256]{1,0:T(8,128)S(1)}, f32[136,256]{1,0:T(8,128)S(1)}, u32[]{:S(2)}, u32[]{:S(2)}) collective-permute-start(f32[136,256]{1,0:T(8,128)S(1)} %get-tuple-element.56), channel_id=1, source_target_pairs={{0,1},{1,0},{64,65},{65,64},{2,3},{3,2},{66,67},{67,66},{4,5},{5,4... | collective-permute-start | bytes 417800 | tf_op jit(solution)/shard_map/ppermute | solution.py:358
  24.3 6.2 %collective-permute-start.7 = (f32[136,256]{1,0:T(8,128)S(1)}, f32[136,256]{1,0:T(8,128)S(1)}, u32[]{:S(2)}, u32[]{:S(2)}) collective-permute-start(f32[136,256]{1,0:T(8,128)S(1)} %get-tuple-element.57), channel_id=1, source_target_pairs={{0,65},{1,64},{64,1},{65,0},{2,67},{3,66},{66,3},{67,2},{4,69},{5,... | collective-permute-start | bytes 417800 | tf_op jit(solution)/shard_map/ppermute | solution.py:358
  32.2 42.1 %all-to-all-start = ((f32[32,72,128]{2,1,0:T(8,128)}), f32[32,72,128]{2,1,0:T(8,128)S(1)}, u32[]{:S(2)}, u32[]{:S(2)}) async-start(f32[32,72,128]{2,1,0:T(8,128)} %shard_map.109), calls=%async_computation | async-start | bytes 2359296 | tf_op jit(solution)/shard_map/all_to_all | solution.py:454
  54.2 4.7 %collective-permute-start.12 = (f32[4,32,128]{2,1,0:T(8,128)S(1)}, f32[4,32,128]{2,1,0:T(8,128)S(1)}, u32[]{:S(2)}, u32[]{:S(2)}) collective-permute-start(f32[4,32,128]{2,1,0:T(8,128)S(1)} %add_add_fusion.4), channel_id=1, source_target_pairs={{0,16},{8,24},{16,0},{24,8},{1,17},{9,25},{17,1},{25,9},{2,18},{10... | collective-permute-start | bytes 196616 | tf_op jit(solution)/shard_map/ppermute | solution.py:358
  55.9 3.8 %collective-permute-start.13 = (f32[4,32,128]{2,1,0:T(8,128)S(1)}, f32[4,32,128]{2,1,0:T(8,128)S(1)}, u32[]{:S(2)}, u32[]{:S(2)}) collective-permute-start(f32[4,32,128]{2,1,0:T(8,128)S(1)} %add_add_fusion.4), channel_id=1, source_target_pairs={{0,8},{8,0},{16,24},{24,16},{1,9},{9,1},{17,25},{25,17},{2,10},{10... | collective-permute-start | bytes 196616 | tf_op jit(solution)/shard_map/ppermute | solution.py:358
  56.2 4.6 %collective-permute-start.14 = (f32[4,32,128]{2,1,0:T(8,128)S(1)}, f32[4,32,128]{2,1,0:T(8,128)S(1)}, u32[]{:S(2)}, u32[]{:S(2)}) collective-permute-start(f32[4,32,128]{2,1,0:T(8,128)S(1)} %add_add_fusion.4), channel_id=1, source_target_pairs={{0,24},{8,16},{16,8},{24,0},{1,25},{9,17},{17,9},{25,1},{2,26},{10... | collective-permute-start | bytes 196616 | tf_op jit(solution)/shard_map/ppermute | solution.py:358
  61.6 2.7 %collective-permute-start.15 = (f32[4,32,128]{2,1,0:T(8,128)S(1)}, f32[4,32,128]{2,1,0:T(8,128)S(1)}, u32[]{:S(2)}, u32[]{:S(2)}) collective-permute-start(f32[4,32,128]{2,1,0:T(8,128)S(1)} %get-tuple-element.68.own), channel_id=1, source_target_pairs={{0,32},{32,0},{1,33},{33,1},{2,34},{34,2},{3,35},{35,3},{4,36},{36... | collective-permute-start | bytes 196616 | tf_op jit(solution)/shard_map/ppermute | solution.py:358
  65.1 6.3 %collective-permute-start.16 = (f32[64,512]{1,0:T(8,128)S(1)}, f32[64,512]{1,0:T(8,128)S(1)}, u32[]{:S(2)}, u32[]{:S(2)}) collective-permute-start(f32[64,512]{1,0:T(8,128)S(1)} %get-tuple-element.74), channel_id=1, source_target_pairs={{0,4},{2,6},{4,0},{6,2},{1,5},{3,7},{5,1},{7,3},{8,12},{10,14},{12... | collective-permute-start | bytes 393224 | tf_op jit(solution)/shard_map/ppermute | solution.py:358
  67.9 6.4 %collective-permute-start.17 = (f32[64,512]{1,0:T(8,128)S(1)}, f32[64,512]{1,0:T(8,128)S(1)}, u32[]{:S(2)}, u32[]{:S(2)}) collective-permute-start(f32[64,512]{1,0:T(8,128)S(1)} %get-tuple-element.75), channel_id=1, source_target_pairs={{0,2},{2,0},{4,6},{6,4},{1,3},{3,1},{5,7},{7,5},{8,10},{10,8},{12,... | collective-permute-start | bytes 393224 | tf_op jit(solution)/shard_map/ppermute | solution.py:358
  68.2 6.2 %collective-permute-start.18 = (f32[64,512]{1,0:T(8,128)S(1)}, f32[64,512]{1,0:T(8,128)S(1)}, u32[]{:S(2)}, u32[]{:S(2)}) collective-permute-start(f32[64,512]{1,0:T(8,128)S(1)} %get-tuple-element.76), channel_id=1, source_target_pairs={{0,6},{2,4},{4,2},{6,0},{1,7},{3,5},{5,3},{7,1},{8,14},{10,12},{12... | collective-permute-start | bytes 393224 | tf_op jit(solution)/shard_map/ppermute | solution.py:358
  74.4 5.4 %collective-permute-start.19 = (f32[64,512]{1,0:T(8,128)S(1)}, f32[64,512]{1,0:T(8,128)S(1)}, u32[]{:S(2)}, u32[]{:S(2)}) collective-permute-start(f32[64,512]{1,0:T(8,128)S(1)} %add_multiply_fusion), channel_id=1, source_target_pairs={{0,64},{1,65},{64,0},{65,1},{2,66},{3,67},{66,2},{67,3},{4,68},{5,... | collective-permute-start | bytes 393224 | tf_op jit(solution)/shard_map/ppermute | solution.py:358
  75.4 6.6 %collective-permute-start.20 = (f32[64,512]{1,0:T(8,128)S(1)}, f32[64,512]{1,0:T(8,128)S(1)}, u32[]{:S(2)}, u32[]{:S(2)}) collective-permute-start(f32[64,512]{1,0:T(8,128)S(1)} %add_multiply_fusion), channel_id=1, source_target_pairs={{0,1},{1,0},{64,65},{65,64},{2,3},{3,2},{66,67},{67,66},{4,5},{5,4... | collective-permute-start | bytes 393224 | tf_op jit(solution)/shard_map/ppermute | solution.py:358
  77.1 6.6 %collective-permute-start.21 = (f32[64,512]{1,0:T(8,128)S(1)}, f32[64,512]{1,0:T(8,128)S(1)}, u32[]{:S(2)}, u32[]{:S(2)}) collective-permute-start(f32[64,512]{1,0:T(8,128)S(1)} %add_multiply_fusion), channel_id=1, source_target_pairs={{0,65},{1,64},{64,1},{65,0},{2,67},{3,66},{66,3},{67,2},{4,69},{5,... | collective-permute-start | bytes 393224 | tf_op jit(solution)/shard_map/ppermute | solution.py:358
  84.0 2.7 %collective-permute-start.22 = (f32[64,256]{1,0:T(8,128)S(1)}, f32[64,256]{1,0:T(8,128)S(1)}, u32[]{:S(2)}, u32[]{:S(2)}) collective-permute-start(f32[64,256]{1,0:T(8,128)S(1)} %shard_map.112), channel_id=1, source_target_pairs={{0,32},{32,0},{1,33},{33,1},{2,34},{34,2},{3,35},{35,3},{4,36},{36... | collective-permute-start | bytes 196616 | tf_op jit(solution)/shard_map/ppermute | solution.py:358
  86.7 4.7 %collective-permute-start.23 = (f32[64,256]{1,0:T(8,128)S(1)}, f32[64,256]{1,0:T(8,128)S(1)}, u32[]{:S(2)}, u32[]{:S(2)}) collective-permute-start(f32[64,256]{1,0:T(8,128)S(1)} %add.82), channel_id=1, source_target_pairs={{0,4},{2,6},{4,0},{6,2},{1,5},{3,7},{5,1},{7,3},{8,12},{10,14},{12... | collective-permute-start | bytes 196616 | tf_op jit(solution)/shard_map/ppermute | solution.py:358
  89.5 3.5 %collective-permute-start.24 = (f32[64,256]{1,0:T(8,128)S(1)}, f32[64,256]{1,0:T(8,128)S(1)}, u32[]{:S(2)}, u32[]{:S(2)}) collective-permute-start(f32[64,256]{1,0:T(8,128)S(1)} %add.82), channel_id=1, source_target_pairs={{0,2},{2,0},{4,6},{6,4},{1,3},{3,1},{5,7},{7,5},{8,10},{10,8},{12,... | collective-permute-start | bytes 196616 | tf_op jit(solution)/shard_map/ppermute | solution.py:358
  89.8 4.3 %collective-permute-start.25 = (f32[64,256]{1,0:T(8,128)S(1)}, f32[64,256]{1,0:T(8,128)S(1)}, u32[]{:S(2)}, u32[]{:S(2)}) collective-permute-start(f32[64,256]{1,0:T(8,128)S(1)} %add.82), channel_id=1, source_target_pairs={{0,6},{2,4},{4,2},{6,0},{1,7},{3,5},{5,3},{7,1},{8,14},{10,12},{12... | collective-permute-start | bytes 196616 | tf_op jit(solution)/shard_map/ppermute | solution.py:358
  94.2 4.7 %collective-permute-start.26 = (f32[64,256]{1,0:T(8,128)S(1)}, f32[64,256]{1,0:T(8,128)S(1)}, u32[]{:S(2)}, u32[]{:S(2)}) collective-permute-start(f32[64,256]{1,0:T(8,128)S(1)} %add_add_fusion.2), channel_id=1, source_target_pairs={{0,16},{8,24},{16,0},{24,8},{1,17},{9,25},{17,1},{25,9},{2,18},{10... | collective-permute-start | bytes 196616 | tf_op jit(solution)/shard_map/ppermute | solution.py:358
  94.9 3.9 %collective-permute-start.27 = (f32[64,256]{1,0:T(8,128)S(1)}, f32[64,256]{1,0:T(8,128)S(1)}, u32[]{:S(2)}, u32[]{:S(2)}) collective-permute-start(f32[64,256]{1,0:T(8,128)S(1)} %add_add_fusion.2), channel_id=1, source_target_pairs={{0,8},{8,0},{16,24},{24,16},{1,9},{9,1},{17,25},{25,17},{2,10},{10... | collective-permute-start | bytes 196616 | tf_op jit(solution)/shard_map/ppermute | solution.py:358
  95.8 4.3 %collective-permute-start.28 = (f32[64,256]{1,0:T(8,128)S(1)}, f32[64,256]{1,0:T(8,128)S(1)}, u32[]{:S(2)}, u32[]{:S(2)}) collective-permute-start(f32[64,256]{1,0:T(8,128)S(1)} %add_add_fusion.2), channel_id=1, source_target_pairs={{0,24},{8,16},{16,8},{24,0},{1,25},{9,17},{17,9},{25,1},{2,26},{10... | collective-permute-start | bytes 196616 | tf_op jit(solution)/shard_map/ppermute | solution.py:358
  100.5 8.9 %collective-permute-start.29 = (f32[64,512]{1,0:T(8,128)S(1)}, f32[64,512]{1,0:T(8,128)S(1)}, u32[]{:S(2)}, u32[]{:S(2)}) collective-permute-start(f32[64,512]{1,0:T(8,128)S(1)} %shard_map.113), channel_id=1, source_target_pairs={{0,64},{1,96},{64,0},{65,32},{32,65},{33,97},{96,1},{97,33},{2,66}... | collective-permute-start | bytes 393224 | tf_op jit(solution)/shard_map/ppermute | solution.py:494
  105.6 6.6 %collective-permute-start.30 = (f32[64,512]{1,0:T(8,128)S(1)}, f32[64,512]{1,0:T(8,128)S(1)}, u32[]{:S(2)}, u32[]{:S(2)}) collective-permute-start(f32[64,512]{1,0:T(8,128)S(1)} %shard_map.113), channel_id=1, source_target_pairs={{0,96},{1,64},{64,32},{65,0},{32,97},{33,65},{96,33},{97,1},{2,98}... | collective-permute-start | bytes 393224 | tf_op jit(solution)/shard_map/ppermute | solution.py:494
  105.6 6.6 %collective-permute-start.31 = (f32[64,512]{1,0:T(8,128)S(1)}, f32[64,512]{1,0:T(8,128)S(1)}, u32[]{:S(2)}, u32[]{:S(2)}) collective-permute-start(f32[64,512]{1,0:T(8,128)S(1)} %shard_map.113), channel_id=1, source_target_pairs={{0,32},{1,0},{64,96},{65,64},{32,33},{33,1},{96,97},{97,65},{2,34}... | collective-permute-start | bytes 393224 | tf_op jit(solution)/shard_map/ppermute | solution.py:494
  106.3 6.6 %collective-permute-start.32 = (f32[64,512]{1,0:T(8,128)S(1)}, f32[64,512]{1,0:T(8,128)S(1)}, u32[]{:S(2)}, u32[]{:S(2)}) collective-permute-start(f32[64,512]{1,0:T(8,128)S(1)} %shard_map.113), channel_id=1, source_target_pairs={{0,0},{1,32},{64,64},{65,96},{32,1},{33,33},{96,65},{97,97},{2,2},... | collective-permute-start | bytes 393224 | tf_op jit(solution)/shard_map/ppermute | solution.py:494
  (3 other events, 24.0 us)
